TPU v7x, 128 devices: a whole 4x4x4 slice. The times are simulated.
128 devices in a mesh: space: 16 (over y, x), band: 8 (over z, core).
Axes of the slice: x: 4, y: 4, z: 4, core: 2. Of those that a mesh axis runs over, the one named last changes fastest.
Arguments:
- vectors: float32 [65536, 1024], P('space', 'band')
- blocks: float32 [256, 7, 256, 256], P('space'), may hold values from -0.125 to 0.125
- neighbours: int32 [256, 7], P('space'), may hold values from 0 to 255, as said below
Outputs:
- rotated: float32 [65536, 1024], P('space', 'band')
Inputs may be any that keep to these rules, and one draw needn't show every extreme that they name: neighbours[e, k] lies within 2 places of e in the cyclic order of the elements; for every e, neighbours[e, 1] = e - 2 and neighbours[e, 2] = e + 2, taken modulo 256.
All inputs are finite; a program needn't handle non-finite values.
Results may differ from a plain program's by a relative error of at most 0.000098.
Values sent between devices are 32-bit elements; how exact they have to be, the bound alone decides.
No kernel may reach another device: no remote copies, remote signals or barrier semaphores. Data moves between devices by JAX's collectives and lax.ppermute only.
A program may use at most 128 MiB of HBM per device.

v0:
```python
import jax
import jax.numpy as jnp
from jax import lax
from jax.sharding import PartitionSpec as P

VECTORS = 1024
REACH = 2


def padded_2(x, sides, width):
    for axis, dim in sides:
        size, length = (lax.axis_size(axis), x.shape[dim])
        up = [(i, (i + 1) % size) for i in range(size)]
        down = [(j, i) for i, j in up]
        last = lax.slice_in_dim(x, length - width, length, axis=dim)
        first = lax.slice_in_dim(x, 0, width, axis=dim)
        before = lax.ppermute(last, axis, up)
        after = lax.ppermute(first, axis, down)
        x = jnp.concatenate([before, x, after], axis=dim)
    return x


def per_device(vectors, blocks, neighbours):
    elem_dev = blocks.shape[0]
    basis = blocks.shape[2]
    panel = vectors.shape[1]
    space_count = lax.axis_size("space")
    total_elements = elem_dev * space_count
    order = total_elements * basis
    first_id = lax.axis_index("space") * elem_dev
    local_ids = jnp.arange(elem_dev, dtype=jnp.int32)
    global_ids = first_id + local_ids
    offsets = (neighbours - global_ids[:, None] + REACH + total_elements) % total_elements - REACH
    slots = local_ids[:, None] + REACH + offsets

    def apply_operator(field):
        padded = padded_2(field, (("space", 0),), REACH * basis)
        padded = padded.reshape(elem_dev + 2 * REACH, basis, panel)
        picked = padded[slots]
        result = jnp.einsum("lkij,lkjm->lim", blocks, picked, precision=lax.Precision.HIGHEST)
        return result.reshape(elem_dev * basis, panel)

    first_step = (apply_operator(vectors) - 0.5 * vectors) / 1.5
    filtered = 2.0 * (apply_operator(first_step) - 0.5 * first_step) / 1.5 - vectors
    identity = jnp.eye(VECTORS, dtype=jnp.float32)
    row_block = lax.all_to_all(filtered, "band", split_axis=0, concat_axis=1, tiled=True)
    local_gram = jnp.dot(
        row_block.T, row_block, precision=lax.Precision.HIGHEST, preferred_element_type=jnp.float32
    )
    gram = lax.psum(local_gram, ("space", "band"))
    scale = jnp.trace(gram) / VECTORS
    normed = gram / scale
    squared = jnp.dot(
        normed, normed, precision=lax.Precision.HIGHEST, preferred_element_type=jnp.float32
    )
    poly = (15.0 * identity - 10.0 * normed + 3.0 * squared) / 8.0
    turned = jnp.dot(
        row_block, poly, precision=lax.Precision.HIGHEST, preferred_element_type=jnp.float32
    )
    turned = turned * jnp.sqrt(order / scale)
    return lax.all_to_all(turned, "band", split_axis=1, concat_axis=0, tiled=True)


def solution(mesh):
    return jax.shard_map(
        per_device,
        mesh=mesh,
        in_specs=(P("space", "band"), P("space", None, None, None), P("space", None)),
        out_specs=P("space", "band"),
        check_vma=False,
    )
```

profile of v0, /device:TPU:1, one launch (start us, length us, event | category | flops | bytes accessed | tf_op | source)
XLA Modules:
  0.0 394.7 jit_solution(10194306985631248399)
XLA Ops:
  6.5 1.1 fusion.27
  7.6 2.1 collective-permute-start
  9.7 3.8 collective-permute-start.1
  14.4 5.0 %collective-permute-done = f32[512,128]{1,0:T(8,128)S(1)} collective-permute-done((f32[512,128]{1,0:T(8,128)S(1)}, f32[512,128]{1,0:T(8,128)S(1)}, u32[]{:S(2)}, u32[]{:S(2)}) %collective-permute-start) | collective-permute-done | bytes 262176 | tf_op jit(solution)/shard_map/ppermute | solution.py:17
  19.4 1.8 pad_maximum_fusion
  21.2 6.7 %gather_fusion = f32[112,256,128]{2,1,0:T(8,128)} fusion(f32[20,256,128]{2,1,0:T(8,128)S(1)} %bitcast.48, s32[1024]{0:T(1024)S(1)} %pad_clamp_fusion), kind=kCustom, calls=%fused_computation | custom fusion | bytes 29360576 | tf_op jit(solution)/shard_map/gather | solution.py:39
  27.9 35.9 %convolution_bitcast_fusion.1 = f32[16,256,128]{1,2,0:T(8,128)} fusion(f32[16,7,256,128]{3,2,1,0:T(8,128)} %bitcast.50, f32[16,7,256,256]{3,2,1,0:T(8,128)} %param.4), kind=kOutput, calls=%fused_computation.28 | convolution fusion | flops 11274289152 | bytes 46137344 | tf_op jit(solution)/shard_map/lkij,lkjm->lim/dot_general | solution.py:40
  63.8 3.0 copy.17
  66.8 1.9 fusion.14
  68.8 4.9 %collective-permute-start.3 = (f32[512,128]{1,0:T(8,128)S(1)}, f32[512,128]{1,0:T(8,128)S(1)}, u32[]{:S(2)}, u32[]{:S(2)}) collective-permute-start(f32[512,128]{1,0:T(8,128)S(1)} %get-tuple-element.6), channel_id=1, source_target_pairs={{8,0},{16,8},{24,16},{32,24},{40,32},{48,40},{56,48},{64,56},{72,6... | collective-permute-start | bytes 786440 | tf_op jit(solution)/shard_map/ppermute | solution.py:18
  73.7 5.0 %collective-permute-done.2 = f32[512,128]{1,0:T(8,128)S(1)} collective-permute-done((f32[512,128]{1,0:T(8,128)S(1)}, f32[512,128]{1,0:T(8,128)S(1)}, u32[]{:S(2)}, u32[]{:S(2)}) %collective-permute-start.2) | collective-permute-done | bytes 262176 | tf_op jit(solution)/shard_map/ppermute | solution.py:17
  78.9 6.7 %gather_fusion.1 = f32[112,256,128]{2,1,0:T(8,128)} fusion(f32[20,256,128]{2,1,0:T(8,128)S(1)} %bitcast.47, s32[1024]{0:T(1024)S(1)} %pad_clamp_fusion), kind=kCustom, calls=%fused_computation.1 | custom fusion | bytes 29360576 | tf_op jit(solution)/shard_map/gather | solution.py:39
  85.6 35.9 %convolution_bitcast_fusion = f32[16,256,128]{1,2,0:T(8,128)} fusion(f32[16,7,256,128]{3,2,1,0:T(8,128)} %bitcast.49, f32[16,7,256,256]{3,2,1,0:T(8,128)} %param.4), kind=kOutput, calls=%fused_computation.27 | convolution fusion | flops 11274289152 | bytes 46137344 | tf_op jit(solution)/shard_map/lkij,lkjm->lim/dot_general | solution.py:40
  121.5 3.1 copy.19
  124.6 4.0 %fusion.8 = f32[4096,128]{1,0:T(8,128)} fusion(f32[4096,128]{1,0:T(8,128)S(1)} %copy-done.1, f32[16,256,128]{2,1,0:T(8,128)} %copy.19, f32[16,256,128]{2,1,0:T(8,128)} %copy.17), kind=kLoop, calls=%fused_computation.16 | loop fusion | flops 3145728 | bytes 8388608 | tf_op jit(solution)/shard_map/sub | solution.py:44
  128.5 2.9 copy.20
  131.4 33.7 %all_to_all.38 = f32[8,512,128]{1,2,0:T(8,128)S(1)} all-to-all(f32[8,512,128]{1,2,0:T(8,128)} %copy.20), channel_id=1, replica_groups=mesh['space'=16,'band'=8] {'band'}, dimensions={0} | all-to-all | bytes 4194304 | tf_op jit(solution)/shard_map/all_to_all | solution.py:46
  165.2 8.3 %fusion.28 = f32[1024,1024]{1,0:T(8,128)} fusion(f32[512,1024]{0,1:T(8,128)S(1)} %bitcast.51), kind=kOutput, calls=%fused_computation.46 | convolution fusion | flops 6442450944 | bytes 6291456 | tf_op jit(solution)/shard_map/dot_general | solution.py:47
  173.5 153.9 %all-reduce.2.cloned.1.call-done = f32[1024,1024]{1,0:T(8,128)} async-done(((f32[1024,1024]{1,0:T(8,128)}), f32[1024,1024]{1,0:T(8,128)}) %all-reduce.2.cloned.1.call-update) | async-done | bytes 4194320 | tf_op jit(solution)/shard_map/psum | solution.py:50
  327.4 2.9 select_reduce_fusion
  331.1 17.4 %fusion.15 = f32[1024,1024]{1,0:T(8,128)S(1)} fusion(f32[1024,1024]{1,0:T(8,128)} %all-reduce.2.cloned.1.call-done, f32[]{:T(128)S(6)} %div.29), kind=kOutput, calls=%fused_computation.26 | convolution fusion | flops 12885950464 | bytes 8388612 | tf_op jit(solution)/shard_map/dot_general | solution.py:53
  348.5 7.2 %multiply_bitcast_fusion = f32[64,8,8,128]{3,2,1,0:T(8,128)S(1)} fusion(f32[512,1024]{0,1:T(8,128)S(1)} %bitcast.52, f32[1024,1024]{1,0:T(8,128)S(1)} %fusion.15, f32[1024,1024]{1,0:T(8,128)S(1)} %copy-done.2, f32[]{:T(128)S(6)} %div.29, f32[]{:T(128)S(6)} %sqrt.3), kind=kOutput, calls=%fused_computation.18 | convolution fusion | flops 6451363840 | bytes 12582920 | tf_op jit(solution)/shard_map/dot_general | solution.py:57
  355.9 30.2 %all_to_all.39 = f32[512,8,128]{2,0,1:T(8,128)S(1)} all-to-all(f32[512,8,128]{2,0,1:T(8,128)S(1)} %bitcast.53), channel_id=1, replica_groups=mesh['space'=16,'band'=8] {'band'}, dimensions={1} | all-to-all | bytes 4194304 | tf_op jit(solution)/shard_map/all_to_all | solution.py:61
  386.1 1.3 copy.29
  (19 shorter events, 1.3 us)
Async XLA Ops:
  6.5 320.9 %all-reduce.2.cloned.1.call-start = ((), (), s32[]{:S(2)}) async-start(), calls=%async_computation.2 | async-start | bytes 8388608 | tf_op jit(solution)/shard_map/psum | solution.py:50
  7.6 11.8 %collective-permute-start = (f32[512,128]{1,0:T(8,128)S(1)}, f32[512,128]{1,0:T(8,128)S(1)}, u32[]{:S(2)}, u32[]{:S(2)}) collective-permute-start(f32[512,128]{1,0:T(8,128)S(1)} %get-tuple-element.7), channel_id=1, source_target_pairs={{0,8},{8,16},{16,24},{24,32},{32,40},{40,48},{48,56},{56,64},{64,7... | collective-permute-start | bytes 786440 | tf_op jit(solution)/shard_map/ppermute | solution.py:17
  9.7 9.7 %collective-permute-start.1 = (f32[512,128]{1,0:T(8,128)S(1)}, f32[512,128]{1,0:T(8,128)S(1)}, u32[]{:S(2)}, u32[]{:S(2)}) collective-permute-start(f32[512,128]{1,0:T(8,128)S(1)} %get-tuple-element.8), channel_id=1, source_target_pairs={{8,0},{16,8},{24,16},{32,24},{40,32},{48,40},{56,48},{64,56},{72,6... | collective-permute-start | bytes 786440 | tf_op jit(solution)/shard_map/ppermute | solution.py:18
  63.8 3.0 copy-start
  68.7 10.0 %collective-permute-start.2 = (f32[512,128]{1,0:T(8,128)S(1)}, f32[512,128]{1,0:T(8,128)S(1)}, u32[]{:S(2)}, u32[]{:S(2)}) collective-permute-start(f32[512,128]{1,0:T(8,128)S(1)} %get-tuple-element.5), channel_id=1, source_target_pairs={{0,8},{8,16},{16,24},{24,32},{32,40},{40,48},{48,56},{56,64},{64,7... | collective-permute-start | bytes 786440 | tf_op jit(solution)/shard_map/ppermute | solution.py:17
  68.8 9.9 %collective-permute-start.3 = (f32[512,128]{1,0:T(8,128)S(1)}, f32[512,128]{1,0:T(8,128)S(1)}, u32[]{:S(2)}, u32[]{:S(2)}) collective-permute-start(f32[512,128]{1,0:T(8,128)S(1)} %get-tuple-element.6), channel_id=1, source_target_pairs={{8,0},{16,8},{24,16},{32,24},{40,32},{48,40},{56,48},{64,56},{72,6... | collective-permute-start | bytes 786440 | tf_op jit(solution)/shard_map/ppermute | solution.py:18
  121.5 3.1 copy-start.1
  331.1 17.4 %copy-start.2 = (f32[1024,1024]{1,0:T(8,128)S(1)}, f32[1024,1024]{1,0:T(8,128)}, u32[]{:S(2)}) copy-start(f32[1024,1024]{1,0:T(8,128)} %all-reduce.2.cloned.1.call-done) | copy-start | bytes 12582916
Sparse Core Ops, SparseCore 0:
  173.6 153.7 all-reduce.1
where the time goes:
time: 402 us; the launch traced here: 395 us
  waiting for transfers between devices  164 us (41%)
  matrix products  105 us (26%)
  blocking collectives  63.9 us (16%)
  local copies, waits for them, and re-layouts  25.2 us (6%)
  between operations  14.7 us (4%)
  other arithmetic  11.4 us (3%)
  starting transfers between devices  10.9 us (3%)
    psum x1, waiting for transfers between devices, per_device(): gram = lax.psum(local_gram, ('space', 'band'))  154 us
    dot_general x2, matrix products, apply_operator(): jnp.einsum('lkij,lkjm->lim', blocks, picked, precision=lax.Precision.HIGH...  71.8 us
    all_to_all x1, blocking collectives, per_device(): lax.all_to_all(filtered, 'band', split_axis=0, concat_axis=1, tiled=True)  33.7 us
    all_to_all x1, blocking collectives, per_device(): lax.all_to_all(turned, 'band', split_axis=1, concat_axis=0, tiled=True)  30.2 us
    dot_general x1, matrix products, per_device(): jnp.dot(normed, normed, precision=lax.Precision.HIGHEST, preferred_elemen...  17.4 us
    gather x2, local copies, waits for them, and re-layouts, apply_operator(): picked = padded[slots]  13.4 us
    ppermute x2, waiting for transfers between devices, padded_2(): before = lax.ppermute(last, axis, up)  9.99 us
    ppermute x2, starting transfers between devices, padded_2(): after = lax.ppermute(first, axis, down)  8.72 us
  transfers between devices with their start and end apart: 5, of which 3 were waited for; matrix products, arithmetic and copies ran while one was open for 0% of the time, Pallas kernels for 0%

commit v1 on v0

v1 whole, which is shorter than its diff:
```python
import functools
import jax
import jax.numpy as jnp
from jax import lax
from jax.experimental import pallas as pl
from jax.experimental.pallas import tpu as pltpu
from jax.sharding import PartitionSpec as P

VECTORS = 1024
REACH = 2
TILE = 256
PAIRS = [(i, j) for i in range(4) for j in range(i, 4)]
F32 = jnp.float32
BF16 = jnp.bfloat16


def split(x):
    hi = x.astype(BF16)
    lo = (x - hi.astype(F32)).astype(BF16)
    return hi, lo


def dot(a, b):
    return jnp.dot(a, b, preferred_element_type=F32)


def operator_kernel(step_kind, edge, elem_dev, slots_ref, blocks_ref, *refs):
    refs = list(refs)
    own_ref = refs.pop(0)
    before_ref = refs.pop(0) if edge else None
    after_ref = refs.pop(0) if edge else None
    base_ref = refs.pop(0) if step_kind == 2 else None
    if edge:
        refs.pop(0)
    out_ref, wide_ref = refs
    step = pl.program_id(0)

    def put(slot, value):
        hi, lo = split(value)
        wide_ref[slot, :, 0:128] = hi
        wide_ref[slot, :, 128:256] = lo

    @pl.when(step == 0)
    def _():
        if edge:
            for r in range(REACH):
                put(r, before_ref[r])
                put(REACH + elem_dev + r, after_ref[r])
            for r in range(2 * REACH):
                put(REACH + r, own_ref[r])
                put(elem_dev - REACH + r, own_ref[elem_dev - 2 * REACH + r])
        else:
            for r in range(elem_dev):
                put(REACH + r, own_ref[r])

    elem = element_of(step, edge, elem_dev)
    highs, lows, wides = [], [], []
    for k in range(7):
        hi, lo = split(blocks_ref[0, k])
        highs.append(hi)
        lows.append(lo)
        wides.append(wide_ref[slots_ref[elem * 7 + k]])
    left = jnp.concatenate(
        [jnp.concatenate(highs, axis=1), jnp.concatenate(lows, axis=1)], axis=0
    )
    prod = dot(left, jnp.concatenate(wides, axis=0))
    total = (prod[256:, 128:] + prod[256:, :128]) + (prod[:256, 128:] + prod[:256, :128])
    own = own_ref[elem]
    if step_kind == 1:
        out_ref[0] = (total - 0.5 * own) / 1.5
    else:
        out_ref[0] = 2.0 * (total - 0.5 * own) / 1.5 - base_ref[0]


def element_of(step, edge, elem_dev):
    if edge:
        return step + jnp.where(step >= REACH, elem_dev - 2 * REACH, 0)
    return step + REACH


def apply_operator(step_kind, edge, slots, blocks, own, halos=(), base=None, into=None):
    elem_dev = own.shape[0]
    count = 2 * REACH if edge else elem_dev - 2 * REACH
    pick = lambda s, *_: element_of(s, edge, elem_dev)
    panel_spec = pl.BlockSpec((1, 256, 128), lambda s, *_: (pick(s), 0, 0))
    whole = lambda x: pl.BlockSpec(x.shape, lambda s, *_: (0, 0, 0), pipeline_mode=pl.Buffered(1))
    args = [slots, blocks, own]
    specs = [
        pl.BlockSpec((1, 7, 256, 256), lambda s, *_: (pick(s), 0, 0, 0)),
        whole(own),
    ]
    if edge:
        args += list(halos)
        specs += [whole(h) for h in halos]
    if step_kind == 2:
        args.append(base)
        specs.append(panel_spec)
    aliases = {}
    if edge:
        aliases = {len(args): 0}
        args.append(into)
        specs.append(pl.BlockSpec(memory_space=pl.ANY))
    return pl.pallas_call(
        functools.partial(operator_kernel, step_kind, edge, elem_dev),
        out_shape=jax.ShapeDtypeStruct(own.shape, F32),
        grid_spec=pltpu.PrefetchScalarGridSpec(
            num_scalar_prefetch=1,
            grid=(count,),
            in_specs=specs,
            out_specs=panel_spec,
            scratch_shapes=[pltpu.VMEM((elem_dev + 2 * REACH, 256, 256), BF16)],
        ),
        input_output_aliases=aliases,
        compiler_params=pltpu.CompilerParams(vmem_limit_bytes=40 << 20),
        name=f"operator{step_kind}{'edge' if edge else 'mid'}",
    )(*args)


def gram_kernel(core_ref, rows_ref, keep_ref, send_ref, hi_ref, lo_ref):
    for b in range(8):
        hi, lo = split(rows_ref[b])
        hi_ref[:, b * 128 : (b + 1) * 128] = hi
        lo_ref[:, b * 128 : (b + 1) * 128] = lo
    core = core_ref[0]
    for n, (i, j) in enumerate(PAIRS):
        a, b = slice(i * TILE, (i + 1) * TILE), slice(j * TILE, (j + 1) * TILE)
        left = jnp.concatenate([hi_ref[:, a], hi_ref[:, a], lo_ref[:, a]], axis=0)
        right = jnp.concatenate([hi_ref[:, b], lo_ref[:, b], hi_ref[:, b]], axis=0)
        block = lax.dot_general(left, right, (((0,), (0,)), ((), ())), preferred_element_type=F32)
        half, at = n // 5, 2 * (n % 5)
        for target, wanted in ((keep_ref, half), (send_ref, 1 - half)):

            @pl.when(core == wanted)
            def _():
                target[at] = block[:, :128]
                target[at + 1] = block[:, 128:]


def local_gram(core, rows):
    half = jax.ShapeDtypeStruct((10, 256, 128), F32)
    vmem = pl.BlockSpec(memory_space=pltpu.VMEM)
    return pl.pallas_call(
        gram_kernel,
        out_shape=(half, half),
        in_specs=[pl.BlockSpec(memory_space=pltpu.SMEM), vmem],
        out_specs=(vmem, vmem),
        scratch_shapes=[pltpu.VMEM((512, 1024), BF16), pltpu.VMEM((512, 1024), BF16)],
        compiler_params=pltpu.CompilerParams(vmem_limit_bytes=40 << 20),
        name="gram",
    )(core, rows)


def turn_kernel(order, core_ref, mine_ref, theirs_ref, rows_ref, out_ref, nh_ref, nl_ref, fh_ref, fl_ref, y_ref):
    first = core_ref[0] == 0
    row = lax.broadcasted_iota(jnp.int32, (256, 128), 0)
    col = lax.broadcasted_iota(jnp.int32, (256, 128), 1)

    def packed(n, h):
        half, at = n // 5, 2 * (n % 5) + h
        here = first if half == 0 else jnp.logical_not(first)
        return jnp.where(here, mine_ref[at], theirs_ref[at])

    diag = jnp.zeros((256, 128), F32)
    for n, (i, j) in enumerate(PAIRS):
        if i == j:
            for h in range(2):
                diag += jnp.where(row == col + 128 * h, packed(n, h), 0.0)
    scale = jnp.sum(diag) / VECTORS
    for n, (i, j) in enumerate(PAIRS):
        for h in range(2):
            hi, lo = split(packed(n, h) / scale)
            c = j * TILE + h * 128
            nh_ref[i * TILE : (i + 1) * TILE, c : c + 128] = hi
            nl_ref[i * TILE : (i + 1) * TILE, c : c + 128] = lo
            if i != j:
                nh_ref[c : c + 128, i * TILE : (i + 1) * TILE] = hi.T
                nl_ref[c : c + 128, i * TILE : (i + 1) * TILE] = lo.T

    def times_normed(hi, lo, j):
        cols = slice(j * TILE, (j + 1) * TILE)
        left = jnp.concatenate([hi, hi, lo], axis=1)
        right = jnp.concatenate([nh_ref[:, cols], nl_ref[:, cols], nh_ref[:, cols]], axis=0)
        return dot(left, right)

    for b in range(8):
        hi, lo = split(rows_ref[b])
        fh_ref[:, b * 128 : (b + 1) * 128] = hi
        fl_ref[:, b * 128 : (b + 1) * 128] = lo
    for j in range(4):
        y_ref[:, j * TILE : (j + 1) * TILE] = times_normed(fh_ref[...], fl_ref[...], j)
    for b in range(8):
        cols = slice(b * 128, (b + 1) * 128)
        hi, lo = split(3.0 * y_ref[:, cols] - 10.0 * rows_ref[b])
        fh_ref[:, cols] = hi
        fl_ref[:, cols] = lo
    stretch = jnp.sqrt(jnp.full((8, 128), order, F32) / scale)[0:1]
    for j in range(4):
        z = times_normed(fh_ref[...], fl_ref[...], j)
        for h in range(2):
            b = 2 * j + h
            out_ref[b] = (15.0 * rows_ref[b] + z[:, h * 128 : (h + 1) * 128]) / 8.0 * stretch


def turn(core, mine, theirs, rows, order):
    vmem = pl.BlockSpec(memory_space=pltpu.VMEM)
    return pl.pallas_call(
        functools.partial(turn_kernel, order),
        out_shape=jax.ShapeDtypeStruct(rows.shape, F32),
        in_specs=[pl.BlockSpec(memory_space=pltpu.SMEM), vmem, vmem, vmem],
        out_specs=vmem,
        scratch_shapes=[
            pltpu.VMEM((1024, 1024), BF16),
            pltpu.VMEM((1024, 1024), BF16),
            pltpu.VMEM((512, 1024), BF16),
            pltpu.VMEM((512, 1024), BF16),
            pltpu.VMEM((512, 1024), F32),
        ],
        compiler_params=pltpu.CompilerParams(vmem_limit_bytes=40 << 20),
        name="turn",
    )(core, mine, theirs, rows)


def halos_of(first, last):
    size = lax.axis_size("space")
    up = [(i, (i + 1) % size) for i in range(size)]
    down = [(j, i) for i, j in up]
    return lax.ppermute(last, "space", up), lax.ppermute(first, "space", down)


def per_device(vectors, blocks, neighbours):
    elem_dev, basis = blocks.shape[0], blocks.shape[2]
    panel = vectors.shape[1]
    space_count, band_count = lax.axis_size("space"), lax.axis_size("band")
    total_elements = elem_dev * space_count
    local_ids = jnp.arange(elem_dev, dtype=jnp.int32)
    global_ids = lax.axis_index("space") * elem_dev + local_ids
    offsets = (neighbours - global_ids[:, None] + REACH + total_elements) % total_elements
    slots = (local_ids[:, None] + offsets).reshape(-1)

    start = vectors.reshape(elem_dev, basis, panel)
    halos = halos_of(start[:REACH], start[-REACH:])
    step = apply_operator(1, False, slots, blocks, start)
    step = apply_operator(1, True, slots, blocks, start, halos, into=step)
    halos = halos_of(step[:REACH], step[-REACH:])
    field = apply_operator(2, False, slots, blocks, step, base=start)
    field = apply_operator(2, True, slots, blocks, step, halos, base=start, into=field)

    share = elem_dev * basis // band_count
    rows = lax.all_to_all(field.reshape(band_count, share, panel), "band", split_axis=0, concat_axis=0, tiled=True)

    core = lax.axis_index("band") % 2
    core_arr = core.reshape(1)
    swap = [(i, i ^ 1) for i in range(band_count)]
    both = ("space", "band")
    groups = [[d for d in range(space_count * band_count) if d % 2 == c] for c in range(2)]
    peers = len(groups[0])
    keep, send = local_gram(core_arr, rows)
    half = keep + lax.ppermute(send, "band", swap)
    pieces = half.reshape(peers, -1, panel)
    pieces = lax.all_to_all(pieces, both, split_axis=0, concat_axis=0, axis_index_groups=groups, tiled=True)
    mine = jnp.sum(pieces, axis=0)
    copies = jnp.broadcast_to(mine[None], pieces.shape)
    copies = lax.all_to_all(copies, both, split_axis=0, concat_axis=0, axis_index_groups=groups, tiled=True)
    mine = copies.reshape(half.shape)
    theirs = lax.ppermute(mine, "band", swap)

    turned = turn(core_arr, mine, theirs, rows, float(total_elements * basis))
    turned = lax.all_to_all(turned, "band", split_axis=0, concat_axis=0, tiled=True)
    return turned.reshape(elem_dev * basis, panel)


def solution(mesh):
    return jax.shard_map(
        per_device,
        mesh=mesh,
        in_specs=(P("space", "band"), P("space", None, None, None), P("space", None)),
        out_specs=P("space", "band"),
        check_vma=False,
    )
```

time: 402 us -> 195 us (0.49); the launches traced: 395 us -> 194 us
  waiting for transfers between devices: 164 us -> 31.5 us
  matrix products: 105 us -> 0 us
  Pallas kernels: 0 us -> 58 us
  local copies, waits for them, and re-layouts: 25.2 us -> 4.27 us
  blocking collectives: 63.9 us -> 81 us
  between operations: 14.7 us -> 0.09 us
  other arithmetic: 11.4 us -> 0.95 us
  starting transfers between devices: 10.9 us -> 18.5 us
    psum x1 -> x0, waiting for transfers between devices: 154 us -> none  [per_device(): gram = lax.psum(local_gram, ('space', 'band'))]
    dot_general x5 -> x0, matrix products: 105 us -> none  [the longest x2 71.8 us: apply_operator(): jnp.einsum('lkij,lkjm->lim', blocks, picked, precision=lax.Precision.HIGH...]
    pallas_call x0 -> x6, Pallas kernels: none -> 58 us  [the longest x4 44 us: apply_operator(): pl.pallas_call(functools.partial(operator_kernel, step_kind, edge, elem_d...]
    all_to_all x0 -> x1, waiting for transfers between devices: none -> 26.2 us  [per_device(): lax.all_to_all(field.reshape(band_count, share, panel), 'band', split_axi...]
    all_to_all x2 -> x3, blocking collectives: 63.9 us -> 81 us  [the longest x1 29 us: per_device(): lax.all_to_all(turned, 'band', split_axis=0, concat_axis=0, tiled=True)]
    gather x2 -> x0, local copies, waits for them, and re-layouts: 13.4 us -> none  [apply_operator(): picked = padded[slots]]
    all_to_all x0 -> x1, starting transfers between devices: none -> 6.88 us  [per_device(): lax.all_to_all(field.reshape(band_count, share, panel), 'band', split_axi...]
    dot_general x2 -> x0, local copies, waits for them, and re-layouts: 6.11 us -> none  [apply_operator(): jnp.einsum('lkij,lkjm->lim', blocks, picked, precision=lax.Precision.HIGH...]
  transfers between devices with their start and end apart: 5 -> 7, of which waited for: 3 -> 3; matrix products, arithmetic and copies ran while one was open for 0% -> 0% of each run, Pallas kernels for 0% -> 16%
where the time goes in v1:
time: 195 us; the launch traced here: 194 us
  blocking collectives  81 us (42%)
  Pallas kernels  58 us (30%)
  waiting for transfers between devices  31.5 us (16%)
  starting transfers between devices  18.5 us (9%)
  local copies, waits for them, and re-layouts  4.27 us (2%)
    pallas_call x4, Pallas kernels, apply_operator(): pl.pallas_call(functools.partial(operator_kernel, step_kind, edge, elem_d...  44 us
    all_to_all x1, blocking collectives, per_device(): lax.all_to_all(turned, 'band', split_axis=0, concat_axis=0, tiled=True)  29 us
    all_to_all x1, blocking collectives, per_device(): lax.all_to_all(pieces, both, split_axis=0, concat_axis=0, axis_index_grou...  27.8 us
    all_to_all x1, waiting for transfers between devices, per_device(): lax.all_to_all(field.reshape(band_count, share, panel), 'band', split_axi...  26.2 us
    all_to_all x1, blocking collectives, per_device(): lax.all_to_all(copies, both, split_axis=0, concat_axis=0, axis_index_grou...  24.2 us
    pallas_call x1, Pallas kernels, turn(): pl.pallas_call(functools.partial(turn_kernel, order), out_shape=jax.Shape...  7.56 us
    ppermute x4, starting transfers between devices, halos_of(): return (lax.ppermute(last, 'space', up), lax.ppermute(first, 'space', down))  7.43 us
    all_to_all x1, starting transfers between devices, per_device(): lax.all_to_all(field.reshape(band_count, share, panel), 'band', split_axi...  6.88 us
  transfers between devices with their start and end apart: 7, of which 3 were waited for; matrix products, arithmetic and copies ran while one was open for 0% of the time, Pallas kernels for 16%

profile of v1, /device:TPU:1, one launch (start us, length us, event | category | flops | bytes accessed | tf_op | source)
XLA Modules:
  0.0 194.4 jit_solution(10860222462795479262)
XLA Ops:
  0.0 1.1 fusion.3
  1.1 2.1 %collective-permute-start = (f32[2,256,128]{2,1,0:T(8,128)S(1)}, f32[2,256,128]{2,1,0:T(8,128)S(1)}, u32[]{:S(2)}, u32[]{:S(2)}) collective-permute-start(f32[2,256,128]{2,1,0:T(8,128)S(1)} %bitcast.17), channel_id=1, source_target_pairs={{0,8},{8,16},{16,24},{24,32},{32,40},{40,48},{48,56},{56,64},{64,7... | collective-permute-start | bytes 786440 | tf_op jit(solution)/shard_map/ppermute | solution.py:227
  3.2 3.8 %collective-permute-start.1 = (f32[2,256,128]{2,1,0:T(8,128)S(1)}, f32[2,256,128]{2,1,0:T(8,128)S(1)}, u32[]{:S(2)}, u32[]{:S(2)}) collective-permute-start(f32[2,256,128]{2,1,0:T(8,128)S(1)} %bitcast.16), channel_id=1, source_target_pairs={{8,0},{16,8},{24,16},{32,24},{40,32},{48,40},{56,48},{64,56},{72,6... | collective-permute-start | bytes 786440 | tf_op jit(solution)/shard_map/ppermute | solution.py:227
  7.0 0.7 fusion.1
  7.9 1.6 copy-done
  9.4 15.2 %operator1mid.1.refs_3_ = f32[16,256,128]{2,1,0:T(8,128)S(1)} custom-call(s32[112]{0:T(128)S(1)} %reshape.29.slots_ref, f32[16,7,256,256]{3,2,1,0:T(8,128)} %blocks_ref.7, f32[16,256,128]{2,1,0:T(8,128)S(1)} %bitcast.8), custom_call_target="tpu_custom_call" | custom-call | tf_op jit(solution)/shard_map/operator1mid/pallas_call | solution.py:103
  24.7 6.0 %operator1edge.1.refs_0_ = f32[16,256,128]{2,1,0:T(8,128)S(1)} custom-call(s32[112]{0:T(128)S(1)} %reshape.29.slots_ref, f32[16,7,256,256]{3,2,1,0:T(8,128)} %blocks_ref.7, f32[16,256,128]{2,1,0:T(8,128)S(1)} %bitcast.9, f32[2,256,128]{2,1,0:T(8,128)S(1)} %collective-permute-done.refs_1_, ...), custom_call_target="tpu_custom_call", output_to_operand_aliasing={{}: (5, {})} | custom-call | tf_op jit(solution)/shard_map/operator1edge/pallas_call | solution.py:103
  30.7 1.5 collective-permute-start.3
  32.2 16.1 %operator2mid.1.refs_4_ = f32[16,256,128]{2,1,0:T(8,128)} custom-call(s32[112]{0:T(128)S(1)} %reshape.29.slots_ref, f32[16,7,256,256]{3,2,1,0:T(8,128)} %blocks_ref.7, f32[16,256,128]{2,1,0:T(8,128)S(1)} %operator1edge.1.refs_0_, f32[16,256,128]{2,1,0:T(8,128)S(1)} %bitcast.10), custom_call_target="tpu_custom_call" | custom-call | tf_op jit(solution)/shard_map/operator2mid/pallas_call | solution.py:103
  48.4 6.7 %operator2edge.1 = f32[16,256,128]{2,1,0:T(8,128)} custom-call(s32[112]{0:T(128)S(1)} %reshape.29.slots_ref, f32[16,7,256,256]{3,2,1,0:T(8,128)} %blocks_ref.7, f32[16,256,128]{2,1,0:T(8,128)S(1)} %operator1edge.1.refs_0_, f32[2,256,128]{2,1,0:T(8,128)S(1)} %collective-permute-done.2.refs_1_, ...), custom_call_target="tpu_custom_call", output_to_operand_aliasing={{}: (6, {})} | custom-call | tf_op jit(solution)/shard_map/operator2edge/pallas_call | solution.py:103
  55.0 6.9 %all-to-all-start = ((f32[8,512,128]{2,1,0:T(8,128)}), f32[8,512,128]{2,1,0:T(8,128)S(1)}, u32[]{:S(2)}, u32[]{:S(2)}) async-start(f32[8,512,128]{2,1,0:T(8,128)} %bitcast.4), calls=%async_computation | async-start | bytes 4194304 | tf_op jit(solution)/shard_map/all_to_all | solution.py:249
  61.9 26.2 %all-to-all-done.rows_ref = f32[8,512,128]{2,1,0:T(8,128)S(1)} async-done(((f32[8,512,128]{2,1,0:T(8,128)}), f32[8,512,128]{2,1,0:T(8,128)S(1)}, u32[]{:S(2)}, u32[]{:S(2)}) %all-to-all-start) | async-done | bytes 2097184 | tf_op jit(solution)/shard_map/all_to_all | solution.py:249
  88.1 6.5 %gram.1 = (f32[10,256,128]{2,1,0:T(8,128)S(1)}, f32[10,256,128]{2,1,0:T(8,128)S(1)}) custom-call(s32[1]{0:T(128)} %bitcast.core_ref, f32[8,512,128]{2,1,0:T(8,128)S(1)} %all-to-all-done.rows_ref), custom_call_target="tpu_custom_call" | custom-call | tf_op jit(solution)/shard_map/gram/pallas_call | solution.py:142
  94.6 1.1 collective-permute-start.4
  95.7 2.7 %collective-permute-done.4 = f32[10,256,128]{2,1,0:T(8,128)S(1)} collective-permute-done((f32[10,256,128]{2,1,0:T(8,128)S(1)}, f32[10,256,128]{2,1,0:T(8,128)S(1)}, u32[]{:S(2)}, u32[]{:S(2)}) %collective-permute-start.4) | collective-permute-done | bytes 1310752 | tf_op jit(solution)/shard_map/ppermute | solution.py:258
  98.3 0.1 add.49
  98.5 27.8 %all_to_all.20 = f32[64,40,128]{2,1,0:T(8,128)S(1)} all-to-all(f32[64,40,128]{2,1,0:T(8,128)S(1)} %bitcast.15), channel_id=1, replica_groups={{0,2,4,6,8,10,12,14,16,18,20,22,24,26,28,30,32,34,36,38,40,42,44,46,48,..., dimensions={0} | all-to-all | bytes 2621440 | tf_op jit(solution)/shard_map/all_to_all | solution.py:260
  126.3 0.1 reduce_sum.9
  126.5 24.2 %all_to_all.21 = f32[64,40,128]{2,1,0:T(8,128)S(1)} all-to-all(f32[64,40,128]{2,1,0:T(8,128)S(1)} %broadcast_in_dim.2), channel_id=1, replica_groups={{0,2,4,6,8,10,12,14,16,18,20,22,24,26,28,30,32,34,36,38,40,42,44,46,48,..., dimensions={0} | all-to-all | bytes 2621440 | tf_op jit(solution)/shard_map/all_to_all | solution.py:263
  150.7 3.2 %collective-permute-start.5 = (f32[10,256,128]{2,1,0:T(8,128)S(1)}, f32[10,256,128]{2,1,0:T(8,128)S(1)}, u32[]{:S(2)}, u32[]{:S(2)}) collective-permute-start(f32[10,256,128]{2,1,0:T(8,128)S(1)} %bitcast.12), channel_id=1, source_target_pairs={{0,1},{1,0},{2,3},{3,2},{4,5},{5,4},{6,7},{7,6},{8,9},{9,8},{10,11... | collective-permute-start | bytes 3932168 | tf_op jit(solution)/shard_map/ppermute | solution.py:265
  153.9 2.7 %collective-permute-done.5.theirs_ref = f32[10,256,128]{2,1,0:T(8,128)S(1)} collective-permute-done((f32[10,256,128]{2,1,0:T(8,128)S(1)}, f32[10,256,128]{2,1,0:T(8,128)S(1)}, u32[]{:S(2)}, u32[]{:S(2)}) %collective-permute-start.5) | collective-permute-done | bytes 1310752 | tf_op jit(solution)/shard_map/ppermute | solution.py:265
  156.5 7.6 %turn.1 = f32[8,512,128]{2,1,0:T(8,128)S(1)} custom-call(s32[1]{0:T(128)} %bitcast.core_ref, f32[10,256,128]{2,1,0:T(8,128)S(1)} %bitcast.13, f32[10,256,128]{2,1,0:T(8,128)S(1)} %collective-permute-done.5.theirs_ref, f32[8,512,128]{2,1,0:T(8,128)S(1)} %all-to-all-done.rows_ref), custom_call_target="tpu_custom_call" | custom-call | tf_op jit(solution)/shard_map/turn/pallas_call | solution.py:206
  164.1 29.0 %all_to_all.22 = f32[8,512,128]{2,1,0:T(8,128)S(1)} all-to-all(f32[8,512,128]{2,1,0:T(8,128)S(1)} %turn.1), channel_id=1, replica_groups=mesh['space'=16,'band'=8] {'band'}, dimensions={0} | all-to-all | bytes 4194304 | tf_op jit(solution)/shard_map/all_to_all | solution.py:268
  193.1 1.3 copy.11
  (11 shorter events, 0.4 us)
Async XLA Ops:
  1.1 23.6 %collective-permute-start = (f32[2,256,128]{2,1,0:T(8,128)S(1)}, f32[2,256,128]{2,1,0:T(8,128)S(1)}, u32[]{:S(2)}, u32[]{:S(2)}) collective-permute-start(f32[2,256,128]{2,1,0:T(8,128)S(1)} %bitcast.17), channel_id=1, source_target_pairs={{0,8},{8,16},{16,24},{24,32},{32,40},{40,48},{48,56},{56,64},{64,7... | collective-permute-start | bytes 786440 | tf_op jit(solution)/shard_map/ppermute | solution.py:227
  3.2 21.5 %collective-permute-start.1 = (f32[2,256,128]{2,1,0:T(8,128)S(1)}, f32[2,256,128]{2,1,0:T(8,128)S(1)}, u32[]{:S(2)}, u32[]{:S(2)}) collective-permute-start(f32[2,256,128]{2,1,0:T(8,128)S(1)} %bitcast.16), channel_id=1, source_target_pairs={{8,0},{16,8},{24,16},{32,24},{40,32},{48,40},{56,48},{64,56},{72,6... | collective-permute-start | bytes 786440 | tf_op jit(solution)/shard_map/ppermute | solution.py:227
  7.8 1.6 copy-start
  30.7 17.7 %collective-permute-start.3 = (f32[2,256,128]{2,1,0:T(8,128)S(1)}, f32[2,256,128]{2,1,0:T(8,128)S(1)}, u32[]{:S(2)}, u32[]{:S(2)}) collective-permute-start(f32[2,256,128]{2,1,0:T(8,128)S(1)} %get-tuple-element.9), channel_id=1, source_target_pairs={{8,0},{16,8},{24,16},{32,24},{40,32},{48,40},{56,48},{64,56},{72,6... | collective-permute-start | bytes 786440 | tf_op jit(solution)/shard_map/ppermute | solution.py:227
  32.2 16.2 %collective-permute-start.2 = (f32[2,256,128]{2,1,0:T(8,128)S(1)}, f32[2,256,128]{2,1,0:T(8,128)S(1)}, u32[]{:S(2)}, u32[]{:S(2)}) collective-permute-start(f32[2,256,128]{2,1,0:T(8,128)S(1)} %get-tuple-element.10), channel_id=1, source_target_pairs={{0,8},{8,16},{16,24},{24,32},{32,40},{40,48},{48,56},{56,64},{64,7... | collective-permute-start | bytes 786440 | tf_op jit(solution)/shard_map/ppermute | solution.py:227
  55.0 33.1 %all-to-all-start = ((f32[8,512,128]{2,1,0:T(8,128)}), f32[8,512,128]{2,1,0:T(8,128)S(1)}, u32[]{:S(2)}, u32[]{:S(2)}) async-start(f32[8,512,128]{2,1,0:T(8,128)} %bitcast.4), calls=%async_computation | async-start | bytes 4194304 | tf_op jit(solution)/shard_map/all_to_all | solution.py:249
  94.6 3.7 %collective-permute-start.4 = (f32[10,256,128]{2,1,0:T(8,128)S(1)}, f32[10,256,128]{2,1,0:T(8,128)S(1)}, u32[]{:S(2)}, u32[]{:S(2)}) collective-permute-start(f32[10,256,128]{2,1,0:T(8,128)S(1)} %get-tuple-element.8), channel_id=1, source_target_pairs={{0,1},{1,0},{2,3},{3,2},{4,5},{5,4},{6,7},{7,6},{8,9},{9,8},{10,11... | collective-permute-start | bytes 3932168 | tf_op jit(solution)/shard_map/ppermute | solution.py:258
  150.7 5.8 %collective-permute-start.5 = (f32[10,256,128]{2,1,0:T(8,128)S(1)}, f32[10,256,128]{2,1,0:T(8,128)S(1)}, u32[]{:S(2)}, u32[]{:S(2)}) collective-permute-start(f32[10,256,128]{2,1,0:T(8,128)S(1)} %bitcast.12), channel_id=1, source_target_pairs={{0,1},{1,0},{2,3},{3,2},{4,5},{5,4},{6,7},{7,6},{8,9},{9,8},{10,11... | collective-permute-start | bytes 3932168 | tf_op jit(solution)/shard_map/ppermute | solution.py:265

commit v2 on v1

--- a/solution.py
+++ b/solution.py
@@ -10,6 +10,11 @@
 REACH = 2
 TILE = 256
 PAIRS = [(i, j) for i in range(4) for j in range(i, 4)]
+SPAN = 2 * REACH + 1
+TOTAL = 256
+RING = 8
+BUILD_LIMIT = 24 << 20
+STEP_LIMIT = 16 << 20
 F32 = jnp.float32
 BF16 = jnp.bfloat16
 
@@ -24,96 +29,169 @@
     return jnp.dot(a, b, preferred_element_type=F32)
 
 
-def operator_kernel(step_kind, edge, elem_dev, slots_ref, blocks_ref, *refs):
+def spread(wide_ref, slot, value):
+    hi, lo = split(value)
+    wide_ref[slot, :, 0:128] = hi
+    wide_ref[slot, :, 128:256] = lo
+
+
+def apply_one(op_ref, wide_ref, elem):
+    near = wide_ref[pl.ds(elem, SPAN)].reshape(SPAN * 256, 256)
+    prod = dot(op_ref[elem], near)
+    return (prod[256:, 128:] + prod[256:, :128]) + (prod[:256, 128:] + prod[:256, :128])
+
+
+def first_of(total, own):
+    return (total - 0.5 * own) / 1.5
+
+
+def second_of(total, own, base):
+    return 2.0 * (total - 0.5 * own) / 1.5 - base
+
+
+def build_kernel(count, near_ref, first_ref, blocks_ref, own_ref, step_ref, op_ref, wide_ref, ring_ref, sums_ref, sem):
+    def fetch(n):
+        elem = lax.rem(n + REACH, count)
+        return pltpu.make_async_copy(blocks_ref.at[elem], ring_ref.at[lax.rem(n, RING)], sem.at[lax.rem(n, RING)])
+
+    for n in range(RING):
+        fetch(n).start()
+    for r in range(count):
+        spread(wide_ref, REACH + r, own_ref[r])
+
+    def combine(n, u):
+        elem = lax.rem(n + REACH, count)
+        at = lax.rem(n, RING)
+        fetch(n).wait()
+        sums_ref[u, 0] = ring_ref[at, 1]
+        sums_ref[u, SPAN - 1] = ring_ref[at, 2]
+        for o in range(1, SPAN - 1):
+            sums_ref[u, o] = jnp.zeros((256, 256), F32)
+        for k in (0, 3, 4, 5, 6):
+            o = lax.rem(near_ref[elem, k] - first_ref[0] - elem + REACH + 2 * TOTAL, TOTAL)
+            sums_ref[u, o] = sums_ref[u, o] + ring_ref[at, k]
+        for o in range(SPAN):
+            hi, lo = split(sums_ref[u, o])
+            op_ref[elem, :256, o * 256 : (o + 1) * 256] = hi
+            op_ref[elem, 256:, o * 256 : (o + 1) * 256] = lo
+        return elem
+
+    def refill(n):
+        @pl.when(n + RING < count)
+        def _():
+            fetch(n + RING).start()
+
+    def inner(g, _):
+        for u in range(2):
+            n = 2 * g + u
+            elem = combine(n, u)
+            refill(n)
+            step_ref[elem] = first_of(apply_one(op_ref, wide_ref, elem), own_ref[elem])
+        return 0
+
+    def outer(n, _):
+        combine(n, 0)
+        return 0
+
+    lax.fori_loop(0, (count - 2 * REACH) // 2, inner, 0)
+    lax.fori_loop(count - 2 * REACH, count, outer, 0)
+
+
+def edges_of(count):
+    return [*range(REACH), *range(count - REACH, count)]
+
+
+def edge_kernel(kind, count, op_ref, own_ref, before_ref, after_ref, *refs):
     refs = list(refs)
-    own_ref = refs.pop(0)
-    before_ref = refs.pop(0) if edge else None
-    after_ref = refs.pop(0) if edge else None
-    base_ref = refs.pop(0) if step_kind == 2 else None
-    if edge:
-        refs.pop(0)
-    out_ref, wide_ref = refs
-    step = pl.program_id(0)
-
-    def put(slot, value):
-        hi, lo = split(value)
-        wide_ref[slot, :, 0:128] = hi
-        wide_ref[slot, :, 128:256] = lo
-
-    @pl.when(step == 0)
-    def _():
-        if edge:
-            for r in range(REACH):
-                put(r, before_ref[r])
-                put(REACH + elem_dev + r, after_ref[r])
-            for r in range(2 * REACH):
-                put(REACH + r, own_ref[r])
-                put(elem_dev - REACH + r, own_ref[elem_dev - 2 * REACH + r])
-        else:
-            for r in range(elem_dev):
-                put(REACH + r, own_ref[r])
-
-    elem = element_of(step, edge, elem_dev)
-    highs, lows, wides = [], [], []
-    for k in range(7):
-        hi, lo = split(blocks_ref[0, k])
-        highs.append(hi)
-        lows.append(lo)
-        wides.append(wide_ref[slots_ref[elem * 7 + k]])
-    left = jnp.concatenate(
-        [jnp.concatenate(highs, axis=1), jnp.concatenate(lows, axis=1)], axis=0
-    )
-    prod = dot(left, jnp.concatenate(wides, axis=0))
-    total = (prod[256:, 128:] + prod[256:, :128]) + (prod[:256, 128:] + prod[:256, :128])
-    own = own_ref[elem]
-    if step_kind == 1:
-        out_ref[0] = (total - 0.5 * own) / 1.5
-    else:
-        out_ref[0] = 2.0 * (total - 0.5 * own) / 1.5 - base_ref[0]
-
-
-def element_of(step, edge, elem_dev):
-    if edge:
-        return step + jnp.where(step >= REACH, elem_dev - 2 * REACH, 0)
-    return step + REACH
-
-
-def apply_operator(step_kind, edge, slots, blocks, own, halos=(), base=None, into=None):
-    elem_dev = own.shape[0]
-    count = 2 * REACH if edge else elem_dev - 2 * REACH
-    pick = lambda s, *_: element_of(s, edge, elem_dev)
-    panel_spec = pl.BlockSpec((1, 256, 128), lambda s, *_: (pick(s), 0, 0))
-    whole = lambda x: pl.BlockSpec(x.shape, lambda s, *_: (0, 0, 0), pipeline_mode=pl.Buffered(1))
-    args = [slots, blocks, own]
-    specs = [
-        pl.BlockSpec((1, 7, 256, 256), lambda s, *_: (pick(s), 0, 0, 0)),
-        whole(own),
-    ]
-    if edge:
-        args += list(halos)
-        specs += [whole(h) for h in halos]
-    if step_kind == 2:
-        args.append(base)
-        specs.append(panel_spec)
-    aliases = {}
-    if edge:
-        aliases = {len(args): 0}
-        args.append(into)
-        specs.append(pl.BlockSpec(memory_space=pl.ANY))
-    return pl.pallas_call(
-        functools.partial(operator_kernel, step_kind, edge, elem_dev),
+    base_ref = refs.pop(0) if kind == 2 else None
+    refs.pop(0)
+    out_ref, wide_ref, made_ref, sem = refs
+    for r in range(REACH):
+        spread(wide_ref, r, before_ref[r])
+        spread(wide_ref, REACH + count + r, after_ref[r])
+    for r in range(2 * REACH):
+        spread(wide_ref, REACH + r, own_ref[r])
+        spread(wide_ref, count - REACH + r, own_ref[count - 2 * REACH + r])
+    copies = []
+    for at, elem in enumerate(edges_of(count)):
+        total = apply_one(op_ref, wide_ref, elem)
+        own = own_ref[elem]
+        made_ref[at] = first_of(total, own) if kind == 1 else second_of(total, own, base_ref[elem])
+        copies.append(pltpu.make_async_copy(made_ref.at[at], out_ref.at[elem], sem.at[at]))
+        copies[-1].start()
+    for copy in copies:
+        copy.wait()
+
+
+def inner_kernel(count, op_ref, own_ref, base_ref, out_ref, wide_ref):
+    for r in range(count):
+        spread(wide_ref, REACH + r, own_ref[r])
+
+    def body(g, _):
+        for u in range(4):
+            elem = REACH + 4 * g + u
+            out_ref[elem] = second_of(apply_one(op_ref, wide_ref, elem), own_ref[elem], base_ref[elem])
+        return 0
+
+    lax.fori_loop(0, (count - 2 * REACH) // 4, body, 0)
+
+
+VMEM_SPEC = pl.BlockSpec(memory_space=pltpu.VMEM)
+SMEM_SPEC = pl.BlockSpec(memory_space=pltpu.SMEM)
+ANY_SPEC = pl.BlockSpec(memory_space=pl.ANY)
+
+
+def build_operator(near, first, blocks, own):
+    count = own.shape[0]
+    return pl.pallas_call(
+        functools.partial(build_kernel, count),
+        out_shape=(
+            jax.ShapeDtypeStruct(own.shape, F32),
+            jax.ShapeDtypeStruct((count, 512, SPAN * 256), BF16),
+        ),
+        in_specs=[SMEM_SPEC, SMEM_SPEC, ANY_SPEC, VMEM_SPEC],
+        out_specs=(VMEM_SPEC, VMEM_SPEC),
+        scratch_shapes=[
+            pltpu.VMEM((count + 2 * REACH, 256, 256), BF16),
+            pltpu.VMEM((RING, 7, 256, 256), F32),
+            pltpu.VMEM((2, SPAN, 256, 256), F32),
+            pltpu.SemaphoreType.DMA((RING,)),
+        ],
+        compiler_params=pltpu.CompilerParams(vmem_limit_bytes=BUILD_LIMIT),
+        name="build",
+    )(near, first, blocks, own)
+
+
+def step_edges(kind, op, own, halos, into, base=None):
+    count = own.shape[0]
+    args = [op, own, *halos] + ([base] if kind == 2 else []) + [into]
+    return pl.pallas_call(
+        functools.partial(edge_kernel, kind, count),
         out_shape=jax.ShapeDtypeStruct(own.shape, F32),
-        grid_spec=pltpu.PrefetchScalarGridSpec(
-            num_scalar_prefetch=1,
-            grid=(count,),
-            in_specs=specs,
-            out_specs=panel_spec,
-            scratch_shapes=[pltpu.VMEM((elem_dev + 2 * REACH, 256, 256), BF16)],
-        ),
-        input_output_aliases=aliases,
-        compiler_params=pltpu.CompilerParams(vmem_limit_bytes=40 << 20),
-        name=f"operator{step_kind}{'edge' if edge else 'mid'}",
+        in_specs=[VMEM_SPEC] * (len(args) - 1) + [ANY_SPEC],
+        out_specs=ANY_SPEC,
+        scratch_shapes=[
+            pltpu.VMEM((count + 2 * REACH, 256, 256), BF16),
+            pltpu.VMEM((2 * REACH, 256, 128), F32),
+            pltpu.SemaphoreType.DMA((2 * REACH,)),
+        ],
+        input_output_aliases={len(args) - 1: 0},
+        compiler_params=pltpu.CompilerParams(vmem_limit_bytes=STEP_LIMIT),
+        name=f"edges{kind}",
     )(*args)
+
+
+def step_inner(op, own, base):
+    count = own.shape[0]
+    return pl.pallas_call(
+        functools.partial(inner_kernel, count),
+        out_shape=jax.ShapeDtypeStruct(own.shape, F32),
+        in_specs=[VMEM_SPEC] * 3,
+        out_specs=VMEM_SPEC,
+        scratch_shapes=[pltpu.VMEM((count + 2 * REACH, 256, 256), BF16)],
+        compiler_params=pltpu.CompilerParams(vmem_limit_bytes=STEP_LIMIT),
+        name="inner",
+    )(op, own, base)
 
 
 def gram_kernel(core_ref, rows_ref, keep_ref, send_ref, hi_ref, lo_ref):
@@ -232,18 +310,15 @@
     panel = vectors.shape[1]
     space_count, band_count = lax.axis_size("space"), lax.axis_size("band")
     total_elements = elem_dev * space_count
-    local_ids = jnp.arange(elem_dev, dtype=jnp.int32)
-    global_ids = lax.axis_index("space") * elem_dev + local_ids
-    offsets = (neighbours - global_ids[:, None] + REACH + total_elements) % total_elements
-    slots = (local_ids[:, None] + offsets).reshape(-1)
+    first = (lax.axis_index("space") * elem_dev).reshape(1)
 
     start = vectors.reshape(elem_dev, basis, panel)
     halos = halos_of(start[:REACH], start[-REACH:])
-    step = apply_operator(1, False, slots, blocks, start)
-    step = apply_operator(1, True, slots, blocks, start, halos, into=step)
+    step, op = build_operator(neighbours, first, blocks, start)
+    step = step_edges(1, op, start, halos, step)
     halos = halos_of(step[:REACH], step[-REACH:])
-    field = apply_operator(2, False, slots, blocks, step, base=start)
-    field = apply_operator(2, True, slots, blocks, step, halos, base=start, into=field)
+    field = step_inner(op, step, start)
+    field = step_edges(2, op, step, halos, field, base=start)
 
     share = elem_dev * basis // band_count
     rows = lax.all_to_all(field.reshape(band_count, share, panel), "band", split_axis=0, concat_axis=0, tiled=True)

time: 195 us -> 180 us (0.923)
  Pallas kernels: 58 us -> 43.4 us
  blocking collectives: 81 us -> 77.2 us
  waiting for transfers between devices: 31.5 us -> 34.9 us
    pallas_call x4, Pallas kernels: 44 us -> 29.2 us  [the longest x1 16.4 us: build_operator(): pl.pallas_call(functools.partial(build_kernel, count), out_shape=(jax.Sha...]
    all_to_all x1, blocking collectives: 27.8 us -> 24.3 us  [per_device(): lax.all_to_all(pieces, both, split_axis=0, concat_axis=0, axis_index_grou...]
    ppermute x4, waiting for transfers between devices: 0.01 us -> 3.35 us  [halos_of(): return (lax.ppermute(last, 'space', up), lax.ppermute(first, 'space', down))]
  transfers between devices with their start and end apart: 7 -> 7, of which waited for: 3 -> 4; matrix products, arithmetic and copies ran while one was open for 0% -> 0% of each run, Pallas kernels for 16% -> 13%
where the time goes in v2:
time: 180 us
  blocking collectives  77.2 us (43%)
  Pallas kernels  43.4 us (24%)
  waiting for transfers between devices  34.9 us (19%)
  starting transfers between devices  19.3 us (11%)
  local copies, waits for them, and re-layouts  4.86 us (3%)
    all_to_all x1, blocking collectives, per_device(): lax.all_to_all(turned, 'band', split_axis=0, concat_axis=0, tiled=True)  29 us
    all_to_all x1, waiting for transfers between devices, per_device(): lax.all_to_all(field.reshape(band_count, share, panel), 'band', split_axi...  26.2 us
    all_to_all x1, blocking collectives, per_device(): lax.all_to_all(pieces, both, split_axis=0, concat_axis=0, axis_index_grou...  24.3 us
    all_to_all x1, blocking collectives, per_device(): lax.all_to_all(copies, both, split_axis=0, concat_axis=0, axis_index_grou...  24 us
    pallas_call x1, Pallas kernels, build_operator(): pl.pallas_call(functools.partial(build_kernel, count), out_shape=(jax.Sha...  16.4 us
    all_to_all x1, starting transfers between devices, per_device(): lax.all_to_all(field.reshape(band_count, share, panel), 'band', split_axi...  7.7 us
    pallas_call x1, Pallas kernels, turn(): pl.pallas_call(functools.partial(turn_kernel, order), out_shape=jax.Shape...  7.49 us
    ppermute x4, starting transfers between devices, halos_of(): return (lax.ppermute(last, 'space', up), lax.ppermute(first, 'space', down))  7.43 us
  transfers between devices with their start and end apart: 7, of which 4 were waited for; matrix products, arithmetic and copies ran while one was open for 0% of the time, Pallas kernels for 13%

profile of v2, /device:TPU:1, one launch (start us, length us, event | category | flops | bytes accessed | tf_op | source)
XLA Modules:
  0.0 180.0 jit_solution(3157192193095330455)
XLA Ops:
  0.0 1.1 fusion.1
  1.1 2.1 %collective-permute-start = (f32[2,256,128]{2,1,0:T(8,128)S(1)}, f32[2,256,128]{2,1,0:T(8,128)S(1)}, u32[]{:S(2)}, u32[]{:S(2)}) collective-permute-start(f32[2,256,128]{2,1,0:T(8,128)S(1)} %bitcast.18), channel_id=1, source_target_pairs={{0,8},{8,16},{16,24},{24,32},{32,40},{40,48},{48,56},{56,64},{64,7... | collective-permute-start | bytes 786440 | tf_op jit(solution)/shard_map/ppermute | solution.py:305
  3.2 3.8 %collective-permute-start.1 = (f32[2,256,128]{2,1,0:T(8,128)S(1)}, f32[2,256,128]{2,1,0:T(8,128)S(1)}, u32[]{:S(2)}, u32[]{:S(2)}) collective-permute-start(f32[2,256,128]{2,1,0:T(8,128)S(1)} %bitcast.17), channel_id=1, source_target_pairs={{8,0},{16,8},{24,16},{32,24},{40,32},{48,40},{56,48},{64,56},{72,6... | collective-permute-start | bytes 786440 | tf_op jit(solution)/shard_map/ppermute | solution.py:305
  7.0 0.8 copy.6.near_ref
  7.7 1.6 copy-done
  9.3 16.4 %build.1 = (f32[16,256,128]{2,1,0:T(8,128)S(1)}, bf16[16,512,1280]{2,1,0:T(8,128)(2,1)S(1)}) custom-call(s32[16,7]{1,0:T(8,128)S(1)} %copy.6.near_ref, s32[1]{0:T(128)} %bitcast.1.first_ref, f32[16,7,256,256]{3,2,1,0:T(8,128)} %blocks_ref.1, f32[16,256,128]{2,1,0:T(8,128)S(1)} %bitcast.9), custom_call_target="tpu_custom_call" | custom-call | tf_op jit(solution)/shard_map/build/pallas_call | solution.py:146
  25.8 4.1 %edges1.1.own_ref = f32[16,256,128]{2,1,0:T(8,128)S(1)} custom-call(bf16[16,512,1280]{2,1,0:T(8,128)(2,1)S(1)} %get-tuple-element.9.op_ref, f32[16,256,128]{2,1,0:T(8,128)S(1)} %bitcast.10, f32[2,256,128]{2,1,0:T(8,128)S(1)} %collective-permute-done.before_ref, f32[2,256,128]{2,1,0:T(8,128)S(1)} %collective-permute-done.1.after_ref, ...), custom_call_target="tpu_custom_call", output_to_operand_aliasing={{}: (4, {})} | custom-call | tf_op jit(solution)/shard_map/edges1/pallas_call | solution.py:168
  30.0 1.5 collective-permute-start.3
  31.5 6.2 %inner.1.refs_1_ = f32[16,256,128]{2,1,0:T(8,128)} custom-call(bf16[16,512,1280]{2,1,0:T(8,128)(2,1)S(1)} %get-tuple-element.9.op_ref, f32[16,256,128]{2,1,0:T(8,128)S(1)} %edges1.1.own_ref, f32[16,256,128]{2,1,0:T(8,128)S(1)} %bitcast.11), custom_call_target="tpu_custom_call" | custom-call | tf_op jit(solution)/shard_map/inner/pallas_call | solution.py:186
  37.7 3.3 %collective-permute-done.2.before_ref = f32[2,256,128]{2,1,0:T(8,128)S(1)} collective-permute-done((f32[2,256,128]{2,1,0:T(8,128)S(1)}, f32[2,256,128]{2,1,0:T(8,128)S(1)}, u32[]{:S(2)}, u32[]{:S(2)}) %collective-permute-start.2) | collective-permute-done | bytes 262176 | tf_op jit(solution)/shard_map/ppermute | solution.py:305
  41.1 2.4 %edges2.1 = f32[16,256,128]{2,1,0:T(8,128)} custom-call(bf16[16,512,1280]{2,1,0:T(8,128)(2,1)S(1)} %get-tuple-element.9.op_ref, f32[16,256,128]{2,1,0:T(8,128)S(1)} %edges1.1.own_ref, f32[2,256,128]{2,1,0:T(8,128)S(1)} %collective-permute-done.2.before_ref, f32[2,256,128]{2,1,0:T(8,128)S(1)} %collective-permute-done.3.after_ref, ...), custom_call_target="tpu_custom_call", output_to_operand_aliasing={{}: (5, {})} | custom-call | tf_op jit(solution)/shard_map/edges2/pallas_call | solution.py:168
  43.5 7.7 %all-to-all-start = ((f32[8,512,128]{2,1,0:T(8,128)}), f32[8,512,128]{2,1,0:T(8,128)S(1)}, u32[]{:S(2)}, u32[]{:S(2)}) async-start(f32[8,512,128]{2,1,0:T(8,128)} %bitcast.5), calls=%async_computation | async-start | bytes 4194304 | tf_op jit(solution)/shard_map/all_to_all | solution.py:324
  51.2 26.2 %all-to-all-done.rows_ref = f32[8,512,128]{2,1,0:T(8,128)S(1)} async-done(((f32[8,512,128]{2,1,0:T(8,128)}), f32[8,512,128]{2,1,0:T(8,128)S(1)}, u32[]{:S(2)}, u32[]{:S(2)}) %all-to-all-start) | async-done | bytes 2097184 | tf_op jit(solution)/shard_map/all_to_all | solution.py:324
  77.4 6.7 %gram.1 = (f32[10,256,128]{2,1,0:T(8,128)S(1)}, f32[10,256,128]{2,1,0:T(8,128)S(1)}) custom-call(s32[1]{0:T(128)} %bitcast.core_ref, f32[8,512,128]{2,1,0:T(8,128)S(1)} %all-to-all-done.rows_ref), custom_call_target="tpu_custom_call" | custom-call | tf_op jit(solution)/shard_map/gram/pallas_call | solution.py:220
  84.1 1.1 collective-permute-start.4
  85.2 2.7 %collective-permute-done.4 = f32[10,256,128]{2,1,0:T(8,128)S(1)} collective-permute-done((f32[10,256,128]{2,1,0:T(8,128)S(1)}, f32[10,256,128]{2,1,0:T(8,128)S(1)}, u32[]{:S(2)}, u32[]{:S(2)}) %collective-permute-start.4) | collective-permute-done | bytes 1310752 | tf_op jit(solution)/shard_map/ppermute | solution.py:333
  87.8 0.1 add.8
  88.0 24.3 %all_to_all.20 = f32[64,40,128]{2,1,0:T(8,128)S(1)} all-to-all(f32[64,40,128]{2,1,0:T(8,128)S(1)} %bitcast.16), channel_id=1, replica_groups={{0,2,4,6,8,10,12,14,16,18,20,22,24,26,28,30,32,34,36,38,40,42,44,46,48,..., dimensions={0} | all-to-all | bytes 2621440 | tf_op jit(solution)/shard_map/all_to_all | solution.py:335
  112.4 24.0 %all_to_all.21 = f32[64,40,128]{2,1,0:T(8,128)S(1)} all-to-all(f32[64,40,128]{2,1,0:T(8,128)S(1)} %broadcast_in_dim.2), channel_id=1, replica_groups={{0,2,4,6,8,10,12,14,16,18,20,22,24,26,28,30,32,34,36,38,40,42,44,46,48,..., dimensions={0} | all-to-all | bytes 2621440 | tf_op jit(solution)/shard_map/all_to_all | solution.py:338
  136.4 3.2 %collective-permute-start.5 = (f32[10,256,128]{2,1,0:T(8,128)S(1)}, f32[10,256,128]{2,1,0:T(8,128)S(1)}, u32[]{:S(2)}, u32[]{:S(2)}) collective-permute-start(f32[10,256,128]{2,1,0:T(8,128)S(1)} %bitcast.13), channel_id=1, source_target_pairs={{0,1},{1,0},{2,3},{3,2},{4,5},{5,4},{6,7},{7,6},{8,9},{9,8},{10,11... | collective-permute-start | bytes 3932168 | tf_op jit(solution)/shard_map/ppermute | solution.py:340
  139.6 2.7 %collective-permute-done.5.theirs_ref = f32[10,256,128]{2,1,0:T(8,128)S(1)} collective-permute-done((f32[10,256,128]{2,1,0:T(8,128)S(1)}, f32[10,256,128]{2,1,0:T(8,128)S(1)}, u32[]{:S(2)}, u32[]{:S(2)}) %collective-permute-start.5) | collective-permute-done | bytes 1310752 | tf_op jit(solution)/shard_map/ppermute | solution.py:340
  142.2 7.5 %turn.1 = f32[8,512,128]{2,1,0:T(8,128)S(1)} custom-call(s32[1]{0:T(128)} %bitcast.core_ref, f32[10,256,128]{2,1,0:T(8,128)S(1)} %bitcast.14, f32[10,256,128]{2,1,0:T(8,128)S(1)} %collective-permute-done.5.theirs_ref, f32[8,512,128]{2,1,0:T(8,128)S(1)} %all-to-all-done.rows_ref), custom_call_target="tpu_custom_call" | custom-call | tf_op jit(solution)/shard_map/turn/pallas_call | solution.py:284
  149.7 29.0 %all_to_all.22 = f32[8,512,128]{2,1,0:T(8,128)S(1)} all-to-all(f32[8,512,128]{2,1,0:T(8,128)S(1)} %turn.1), channel_id=1, replica_groups=mesh['space'=16,'band'=8] {'band'}, dimensions={0} | all-to-all | bytes 4194304 | tf_op jit(solution)/shard_map/all_to_all | solution.py:343
  178.7 1.3 copy.10
  (8 shorter events, 0.3 us)
Async XLA Ops:
  1.1 24.7 %collective-permute-start = (f32[2,256,128]{2,1,0:T(8,128)S(1)}, f32[2,256,128]{2,1,0:T(8,128)S(1)}, u32[]{:S(2)}, u32[]{:S(2)}) collective-permute-start(f32[2,256,128]{2,1,0:T(8,128)S(1)} %bitcast.18), channel_id=1, source_target_pairs={{0,8},{8,16},{16,24},{24,32},{32,40},{40,48},{48,56},{56,64},{64,7... | collective-permute-start | bytes 786440 | tf_op jit(solution)/shard_map/ppermute | solution.py:305
  3.2 22.6 %collective-permute-start.1 = (f32[2,256,128]{2,1,0:T(8,128)S(1)}, f32[2,256,128]{2,1,0:T(8,128)S(1)}, u32[]{:S(2)}, u32[]{:S(2)}) collective-permute-start(f32[2,256,128]{2,1,0:T(8,128)S(1)} %bitcast.17), channel_id=1, source_target_pairs={{8,0},{16,8},{24,16},{32,24},{40,32},{48,40},{56,48},{64,56},{72,6... | collective-permute-start | bytes 786440 | tf_op jit(solution)/shard_map/ppermute | solution.py:305
  7.7 1.6 copy-start
  30.0 7.8 %collective-permute-start.3 = (f32[2,256,128]{2,1,0:T(8,128)S(1)}, f32[2,256,128]{2,1,0:T(8,128)S(1)}, u32[]{:S(2)}, u32[]{:S(2)}) collective-permute-start(f32[2,256,128]{2,1,0:T(8,128)S(1)} %get-tuple-element.13), channel_id=1, source_target_pairs={{8,0},{16,8},{24,16},{32,24},{40,32},{48,40},{56,48},{64,56},{72,6... | collective-permute-start | bytes 786440 | tf_op jit(solution)/shard_map/ppermute | solution.py:305
  31.4 9.7 %collective-permute-start.2 = (f32[2,256,128]{2,1,0:T(8,128)S(1)}, f32[2,256,128]{2,1,0:T(8,128)S(1)}, u32[]{:S(2)}, u32[]{:S(2)}) collective-permute-start(f32[2,256,128]{2,1,0:T(8,128)S(1)} %get-tuple-element.14), channel_id=1, source_target_pairs={{0,8},{8,16},{16,24},{24,32},{32,40},{40,48},{48,56},{56,64},{64,7... | collective-permute-start | bytes 786440 | tf_op jit(solution)/shard_map/ppermute | solution.py:305
  43.5 33.9 %all-to-all-start = ((f32[8,512,128]{2,1,0:T(8,128)}), f32[8,512,128]{2,1,0:T(8,128)S(1)}, u32[]{:S(2)}, u32[]{:S(2)}) async-start(f32[8,512,128]{2,1,0:T(8,128)} %bitcast.5), calls=%async_computation | async-start | bytes 4194304 | tf_op jit(solution)/shard_map/all_to_all | solution.py:324
  84.1 3.7 %collective-permute-start.4 = (f32[10,256,128]{2,1,0:T(8,128)S(1)}, f32[10,256,128]{2,1,0:T(8,128)S(1)}, u32[]{:S(2)}, u32[]{:S(2)}) collective-permute-start(f32[10,256,128]{2,1,0:T(8,128)S(1)} %get-tuple-element.12), channel_id=1, source_target_pairs={{0,1},{1,0},{2,3},{3,2},{4,5},{5,4},{6,7},{7,6},{8,9},{9,8},{10,11... | collective-permute-start | bytes 3932168 | tf_op jit(solution)/shard_map/ppermute | solution.py:333
  136.4 5.8 %collective-permute-start.5 = (f32[10,256,128]{2,1,0:T(8,128)S(1)}, f32[10,256,128]{2,1,0:T(8,128)S(1)}, u32[]{:S(2)}, u32[]{:S(2)}) collective-permute-start(f32[10,256,128]{2,1,0:T(8,128)S(1)} %bitcast.13), channel_id=1, source_target_pairs={{0,1},{1,0},{2,3},{3,2},{4,5},{5,4},{6,7},{7,6},{8,9},{9,8},{10,11... | collective-permute-start | bytes 3932168 | tf_op jit(solution)/shard_map/ppermute | solution.py:340

commit v3 on v0

v3 whole, which is shorter than its diff:
```python
import functools
import jax
import jax.numpy as jnp
from jax import lax
from jax.experimental import pallas as pl
from jax.experimental.pallas import tpu as pltpu
from jax.sharding import PartitionSpec as P

VECTORS = 1024
REACH = 2
TILE = 256
PAIRS = [(i, j) for i in range(4) for j in range(i, 4)]
SPAN = 2 * REACH + 1
TOTAL = 256
RING = 8
BUILD_LIMIT = 26 << 20
STEP_LIMIT = 16 << 20
TURN_LIMIT = 32 << 20
F32 = jnp.float32
BF16 = jnp.bfloat16


def split(x):
    hi = x.astype(BF16)
    lo = (x - hi.astype(F32)).astype(BF16)
    return hi, lo


def dot(a, b):
    return jnp.dot(a, b, preferred_element_type=F32)


def spread(wide_ref, slot, value):
    hi, lo = split(value)
    wide_ref[slot, :, 0:128] = hi
    wide_ref[slot, :, 128:256] = lo


def apply_one(op_ref, wide_ref, elem):
    near = wide_ref[pl.ds(elem, SPAN)].reshape(SPAN * 256, 256)
    prod = dot(op_ref[elem], near)
    return (prod[256:, 128:] + prod[256:, :128]) + (prod[:256, 128:] + prod[:256, :128])


def first_of(total, own):
    return (total - 0.5 * own) / 1.5


def second_of(total, own, base):
    return 2.0 * (total - 0.5 * own) / 1.5 - base


def build_kernel(count, near_ref, at_ref, blocks_ref, vectors_ref, step_ref, op_ref, wide_ref, ring_ref, sums_ref, own_ref, sem, own_sem):
    def fetch(n):
        elem = lax.rem(n + REACH, count)
        return pltpu.make_async_copy(blocks_ref.at[elem], ring_ref.at[lax.rem(n, RING)], sem.at[lax.rem(n, RING)])

    first = (at_ref[1] * 4 + at_ref[0]) * count
    load = pltpu.make_async_copy(vectors_ref, own_ref, own_sem)
    load.start()
    for n in range(RING):
        fetch(n).start()
    load.wait()
    for r in range(count):
        spread(wide_ref, REACH + r, own_ref[r])

    def combine(n, u):
        elem = lax.rem(n + REACH, count)
        at = lax.rem(n, RING)
        fetch(n).wait()
        sums_ref[u, 0] = ring_ref[at, 1]
        sums_ref[u, SPAN - 1] = ring_ref[at, 2]
        for o in range(1, SPAN - 1):
            sums_ref[u, o] = jnp.zeros((256, 256), F32)
        for k in (0, 3, 4, 5, 6):
            o = lax.rem(near_ref[k, elem] - first - elem + REACH + 2 * TOTAL, TOTAL)
            sums_ref[u, o] = sums_ref[u, o] + ring_ref[at, k]
        for o in range(SPAN):
            hi, lo = split(sums_ref[u, o])
            op_ref[elem, :256, o * 256 : (o + 1) * 256] = hi
            op_ref[elem, 256:, o * 256 : (o + 1) * 256] = lo
        return elem

    def refill(n):
        @pl.when(n + RING < count)
        def _():
            fetch(n + RING).start()

    def inner(g, _):
        for u in range(2):
            n = 2 * g + u
            elem = combine(n, u)
            refill(n)
            step_ref[elem - REACH] = first_of(apply_one(op_ref, wide_ref, elem), own_ref[elem])
        return 0

    def outer(n, _):
        combine(n, 0)
        return 0

    lax.fori_loop(0, (count - 2 * REACH) // 2, inner, 0)
    lax.fori_loop(count - 2 * REACH, count, outer, 0)


def edges_of(count):
    return [*range(REACH), *range(count - REACH, count)]


def first_edge_kernel(count, op_ref, own_ref, before_ref, after_ref, low_ref, high_ref, wide_ref):
    for r in range(REACH):
        spread(wide_ref, r, before_ref[r])
        spread(wide_ref, REACH + count + r, after_ref[r])
    for r in range(2 * REACH):
        spread(wide_ref, REACH + r, own_ref[r])
        spread(wide_ref, count - REACH + r, own_ref[count - 2 * REACH + r])
    for at, elem in enumerate(edges_of(count)):
        out_ref = low_ref if at < REACH else high_ref
        out_ref[at % REACH] = first_of(apply_one(op_ref, wide_ref, elem), own_ref[elem])


def side_of(elem, count, c):
    return lax.rem(elem // (count // 2) + c, 2), lax.rem(elem, count // 2)


def second_edge_kernel(count, at_ref, op_ref, mid_ref, low_ref, high_ref, before_ref, after_ref, base_ref, _, out_ref, wide_ref, made_ref, sem):
    for r in range(REACH):
        spread(wide_ref, r, before_ref[r])
        spread(wide_ref, REACH + r, low_ref[r])
        spread(wide_ref, 2 * REACH + r, mid_ref[r])
        spread(wide_ref, count - REACH + r, mid_ref[count - 3 * REACH + r])
        spread(wide_ref, count + r, high_ref[r])
        spread(wide_ref, REACH + count + r, after_ref[r])
    copies = []
    for at, elem in enumerate(edges_of(count)):
        own = (low_ref if at < REACH else high_ref)[at % REACH]
        made_ref[at] = second_of(apply_one(op_ref, wide_ref, elem), own, base_ref[elem])
        side, place = side_of(elem, count, at_ref[3])
        copies.append(pltpu.make_async_copy(made_ref.at[at], out_ref.at[side, place], sem.at[at]))
        copies[-1].start()
    for copy in copies:
        copy.wait()


def inner_kernel(count, at_ref, op_ref, mid_ref, low_ref, high_ref, base_ref, out_ref, wide_ref):
    for r in range(REACH):
        spread(wide_ref, REACH + r, low_ref[r])
        spread(wide_ref, count + r, high_ref[r])
    for r in range(count - 2 * REACH):
        spread(wide_ref, 2 * REACH + r, mid_ref[r])

    def body(g, _):
        for u in range(4):
            at = 4 * g + u
            elem = REACH + at
            side, place = side_of(elem, count, at_ref[3])
            out_ref[side, place] = second_of(apply_one(op_ref, wide_ref, elem), mid_ref[at], base_ref[elem])
        return 0

    lax.fori_loop(0, (count - 2 * REACH) // 4, body, 0)


VMEM_SPEC = pl.BlockSpec(memory_space=pltpu.VMEM)
SMEM_SPEC = pl.BlockSpec(memory_space=pltpu.SMEM)
ANY_SPEC = pl.BlockSpec(memory_space=pl.ANY)
HBM_SPEC = pl.BlockSpec(memory_space=pltpu.HBM)


def shaped(*shape, dtype=F32):
    return jax.ShapeDtypeStruct(shape, dtype)


def call(kernel, name, outs, specs, scratch, args, limit, **kwargs):
    return pl.pallas_call(
        kernel,
        out_shape=outs,
        in_specs=specs,
        out_specs=kwargs.pop("out_specs", jax.tree.map(lambda _: VMEM_SPEC, outs)),
        scratch_shapes=scratch,
        compiler_params=pltpu.CompilerParams(vmem_limit_bytes=limit),
        name=name,
        **kwargs,
    )(*args)


def wide_scratch(count):
    return pltpu.VMEM((count + 2 * REACH, 256, 256), BF16)


def build_operator(near, here, blocks, own):
    count = own.shape[0]
    return call(
        functools.partial(build_kernel, count),
        "build",
        (shaped(count - 2 * REACH, 256, 128), shaped(count, 512, SPAN * 256, dtype=BF16)),
        [SMEM_SPEC, SMEM_SPEC, HBM_SPEC, HBM_SPEC],
        [
            wide_scratch(count),
            pltpu.VMEM((RING, 7, 256, 256), F32),
            pltpu.VMEM((2, SPAN, 256, 256), F32),
            pltpu.VMEM(own.shape, F32),
            pltpu.SemaphoreType.DMA((RING,)),
            pltpu.SemaphoreType.DMA,
        ],
        (near, here, blocks, own),
        BUILD_LIMIT,
    )


def first_edges(op, own, halos):
    count = own.shape[0]
    edge = shaped(REACH, 256, 128)
    return call(
        functools.partial(first_edge_kernel, count), "edges1", (edge, edge), [VMEM_SPEC] * 4,
        [wide_scratch(count)], (op, own, *halos), STEP_LIMIT,
    )


def second_inner(here, op, mid, low, high, base):
    count = base.shape[0]
    return call(
        functools.partial(inner_kernel, count), "inner", shaped(2, count // 2, 256, 128), [SMEM_SPEC] + [VMEM_SPEC] * 5,
        [wide_scratch(count)], (here, op, mid, low, high, base), STEP_LIMIT,
    )


def second_edges(here, op, mid, low, high, halos, base, into):
    count = base.shape[0]
    return call(
        functools.partial(second_edge_kernel, count), "edges2", shaped(*into.shape),
        [SMEM_SPEC] + [VMEM_SPEC] * 7 + [ANY_SPEC],
        [wide_scratch(count), pltpu.VMEM((2 * REACH, 256, 128), F32), pltpu.SemaphoreType.DMA((2 * REACH,))],
        (here, op, mid, low, high, *halos, base, into), STEP_LIMIT,
        out_specs=ANY_SPEC, input_output_aliases={8: 0},
    )


def pair_kernel(at_ref, both_ref, got_ref, *out_refs):
    z = at_ref[2]
    for k in range(4):
        chip = lax.rem(z + k, 4)
        out_refs[k][0] = both_ref[0, chip]
        out_refs[k][1] = got_ref[chip]


def share_kernel(axis, count, at_ref, *refs):
    ins, outs, sum_ref = refs[:count], refs[count:-1], refs[-1]
    total = ins[0][...]
    for ref in ins[1:]:
        total = total + ref[...]
    sum_ref[...] = total
    size = outs[0].shape[0]
    for k in range(4):
        part = lax.rem(at_ref[axis] + k, 4)
        outs[k][...] = sum_ref[pl.ds(pl.multiple_of(part * size, size), size)]


def shares(here, axis, shift, arrays):
    size, panel = arrays[0].shape
    part = shaped(size // 4, panel)
    outs = call(
        functools.partial(share_kernel, axis, len(arrays)), f"share{axis}", (part,) * 4,
        [SMEM_SPEC] + [VMEM_SPEC] * len(arrays), [pltpu.VMEM((size, panel), F32)], (here, *arrays), STEP_LIMIT,
    )
    got = {k: shift(outs[k], k) for k in SHIFTS}
    return [outs[0]] + [got[k] for k in (1, 2, 3)]


def lanes(start, size):
    return pl.ds(pl.multiple_of(start, size), size)


def half_of_gram(half, hi_ref, lo_ref, out_ref):
    for m in range(5):
        (i0, j0), (i1, j1) = PAIRS[m], PAIRS[m + 5]
        i = lanes(jnp.where(half == 0, i0, i1) * TILE, TILE)
        j = lanes(jnp.where(half == 0, j0, j1) * TILE, TILE)
        left_hi, right_hi = hi_ref[:, i], hi_ref[:, j]
        left = jnp.concatenate([left_hi, left_hi, lo_ref[:, i]], axis=0)
        right = jnp.concatenate([right_hi, lo_ref[:, j], right_hi], axis=0)
        block = lax.dot_general(left, right, (((0,), (0,)), ((), ())), preferred_element_type=F32)
        out_ref[2 * m] = block[:, :128]
        out_ref[2 * m + 1] = block[:, 128:]


def gram_send_kernel(at_ref, *refs):
    parts, (rows_ref, hi_ref, lo_ref, out_ref) = refs[:4], refs[4:]
    z, c = at_ref[2], at_ref[3]
    for k in range(4):
        for j in range(2):
            band = lax.rem(z + 4 - k, 4) * 2 + lax.rem(c + j, 2)
            value = parts[k][j]
            rows_ref[band] = value
            hi, lo = split(value)
            hi_ref[:, lanes(band * 128, 128)] = hi
            lo_ref[:, lanes(band * 128, 128)] = lo
    half_of_gram(1 - c, hi_ref, lo_ref, out_ref)


def gram_keep_kernel(at_ref, hi_ref, lo_ref, out_ref):
    half_of_gram(at_ref[3], hi_ref, lo_ref, out_ref)


def times_normed(hi, lo, nh, nl):
    return dot(jnp.concatenate([hi, hi, lo], axis=1), jnp.concatenate([nh, nl, nh], axis=0))


def normed_kernel(order, at_ref, mine_ref, theirs_ref, rows_ref, hi_ref, lo_ref, nh_ref, nl_ref, gh_ref, gl_ref, stretch_ref, gram_ref, y_ref):
    x, y, c = at_ref[0], at_ref[1], at_ref[3]
    for kx in range(4):
        for ky in range(4):
            piece = lax.rem(x + 4 - kx, 4) * 4 + lax.rem(y + 4 - ky, 4)
            rows = pl.ds(pl.multiple_of(piece * 160, 160), 160)
            gram_ref[c, rows] = mine_ref[kx * 4 + ky]
            gram_ref[1 - c, rows] = theirs_ref[kx * 4 + ky]

    def packed(n, h):
        at = 2 * (n % 5) + h
        return gram_ref[n // 5, at * 256 : (at + 1) * 256]

    row = lax.broadcasted_iota(jnp.int32, (256, 128), 0)
    col = lax.broadcasted_iota(jnp.int32, (256, 128), 1)
    diag = jnp.zeros((256, 128), F32)
    for n, (i, j) in enumerate(PAIRS):
        if i == j:
            for h in range(2):
                diag += jnp.where(row == col + 128 * h, packed(n, h), 0.0)
    scale = jnp.sum(diag) / VECTORS
    for n, (i, j) in enumerate(PAIRS):
        for h in range(2):
            hi, lo = split(packed(n, h) / scale)
            at = j * TILE + h * 128
            nh_ref[i * TILE : (i + 1) * TILE, at : at + 128] = hi
            nl_ref[i * TILE : (i + 1) * TILE, at : at + 128] = lo
            if i != j:
                nh_ref[at : at + 128, i * TILE : (i + 1) * TILE] = hi.T
                nl_ref[at : at + 128, i * TILE : (i + 1) * TILE] = lo.T
    for j in range(4):
        cols = slice(j * TILE, (j + 1) * TILE)
        y_ref[:, cols] = times_normed(hi_ref[...], lo_ref[...], nh_ref[:, cols], nl_ref[:, cols])
    for b in range(8):
        cols = slice(b * 128, (b + 1) * 128)
        hi, lo = split(3.0 * y_ref[:, cols] - 10.0 * rows_ref[b])
        gh_ref[:, cols] = hi
        gl_ref[:, cols] = lo
    stretch_ref[...] = jnp.sqrt(jnp.full((8, 128), order, F32) / scale)


def turned_kernel(k, at_ref, rows_ref, gh_ref, gl_ref, nh_ref, nl_ref, stretch_ref, out_ref):
    z, c = at_ref[2], at_ref[3]
    chip = lax.rem(z + k, 4)
    cols = lanes(chip * TILE, TILE)
    prod = times_normed(gh_ref[...], gl_ref[...], nh_ref[:, cols], nl_ref[:, cols])
    for j in range(2):
        part = 15.0 * rows_ref[2 * chip + j] + prod[:, j * 128 : (j + 1) * 128]
        out_ref[lax.rem(c + j, 2)] = part / 8.0 * stretch_ref[0:1]


def place_kernel(at_ref, *refs):
    parts, got_ref, out_ref, sem = refs[:4], refs[4], refs[5], refs[6]
    z, c = at_ref[2], at_ref[3]
    copies = []
    for k in range(4):
        chip = lax.rem(z + 4 - k, 4)
        copies.append(pltpu.make_async_copy(parts[k].at[0], out_ref.at[c * 4 + chip], sem.at[k]))
        copies.append(pltpu.make_async_copy(got_ref.at[k], out_ref.at[(1 - c) * 4 + chip], sem.at[4 + k]))
    for copy in copies:
        copy.start()
    for copy in copies:
        copy.wait()


SHIFTS = (2, 1, 3)


def swap_cores(x):
    return lax.ppermute(x, "band", [(i, i ^ 1) for i in range(8)])


def shift_z(x, k):
    return lax.ppermute(x, "band", [(i, (i + 2 * k) % 8) for i in range(8)])


def shift_x(x, k):
    return lax.ppermute(x, "space", [(i, (i & 12) | ((i + k) & 3)) for i in range(16)])


def shift_y(x, k):
    return lax.ppermute(x, "space", [(i, (i + 4 * k) % 16) for i in range(16)])


def gathered(x, shift):
    got = {k: shift(x, k) for k in SHIFTS}
    return jnp.stack([x] + [got[k] for k in (1, 2, 3)])


def halos_of(first, last):
    size = lax.axis_size("space")
    up = [(i, (i + 1) % size) for i in range(size)]
    down = [(j, i) for i, j in up]
    return lax.ppermute(last, "space", up), lax.ppermute(first, "space", down)


def per_device(vectors, blocks, neighbours):
    elem_dev, basis = blocks.shape[0], blocks.shape[2]
    panel = vectors.shape[1]
    order = float(elem_dev * basis * lax.axis_size("space"))
    space, band = lax.axis_index("space"), lax.axis_index("band")
    x, y, z, c = space & 3, space >> 2, band >> 1, band & 1
    here = jnp.stack([x, y, z, c]).astype(jnp.int32)

    start = vectors.reshape(elem_dev, basis, panel)
    halos = halos_of(start[:REACH], start[-REACH:])
    mid, op = build_operator(neighbours.T, here, blocks, start)
    low, high = first_edges(op, start, halos)
    halos = halos_of(low, high)
    field = second_inner(here, op, mid, low, high, start)
    field = second_edges(here, op, mid, low, high, halos, start, field)

    share = elem_dev * basis // 8
    both = field.reshape(2, 4, share, panel)
    got = swap_cores(both[1])
    pairs = call(
        pair_kernel, "pair", (shaped(2, share, panel),) * 4, [SMEM_SPEC] + [VMEM_SPEC] * 2, [], (here, both, got), STEP_LIMIT
    )
    parts = {k: shift_z(pairs[k], k) for k in SHIFTS}
    parts[0] = pairs[0]
    half = shaped(10, 256, 128)
    wide = shaped(share, VECTORS, dtype=BF16)
    rows, hi, lo, send = call(
        gram_send_kernel, "gram1", (shaped(8, share, panel), wide, wide, half), [SMEM_SPEC] + [VMEM_SPEC] * 4, [],
        (here, *(parts[k] for k in range(4))), STEP_LIMIT,
    )
    theirs = swap_cores(send)
    keep = call(gram_keep_kernel, "gram2", half, [SMEM_SPEC] + [VMEM_SPEC] * 2, [], (here, hi, lo), STEP_LIMIT)
    pieces = shares(here, 0, shift_x, [keep.reshape(2560, panel), theirs.reshape(2560, panel)])
    pieces = shares(here, 1, shift_y, pieces)
    piece = (pieces[0] + pieces[1]) + (pieces[2] + pieces[3])
    got = [shift_z(piece, k) for k in SHIFTS]
    piece = piece + got[0] + (got[1] + got[2])
    mine = gathered(gathered(piece, shift_y), shift_x).reshape(16, 160, panel)
    theirs = swap_cores(mine)

    square = shaped(VECTORS, VECTORS, dtype=BF16)
    nh, nl, gh, gl, stretch = call(
        functools.partial(normed_kernel, order), "normed", (square, square, wide, wide, shaped(8, 128)),
        [SMEM_SPEC] + [VMEM_SPEC] * 5, [pltpu.VMEM((2, 2560, 128), F32), pltpu.VMEM((share, VECTORS), F32)],
        (here, mine, theirs, rows, hi, lo), TURN_LIMIT,
    )
    turned = [
        call(
            functools.partial(turned_kernel, k), f"turned{k}", shaped(2, share, panel), [SMEM_SPEC] + [VMEM_SPEC] * 6, [],
            (here, rows, gh, gl, nh, nl, stretch), STEP_LIMIT,
        )
        for k in range(4)
    ]
    parts = {k: shift_z(turned[k], k) for k in SHIFTS}
    parts[0] = turned[0]
    got = swap_cores(jnp.stack([parts[k][1] for k in range(4)]))
    placed = call(
        place_kernel, "place", shaped(8, share, panel), [SMEM_SPEC] + [ANY_SPEC] * 5, [pltpu.SemaphoreType.DMA((8,))],
        (here, *(parts[k] for k in range(4)), got), STEP_LIMIT, out_specs=ANY_SPEC,
    )
    return placed.reshape(elem_dev * basis, panel)


def solution(mesh):
    return jax.shard_map(
        per_device,
        mesh=mesh,
        in_specs=(P("space", "band"), P("space", None, None, None), P("space", None)),
        out_specs=P("space", "band"),
        check_vma=False,
    )
```

time: 402 us -> 187 us (0.47); the launches traced: 395 us -> 187 us
  matrix products: 105 us -> 0 us
  waiting for transfers between devices: 164 us -> 91.3 us
  blocking collectives: 63.9 us -> 0 us
  Pallas kernels: 0 us -> 48.5 us
  starting transfers between devices: 10.9 us -> 43.2 us
  local copies, waits for them, and re-layouts: 25.2 us -> 3.48 us
  between operations: 14.7 us -> 0.42 us
  other arithmetic: 11.4 us -> 0.34 us
    psum x1 -> x0, waiting for transfers between devices: 154 us -> none  [per_device(): gram = lax.psum(local_gram, ('space', 'band'))]
    dot_general x5 -> x0, matrix products: 105 us -> none  [the longest x2 71.8 us: apply_operator(): jnp.einsum('lkij,lkjm->lim', blocks, picked, precision=lax.Precision.HIGH...]
    ppermute x4 -> x29, waiting for transfers between devices: 9.99 us -> 91.3 us  [the longest x9 45.3 us: shift_z(): return lax.ppermute(x, 'band', [(i, (i + 2 * k) % 8) for i in range(8)])]
    all_to_all x2 -> x0, blocking collectives: 63.9 us -> none  [the longest x1 33.7 us: per_device(): lax.all_to_all(filtered, 'band', split_axis=0, concat_axis=1, tiled=True)]
    pallas_call x0 -> x15, Pallas kernels: none -> 48.5 us  [call(): pl.pallas_call(kernel, out_shape=outs, in_specs=specs, out_specs=kwargs.p...]
    ppermute x4 -> x29, starting transfers between devices: 10.9 us -> 43.2 us  [the longest x9 12.8 us: shift_z(): return lax.ppermute(x, 'band', [(i, (i + 2 * k) % 8) for i in range(8)])]
    gather x2 -> x0, local copies, waits for them, and re-layouts: 13.4 us -> none  [apply_operator(): picked = padded[slots]]
    dot_general x2 -> x0, local copies, waits for them, and re-layouts: 6.11 us -> none  [apply_operator(): jnp.einsum('lkij,lkjm->lim', blocks, picked, precision=lax.Precision.HIGH...]
  transfers between devices with their start and end apart: 5 -> 29, of which waited for: 3 -> 21; matrix products, arithmetic and copies ran while one was open for 0% -> 0% of each run, Pallas kernels for 0% -> 15%
where the time goes in v3:
time: 187 us
  waiting for transfers between devices  91.3 us (49%)
  Pallas kernels  48.5 us (26%)
  starting transfers between devices  43.2 us (23%)
  local copies, waits for them, and re-layouts  3.48 us (2%)
    pallas_call x15, Pallas kernels, call(): pl.pallas_call(kernel, out_shape=outs, in_specs=specs, out_specs=kwargs.p...  48.5 us
    ppermute x9, waiting for transfers between devices, shift_z(): return lax.ppermute(x, 'band', [(i, (i + 2 * k) % 8) for i in range(8)])  45.3 us
    ppermute x6, waiting for transfers between devices, shift_x(): lax.ppermute(x, 'space', [(i, i & 12 | i + k & 3) for i in range(16)])  25.9 us
    ppermute x9, starting transfers between devices, shift_z(): return lax.ppermute(x, 'band', [(i, (i + 2 * k) % 8) for i in range(8)])  12.8 us
    ppermute x4, starting transfers between devices, swap_cores(): return lax.ppermute(x, 'band', [(i, i ^ 1) for i in range(8)])  9.5 us
    ppermute x6, waiting for transfers between devices, shift_y(): return lax.ppermute(x, 'space', [(i, (i + 4 * k) % 16) for i in range(16)])  8.09 us
    ppermute x4, waiting for transfers between devices, swap_cores(): return lax.ppermute(x, 'band', [(i, i ^ 1) for i in range(8)])  8.04 us
    ppermute x6, starting transfers between devices, shift_x(): lax.ppermute(x, 'space', [(i, i & 12 | i + k & 3) for i in range(16)])  7.71 us
  transfers between devices with their start and end apart: 29, of which 21 were waited for; matrix products, arithmetic and copies ran while one was open for 0% of the time, Pallas kernels for 15%

profile of v3, /device:TPU:1, one launch (start us, length us, event | category | flops | bytes accessed | tf_op | source)
XLA Modules:
  0.0 187.2 jit_solution(1052581108369098059)
XLA Ops:
  3.2 3.8 %collective-permute-start.1 = (f32[2,256,128]{2,1,0:T(8,128)S(1)}, f32[2,256,128]{2,1,0:T(8,128)S(1)}, u32[]{:S(2)}, u32[]{:S(2)}) collective-permute-start(f32[2,256,128]{2,1,0:T(8,128)S(1)} %bitcast.38), channel_id=1, source_target_pairs={{8,0},{16,8},{24,16},{32,24},{40,32},{48,40},{56,48},{64,56},{72,6... | collective-permute-start | bytes 786440 | tf_op jit(solution)/shard_map/ppermute | solution.py:400
  9.3 16.5 %build.1 = (f32[12,256,128]{2,1,0:T(8,128)S(1)}, bf16[16,512,1280]{2,1,0:T(8,128)(2,1)S(1)}) custom-call(s32[7,16]{1,0:T(8,128)S(1)} %bitcast.32, s32[4]{0:T(128)S(1)} %pad_add_fusion.at_ref, f32[16,7,256,256]{3,2,1,0:T(8,128)} %blocks_ref.1, f32[16,256,128]{2,1,0:T(8,128)S(1)} %bitcast.23), custom_call_target="tpu_custom_call" | custom-call | tf_op jit(solution)/shard_map/build/pallas_call | solution.py:173
  29.1 5.6 %inner.1._ = f32[2,8,256,128]{3,2,1,0:T(8,128)S(1)} custom-call(s32[4]{0:T(128)S(1)} %pad_add_fusion.at_ref, bf16[16,512,1280]{2,1,0:T(8,128)(2,1)S(1)} %get-tuple-element.30.op_ref, f32[12,256,128]{2,1,0:T(8,128)S(1)} %get-tuple-element.31.mid_ref, f32[2,256,128]{2,1,0:T(8,128)S(1)} %get-tuple-element.32.low_ref, ...), custom_call_target="tpu_custom_call" | custom-call | tf_op jit(solution)/shard_map/inner/pallas_call | solution.py:173
  34.8 4.0 %collective-permute-done.2.before_ref = f32[2,256,128]{2,1,0:T(8,128)S(1)} collective-permute-done((f32[2,256,128]{2,1,0:T(8,128)S(1)}, f32[2,256,128]{2,1,0:T(8,128)S(1)}, u32[]{:S(2)}, u32[]{:S(2)}) %collective-permute-start.2) | collective-permute-done | bytes 262176 | tf_op jit(solution)/shard_map/ppermute | solution.py:400
  38.7 4.8 %edges2.1 = f32[2,8,256,128]{3,2,1,0:T(8,128)S(1)} custom-call(s32[4]{0:T(128)S(1)} %pad_add_fusion.at_ref, bf16[16,512,1280]{2,1,0:T(8,128)(2,1)S(1)} %get-tuple-element.30.op_ref, f32[12,256,128]{2,1,0:T(8,128)S(1)} %get-tuple-element.31.mid_ref, f32[2,256,128]{2,1,0:T(8,128)S(1)} %get-tuple-element.32.low_ref, ...), custom_call_target="tpu_custom_call", output_to_operand_aliasing={{}: (8, {})} | custom-call | tf_op jit(solution)/shard_map/edges2/pallas_call | solution.py:173
  43.6 2.4 %collective-permute-start.4 = (f32[4,512,128]{2,1,0:T(8,128)S(1)}, f32[4,512,128]{2,1,0:T(8,128)S(1)}, u32[]{:S(2)}, u32[]{:S(2)}) collective-permute-start(f32[4,512,128]{2,1,0:T(8,128)S(1)} %bitcast.33), channel_id=1, source_target_pairs={{0,1},{1,0},{2,3},{3,2},{4,5},{5,4},{6,7},{7,6},{8,9},{9,8},{10,11... | collective-permute-start | bytes 3145736 | tf_op jit(solution)/shard_map/ppermute | solution.py:376
  50.8 3.3 %collective-permute-start.6 = (f32[2,512,128]{2,1,0:T(8,128)S(1)}, f32[2,512,128]{2,1,0:T(8,128)S(1)}, u32[]{:S(2)}, u32[]{:S(2)}) collective-permute-start(f32[2,512,128]{2,1,0:T(8,128)S(1)} %get-tuple-element.36), channel_id=1, source_target_pairs={{0,4},{1,5},{2,6},{3,7},{4,0},{5,1},{6,2},{7,3},{8,12},{9,13},{10,... | collective-permute-start | bytes 1572872 | tf_op jit(solution)/shard_map/ppermute | solution.py:380
  54.8 10.0 %collective-permute-done.5.refs_1_ = f32[2,512,128]{2,1,0:T(8,128)S(1)} collective-permute-done((f32[2,512,128]{2,1,0:T(8,128)S(1)}, f32[2,512,128]{2,1,0:T(8,128)S(1)}, u32[]{:S(2)}, u32[]{:S(2)}) %collective-permute-start.5) | collective-permute-done | bytes 524320 | tf_op jit(solution)/shard_map/ppermute | solution.py:380
  64.8 12.1 %collective-permute-done.6.refs_2_ = f32[2,512,128]{2,1,0:T(8,128)S(1)} collective-permute-done((f32[2,512,128]{2,1,0:T(8,128)S(1)}, f32[2,512,128]{2,1,0:T(8,128)S(1)}, u32[]{:S(2)}, u32[]{:S(2)}) %collective-permute-start.6) | collective-permute-done | bytes 524320 | tf_op jit(solution)/shard_map/ppermute | solution.py:380
  77.0 2.8 %gram1.1 = (f32[8,512,128]{2,1,0:T(8,128)S(1)}, bf16[512,1024]{1,0:T(8,128)(2,1)S(1)}, bf16[512,1024]{1,0:T(8,128)(2,1)S(1)}, f32[10,256,128]{2,1,0:T(8,128)S(1)}) custom-call(s32[4]{0:T(128)S(1)} %pad_add_fusion.at_ref, f32[2,512,128]{2,1,0:T(8,128)S(1)} %get-tuple-element.34.refs_0_, f32[2,512,128]{2,1,0:T(8,128)S(1)} %collective-permute-done.5.refs_1_, ...), custom_call_target="tpu_custom_call" | custom-call | tf_op jit(solution)/shard_map/gram1/pallas_call | solution.py:173
  84.7 2.6 %collective-permute-start.11 = (f32[640,128]{1,0:T(8,128)S(1)}, f32[640,128]{1,0:T(8,128)S(1)}, u32[]{:S(2)}, u32[]{:S(2)}) collective-permute-start(f32[640,128]{1,0:T(8,128)S(1)} %get-tuple-element.45), channel_id=1, source_target_pairs={{0,24},{8,0},{16,8},{24,16},{32,56},{40,32},{48,40},{56,48},{64,88... | collective-permute-start | bytes 983048 | tf_op jit(solution)/shard_map/ppermute | solution.py:384
  87.2 14.4 %collective-permute-done.9.refs_1_ = f32[640,128]{1,0:T(8,128)S(1)} collective-permute-done((f32[640,128]{1,0:T(8,128)S(1)}, f32[640,128]{1,0:T(8,128)S(1)}, u32[]{:S(2)}, u32[]{:S(2)}) %collective-permute-start.9) | collective-permute-done | bytes 327712 | tf_op jit(solution)/shard_map/ppermute | solution.py:384
  105.5 2.7 %collective-permute-done.12 = f32[160,128]{1,0:T(8,128)S(1)} collective-permute-done((f32[160,128]{1,0:T(8,128)S(1)}, f32[160,128]{1,0:T(8,128)S(1)}, u32[]{:S(2)}, u32[]{:S(2)}) %collective-permute-start.12) | collective-permute-done | bytes 81952 | tf_op jit(solution)/shard_map/ppermute | solution.py:388
  112.6 3.8 %collective-permute-done.16 = f32[160,128]{1,0:T(8,128)S(1)} collective-permute-done((f32[160,128]{1,0:T(8,128)S(1)}, f32[160,128]{1,0:T(8,128)S(1)}, u32[]{:S(2)}, u32[]{:S(2)}) %collective-permute-start.16) | collective-permute-done | bytes 81952 | tf_op jit(solution)/shard_map/ppermute | solution.py:380
  120.6 2.5 %collective-permute-done.19 = f32[160,128]{1,0:T(8,128)S(1)} collective-permute-done((f32[160,128]{1,0:T(8,128)S(1)}, f32[160,128]{1,0:T(8,128)S(1)}, u32[]{:S(2)}, u32[]{:S(2)}) %collective-permute-start.19) | collective-permute-done | bytes 81952 | tf_op jit(solution)/shard_map/ppermute | solution.py:388
  124.9 3.2 %collective-permute-start.21 = (f32[4,160,128]{2,1,0:T(8,128)S(1)}, f32[4,160,128]{2,1,0:T(8,128)S(1)}, u32[]{:S(2)}, u32[]{:S(2)}) collective-permute-start(f32[4,160,128]{2,1,0:T(8,128)S(1)} %get-tuple-element.58), channel_id=1, source_target_pairs={{0,8},{8,16},{16,24},{24,0},{32,40},{40,48},{48,56},{56,32},{64,72... | collective-permute-start | bytes 983048 | tf_op jit(solution)/shard_map/ppermute | solution.py:384
  129.0 2.6 %collective-permute-done.22 = f32[4,160,128]{2,1,0:T(8,128)S(1)} collective-permute-done((f32[4,160,128]{2,1,0:T(8,128)S(1)}, f32[4,160,128]{2,1,0:T(8,128)S(1)}, u32[]{:S(2)}, u32[]{:S(2)}) %collective-permute-start.22) | collective-permute-done | bytes 327712 | tf_op jit(solution)/shard_map/ppermute | solution.py:384
  131.6 7.7 %collective-permute-done.21 = f32[4,160,128]{2,1,0:T(8,128)S(1)} collective-permute-done((f32[4,160,128]{2,1,0:T(8,128)S(1)}, f32[4,160,128]{2,1,0:T(8,128)S(1)}, u32[]{:S(2)}, u32[]{:S(2)}) %collective-permute-start.21) | collective-permute-done | bytes 327712 | tf_op jit(solution)/shard_map/ppermute | solution.py:384
  140.2 4.1 %collective-permute-start.24 = (f32[16,160,128]{2,1,0:T(8,128)S(1)}, f32[16,160,128]{2,1,0:T(8,128)S(1)}, u32[]{:S(2)}, u32[]{:S(2)}) collective-permute-start(f32[16,160,128]{2,1,0:T(8,128)S(1)} %bitcast.29), channel_id=1, source_target_pairs={{0,1},{1,0},{2,3},{3,2},{4,5},{5,4},{6,7},{7,6},{8,9},{9,8},{10,11... | collective-permute-start | bytes 3932168 | tf_op jit(solution)/shard_map/ppermute | solution.py:376
  144.3 2.7 %collective-permute-done.24.theirs_ref = f32[16,160,128]{2,1,0:T(8,128)S(1)} collective-permute-done((f32[16,160,128]{2,1,0:T(8,128)S(1)}, f32[16,160,128]{2,1,0:T(8,128)S(1)}, u32[]{:S(2)}, u32[]{:S(2)}) %collective-permute-start.24) | collective-permute-done | bytes 1310752 | tf_op jit(solution)/shard_map/ppermute | solution.py:376
  146.9 5.0 %normed.1 = (bf16[1024,1024]{1,0:T(8,128)(2,1)S(1)}, bf16[1024,1024]{1,0:T(8,128)(2,1)S(1)}, bf16[512,1024]{1,0:T(8,128)(2,1)S(1)}, bf16[512,1024]{1,0:T(8,128)(2,1)S(1)}, f32[8,128]{1,0:T(8,128)S(1)}) custom-call(s32[4]{0:T(128)S(1)} %pad_add_fusion.at_ref, f32[16,160,128]{2,1,0:T(8,128)S(1)} %bitcast.30, ...), custom_call_target="tpu_custom_call" | custom-call | tf_op jit(solution)/shard_map/normed/pallas_call | solution.py:173
  155.7 3.0 %collective-permute-start.26 = (f32[2,512,128]{2,1,0:T(8,128)S(1)}, f32[2,512,128]{2,1,0:T(8,128)S(1)}, u32[]{:S(2)}, u32[]{:S(2)}) collective-permute-start(f32[2,512,128]{2,1,0:T(8,128)S(1)} %turned2.1), channel_id=1, source_target_pairs={{0,4},{1,5},{2,6},{3,7},{4,0},{5,1},{6,2},{7,3},{8,12},{9,13},{10,... | collective-permute-start | bytes 1572872 | tf_op jit(solution)/shard_map/ppermute | solution.py:380
  161.8 6.1 %collective-permute-done.25.refs_1_ = f32[2,512,128]{2,1,0:T(8,128)S(1)} collective-permute-done((f32[2,512,128]{2,1,0:T(8,128)S(1)}, f32[2,512,128]{2,1,0:T(8,128)S(1)}, u32[]{:S(2)}, u32[]{:S(2)}) %collective-permute-start.25) | collective-permute-done | bytes 524320 | tf_op jit(solution)/shard_map/ppermute | solution.py:380
  168.0 11.9 %collective-permute-done.26.refs_2_ = f32[2,512,128]{2,1,0:T(8,128)S(1)} collective-permute-done((f32[2,512,128]{2,1,0:T(8,128)S(1)}, f32[2,512,128]{2,1,0:T(8,128)S(1)}, u32[]{:S(2)}, u32[]{:S(2)}) %collective-permute-start.26) | collective-permute-done | bytes 524320 | tf_op jit(solution)/shard_map/ppermute | solution.py:380
  (65 shorter events, 49.1 us)
Async XLA Ops:
  1.1 24.8 %collective-permute-start = (f32[2,256,128]{2,1,0:T(8,128)S(1)}, f32[2,256,128]{2,1,0:T(8,128)S(1)}, u32[]{:S(2)}, u32[]{:S(2)}) collective-permute-start(f32[2,256,128]{2,1,0:T(8,128)S(1)} %bitcast.39), channel_id=1, source_target_pairs={{0,8},{8,16},{16,24},{24,32},{32,40},{40,48},{48,56},{56,64},{64,7... | collective-permute-start | bytes 786440 | tf_op jit(solution)/shard_map/ppermute | solution.py:400
  3.2 22.7 %collective-permute-start.1 = (f32[2,256,128]{2,1,0:T(8,128)S(1)}, f32[2,256,128]{2,1,0:T(8,128)S(1)}, u32[]{:S(2)}, u32[]{:S(2)}) collective-permute-start(f32[2,256,128]{2,1,0:T(8,128)S(1)} %bitcast.38), channel_id=1, source_target_pairs={{8,0},{16,8},{24,16},{32,24},{40,32},{48,40},{56,48},{64,56},{72,6... | collective-permute-start | bytes 786440 | tf_op jit(solution)/shard_map/ppermute | solution.py:400
  27.6 7.1 %collective-permute-start.3 = (f32[2,256,128]{2,1,0:T(8,128)S(1)}, f32[2,256,128]{2,1,0:T(8,128)S(1)}, u32[]{:S(2)}, u32[]{:S(2)}) collective-permute-start(f32[2,256,128]{2,1,0:T(8,128)S(1)} %get-tuple-element.32.low_ref), channel_id=1, source_target_pairs={{8,0},{16,8},{24,16},{32,24},{40,32},{48,40},{56,48},{64,56},{72,6... | collective-permute-start | bytes 786440 | tf_op jit(solution)/shard_map/ppermute | solution.py:400
  29.1 9.7 %collective-permute-start.2 = (f32[2,256,128]{2,1,0:T(8,128)S(1)}, f32[2,256,128]{2,1,0:T(8,128)S(1)}, u32[]{:S(2)}, u32[]{:S(2)}) collective-permute-start(f32[2,256,128]{2,1,0:T(8,128)S(1)} %get-tuple-element.33.high_ref), channel_id=1, source_target_pairs={{0,8},{8,16},{16,24},{24,32},{32,40},{40,48},{48,56},{56,64},{64,7... | collective-permute-start | bytes 786440 | tf_op jit(solution)/shard_map/ppermute | solution.py:400
  43.6 4.7 %collective-permute-start.4 = (f32[4,512,128]{2,1,0:T(8,128)S(1)}, f32[4,512,128]{2,1,0:T(8,128)S(1)}, u32[]{:S(2)}, u32[]{:S(2)}) collective-permute-start(f32[4,512,128]{2,1,0:T(8,128)S(1)} %bitcast.33), channel_id=1, source_target_pairs={{0,1},{1,0},{2,3},{3,2},{4,5},{5,4},{6,7},{7,6},{8,9},{9,8},{10,11... | collective-permute-start | bytes 3145736 | tf_op jit(solution)/shard_map/ppermute | solution.py:376
  49.1 15.8 %collective-permute-start.5 = (f32[2,512,128]{2,1,0:T(8,128)S(1)}, f32[2,512,128]{2,1,0:T(8,128)S(1)}, u32[]{:S(2)}, u32[]{:S(2)}) collective-permute-start(f32[2,512,128]{2,1,0:T(8,128)S(1)} %get-tuple-element.35), channel_id=1, source_target_pairs={{0,2},{1,3},{2,4},{3,5},{4,6},{5,7},{6,0},{7,1},{8,10},{9,11},{10,... | collective-permute-start | bytes 1572872 | tf_op jit(solution)/shard_map/ppermute | solution.py:380
  50.8 26.2 %collective-permute-start.6 = (f32[2,512,128]{2,1,0:T(8,128)S(1)}, f32[2,512,128]{2,1,0:T(8,128)S(1)}, u32[]{:S(2)}, u32[]{:S(2)}) collective-permute-start(f32[2,512,128]{2,1,0:T(8,128)S(1)} %get-tuple-element.36), channel_id=1, source_target_pairs={{0,4},{1,5},{2,6},{3,7},{4,0},{5,1},{6,2},{7,3},{8,12},{9,13},{10,... | collective-permute-start | bytes 1572872 | tf_op jit(solution)/shard_map/ppermute | solution.py:380
  54.1 22.9 %collective-permute-start.7 = (f32[2,512,128]{2,1,0:T(8,128)S(1)}, f32[2,512,128]{2,1,0:T(8,128)S(1)}, u32[]{:S(2)}, u32[]{:S(2)}) collective-permute-start(f32[2,512,128]{2,1,0:T(8,128)S(1)} %get-tuple-element.37), channel_id=1, source_target_pairs={{0,6},{1,7},{2,0},{3,1},{4,2},{5,3},{6,4},{7,5},{8,14},{9,15},{10,... | collective-permute-start | bytes 1572872 | tf_op jit(solution)/shard_map/ppermute | solution.py:380
  84.5 17.2 %collective-permute-start.9 = (f32[640,128]{1,0:T(8,128)S(1)}, f32[640,128]{1,0:T(8,128)S(1)}, u32[]{:S(2)}, u32[]{:S(2)}) collective-permute-start(f32[640,128]{1,0:T(8,128)S(1)} %get-tuple-element.43), channel_id=1, source_target_pairs={{0,8},{8,16},{16,24},{24,0},{32,40},{40,48},{48,56},{56,32},{64,72... | collective-permute-start | bytes 983048 | tf_op jit(solution)/shard_map/ppermute | solution.py:384
  84.6 17.1 %collective-permute-start.10 = (f32[640,128]{1,0:T(8,128)S(1)}, f32[640,128]{1,0:T(8,128)S(1)}, u32[]{:S(2)}, u32[]{:S(2)}) collective-permute-start(f32[640,128]{1,0:T(8,128)S(1)} %get-tuple-element.44), channel_id=1, source_target_pairs={{0,16},{8,24},{16,0},{24,8},{32,48},{40,56},{48,32},{56,40},{64,80... | collective-permute-start | bytes 983048 | tf_op jit(solution)/shard_map/ppermute | solution.py:384
  84.7 17.4 %collective-permute-start.11 = (f32[640,128]{1,0:T(8,128)S(1)}, f32[640,128]{1,0:T(8,128)S(1)}, u32[]{:S(2)}, u32[]{:S(2)}) collective-permute-start(f32[640,128]{1,0:T(8,128)S(1)} %get-tuple-element.45), channel_id=1, source_target_pairs={{0,24},{8,0},{16,8},{24,16},{32,56},{40,32},{48,40},{56,48},{64,88... | collective-permute-start | bytes 983048 | tf_op jit(solution)/shard_map/ppermute | solution.py:384
  102.7 5.4 %collective-permute-start.12 = (f32[160,128]{1,0:T(8,128)S(1)}, f32[160,128]{1,0:T(8,128)S(1)}, u32[]{:S(2)}, u32[]{:S(2)}) collective-permute-start(f32[160,128]{1,0:T(8,128)S(1)} %get-tuple-element.47), channel_id=1, source_target_pairs={{0,32},{8,40},{16,48},{24,56},{32,64},{40,72},{48,80},{56,88},{64,... | collective-permute-start | bytes 245768 | tf_op jit(solution)/shard_map/ppermute | solution.py:388
  102.8 5.4 %collective-permute-start.13 = (f32[160,128]{1,0:T(8,128)S(1)}, f32[160,128]{1,0:T(8,128)S(1)}, u32[]{:S(2)}, u32[]{:S(2)}) collective-permute-start(f32[160,128]{1,0:T(8,128)S(1)} %get-tuple-element.48), channel_id=1, source_target_pairs={{0,64},{8,72},{16,80},{24,88},{32,96},{40,104},{48,112},{56,120},{... | collective-permute-start | bytes 245768 | tf_op jit(solution)/shard_map/ppermute | solution.py:388
  103.2 5.8 %collective-permute-start.14 = (f32[160,128]{1,0:T(8,128)S(1)}, f32[160,128]{1,0:T(8,128)S(1)}, u32[]{:S(2)}, u32[]{:S(2)}) collective-permute-start(f32[160,128]{1,0:T(8,128)S(1)} %get-tuple-element.49), channel_id=1, source_target_pairs={{0,96},{8,104},{16,112},{24,120},{32,0},{40,8},{48,16},{56,24},{64... | collective-permute-start | bytes 245768 | tf_op jit(solution)/shard_map/ppermute | solution.py:388
  111.0 5.4 %collective-permute-start.16 = (f32[160,128]{1,0:T(8,128)S(1)}, f32[160,128]{1,0:T(8,128)S(1)}, u32[]{:S(2)}, u32[]{:S(2)}) collective-permute-start(f32[160,128]{1,0:T(8,128)S(1)} %add_add_fusion.1), channel_id=1, source_target_pairs={{0,2},{1,3},{2,4},{3,5},{4,6},{5,7},{6,0},{7,1},{8,10},{9,11},{10,... | collective-permute-start | bytes 245768 | tf_op jit(solution)/shard_map/ppermute | solution.py:380
  111.0 5.4 %collective-permute-start.15 = (f32[160,128]{1,0:T(8,128)S(1)}, f32[160,128]{1,0:T(8,128)S(1)}, u32[]{:S(2)}, u32[]{:S(2)}) collective-permute-start(f32[160,128]{1,0:T(8,128)S(1)} %add_add_fusion.1), channel_id=1, source_target_pairs={{0,4},{1,5},{2,6},{3,7},{4,0},{5,1},{6,2},{7,3},{8,12},{9,13},{10,... | collective-permute-start | bytes 245768 | tf_op jit(solution)/shard_map/ppermute | solution.py:380
  118.3 4.8 %collective-permute-start.19 = (f32[160,128]{1,0:T(8,128)S(1)}, f32[160,128]{1,0:T(8,128)S(1)}, u32[]{:S(2)}, u32[]{:S(2)}) collective-permute-start(f32[160,128]{1,0:T(8,128)S(1)} %add_add_fusion), channel_id=1, source_target_pairs={{0,64},{8,72},{16,80},{24,88},{32,96},{40,104},{48,112},{56,120},{... | collective-permute-start | bytes 245768 | tf_op jit(solution)/shard_map/ppermute | solution.py:388
  124.0 7.6 %collective-permute-start.22 = (f32[4,160,128]{2,1,0:T(8,128)S(1)}, f32[4,160,128]{2,1,0:T(8,128)S(1)}, u32[]{:S(2)}, u32[]{:S(2)}) collective-permute-start(f32[4,160,128]{2,1,0:T(8,128)S(1)} %get-tuple-element.58), channel_id=1, source_target_pairs={{0,16},{8,24},{16,0},{24,8},{32,48},{40,56},{48,32},{56,40},{64,80... | collective-permute-start | bytes 983048 | tf_op jit(solution)/shard_map/ppermute | solution.py:384
  124.9 14.4 %collective-permute-start.21 = (f32[4,160,128]{2,1,0:T(8,128)S(1)}, f32[4,160,128]{2,1,0:T(8,128)S(1)}, u32[]{:S(2)}, u32[]{:S(2)}) collective-permute-start(f32[4,160,128]{2,1,0:T(8,128)S(1)} %get-tuple-element.58), channel_id=1, source_target_pairs={{0,8},{8,16},{16,24},{24,0},{32,40},{40,48},{48,56},{56,32},{64,72... | collective-permute-start | bytes 983048 | tf_op jit(solution)/shard_map/ppermute | solution.py:384
  128.1 11.9 %collective-permute-start.23 = (f32[4,160,128]{2,1,0:T(8,128)S(1)}, f32[4,160,128]{2,1,0:T(8,128)S(1)}, u32[]{:S(2)}, u32[]{:S(2)}) collective-permute-start(f32[4,160,128]{2,1,0:T(8,128)S(1)} %get-tuple-element.58), channel_id=1, source_target_pairs={{0,24},{8,0},{16,8},{24,16},{32,56},{40,32},{48,40},{56,48},{64,88... | collective-permute-start | bytes 983048 | tf_op jit(solution)/shard_map/ppermute | solution.py:384
  140.2 6.8 %collective-permute-start.24 = (f32[16,160,128]{2,1,0:T(8,128)S(1)}, f32[16,160,128]{2,1,0:T(8,128)S(1)}, u32[]{:S(2)}, u32[]{:S(2)}) collective-permute-start(f32[16,160,128]{2,1,0:T(8,128)S(1)} %bitcast.29), channel_id=1, source_target_pairs={{0,1},{1,0},{2,3},{3,2},{4,5},{5,4},{6,7},{7,6},{8,9},{9,8},{10,11... | collective-permute-start | bytes 3932168 | tf_op jit(solution)/shard_map/ppermute | solution.py:376
  153.6 14.4 %collective-permute-start.25 = (f32[2,512,128]{2,1,0:T(8,128)S(1)}, f32[2,512,128]{2,1,0:T(8,128)S(1)}, u32[]{:S(2)}, u32[]{:S(2)}) collective-permute-start(f32[2,512,128]{2,1,0:T(8,128)S(1)} %turned1.1), channel_id=1, source_target_pairs={{0,2},{1,3},{2,4},{3,5},{4,6},{5,7},{6,0},{7,1},{8,10},{9,11},{10,... | collective-permute-start | bytes 1572872 | tf_op jit(solution)/shard_map/ppermute | solution.py:380
  155.7 24.2 %collective-permute-start.26 = (f32[2,512,128]{2,1,0:T(8,128)S(1)}, f32[2,512,128]{2,1,0:T(8,128)S(1)}, u32[]{:S(2)}, u32[]{:S(2)}) collective-permute-start(f32[2,512,128]{2,1,0:T(8,128)S(1)} %turned2.1), channel_id=1, source_target_pairs={{0,4},{1,5},{2,6},{3,7},{4,0},{5,1},{6,2},{7,3},{8,12},{9,13},{10,... | collective-permute-start | bytes 1572872 | tf_op jit(solution)/shard_map/ppermute | solution.py:380
  160.2 21.0 %collective-permute-start.27 = (f32[2,512,128]{2,1,0:T(8,128)S(1)}, f32[2,512,128]{2,1,0:T(8,128)S(1)}, u32[]{:S(2)}, u32[]{:S(2)}) collective-permute-start(f32[2,512,128]{2,1,0:T(8,128)S(1)} %turned3.1), channel_id=1, source_target_pairs={{0,6},{1,7},{2,0},{3,1},{4,2},{5,3},{6,4},{7,5},{8,14},{9,15},{10,... | collective-permute-start | bytes 1572872 | tf_op jit(solution)/shard_map/ppermute | solution.py:380
  (7 other events, 22.3 us)

commit v4 on v3

--- a/solution.py
+++ b/solution.py
@@ -5,6 +5,7 @@
 from jax.experimental import pallas as pl
 from jax.experimental.pallas import tpu as pltpu
 from jax.sharding import PartitionSpec as P
+
 
 VECTORS = 1024
 REACH = 2
@@ -15,6 +16,7 @@
 RING = 8
 BUILD_LIMIT = 26 << 20
 STEP_LIMIT = 16 << 20
+OPERATOR_LIMIT = 8 << 20
 TURN_LIMIT = 32 << 20
 F32 = jnp.float32
 BF16 = jnp.bfloat16
@@ -118,11 +120,8 @@
         out_ref[at % REACH] = first_of(apply_one(op_ref, wide_ref, elem), own_ref[elem])
 
 
-def side_of(elem, count, c):
-    return lax.rem(elem // (count // 2) + c, 2), lax.rem(elem, count // 2)
-
-
-def second_edge_kernel(count, at_ref, op_ref, mid_ref, low_ref, high_ref, before_ref, after_ref, base_ref, _, out_ref, wide_ref, made_ref, sem):
+def second_edge_kernel(count, at_ref, op_ref, mid_ref, low_ref, high_ref, before_ref, after_ref, base_ref, done_ref, *refs):
+    own_refs, (other_ref, wide_ref, all_ref) = refs[:4], refs[4:]
     for r in range(REACH):
         spread(wide_ref, r, before_ref[r])
         spread(wide_ref, REACH + r, low_ref[r])
@@ -130,18 +129,21 @@
         spread(wide_ref, count - REACH + r, mid_ref[count - 3 * REACH + r])
         spread(wide_ref, count + r, high_ref[r])
         spread(wide_ref, REACH + count + r, after_ref[r])
-    copies = []
     for at, elem in enumerate(edges_of(count)):
         own = (low_ref if at < REACH else high_ref)[at % REACH]
-        made_ref[at] = second_of(apply_one(op_ref, wide_ref, elem), own, base_ref[elem])
-        side, place = side_of(elem, count, at_ref[3])
-        copies.append(pltpu.make_async_copy(made_ref.at[at], out_ref.at[side, place], sem.at[at]))
-        copies[-1].start()
-    for copy in copies:
-        copy.wait()
-
-
-def inner_kernel(count, at_ref, op_ref, mid_ref, low_ref, high_ref, base_ref, out_ref, wide_ref):
+        all_ref[elem] = second_of(apply_one(op_ref, wide_ref, elem), own, base_ref[elem])
+    for at in range(count - 2 * REACH):
+        all_ref[REACH + at] = done_ref[at]
+    z, c = at_ref[2], at_ref[3]
+    half = count // 2
+    for k in range(4):
+        chip = lax.rem(z + k, 4)
+        for r in range(2):
+            other_ref[k, r * 256 : (r + 1) * 256] = all_ref[(1 - c) * half + chip * 2 + r]
+            own_refs[k][r * 256 : (r + 1) * 256] = all_ref[c * half + chip * 2 + r]
+
+
+def inner_kernel(count, op_ref, mid_ref, low_ref, high_ref, base_ref, out_ref, wide_ref):
     for r in range(REACH):
         spread(wide_ref, REACH + r, low_ref[r])
         spread(wide_ref, count + r, high_ref[r])
@@ -152,8 +154,7 @@
         for u in range(4):
             at = 4 * g + u
             elem = REACH + at
-            side, place = side_of(elem, count, at_ref[3])
-            out_ref[side, place] = second_of(apply_one(op_ref, wide_ref, elem), mid_ref[at], base_ref[elem])
+            out_ref[at] = second_of(apply_one(op_ref, wide_ref, elem), mid_ref[at], base_ref[elem])
         return 0
 
     lax.fori_loop(0, (count - 2 * REACH) // 4, body, 0)
@@ -169,7 +170,7 @@
     return jax.ShapeDtypeStruct(shape, dtype)
 
 
-def call(kernel, name, outs, specs, scratch, args, limit, **kwargs):
+def call(kernel, outs, specs, scratch, args, limit, **kwargs):
     return pl.pallas_call(
         kernel,
         out_shape=outs,
@@ -177,7 +178,6 @@
         out_specs=kwargs.pop("out_specs", jax.tree.map(lambda _: VMEM_SPEC, outs)),
         scratch_shapes=scratch,
         compiler_params=pltpu.CompilerParams(vmem_limit_bytes=limit),
-        name=name,
         **kwargs,
     )(*args)
 
@@ -190,7 +190,6 @@
     count = own.shape[0]
     return call(
         functools.partial(build_kernel, count),
-        "build",
         (shaped(count - 2 * REACH, 256, 128), shaped(count, 512, SPAN * 256, dtype=BF16)),
         [SMEM_SPEC, SMEM_SPEC, HBM_SPEC, HBM_SPEC],
         [
@@ -210,36 +209,41 @@
     count = own.shape[0]
     edge = shaped(REACH, 256, 128)
     return call(
-        functools.partial(first_edge_kernel, count), "edges1", (edge, edge), [VMEM_SPEC] * 4,
-        [wide_scratch(count)], (op, own, *halos), STEP_LIMIT,
-    )
-
-
-def second_inner(here, op, mid, low, high, base):
+        functools.partial(first_edge_kernel, count), (edge, edge), [VMEM_SPEC] * 4,
+        [wide_scratch(count)], (op, own, *halos), OPERATOR_LIMIT,
+    )
+
+
+def second_inner(op, mid, low, high, base):
     count = base.shape[0]
     return call(
-        functools.partial(inner_kernel, count), "inner", shaped(2, count // 2, 256, 128), [SMEM_SPEC] + [VMEM_SPEC] * 5,
-        [wide_scratch(count)], (here, op, mid, low, high, base), STEP_LIMIT,
-    )
-
-
-def second_edges(here, op, mid, low, high, halos, base, into):
+        functools.partial(inner_kernel, count), shaped(*mid.shape), [VMEM_SPEC] * 5,
+        [wide_scratch(count)], (op, mid, low, high, base), OPERATOR_LIMIT,
+    )
+
+
+def second_edges(here, op, mid, low, high, halos, base, done):
     count = base.shape[0]
-    return call(
-        functools.partial(second_edge_kernel, count), "edges2", shaped(*into.shape),
-        [SMEM_SPEC] + [VMEM_SPEC] * 7 + [ANY_SPEC],
-        [wide_scratch(count), pltpu.VMEM((2 * REACH, 256, 128), F32), pltpu.SemaphoreType.DMA((2 * REACH,))],
-        (here, op, mid, low, high, *halos, base, into), STEP_LIMIT,
-        out_specs=ANY_SPEC, input_output_aliases={8: 0},
-    )
-
-
-def pair_kernel(at_ref, both_ref, got_ref, *out_refs):
-    z = at_ref[2]
-    for k in range(4):
-        chip = lax.rem(z + k, 4)
-        out_refs[k][0] = both_ref[0, chip]
-        out_refs[k][1] = got_ref[chip]
+    chunk = shaped(512, 128)
+    outs = call(
+        functools.partial(second_edge_kernel, count), (chunk,) * 4 + (shaped(4, 512, 128),),
+        [SMEM_SPEC] + [VMEM_SPEC] * 8,
+        [wide_scratch(count), pltpu.VMEM(base.shape, F32)],
+        (here, op, mid, low, high, *halos, base, done), OPERATOR_LIMIT,
+    )
+    return outs[:4], outs[4]
+
+
+def bulk_kernel(*refs):
+    own_refs, got_ref, out_refs = refs[:4], refs[4], refs[5:]
+    for k in range(1, 4):
+        for i, m in enumerate(chunks_for(k)):
+            out_refs[k - 1][i, 0] = own_refs[m][...]
+            out_refs[k - 1][i, 1] = got_ref[m]
+
+
+def chunks_for(k):
+    return [m for m in range(4) if m != k]
 
 
 def share_kernel(axis, count, at_ref, *refs):
@@ -258,7 +262,7 @@
     size, panel = arrays[0].shape
     part = shaped(size // 4, panel)
     outs = call(
-        functools.partial(share_kernel, axis, len(arrays)), f"share{axis}", (part,) * 4,
+        functools.partial(share_kernel, axis, len(arrays)), (part,) * 4,
         [SMEM_SPEC] + [VMEM_SPEC] * len(arrays), [pltpu.VMEM((size, panel), F32)], (here, *arrays), STEP_LIMIT,
     )
     got = {k: shift(outs[k], k) for k in SHIFTS}
@@ -283,14 +287,12 @@
 
 
 def gram_send_kernel(at_ref, *refs):
-    parts, (rows_ref, hi_ref, lo_ref, out_ref) = refs[:4], refs[4:]
+    owns, gots, (hi_ref, lo_ref, out_ref) = refs[:4], refs[4:8], refs[8:]
     z, c = at_ref[2], at_ref[3]
     for k in range(4):
         for j in range(2):
             band = lax.rem(z + 4 - k, 4) * 2 + lax.rem(c + j, 2)
-            value = parts[k][j]
-            rows_ref[band] = value
-            hi, lo = split(value)
+            hi, lo = split((owns, gots)[j][k][...])
             hi_ref[:, lanes(band * 128, 128)] = hi
             lo_ref[:, lanes(band * 128, 128)] = lo
     half_of_gram(1 - c, hi_ref, lo_ref, out_ref)
@@ -304,14 +306,14 @@
     return dot(jnp.concatenate([hi, hi, lo], axis=1), jnp.concatenate([nh, nl, nh], axis=0))
 
 
-def normed_kernel(order, at_ref, mine_ref, theirs_ref, rows_ref, hi_ref, lo_ref, nh_ref, nl_ref, gh_ref, gl_ref, stretch_ref, gram_ref, y_ref):
-    x, y, c = at_ref[0], at_ref[1], at_ref[3]
-    for kx in range(4):
-        for ky in range(4):
-            piece = lax.rem(x + 4 - kx, 4) * 4 + lax.rem(y + 4 - ky, 4)
+def poly_kernel(order, at_ref, mine_ref, theirs_ref, ph_ref, pl_ref, stretch_ref, gram_ref, nh_ref, nl_ref, poly_ref):
+    x, y, z, c = at_ref[0], at_ref[1], at_ref[2], at_ref[3]
+    for ky in range(4):
+        for kx in range(4):
+            piece = lax.rem(y + 4 - ky, 4) * 4 + lax.rem(x + 4 - kx, 4)
             rows = pl.ds(pl.multiple_of(piece * 160, 160), 160)
-            gram_ref[c, rows] = mine_ref[kx * 4 + ky]
-            gram_ref[1 - c, rows] = theirs_ref[kx * 4 + ky]
+            gram_ref[c, rows] = mine_ref[ky * 4 + kx]
+            gram_ref[1 - c, rows] = theirs_ref[ky * 4 + kx]
 
     def packed(n, h):
         at = 2 * (n % 5) + h
@@ -334,34 +336,61 @@
             if i != j:
                 nh_ref[at : at + 128, i * TILE : (i + 1) * TILE] = hi.T
                 nl_ref[at : at + 128, i * TILE : (i + 1) * TILE] = lo.T
-    for j in range(4):
-        cols = slice(j * TILE, (j + 1) * TILE)
-        y_ref[:, cols] = times_normed(hi_ref[...], lo_ref[...], nh_ref[:, cols], nl_ref[:, cols])
-    for b in range(8):
-        cols = slice(b * 128, (b + 1) * 128)
-        hi, lo = split(3.0 * y_ref[:, cols] - 10.0 * rows_ref[b])
-        gh_ref[:, cols] = hi
-        gl_ref[:, cols] = lo
     stretch_ref[...] = jnp.sqrt(jnp.full((8, 128), order, F32) / scale)
-
-
-def turned_kernel(k, at_ref, rows_ref, gh_ref, gl_ref, nh_ref, nl_ref, stretch_ref, out_ref):
-    z, c = at_ref[2], at_ref[3]
-    chip = lax.rem(z + k, 4)
-    cols = lanes(chip * TILE, TILE)
-    prod = times_normed(gh_ref[...], gl_ref[...], nh_ref[:, cols], nl_ref[:, cols])
+    right = []
     for j in range(2):
-        part = 15.0 * rows_ref[2 * chip + j] + prod[:, j * 128 : (j + 1) * 128]
-        out_ref[lax.rem(c + j, 2)] = part / 8.0 * stretch_ref[0:1]
-
-
-def place_kernel(at_ref, *refs):
-    parts, got_ref, out_ref, sem = refs[:4], refs[4], refs[5], refs[6]
+        band = lanes((2 * z + lax.rem(c + j, 2)) * 128, 128)
+        right.append((nh_ref[:, band], nl_ref[:, band]))
+    nh = jnp.concatenate([right[0][0], right[1][0]], axis=1)
+    nl = jnp.concatenate([right[0][1], right[1][1]], axis=1)
+    squared = times_normed(nh_ref[...], nl_ref[...], nh, nl)
+    poly_ref[...] = 3.0 * squared - 10.0 * (nh.astype(F32) + nl.astype(F32))
+    for q in range(4):
+        for j in range(2):
+            band = lax.rem(z + q, 4) * 2 + lax.rem(c + j, 2)
+            part = poly_ref[pl.ds(pl.multiple_of(band * 128, 128), 128)]
+            if q == 0:
+                r = lax.broadcasted_iota(jnp.int32, (128, 256), 0)
+                l = lax.broadcasted_iota(jnp.int32, (128, 256), 1)
+                part = part + jnp.where(l == r + 128 * j, 15.0, 0.0)
+            hi, lo = split(part / 8.0)
+            at = q * 256 + j * 128
+            ph_ref[at : at + 128] = hi
+            pl_ref[at : at + 128] = lo
+
+
+def turned_kernel(*refs):
+    owns, got_ref, part_owns, part_gots, bulks = refs[:4], refs[4], refs[5:8], refs[8:11], refs[11:14]
+    ph_ref, pl_ref, stretch_ref, mine_ref, theirs_ref = refs[14:]
+
+    def piece(r, q, j):
+        k = (4 - q) % 4
+        if q == 0:
+            return owns[r][...] if j == 0 else got_ref[r]
+        if r == 0:
+            return (part_owns, part_gots)[j][k - 1][...]
+        return bulks[k - 1][chunks_for(k).index((r + k) % 4), j]
+
+    ph, low = ph_ref[...], pl_ref[...]
+    for r in range(4):
+        highs, lows = [], []
+        for q in range(4):
+            for j in range(2):
+                hi, lo = split(piece(r, q, j))
+                highs.append(hi)
+                lows.append(lo)
+        out = times_normed(jnp.concatenate(highs, axis=1), jnp.concatenate(lows, axis=1), ph, low)
+        stretch = stretch_ref[0:1]
+        mine_ref[r] = out[:, :128] * stretch
+        theirs_ref[r] = out[:, 128:] * stretch
+
+
+def place_kernel(at_ref, mine_ref, got_ref, out_ref, sem):
     z, c = at_ref[2], at_ref[3]
     copies = []
     for k in range(4):
-        chip = lax.rem(z + 4 - k, 4)
-        copies.append(pltpu.make_async_copy(parts[k].at[0], out_ref.at[c * 4 + chip], sem.at[k]))
+        chip = lax.rem(z + k, 4)
+        copies.append(pltpu.make_async_copy(mine_ref.at[k], out_ref.at[c * 4 + chip], sem.at[k]))
         copies.append(pltpu.make_async_copy(got_ref.at[k], out_ref.at[(1 - c) * 4 + chip], sem.at[4 + k]))
     for copy in copies:
         copy.start()
@@ -400,7 +429,7 @@
     return lax.ppermute(last, "space", up), lax.ppermute(first, "space", down)
 
 
-def per_device(vectors, blocks, neighbours):
+def steps(vectors, blocks, neighbours):
     elem_dev, basis = blocks.shape[0], blocks.shape[2]
     panel = vectors.shape[1]
     order = float(elem_dev * basis * lax.axis_size("space"))
@@ -413,59 +442,67 @@
     mid, op = build_operator(neighbours.T, here, blocks, start)
     low, high = first_edges(op, start, halos)
     halos = halos_of(low, high)
-    field = second_inner(here, op, mid, low, high, start)
-    field = second_edges(here, op, mid, low, high, halos, start, field)
+    done = second_inner(op, mid, low, high, start)
+    own, other = second_edges(here, op, mid, low, high, halos, start, done)
 
     share = elem_dev * basis // 8
-    both = field.reshape(2, 4, share, panel)
-    got = swap_cores(both[1])
-    pairs = call(
-        pair_kernel, "pair", (shaped(2, share, panel),) * 4, [SMEM_SPEC] + [VMEM_SPEC] * 2, [], (here, both, got), STEP_LIMIT
-    )
-    parts = {k: shift_z(pairs[k], k) for k in SHIFTS}
-    parts[0] = pairs[0]
+    got = swap_cores(other)
+    part_own = {k: shift_z(own[k], k) for k in SHIFTS}
+    part_got = {k: shift_z(got[k], k) for k in SHIFTS}
+    part_own[0], part_got[0] = own[0], got[0]
+    part_own = [part_own[k] for k in range(4)]
+    part_got = [part_got[k] for k in range(4)]
+
+    late_own, late_got, part_own, part_got = lax.optimization_barrier((own, got, part_own, part_got))
+    bulks = call(bulk_kernel, (shaped(3, 2, share, panel),) * 3, [VMEM_SPEC] * 5, [], (*late_own, late_got), STEP_LIMIT)
+    sent = []
+    for k in (1, 2, 3):
+        sent.append(shift_z(bulks[k - 1], k))
+    bulks = sent
+
     half = shaped(10, 256, 128)
     wide = shaped(share, VECTORS, dtype=BF16)
-    rows, hi, lo, send = call(
-        gram_send_kernel, "gram1", (shaped(8, share, panel), wide, wide, half), [SMEM_SPEC] + [VMEM_SPEC] * 4, [],
-        (here, *(parts[k] for k in range(4))), STEP_LIMIT,
+    hi, lo, send = call(
+        gram_send_kernel, (wide, wide, half), [SMEM_SPEC] + [VMEM_SPEC] * 8, [],
+        (here, *part_own, *part_got), STEP_LIMIT,
     )
     theirs = swap_cores(send)
-    keep = call(gram_keep_kernel, "gram2", half, [SMEM_SPEC] + [VMEM_SPEC] * 2, [], (here, hi, lo), STEP_LIMIT)
-    pieces = shares(here, 0, shift_x, [keep.reshape(2560, panel), theirs.reshape(2560, panel)])
-    pieces = shares(here, 1, shift_y, pieces)
+    keep = call(gram_keep_kernel, half, [SMEM_SPEC] + [VMEM_SPEC] * 2, [], (here, hi, lo), STEP_LIMIT)
+    pieces = shares(here, 1, shift_y, [keep.reshape(2560, panel), theirs.reshape(2560, panel)])
+    pieces = shares(here, 0, shift_x, pieces)
     piece = (pieces[0] + pieces[1]) + (pieces[2] + pieces[3])
-    got = [shift_z(piece, k) for k in SHIFTS]
-    piece = piece + got[0] + (got[1] + got[2])
-    mine = gathered(gathered(piece, shift_y), shift_x).reshape(16, 160, panel)
+    sums = [shift_z(piece, k) for k in SHIFTS]
+    piece = piece + sums[0] + (sums[1] + sums[2])
+    mine = gathered(gathered(piece, shift_x), shift_y).reshape(16, 160, panel)
     theirs = swap_cores(mine)
 
-    square = shaped(VECTORS, VECTORS, dtype=BF16)
-    nh, nl, gh, gl, stretch = call(
-        functools.partial(normed_kernel, order), "normed", (square, square, wide, wide, shaped(8, 128)),
-        [SMEM_SPEC] + [VMEM_SPEC] * 5, [pltpu.VMEM((2, 2560, 128), F32), pltpu.VMEM((share, VECTORS), F32)],
-        (here, mine, theirs, rows, hi, lo), TURN_LIMIT,
-    )
-    turned = [
-        call(
-            functools.partial(turned_kernel, k), f"turned{k}", shaped(2, share, panel), [SMEM_SPEC] + [VMEM_SPEC] * 6, [],
-            (here, rows, gh, gl, nh, nl, stretch), STEP_LIMIT,
-        )
-        for k in range(4)
-    ]
-    parts = {k: shift_z(turned[k], k) for k in SHIFTS}
-    parts[0] = turned[0]
-    got = swap_cores(jnp.stack([parts[k][1] for k in range(4)]))
+    poly = shaped(VECTORS, TILE, dtype=BF16)
+    ph, low, stretch = call(
+        functools.partial(poly_kernel, order), (poly, poly, shaped(8, 128)), [SMEM_SPEC] + [VMEM_SPEC] * 2,
+        [
+            pltpu.VMEM((2, 2560, 128), F32),
+            pltpu.VMEM((VECTORS, VECTORS), BF16),
+            pltpu.VMEM((VECTORS, VECTORS), BF16),
+            pltpu.VMEM((VECTORS, TILE), F32),
+        ],
+        (here, mine, theirs), TURN_LIMIT,
+    )
+    quarter = shaped(4, share, panel)
+    mine, theirs = call(
+        turned_kernel, (quarter, quarter), [VMEM_SPEC] * 17, [],
+        (*own, got, *part_own[1:], *part_got[1:], *bulks, ph, low, stretch), TURN_LIMIT,
+    )
+    theirs = swap_cores(theirs)
     placed = call(
-        place_kernel, "place", shaped(8, share, panel), [SMEM_SPEC] + [ANY_SPEC] * 5, [pltpu.SemaphoreType.DMA((8,))],
-        (here, *(parts[k] for k in range(4)), got), STEP_LIMIT, out_specs=ANY_SPEC,
+        place_kernel, shaped(8, share, panel), [SMEM_SPEC] + [ANY_SPEC] * 2, [pltpu.SemaphoreType.DMA((8,))],
+        (here, mine, theirs), STEP_LIMIT, out_specs=ANY_SPEC,
     )
     return placed.reshape(elem_dev * basis, panel)
 
 
 def solution(mesh):
     return jax.shard_map(
-        per_device,
+        steps,
         mesh=mesh,
         in_specs=(P("space", "band"), P("space", None, None, None), P("space", None)),
         out_specs=P("space", "band"),

time: 187 us -> 204 us (1.091)
  waiting for transfers between devices: 91.3 us -> 113 us
  Pallas kernels: 48.5 us -> 41.3 us
  starting transfers between devices: 43.2 us -> 46.3 us
    ppermute x9 -> x12, waiting for transfers between devices: 45.3 us -> 73.7 us  [shift_z(): return lax.ppermute(x, 'band', [(i, (i + 2 * k) % 8) for i in range(8)])]
    ppermute x6, waiting for transfers between devices: 25.9 us -> 8.09 us  [shift_x(): lax.ppermute(x, 'space', [(i, i & 12 | i + k & 3) for i in range(16)])]
    ppermute x6, waiting for transfers between devices: 8.09 us -> 20.5 us  [shift_y(): return lax.ppermute(x, 'space', [(i, (i + 4 * k) % 16) for i in range(16)])]
    pallas_call x15 -> x12, Pallas kernels: 48.5 us -> 41.3 us  [call(): pl.pallas_call(kernel, out_shape=outs, in_specs=specs, out_specs=kwargs.p...]
    ppermute x9 -> x12, starting transfers between devices: 12.8 us -> 16.5 us  [shift_z(): return lax.ppermute(x, 'band', [(i, (i + 2 * k) % 8) for i in range(8)])]
    ppermute x4, waiting for transfers between devices: 8.04 us -> 5.76 us  [swap_cores(): return lax.ppermute(x, 'band', [(i, i ^ 1) for i in range(8)])]
    ppermute x6, starting transfers between devices: 5.77 us -> 7.84 us  [shift_y(): return lax.ppermute(x, 'space', [(i, (i + 4 * k) % 16) for i in range(16)])]
  transfers between devices with their start and end apart: 29 -> 32, of which waited for: 21 -> 24; matrix products, arithmetic and copies ran while one was open for 0% -> 0% of each run, Pallas kernels for 15% -> 13%
where the time goes in v4:
time: 204 us
  waiting for transfers between devices  113 us (55%)
  starting transfers between devices  46.3 us (23%)
  Pallas kernels  41.3 us (20%)
  local copies, waits for them, and re-layouts  3.41 us (2%)
    ppermute x12, waiting for transfers between devices, shift_z(): return lax.ppermute(x, 'band', [(i, (i + 2 * k) % 8) for i in range(8)])  73.7 us
    pallas_call x12, Pallas kernels, call(): pl.pallas_call(kernel, out_shape=outs, in_specs=specs, out_specs=kwargs.p...  41.3 us
    ppermute x6, waiting for transfers between devices, shift_y(): return lax.ppermute(x, 'space', [(i, (i + 4 * k) % 16) for i in range(16)])  20.5 us
    ppermute x12, starting transfers between devices, shift_z(): return lax.ppermute(x, 'band', [(i, (i + 2 * k) % 8) for i in range(8)])  16.5 us
    ppermute x4, starting transfers between devices, swap_cores(): return lax.ppermute(x, 'band', [(i, i ^ 1) for i in range(8)])  8.81 us
    ppermute x6, waiting for transfers between devices, shift_x(): lax.ppermute(x, 'space', [(i, i & 12 | i + k & 3) for i in range(16)])  8.09 us
    ppermute x6, starting transfers between devices, shift_y(): return lax.ppermute(x, 'space', [(i, (i + 4 * k) % 16) for i in range(16)])  7.84 us
    ppermute x4, starting transfers between devices, halos_of(): return (lax.ppermute(last, 'space', up), lax.ppermute(first, 'space', down))  7.43 us
  transfers between devices with their start and end apart: 32, of which 24 were waited for; matrix products, arithmetic and copies ran while one was open for 0% of the time, Pallas kernels for 13%

profile of v4, /device:TPU:1, one launch (start us, length us, event | category | flops | bytes accessed | tf_op | source)
XLA Modules:
  0.0 204.2 jit_solution(107206068803276038)
XLA Ops:
  3.2 3.8 %collective-permute-start.1 = (f32[2,256,128]{2,1,0:T(8,128)S(1)}, f32[2,256,128]{2,1,0:T(8,128)S(1)}, u32[]{:S(2)}, u32[]{:S(2)}) collective-permute-start(f32[2,256,128]{2,1,0:T(8,128)S(1)} %bitcast.42), channel_id=1, source_target_pairs={{8,0},{16,8},{24,16},{32,24},{40,32},{48,40},{56,48},{64,56},{72,6... | collective-permute-start | bytes 786440 | tf_op jit(solution)/shard_map/ppermute | solution.py:429
  9.3 16.5 %shard_map.37 = (f32[12,256,128]{2,1,0:T(8,128)S(1)}, bf16[16,512,1280]{2,1,0:T(8,128)(2,1)S(1)}) custom-call(s32[7,16]{1,0:T(8,128)S(1)} %bitcast.37, s32[4]{0:T(128)S(1)} %pad_add_fusion.at_ref, f32[16,7,256,256]{3,2,1,0:T(8,128)} %blocks_ref.1, f32[16,256,128]{2,1,0:T(8,128)S(1)} %bitcast.29), custom_call_target="tpu_custom_call" | custom-call | tf_op jit(solution)/shard_map/pallas_call | solution.py:174
  29.1 5.0 %shard_map.39.done_ref = f32[12,256,128]{2,1,0:T(8,128)S(1)} custom-call(bf16[16,512,1280]{2,1,0:T(8,128)(2,1)S(1)} %get-tuple-element.46.op_ref, f32[12,256,128]{2,1,0:T(8,128)S(1)} %get-tuple-element.47.mid_ref, f32[2,256,128]{2,1,0:T(8,128)S(1)} %get-tuple-element.48.low_ref, f32[2,256,128]{2,1,0:T(8,128)S(1)} %get-tuple-element.49.high_ref, ...), custom_call_target="tpu_custom_call" | custom-call | tf_op jit(solution)/shard_map/pallas_call | solution.py:174
  34.6 4.1 %collective-permute-done.2.before_ref = f32[2,256,128]{2,1,0:T(8,128)S(1)} collective-permute-done((f32[2,256,128]{2,1,0:T(8,128)S(1)}, f32[2,256,128]{2,1,0:T(8,128)S(1)}, u32[]{:S(2)}, u32[]{:S(2)}) %collective-permute-start.2) | collective-permute-done | bytes 262176 | tf_op jit(solution)/shard_map/ppermute | solution.py:429
  45.3 3.3 %collective-permute-start.6 = (f32[512,128]{1,0:T(8,128)S(1)}, f32[512,128]{1,0:T(8,128)S(1)}, u32[]{:S(2)}, u32[]{:S(2)}) collective-permute-start(f32[512,128]{1,0:T(8,128)S(1)} %get-tuple-element.63.refs_2_), channel_id=1, source_target_pairs={{0,4},{1,5},{2,6},{3,7},{4,0},{5,1},{6,2},{7,3},{8,12},{9,13},{10,... | collective-permute-start | bytes 786440 | tf_op jit(solution)/shard_map/ppermute | solution.py:409
  54.0 6.6 %collective-permute-done.6.refs_2_.refs_6_ = f32[512,128]{1,0:T(8,128)S(1)} collective-permute-done((f32[512,128]{1,0:T(8,128)S(1)}, f32[512,128]{1,0:T(8,128)S(1)}, u32[]{:S(2)}, u32[]{:S(2)}) %collective-permute-start.6) | collective-permute-done | bytes 262176 | tf_op jit(solution)/shard_map/ppermute | solution.py:409
  60.6 4.9 %collective-permute-done.10.refs_7_.refs_10_ = f32[512,128]{1,0:T(8,128)S(1)} collective-permute-done((f32[512,128]{1,0:T(8,128)S(1)}, f32[512,128]{1,0:T(8,128)S(1)}, u32[]{:S(2)}, u32[]{:S(2)}) %collective-permute-start.10) | collective-permute-done | bytes 262176 | tf_op jit(solution)/shard_map/ppermute | solution.py:409
  66.2 6.0 %collective-permute-done.8.refs_5_.refs_8_ = f32[512,128]{1,0:T(8,128)S(1)} collective-permute-done((f32[512,128]{1,0:T(8,128)S(1)}, f32[512,128]{1,0:T(8,128)S(1)}, u32[]{:S(2)}, u32[]{:S(2)}) %collective-permute-start.8) | collective-permute-done | bytes 262176 | tf_op jit(solution)/shard_map/ppermute | solution.py:409
  72.2 2.6 %shard_map.42 = (bf16[512,1024]{1,0:T(8,128)(2,1)S(1)}, bf16[512,1024]{1,0:T(8,128)(2,1)S(1)}, f32[10,256,128]{2,1,0:T(8,128)S(1)}) custom-call(s32[4]{0:T(128)S(1)} %pad_add_fusion.at_ref, f32[512,128]{1,0:T(8,128)S(1)} %get-tuple-element.69.refs_0_, f32[512,128]{1,0:T(8,128)S(1)} %collective-permute-done.5.refs_1_.refs_5_, ...), custom_call_target="tpu_custom_call" | custom-call | tf_op jit(solution)/shard_map/pallas_call | solution.py:174
  81.6 14.4 %collective-permute-done.15.refs_1_ = f32[640,128]{1,0:T(8,128)S(1)} collective-permute-done((f32[640,128]{1,0:T(8,128)S(1)}, f32[640,128]{1,0:T(8,128)S(1)}, u32[]{:S(2)}, u32[]{:S(2)}) %collective-permute-start.15) | collective-permute-done | bytes 327712 | tf_op jit(solution)/shard_map/ppermute | solution.py:417
  97.3 2.6 %collective-permute-start.20 = (f32[160,128]{1,0:T(8,128)S(1)}, f32[160,128]{1,0:T(8,128)S(1)}, u32[]{:S(2)}, u32[]{:S(2)}) collective-permute-start(f32[160,128]{1,0:T(8,128)S(1)} %get-tuple-element.81), channel_id=1, source_target_pairs={{0,24},{8,0},{16,8},{24,16},{32,56},{40,32},{48,40},{56,48},{64,88... | collective-permute-start | bytes 245768 | tf_op jit(solution)/shard_map/ppermute | solution.py:413
  99.9 2.7 %collective-permute-done.18 = f32[160,128]{1,0:T(8,128)S(1)} collective-permute-done((f32[160,128]{1,0:T(8,128)S(1)}, f32[160,128]{1,0:T(8,128)S(1)}, u32[]{:S(2)}, u32[]{:S(2)}) %collective-permute-start.18) | collective-permute-done | bytes 81952 | tf_op jit(solution)/shard_map/ppermute | solution.py:413
  106.9 3.9 %collective-permute-done.22 = f32[160,128]{1,0:T(8,128)S(1)} collective-permute-done((f32[160,128]{1,0:T(8,128)S(1)}, f32[160,128]{1,0:T(8,128)S(1)}, u32[]{:S(2)}, u32[]{:S(2)}) %collective-permute-start.22) | collective-permute-done | bytes 81952 | tf_op jit(solution)/shard_map/ppermute | solution.py:409
  114.9 2.5 %collective-permute-done.25 = f32[160,128]{1,0:T(8,128)S(1)} collective-permute-done((f32[160,128]{1,0:T(8,128)S(1)}, f32[160,128]{1,0:T(8,128)S(1)}, u32[]{:S(2)}, u32[]{:S(2)}) %collective-permute-start.25) | collective-permute-done | bytes 81952 | tf_op jit(solution)/shard_map/ppermute | solution.py:413
  119.3 3.2 %collective-permute-start.27 = (f32[4,160,128]{2,1,0:T(8,128)S(1)}, f32[4,160,128]{2,1,0:T(8,128)S(1)}, u32[]{:S(2)}, u32[]{:S(2)}) collective-permute-start(f32[4,160,128]{2,1,0:T(8,128)S(1)} %get-tuple-element.94), channel_id=1, source_target_pairs={{0,32},{8,40},{16,48},{24,56},{32,64},{40,72},{48,80},{56,88},{64,... | collective-permute-start | bytes 983048 | tf_op jit(solution)/shard_map/ppermute | solution.py:417
  123.9 2.9 %collective-permute-start.12 = (f32[3,2,512,128]{3,2,1,0:T(8,128)S(1)}, f32[3,2,512,128]{3,2,1,0:T(8,128)S(1)}, u32[]{:S(2)}, u32[]{:S(2)}) collective-permute-start(f32[3,2,512,128]{3,2,1,0:T(8,128)S(1)} %get-tuple-element.67), channel_id=1, source_target_pairs={{0,4},{1,5},{2,6},{3,7},{4,0},{5,1},{6,2},{7,3},{8,12},{9,13},{10,... | collective-permute-start | bytes 4718600 | tf_op jit(solution)/shard_map/ppermute | solution.py:409
  128.8 4.9 %collective-permute-done.27 = f32[4,160,128]{2,1,0:T(8,128)S(1)} collective-permute-done((f32[4,160,128]{2,1,0:T(8,128)S(1)}, f32[4,160,128]{2,1,0:T(8,128)S(1)}, u32[]{:S(2)}, u32[]{:S(2)}) %collective-permute-start.27) | collective-permute-done | bytes 327712 | tf_op jit(solution)/shard_map/ppermute | solution.py:417
  134.5 4.1 %collective-permute-start.30 = (f32[16,160,128]{2,1,0:T(8,128)S(1)}, f32[16,160,128]{2,1,0:T(8,128)S(1)}, u32[]{:S(2)}, u32[]{:S(2)}) collective-permute-start(f32[16,160,128]{2,1,0:T(8,128)S(1)} %bitcast.33), channel_id=1, source_target_pairs={{0,1},{1,0},{2,3},{3,2},{4,5},{5,4},{6,7},{7,6},{8,9},{9,8},{10,11... | collective-permute-start | bytes 3932168 | tf_op jit(solution)/shard_map/ppermute | solution.py:405
  138.6 2.7 %collective-permute-done.30.theirs_ref = f32[16,160,128]{2,1,0:T(8,128)S(1)} collective-permute-done((f32[16,160,128]{2,1,0:T(8,128)S(1)}, f32[16,160,128]{2,1,0:T(8,128)S(1)}, u32[]{:S(2)}, u32[]{:S(2)}) %collective-permute-start.30) | collective-permute-done | bytes 1310752 | tf_op jit(solution)/shard_map/ppermute | solution.py:405
  141.3 3.9 %shard_map.46 = (bf16[1024,256]{1,0:T(8,128)(2,1)S(1)}, bf16[1024,256]{1,0:T(8,128)(2,1)S(1)}, f32[8,128]{1,0:T(8,128)S(1)}) custom-call(s32[4]{0:T(128)S(1)} %pad_add_fusion.at_ref, f32[16,160,128]{2,1,0:T(8,128)S(1)} %bitcast.34, f32[16,160,128]{2,1,0:T(8,128)S(1)} %collective-permute-done.30.theirs_ref), custom_call_target="tpu_custom_call" | custom-call | tf_op jit(solution)/shard_map/pallas_call | solution.py:174
  145.2 11.3 %collective-permute-done.11.refs_11_ = f32[3,2,512,128]{3,2,1,0:T(8,128)S(1)} collective-permute-done((f32[3,2,512,128]{3,2,1,0:T(8,128)S(1)}, f32[3,2,512,128]{3,2,1,0:T(8,128)S(1)}, u32[]{:S(2)}, u32[]{:S(2)}) %collective-permute-start.11) | collective-permute-done | bytes 1572896 | tf_op jit(solution)/shard_map/ppermute | solution.py:409
  156.5 33.1 %collective-permute-done.12.refs_12_ = f32[3,2,512,128]{3,2,1,0:T(8,128)S(1)} collective-permute-done((f32[3,2,512,128]{3,2,1,0:T(8,128)S(1)}, f32[3,2,512,128]{3,2,1,0:T(8,128)S(1)}, u32[]{:S(2)}, u32[]{:S(2)}) %collective-permute-start.12) | collective-permute-done | bytes 1572896 | tf_op jit(solution)/shard_map/ppermute | solution.py:409
  189.5 5.1 %collective-permute-done.13.refs_13_ = f32[3,2,512,128]{3,2,1,0:T(8,128)S(1)} collective-permute-done((f32[3,2,512,128]{3,2,1,0:T(8,128)S(1)}, f32[3,2,512,128]{3,2,1,0:T(8,128)S(1)}, u32[]{:S(2)}, u32[]{:S(2)}) %collective-permute-start.13) | collective-permute-done | bytes 1572896 | tf_op jit(solution)/shard_map/ppermute | solution.py:409
  194.6 3.6 %shard_map.47 = (f32[4,512,128]{2,1,0:T(8,128)S(1)}, f32[4,512,128]{2,1,0:T(8,128)S(1)}) custom-call(f32[512,128]{1,0:T(8,128)S(1)} %get-tuple-element.69.refs_0_, f32[512,128]{1,0:T(8,128)S(1)} %get-tuple-element.62.refs_1_, f32[512,128]{1,0:T(8,128)S(1)} %get-tuple-element.63.refs_2_, f32[512,128]{1,0:T(8,128)S(1)} %get-tuple-element.64.refs_3_, ...), custom_call_target="tpu_custom_call" | custom-call | tf_op jit(solution)/shard_map/pallas_call | solution.py:174
  (63 shorter events, 50.2 us)
Async XLA Ops:
  1.1 24.8 %collective-permute-start = (f32[2,256,128]{2,1,0:T(8,128)S(1)}, f32[2,256,128]{2,1,0:T(8,128)S(1)}, u32[]{:S(2)}, u32[]{:S(2)}) collective-permute-start(f32[2,256,128]{2,1,0:T(8,128)S(1)} %bitcast.43), channel_id=1, source_target_pairs={{0,8},{8,16},{16,24},{24,32},{32,40},{40,48},{48,56},{56,64},{64,7... | collective-permute-start | bytes 786440 | tf_op jit(solution)/shard_map/ppermute | solution.py:429
  3.2 22.7 %collective-permute-start.1 = (f32[2,256,128]{2,1,0:T(8,128)S(1)}, f32[2,256,128]{2,1,0:T(8,128)S(1)}, u32[]{:S(2)}, u32[]{:S(2)}) collective-permute-start(f32[2,256,128]{2,1,0:T(8,128)S(1)} %bitcast.42), channel_id=1, source_target_pairs={{8,0},{16,8},{24,16},{32,24},{40,32},{48,40},{56,48},{64,56},{72,6... | collective-permute-start | bytes 786440 | tf_op jit(solution)/shard_map/ppermute | solution.py:429
  27.6 7.0 %collective-permute-start.3 = (f32[2,256,128]{2,1,0:T(8,128)S(1)}, f32[2,256,128]{2,1,0:T(8,128)S(1)}, u32[]{:S(2)}, u32[]{:S(2)}) collective-permute-start(f32[2,256,128]{2,1,0:T(8,128)S(1)} %get-tuple-element.48.low_ref), channel_id=1, source_target_pairs={{8,0},{16,8},{24,16},{32,24},{40,32},{48,40},{56,48},{64,56},{72,6... | collective-permute-start | bytes 786440 | tf_op jit(solution)/shard_map/ppermute | solution.py:429
  29.1 9.7 %collective-permute-start.2 = (f32[2,256,128]{2,1,0:T(8,128)S(1)}, f32[2,256,128]{2,1,0:T(8,128)S(1)}, u32[]{:S(2)}, u32[]{:S(2)}) collective-permute-start(f32[2,256,128]{2,1,0:T(8,128)S(1)} %get-tuple-element.49.high_ref), channel_id=1, source_target_pairs={{0,8},{8,16},{16,24},{24,32},{32,40},{40,48},{48,56},{56,64},{64,7... | collective-permute-start | bytes 786440 | tf_op jit(solution)/shard_map/ppermute | solution.py:429
  41.2 8.1 %collective-permute-start.4 = (f32[4,512,128]{2,1,0:T(8,128)S(1)}, f32[4,512,128]{2,1,0:T(8,128)S(1)}, u32[]{:S(2)}, u32[]{:S(2)}) collective-permute-start(f32[4,512,128]{2,1,0:T(8,128)S(1)} %get-tuple-element.54), channel_id=1, source_target_pairs={{0,1},{1,0},{2,3},{3,2},{4,5},{5,4},{6,7},{7,6},{8,9},{9,8},{10,11... | collective-permute-start | bytes 3145736 | tf_op jit(solution)/shard_map/ppermute | solution.py:405
  43.7 10.3 %collective-permute-start.5 = (f32[512,128]{1,0:T(8,128)S(1)}, f32[512,128]{1,0:T(8,128)S(1)}, u32[]{:S(2)}, u32[]{:S(2)}) collective-permute-start(f32[512,128]{1,0:T(8,128)S(1)} %get-tuple-element.62.refs_1_), channel_id=1, source_target_pairs={{0,2},{1,3},{2,4},{3,5},{4,6},{5,7},{6,0},{7,1},{8,10},{9,11},{10,... | collective-permute-start | bytes 786440 | tf_op jit(solution)/shard_map/ppermute | solution.py:409
  45.3 15.3 %collective-permute-start.6 = (f32[512,128]{1,0:T(8,128)S(1)}, f32[512,128]{1,0:T(8,128)S(1)}, u32[]{:S(2)}, u32[]{:S(2)}) collective-permute-start(f32[512,128]{1,0:T(8,128)S(1)} %get-tuple-element.63.refs_2_), channel_id=1, source_target_pairs={{0,4},{1,5},{2,6},{3,7},{4,0},{5,1},{6,2},{7,3},{8,12},{9,13},{10,... | collective-permute-start | bytes 786440 | tf_op jit(solution)/shard_map/ppermute | solution.py:409
  48.6 12.0 %collective-permute-start.7 = (f32[512,128]{1,0:T(8,128)S(1)}, f32[512,128]{1,0:T(8,128)S(1)}, u32[]{:S(2)}, u32[]{:S(2)}) collective-permute-start(f32[512,128]{1,0:T(8,128)S(1)} %get-tuple-element.64.refs_3_), channel_id=1, source_target_pairs={{0,6},{1,7},{2,0},{3,1},{4,2},{5,3},{6,4},{7,5},{8,14},{9,15},{10,... | collective-permute-start | bytes 786440 | tf_op jit(solution)/shard_map/ppermute | solution.py:409
  49.4 16.1 %collective-permute-start.10 = (f32[512,128]{1,0:T(8,128)S(1)}, f32[512,128]{1,0:T(8,128)S(1)}, u32[]{:S(2)}, u32[]{:S(2)}) collective-permute-start(f32[512,128]{1,0:T(8,128)S(1)} %get-tuple-element.89), channel_id=1, source_target_pairs={{0,6},{1,7},{2,0},{3,1},{4,2},{5,3},{6,4},{7,5},{8,14},{9,15},{10,... | collective-permute-start | bytes 786440 | tf_op jit(solution)/shard_map/ppermute | solution.py:409
  49.9 16.4 %collective-permute-start.9 = (f32[512,128]{1,0:T(8,128)S(1)}, f32[512,128]{1,0:T(8,128)S(1)}, u32[]{:S(2)}, u32[]{:S(2)}) collective-permute-start(f32[512,128]{1,0:T(8,128)S(1)} %get-tuple-element.90), channel_id=1, source_target_pairs={{0,4},{1,5},{2,6},{3,7},{4,0},{5,1},{6,2},{7,3},{8,12},{9,13},{10,... | collective-permute-start | bytes 786440 | tf_op jit(solution)/shard_map/ppermute | solution.py:409
  54.0 18.2 %collective-permute-start.8 = (f32[512,128]{1,0:T(8,128)S(1)}, f32[512,128]{1,0:T(8,128)S(1)}, u32[]{:S(2)}, u32[]{:S(2)}) collective-permute-start(f32[512,128]{1,0:T(8,128)S(1)} %get-tuple-element.91), channel_id=1, source_target_pairs={{0,2},{1,3},{2,4},{3,5},{4,6},{5,7},{6,0},{7,1},{8,10},{9,11},{10,... | collective-permute-start | bytes 786440 | tf_op jit(solution)/shard_map/ppermute | solution.py:409
  78.9 17.2 %collective-permute-start.15 = (f32[640,128]{1,0:T(8,128)S(1)}, f32[640,128]{1,0:T(8,128)S(1)}, u32[]{:S(2)}, u32[]{:S(2)}) collective-permute-start(f32[640,128]{1,0:T(8,128)S(1)} %get-tuple-element.75), channel_id=1, source_target_pairs={{0,32},{8,40},{16,48},{24,56},{32,64},{40,72},{48,80},{56,88},{64,... | collective-permute-start | bytes 983048 | tf_op jit(solution)/shard_map/ppermute | solution.py:417
  78.9 17.1 %collective-permute-start.16 = (f32[640,128]{1,0:T(8,128)S(1)}, f32[640,128]{1,0:T(8,128)S(1)}, u32[]{:S(2)}, u32[]{:S(2)}) collective-permute-start(f32[640,128]{1,0:T(8,128)S(1)} %get-tuple-element.76), channel_id=1, source_target_pairs={{0,64},{8,72},{16,80},{24,88},{32,96},{40,104},{48,112},{56,120},{... | collective-permute-start | bytes 983048 | tf_op jit(solution)/shard_map/ppermute | solution.py:417
  79.4 17.1 %collective-permute-start.17 = (f32[640,128]{1,0:T(8,128)S(1)}, f32[640,128]{1,0:T(8,128)S(1)}, u32[]{:S(2)}, u32[]{:S(2)}) collective-permute-start(f32[640,128]{1,0:T(8,128)S(1)} %get-tuple-element.77), channel_id=1, source_target_pairs={{0,96},{8,104},{16,112},{24,120},{32,0},{40,8},{48,16},{56,24},{64... | collective-permute-start | bytes 983048 | tf_op jit(solution)/shard_map/ppermute | solution.py:417
  97.1 5.4 %collective-permute-start.18 = (f32[160,128]{1,0:T(8,128)S(1)}, f32[160,128]{1,0:T(8,128)S(1)}, u32[]{:S(2)}, u32[]{:S(2)}) collective-permute-start(f32[160,128]{1,0:T(8,128)S(1)} %get-tuple-element.79), channel_id=1, source_target_pairs={{0,8},{8,16},{16,24},{24,0},{32,40},{40,48},{48,56},{56,32},{64,72... | collective-permute-start | bytes 245768 | tf_op jit(solution)/shard_map/ppermute | solution.py:413
  97.3 6.1 %collective-permute-start.20 = (f32[160,128]{1,0:T(8,128)S(1)}, f32[160,128]{1,0:T(8,128)S(1)}, u32[]{:S(2)}, u32[]{:S(2)}) collective-permute-start(f32[160,128]{1,0:T(8,128)S(1)} %get-tuple-element.81), channel_id=1, source_target_pairs={{0,24},{8,0},{16,8},{24,16},{32,56},{40,32},{48,40},{56,48},{64,88... | collective-permute-start | bytes 245768 | tf_op jit(solution)/shard_map/ppermute | solution.py:413
  105.4 5.4 %collective-permute-start.22 = (f32[160,128]{1,0:T(8,128)S(1)}, f32[160,128]{1,0:T(8,128)S(1)}, u32[]{:S(2)}, u32[]{:S(2)}) collective-permute-start(f32[160,128]{1,0:T(8,128)S(1)} %add_add_fusion.1), channel_id=1, source_target_pairs={{0,2},{1,3},{2,4},{3,5},{4,6},{5,7},{6,0},{7,1},{8,10},{9,11},{10,... | collective-permute-start | bytes 245768 | tf_op jit(solution)/shard_map/ppermute | solution.py:409
  118.4 8.4 %collective-permute-start.28 = (f32[4,160,128]{2,1,0:T(8,128)S(1)}, f32[4,160,128]{2,1,0:T(8,128)S(1)}, u32[]{:S(2)}, u32[]{:S(2)}) collective-permute-start(f32[4,160,128]{2,1,0:T(8,128)S(1)} %get-tuple-element.94), channel_id=1, source_target_pairs={{0,64},{8,72},{16,80},{24,88},{32,96},{40,104},{48,112},{56,120},{... | collective-permute-start | bytes 983048 | tf_op jit(solution)/shard_map/ppermute | solution.py:417
  119.3 14.4 %collective-permute-start.27 = (f32[4,160,128]{2,1,0:T(8,128)S(1)}, f32[4,160,128]{2,1,0:T(8,128)S(1)}, u32[]{:S(2)}, u32[]{:S(2)}) collective-permute-start(f32[4,160,128]{2,1,0:T(8,128)S(1)} %get-tuple-element.94), channel_id=1, source_target_pairs={{0,32},{8,40},{16,48},{24,56},{32,64},{40,72},{48,80},{56,88},{64,... | collective-permute-start | bytes 983048 | tf_op jit(solution)/shard_map/ppermute | solution.py:417
  122.5 11.9 %collective-permute-start.29 = (f32[4,160,128]{2,1,0:T(8,128)S(1)}, f32[4,160,128]{2,1,0:T(8,128)S(1)}, u32[]{:S(2)}, u32[]{:S(2)}) collective-permute-start(f32[4,160,128]{2,1,0:T(8,128)S(1)} %get-tuple-element.94), channel_id=1, source_target_pairs={{0,96},{8,104},{16,112},{24,120},{32,0},{40,8},{48,16},{56,24},{64... | collective-permute-start | bytes 983048 | tf_op jit(solution)/shard_map/ppermute | solution.py:417
  123.8 32.7 %collective-permute-start.11 = (f32[3,2,512,128]{3,2,1,0:T(8,128)S(1)}, f32[3,2,512,128]{3,2,1,0:T(8,128)S(1)}, u32[]{:S(2)}, u32[]{:S(2)}) collective-permute-start(f32[3,2,512,128]{3,2,1,0:T(8,128)S(1)} %get-tuple-element.66), channel_id=1, source_target_pairs={{0,2},{1,3},{2,4},{3,5},{4,6},{5,7},{6,0},{7,1},{8,10},{9,11},{10,... | collective-permute-start | bytes 4718600 | tf_op jit(solution)/shard_map/ppermute | solution.py:409
  123.9 65.6 %collective-permute-start.12 = (f32[3,2,512,128]{3,2,1,0:T(8,128)S(1)}, f32[3,2,512,128]{3,2,1,0:T(8,128)S(1)}, u32[]{:S(2)}, u32[]{:S(2)}) collective-permute-start(f32[3,2,512,128]{3,2,1,0:T(8,128)S(1)} %get-tuple-element.67), channel_id=1, source_target_pairs={{0,4},{1,5},{2,6},{3,7},{4,0},{5,1},{6,2},{7,3},{8,12},{9,13},{10,... | collective-permute-start | bytes 4718600 | tf_op jit(solution)/shard_map/ppermute | solution.py:409
  126.8 67.8 %collective-permute-start.13 = (f32[3,2,512,128]{3,2,1,0:T(8,128)S(1)}, f32[3,2,512,128]{3,2,1,0:T(8,128)S(1)}, u32[]{:S(2)}, u32[]{:S(2)}) collective-permute-start(f32[3,2,512,128]{3,2,1,0:T(8,128)S(1)} %get-tuple-element.68), channel_id=1, source_target_pairs={{0,6},{1,7},{2,0},{3,1},{4,2},{5,3},{6,4},{7,5},{8,14},{9,15},{10,... | collective-permute-start | bytes 4718600 | tf_op jit(solution)/shard_map/ppermute | solution.py:409
  134.5 6.8 %collective-permute-start.30 = (f32[16,160,128]{2,1,0:T(8,128)S(1)}, f32[16,160,128]{2,1,0:T(8,128)S(1)}, u32[]{:S(2)}, u32[]{:S(2)}) collective-permute-start(f32[16,160,128]{2,1,0:T(8,128)S(1)} %bitcast.33), channel_id=1, source_target_pairs={{0,1},{1,0},{2,3},{3,2},{4,5},{5,4},{6,7},{7,6},{8,9},{9,8},{10,11... | collective-permute-start | bytes 3932168 | tf_op jit(solution)/shard_map/ppermute | solution.py:405
  (10 other events, 37.1 us)

commit v5 on v4

--- a/solution.py
+++ b/solution.py
@@ -246,27 +246,20 @@
     return [m for m in range(4) if m != k]
 
 
-def share_kernel(axis, count, at_ref, *refs):
-    ins, outs, sum_ref = refs[:count], refs[count:-1], refs[-1]
-    total = ins[0][...]
-    for ref in ins[1:]:
-        total = total + ref[...]
-    sum_ref[...] = total
-    size = outs[0].shape[0]
-    for k in range(4):
-        part = lax.rem(at_ref[axis] + k, 4)
-        outs[k][...] = sum_ref[pl.ds(pl.multiple_of(part * size, size), size)]
-
-
-def shares(here, axis, shift, arrays):
-    size, panel = arrays[0].shape
-    part = shaped(size // 4, panel)
-    outs = call(
-        functools.partial(share_kernel, axis, len(arrays)), (part,) * 4,
-        [SMEM_SPEC] + [VMEM_SPEC] * len(arrays), [pltpu.VMEM((size, panel), F32)], (here, *arrays), STEP_LIMIT,
-    )
-    got = {k: shift(outs[k], k) for k in SHIFTS}
-    return [outs[0]] + [got[k] for k in (1, 2, 3)]
+def add_kernel(a_ref, b_ref, out_ref):
+    out_ref[...] = a_ref[...] + b_ref[...]
+
+
+def fold_kernel(parts_ref, out_ref):
+    total = parts_ref[0]
+    for at in range(1, parts_ref.shape[0]):
+        total = total + parts_ref[at]
+    out_ref[...] = total
+
+
+def copy_kernel(piece_ref, out_ref):
+    for at in range(out_ref.shape[0]):
+        out_ref[at] = piece_ref[...]
 
 
 def lanes(start, size):
@@ -307,11 +300,10 @@
 
 
 def poly_kernel(order, at_ref, mine_ref, theirs_ref, ph_ref, pl_ref, stretch_ref, gram_ref, nh_ref, nl_ref, poly_ref):
-    x, y, z, c = at_ref[0], at_ref[1], at_ref[2], at_ref[3]
+    z, c = at_ref[2], at_ref[3]
     for ky in range(4):
         for kx in range(4):
-            piece = lax.rem(y + 4 - ky, 4) * 4 + lax.rem(x + 4 - kx, 4)
-            rows = pl.ds(pl.multiple_of(piece * 160, 160), 160)
+            rows = slice((ky * 4 + kx) * 160, (ky * 4 + kx + 1) * 160)
             gram_ref[c, rows] = mine_ref[ky * 4 + kx]
             gram_ref[1 - c, rows] = theirs_ref[ky * 4 + kx]
 
@@ -409,19 +401,6 @@
     return lax.ppermute(x, "band", [(i, (i + 2 * k) % 8) for i in range(8)])
 
 
-def shift_x(x, k):
-    return lax.ppermute(x, "space", [(i, (i & 12) | ((i + k) & 3)) for i in range(16)])
-
-
-def shift_y(x, k):
-    return lax.ppermute(x, "space", [(i, (i + 4 * k) % 16) for i in range(16)])
-
-
-def gathered(x, shift):
-    got = {k: shift(x, k) for k in SHIFTS}
-    return jnp.stack([x] + [got[k] for k in (1, 2, 3)])
-
-
 def halos_of(first, last):
     size = lax.axis_size("space")
     up = [(i, (i + 1) % size) for i in range(size)]
@@ -455,10 +434,9 @@
 
     late_own, late_got, part_own, part_got = lax.optimization_barrier((own, got, part_own, part_got))
     bulks = call(bulk_kernel, (shaped(3, 2, share, panel),) * 3, [VMEM_SPEC] * 5, [], (*late_own, late_got), STEP_LIMIT)
-    sent = []
-    for k in (1, 2, 3):
-        sent.append(shift_z(bulks[k - 1], k))
-    bulks = sent
+    sent = {}
+    for k in (1, 3):
+        sent[k] = shift_z(bulks[k - 1], k)
 
     half = shaped(10, 256, 128)
     wide = shaped(share, VECTORS, dtype=BF16)
@@ -468,12 +446,17 @@
     )
     theirs = swap_cores(send)
     keep = call(gram_keep_kernel, half, [SMEM_SPEC] + [VMEM_SPEC] * 2, [], (here, hi, lo), STEP_LIMIT)
-    pieces = shares(here, 1, shift_y, [keep.reshape(2560, panel), theirs.reshape(2560, panel)])
-    pieces = shares(here, 0, shift_x, pieces)
-    piece = (pieces[0] + pieces[1]) + (pieces[2] + pieces[3])
+    total = call(add_kernel, half, [VMEM_SPEC] * 2, [], (keep, theirs), STEP_LIMIT)
+    pieces = total.reshape(16, 160, panel)
+    pieces = lax.all_to_all(pieces, "space", split_axis=0, concat_axis=0, tiled=True)
+    piece = call(fold_kernel, shaped(160, panel), [VMEM_SPEC], [], (pieces,), STEP_LIMIT)
     sums = [shift_z(piece, k) for k in SHIFTS]
     piece = piece + sums[0] + (sums[1] + sums[2])
-    mine = gathered(gathered(piece, shift_x), shift_y).reshape(16, 160, panel)
+    late, piece = lax.optimization_barrier((bulks[1], piece))
+    sent[2] = shift_z(late, 2)
+    bulks = [sent[k] for k in (1, 2, 3)]
+    copies = call(copy_kernel, shaped(*pieces.shape), [VMEM_SPEC], [], (piece,), STEP_LIMIT)
+    mine = lax.all_to_all(copies, "space", split_axis=0, concat_axis=0, tiled=True)
     theirs = swap_cores(mine)
 
     poly = shaped(VECTORS, TILE, dtype=BF16)

time: 204 us -> 196 us (0.961)
  waiting for transfers between devices: 113 us -> 85.1 us
  blocking collectives: 0 us -> 22.2 us
  starting transfers between devices: 46.3 us -> 37.5 us
  local copies, waits for them, and re-layouts: 3.41 us -> 8.09 us
    ppermute x12 -> x0, waiting for transfers between devices: 28.5 us -> none  [the longest x6 20.5 us: shift_y(): return lax.ppermute(x, 'space', [(i, (i + 4 * k) % 16) for i in range(16)])]
    all_to_all x0 -> x1, blocking collectives: none -> 22.2 us  [steps(): lax.all_to_all(pieces, 'space', split_axis=0, concat_axis=0, tiled=True)]
    all_to_all x0 -> x1, waiting for transfers between devices: none -> 13.7 us  [steps(): lax.all_to_all(copies, 'space', split_axis=0, concat_axis=0, tiled=True)]
    ppermute x12 -> x0, starting transfers between devices: 13.6 us -> none  [the longest x6 7.84 us: shift_y(): return lax.ppermute(x, 'space', [(i, (i + 4 * k) % 16) for i in range(16)])]
    ppermute x12, waiting for transfers between devices: 73.7 us -> 61 us  [shift_z(): return lax.ppermute(x, 'band', [(i, (i + 2 * k) % 8) for i in range(8)])]
    unnamed x4 -> x36, local copies, waits for them, and re-layouts: 2.28 us -> 6.96 us
    all_to_all x0 -> x1, starting transfers between devices: none -> 3.7 us  [steps(): lax.all_to_all(copies, 'space', split_axis=0, concat_axis=0, tiled=True)]
    ppermute x4, starting transfers between devices: 8.81 us -> 11.4 us  [swap_cores(): return lax.ppermute(x, 'band', [(i, i ^ 1) for i in range(8)])]
  transfers between devices with their start and end apart: 32 -> 21, of which waited for: 24 -> 16; matrix products, arithmetic and copies ran while one was open for 0% -> 0% of each run, Pallas kernels for 13% -> 14%
where the time goes in v5:
time: 196 us
  waiting for transfers between devices  85.1 us (43%)
  Pallas kernels  42.4 us (22%)
  starting transfers between devices  37.5 us (19%)
  blocking collectives  22.2 us (11%)
  local copies, waits for them, and re-layouts  8.09 us (4%)
    ppermute x12, waiting for transfers between devices, shift_z(): return lax.ppermute(x, 'band', [(i, (i + 2 * k) % 8) for i in range(8)])  61 us
    pallas_call x13, Pallas kernels, call(): pl.pallas_call(kernel, out_shape=outs, in_specs=specs, out_specs=kwargs.p...  42.4 us
    all_to_all x1, blocking collectives, steps(): lax.all_to_all(pieces, 'space', split_axis=0, concat_axis=0, tiled=True)  22.2 us
    ppermute x12, starting transfers between devices, shift_z(): return lax.ppermute(x, 'band', [(i, (i + 2 * k) % 8) for i in range(8)])  15 us
    all_to_all x1, waiting for transfers between devices, steps(): lax.all_to_all(copies, 'space', split_axis=0, concat_axis=0, tiled=True)  13.7 us
    ppermute x4, starting transfers between devices, swap_cores(): return lax.ppermute(x, 'band', [(i, i ^ 1) for i in range(8)])  11.4 us
    ppermute x4, starting transfers between devices, halos_of(): return (lax.ppermute(last, 'space', up), lax.ppermute(first, 'space', down))  7.43 us
    unnamed x36, local copies, waits for them, and re-layouts  6.96 us
  transfers between devices with their start and end apart: 21, of which 16 were waited for; matrix products, arithmetic and copies ran while one was open for 0% of the time, Pallas kernels for 14%

profile of v5, /device:TPU:1, one launch (start us, length us, event | category | flops | bytes accessed | tf_op | source)
XLA Modules:
  0.0 195.9 jit_solution(9239450081987088251)
XLA Ops:
  1.1 2.1 %collective-permute-start = (f32[2,256,128]{2,1,0:T(8,128)S(1)}, f32[2,256,128]{2,1,0:T(8,128)S(1)}, u32[]{:S(2)}, u32[]{:S(2)}) collective-permute-start(f32[2,256,128]{2,1,0:T(8,128)S(1)} %bitcast.25), channel_id=1, source_target_pairs={{0,8},{8,16},{16,24},{24,32},{32,40},{40,48},{48,56},{56,64},{64,7... | collective-permute-start | bytes 786440 | tf_op jit(solution)/shard_map/ppermute | solution.py:408
  3.2 3.8 %collective-permute-start.1 = (f32[2,256,128]{2,1,0:T(8,128)S(1)}, f32[2,256,128]{2,1,0:T(8,128)S(1)}, u32[]{:S(2)}, u32[]{:S(2)}) collective-permute-start(f32[2,256,128]{2,1,0:T(8,128)S(1)} %bitcast.24), channel_id=1, source_target_pairs={{8,0},{16,8},{24,16},{32,24},{40,32},{48,40},{56,48},{64,56},{72,6... | collective-permute-start | bytes 786440 | tf_op jit(solution)/shard_map/ppermute | solution.py:408
  9.3 16.5 %shard_map.37 = (f32[12,256,128]{2,1,0:T(8,128)S(1)}, bf16[16,512,1280]{2,1,0:T(8,128)(2,1)S(1)}) custom-call(s32[7,16]{1,0:T(8,128)S(1)} %bitcast.23, s32[4]{0:T(128)S(1)} %pad_add_fusion.at_ref, f32[16,7,256,256]{3,2,1,0:T(8,128)} %blocks_ref.1, f32[16,256,128]{2,1,0:T(8,128)S(1)} %bitcast.18), custom_call_target="tpu_custom_call" | custom-call | tf_op jit(solution)/shard_map/pallas_call | solution.py:174
  29.2 4.9 %shard_map.39.done_ref = f32[12,256,128]{2,1,0:T(8,128)S(1)} custom-call(bf16[16,512,1280]{2,1,0:T(8,128)(2,1)S(1)} %get-tuple-element.40.op_ref, f32[12,256,128]{2,1,0:T(8,128)S(1)} %get-tuple-element.41.mid_ref, f32[2,256,128]{2,1,0:T(8,128)S(1)} %get-tuple-element.42.low_ref, f32[2,256,128]{2,1,0:T(8,128)S(1)} %get-tuple-element.43.high_ref, ...), custom_call_target="tpu_custom_call" | custom-call | tf_op jit(solution)/shard_map/pallas_call | solution.py:174
  34.6 4.1 %collective-permute-done.2.before_ref = f32[2,256,128]{2,1,0:T(8,128)S(1)} collective-permute-done((f32[2,256,128]{2,1,0:T(8,128)S(1)}, f32[2,256,128]{2,1,0:T(8,128)S(1)}, u32[]{:S(2)}, u32[]{:S(2)}) %collective-permute-start.2) | collective-permute-done | bytes 262176 | tf_op jit(solution)/shard_map/ppermute | solution.py:408
  38.7 2.5 %shard_map.40 = (f32[512,128]{1,0:T(8,128)S(1)}, f32[512,128]{1,0:T(8,128)S(1)}, f32[512,128]{1,0:T(8,128)S(1)}, f32[512,128]{1,0:T(8,128)S(1)}, f32[4,512,128]{2,1,0:T(8,128)S(1)}) custom-call(s32[4]{0:T(128)S(1)} %pad_add_fusion.at_ref, bf16[16,512,1280]{2,1,0:T(8,128)(2,1)S(1)} %get-tuple-element.40.op_ref, ...), custom_call_target="tpu_custom_call" | custom-call | tf_op jit(solution)/shard_map/pallas_call | solution.py:174
  41.3 2.4 %collective-permute-start.4 = (f32[4,512,128]{2,1,0:T(8,128)S(1)}, f32[4,512,128]{2,1,0:T(8,128)S(1)}, u32[]{:S(2)}, u32[]{:S(2)}) collective-permute-start(f32[4,512,128]{2,1,0:T(8,128)S(1)} %get-tuple-element.48), channel_id=1, source_target_pairs={{0,1},{1,0},{2,3},{3,2},{4,5},{5,4},{6,7},{7,6},{8,9},{9,8},{10,11... | collective-permute-start | bytes 3145736 | tf_op jit(solution)/shard_map/ppermute | solution.py:397
  45.4 3.3 %collective-permute-start.6 = (f32[512,128]{1,0:T(8,128)S(1)}, f32[512,128]{1,0:T(8,128)S(1)}, u32[]{:S(2)}, u32[]{:S(2)}) collective-permute-start(f32[512,128]{1,0:T(8,128)S(1)} %get-tuple-element.57.refs_2_), channel_id=1, source_target_pairs={{0,4},{1,5},{2,6},{3,7},{4,0},{5,1},{6,2},{7,3},{8,12},{9,13},{10,... | collective-permute-start | bytes 786440 | tf_op jit(solution)/shard_map/ppermute | solution.py:401
  49.9 2.2 %collective-permute-start.9 = (f32[512,128]{1,0:T(8,128)S(1)}, f32[512,128]{1,0:T(8,128)S(1)}, u32[]{:S(2)}, u32[]{:S(2)}) collective-permute-start(f32[512,128]{1,0:T(8,128)S(1)} %get-tuple-element.78), channel_id=1, source_target_pairs={{0,4},{1,5},{2,6},{3,7},{4,0},{5,1},{6,2},{7,3},{8,12},{9,13},{10,... | collective-permute-start | bytes 786440 | tf_op jit(solution)/shard_map/ppermute | solution.py:401
  54.1 6.6 %collective-permute-done.6.refs_2_.refs_6_ = f32[512,128]{1,0:T(8,128)S(1)} collective-permute-done((f32[512,128]{1,0:T(8,128)S(1)}, f32[512,128]{1,0:T(8,128)S(1)}, u32[]{:S(2)}, u32[]{:S(2)}) %collective-permute-start.6) | collective-permute-done | bytes 262176 | tf_op jit(solution)/shard_map/ppermute | solution.py:401
  60.6 4.9 %collective-permute-done.10.refs_7_.refs_10_ = f32[512,128]{1,0:T(8,128)S(1)} collective-permute-done((f32[512,128]{1,0:T(8,128)S(1)}, f32[512,128]{1,0:T(8,128)S(1)}, u32[]{:S(2)}, u32[]{:S(2)}) %collective-permute-start.10) | collective-permute-done | bytes 262176 | tf_op jit(solution)/shard_map/ppermute | solution.py:401
  66.3 6.0 %collective-permute-done.8.refs_5_.refs_8_ = f32[512,128]{1,0:T(8,128)S(1)} collective-permute-done((f32[512,128]{1,0:T(8,128)S(1)}, f32[512,128]{1,0:T(8,128)S(1)}, u32[]{:S(2)}, u32[]{:S(2)}) %collective-permute-start.8) | collective-permute-done | bytes 262176 | tf_op jit(solution)/shard_map/ppermute | solution.py:401
  72.3 2.6 %shard_map.42 = (bf16[512,1024]{1,0:T(8,128)(2,1)S(1)}, bf16[512,1024]{1,0:T(8,128)(2,1)S(1)}, f32[10,256,128]{2,1,0:T(8,128)S(1)}) custom-call(s32[4]{0:T(128)S(1)} %pad_add_fusion.at_ref, f32[512,128]{1,0:T(8,128)S(1)} %get-tuple-element.62.refs_0_, f32[512,128]{1,0:T(8,128)S(1)} %collective-permute-done.5.refs_1_.refs_5_, ...), custom_call_target="tpu_custom_call" | custom-call | tf_op jit(solution)/shard_map/pallas_call | solution.py:174
  78.3 22.2 %all_to_all.10.parts_ref = f32[16,160,128]{2,1,0:T(8,128)S(1)} all-to-all(f32[16,160,128]{2,1,0:T(8,128)S(1)} %bitcast.22), channel_id=1, replica_groups=mesh['space'=16,'band'=8] {'space'}, dimensions={0} | all-to-all | bytes 2621440 | tf_op jit(solution)/shard_map/all_to_all | solution.py:451
  109.2 3.7 %all-to-all-start.1 = ((f32[16,160,128]{2,1,0:T(8,128)}), f32[16,160,128]{2,1,0:T(8,128)S(1)}, u32[]{:S(2)}, u32[]{:S(2)}) async-start(f32[16,160,128]{2,1,0:T(8,128)} %copy-done.1), calls=%async_computation.1 | async-start | bytes 2621440 | tf_op jit(solution)/shard_map/all_to_all | solution.py:459
  116.5 13.7 %all-to-all-done.1.mine_ref = f32[16,160,128]{2,1,0:T(8,128)S(1)} async-done(((f32[16,160,128]{2,1,0:T(8,128)}), f32[16,160,128]{2,1,0:T(8,128)S(1)}, u32[]{:S(2)}, u32[]{:S(2)}) %all-to-all-start.1) | async-done | bytes 1310752 | tf_op jit(solution)/shard_map/all_to_all | solution.py:459
  130.2 4.4 %collective-permute-start.18 = (f32[16,160,128]{2,1,0:T(8,128)S(1)}, f32[16,160,128]{2,1,0:T(8,128)S(1)}, u32[]{:S(2)}, u32[]{:S(2)}) collective-permute-start(f32[16,160,128]{2,1,0:T(8,128)S(1)} %all-to-all-done.1.mine_ref), channel_id=1, source_target_pairs={{0,1},{1,0},{2,3},{3,2},{4,5},{5,4},{6,7},{7,6},{8,9},{9,8},{10,11... | collective-permute-start | bytes 3932168 | tf_op jit(solution)/shard_map/ppermute | solution.py:397
  134.6 2.7 %collective-permute-done.18.theirs_ref = f32[16,160,128]{2,1,0:T(8,128)S(1)} collective-permute-done((f32[16,160,128]{2,1,0:T(8,128)S(1)}, f32[16,160,128]{2,1,0:T(8,128)S(1)}, u32[]{:S(2)}, u32[]{:S(2)}) %collective-permute-start.18) | collective-permute-done | bytes 1310752 | tf_op jit(solution)/shard_map/ppermute | solution.py:397
  137.3 3.9 %shard_map.47 = (bf16[1024,256]{1,0:T(8,128)(2,1)S(1)}, bf16[1024,256]{1,0:T(8,128)(2,1)S(1)}, f32[8,128]{1,0:T(8,128)S(1)}) custom-call(s32[4]{0:T(128)S(1)} %pad_add_fusion.at_ref, f32[16,160,128]{2,1,0:T(8,128)S(1)} %all-to-all-done.1.mine_ref, f32[16,160,128]{2,1,0:T(8,128)S(1)} %collective-permute-done.18.theirs_ref), custom_call_target="tpu_custom_call" | custom-call | tf_op jit(solution)/shard_map/pallas_call | solution.py:174
  141.2 6.7 %collective-permute-done.11.refs_11_ = f32[3,2,512,128]{3,2,1,0:T(8,128)} collective-permute-done((f32[3,2,512,128]{3,2,1,0:T(8,128)}, f32[3,2,512,128]{3,2,1,0:T(8,128)}, u32[]{:S(2)}, u32[]{:S(2)}) %collective-permute-start.11) | collective-permute-done | bytes 1572896 | tf_op jit(solution)/shard_map/ppermute | solution.py:401
  148.4 33.2 %collective-permute-done.16.refs_12_ = f32[3,2,512,128]{3,2,1,0:T(8,128)} collective-permute-done((f32[3,2,512,128]{3,2,1,0:T(8,128)}, f32[3,2,512,128]{3,2,1,0:T(8,128)}, u32[]{:S(2)}, u32[]{:S(2)}) %collective-permute-start.16) | collective-permute-done | bytes 1572896 | tf_op jit(solution)/shard_map/ppermute | solution.py:401
  181.6 5.8 %shard_map.48 = (f32[4,512,128]{2,1,0:T(8,128)S(1)}, f32[4,512,128]{2,1,0:T(8,128)S(1)}) custom-call(f32[512,128]{1,0:T(8,128)S(1)} %get-tuple-element.62.refs_0_, f32[512,128]{1,0:T(8,128)S(1)} %copy-done.9, f32[512,128]{1,0:T(8,128)S(1)} %copy-done.11, f32[512,128]{1,0:T(8,128)S(1)} %copy-done.13, f32[4,512,128]{2,1,0:T(8,128)S(1)} %collective-permute-done.4.refs_4_, ...), custom_call_target="tpu_custom_call" | custom-call | tf_op jit(solution)/shard_map/pallas_call | solution.py:174
  187.5 4.0 %collective-permute-start.19 = (f32[4,512,128]{2,1,0:T(8,128)S(1)}, f32[4,512,128]{2,1,0:T(8,128)S(1)}, u32[]{:S(2)}, u32[]{:S(2)}) collective-permute-start(f32[4,512,128]{2,1,0:T(8,128)S(1)} %get-tuple-element.74), channel_id=1, source_target_pairs={{0,1},{1,0},{2,3},{3,2},{4,5},{5,4},{6,7},{7,6},{8,9},{9,8},{10,11... | collective-permute-start | bytes 3145736 | tf_op jit(solution)/shard_map/ppermute | solution.py:397
  191.5 2.3 %collective-permute-done.19.got_ref = f32[4,512,128]{2,1,0:T(8,128)S(1)} collective-permute-done((f32[4,512,128]{2,1,0:T(8,128)S(1)}, f32[4,512,128]{2,1,0:T(8,128)S(1)}, u32[]{:S(2)}, u32[]{:S(2)}) %collective-permute-start.19) | collective-permute-done | bytes 1048608 | tf_op jit(solution)/shard_map/ppermute | solution.py:397
  (72 shorter events, 30.9 us)
Async XLA Ops:
  1.1 24.8 %collective-permute-start = (f32[2,256,128]{2,1,0:T(8,128)S(1)}, f32[2,256,128]{2,1,0:T(8,128)S(1)}, u32[]{:S(2)}, u32[]{:S(2)}) collective-permute-start(f32[2,256,128]{2,1,0:T(8,128)S(1)} %bitcast.25), channel_id=1, source_target_pairs={{0,8},{8,16},{16,24},{24,32},{32,40},{40,48},{48,56},{56,64},{64,7... | collective-permute-start | bytes 786440 | tf_op jit(solution)/shard_map/ppermute | solution.py:408
  3.2 22.7 %collective-permute-start.1 = (f32[2,256,128]{2,1,0:T(8,128)S(1)}, f32[2,256,128]{2,1,0:T(8,128)S(1)}, u32[]{:S(2)}, u32[]{:S(2)}) collective-permute-start(f32[2,256,128]{2,1,0:T(8,128)S(1)} %bitcast.24), channel_id=1, source_target_pairs={{8,0},{16,8},{24,16},{32,24},{40,32},{48,40},{56,48},{64,56},{72,6... | collective-permute-start | bytes 786440 | tf_op jit(solution)/shard_map/ppermute | solution.py:408
  27.6 7.0 %collective-permute-start.3 = (f32[2,256,128]{2,1,0:T(8,128)S(1)}, f32[2,256,128]{2,1,0:T(8,128)S(1)}, u32[]{:S(2)}, u32[]{:S(2)}) collective-permute-start(f32[2,256,128]{2,1,0:T(8,128)S(1)} %get-tuple-element.42.low_ref), channel_id=1, source_target_pairs={{8,0},{16,8},{24,16},{32,24},{40,32},{48,40},{56,48},{64,56},{72,6... | collective-permute-start | bytes 786440 | tf_op jit(solution)/shard_map/ppermute | solution.py:408
  29.1 9.7 %collective-permute-start.2 = (f32[2,256,128]{2,1,0:T(8,128)S(1)}, f32[2,256,128]{2,1,0:T(8,128)S(1)}, u32[]{:S(2)}, u32[]{:S(2)}) collective-permute-start(f32[2,256,128]{2,1,0:T(8,128)S(1)} %get-tuple-element.43.high_ref), channel_id=1, source_target_pairs={{0,8},{8,16},{16,24},{24,32},{32,40},{40,48},{48,56},{56,64},{64,7... | collective-permute-start | bytes 786440 | tf_op jit(solution)/shard_map/ppermute | solution.py:408
  41.2 62.5 %copy-start.8 = (f32[512,128]{1,0:T(8,128)}, f32[512,128]{1,0:T(8,128)S(1)}, u32[]{:S(2)}) copy-start(f32[512,128]{1,0:T(8,128)S(1)} %get-tuple-element.56.refs_1_) | copy-start | bytes 786436
  41.2 62.5 %copy-start.10 = (f32[512,128]{1,0:T(8,128)}, f32[512,128]{1,0:T(8,128)S(1)}, u32[]{:S(2)}) copy-start(f32[512,128]{1,0:T(8,128)S(1)} %get-tuple-element.57.refs_2_) | copy-start | bytes 786436
  41.3 62.5 %copy-start.12 = (f32[512,128]{1,0:T(8,128)}, f32[512,128]{1,0:T(8,128)S(1)}, u32[]{:S(2)}) copy-start(f32[512,128]{1,0:T(8,128)S(1)} %get-tuple-element.58.refs_3_) | copy-start | bytes 786436
  41.3 8.1 %collective-permute-start.4 = (f32[4,512,128]{2,1,0:T(8,128)S(1)}, f32[4,512,128]{2,1,0:T(8,128)S(1)}, u32[]{:S(2)}, u32[]{:S(2)}) collective-permute-start(f32[4,512,128]{2,1,0:T(8,128)S(1)} %get-tuple-element.48), channel_id=1, source_target_pairs={{0,1},{1,0},{2,3},{3,2},{4,5},{5,4},{6,7},{7,6},{8,9},{9,8},{10,11... | collective-permute-start | bytes 3145736 | tf_op jit(solution)/shard_map/ppermute | solution.py:397
  43.7 10.4 %collective-permute-start.5 = (f32[512,128]{1,0:T(8,128)S(1)}, f32[512,128]{1,0:T(8,128)S(1)}, u32[]{:S(2)}, u32[]{:S(2)}) collective-permute-start(f32[512,128]{1,0:T(8,128)S(1)} %get-tuple-element.56.refs_1_), channel_id=1, source_target_pairs={{0,2},{1,3},{2,4},{3,5},{4,6},{5,7},{6,0},{7,1},{8,10},{9,11},{10,... | collective-permute-start | bytes 786440 | tf_op jit(solution)/shard_map/ppermute | solution.py:401
  45.4 15.3 %collective-permute-start.6 = (f32[512,128]{1,0:T(8,128)S(1)}, f32[512,128]{1,0:T(8,128)S(1)}, u32[]{:S(2)}, u32[]{:S(2)}) collective-permute-start(f32[512,128]{1,0:T(8,128)S(1)} %get-tuple-element.57.refs_2_), channel_id=1, source_target_pairs={{0,4},{1,5},{2,6},{3,7},{4,0},{5,1},{6,2},{7,3},{8,12},{9,13},{10,... | collective-permute-start | bytes 786440 | tf_op jit(solution)/shard_map/ppermute | solution.py:401
  48.7 12.0 %collective-permute-start.7 = (f32[512,128]{1,0:T(8,128)S(1)}, f32[512,128]{1,0:T(8,128)S(1)}, u32[]{:S(2)}, u32[]{:S(2)}) collective-permute-start(f32[512,128]{1,0:T(8,128)S(1)} %get-tuple-element.58.refs_3_), channel_id=1, source_target_pairs={{0,6},{1,7},{2,0},{3,1},{4,2},{5,3},{6,4},{7,5},{8,14},{9,15},{10,... | collective-permute-start | bytes 786440 | tf_op jit(solution)/shard_map/ppermute | solution.py:401
  49.5 16.1 %collective-permute-start.10 = (f32[512,128]{1,0:T(8,128)S(1)}, f32[512,128]{1,0:T(8,128)S(1)}, u32[]{:S(2)}, u32[]{:S(2)}) collective-permute-start(f32[512,128]{1,0:T(8,128)S(1)} %get-tuple-element.77), channel_id=1, source_target_pairs={{0,6},{1,7},{2,0},{3,1},{4,2},{5,3},{6,4},{7,5},{8,14},{9,15},{10,... | collective-permute-start | bytes 786440 | tf_op jit(solution)/shard_map/ppermute | solution.py:401
  49.9 16.4 %collective-permute-start.9 = (f32[512,128]{1,0:T(8,128)S(1)}, f32[512,128]{1,0:T(8,128)S(1)}, u32[]{:S(2)}, u32[]{:S(2)}) collective-permute-start(f32[512,128]{1,0:T(8,128)S(1)} %get-tuple-element.78), channel_id=1, source_target_pairs={{0,4},{1,5},{2,6},{3,7},{4,0},{5,1},{6,2},{7,3},{8,12},{9,13},{10,... | collective-permute-start | bytes 786440 | tf_op jit(solution)/shard_map/ppermute | solution.py:401
  54.1 18.2 %collective-permute-start.8 = (f32[512,128]{1,0:T(8,128)S(1)}, f32[512,128]{1,0:T(8,128)S(1)}, u32[]{:S(2)}, u32[]{:S(2)}) collective-permute-start(f32[512,128]{1,0:T(8,128)S(1)} %get-tuple-element.79), channel_id=1, source_target_pairs={{0,2},{1,3},{2,4},{3,5},{4,6},{5,7},{6,0},{7,1},{8,10},{9,11},{10,... | collective-permute-start | bytes 786440 | tf_op jit(solution)/shard_map/ppermute | solution.py:401
  74.9 3.3 %collective-permute-start.12 = (f32[10,256,128]{2,1,0:T(8,128)S(1)}, f32[10,256,128]{2,1,0:T(8,128)S(1)}, u32[]{:S(2)}, u32[]{:S(2)}) collective-permute-start(f32[10,256,128]{2,1,0:T(8,128)S(1)} %get-tuple-element.66), channel_id=1, source_target_pairs={{0,1},{1,0},{2,3},{3,2},{4,5},{5,4},{6,7},{7,6},{8,9},{9,8},{10,11... | collective-permute-start | bytes 3932168 | tf_op jit(solution)/shard_map/ppermute | solution.py:397
  100.6 7.1 %collective-permute-start.15 = (f32[160,128]{1,0:T(8,128)S(1)}, f32[160,128]{1,0:T(8,128)S(1)}, u32[]{:S(2)}, u32[]{:S(2)}) collective-permute-start(f32[160,128]{1,0:T(8,128)S(1)} %shard_map.45), channel_id=1, source_target_pairs={{0,6},{1,7},{2,0},{3,1},{4,2},{5,3},{6,4},{7,5},{8,14},{9,15},{10,... | collective-permute-start | bytes 245768 | tf_op jit(solution)/shard_map/ppermute | solution.py:401
  102.5 5.2 %collective-permute-start.14 = (f32[160,128]{1,0:T(8,128)S(1)}, f32[160,128]{1,0:T(8,128)S(1)}, u32[]{:S(2)}, u32[]{:S(2)}) collective-permute-start(f32[160,128]{1,0:T(8,128)S(1)} %shard_map.45), channel_id=1, source_target_pairs={{0,2},{1,3},{2,4},{3,5},{4,6},{5,7},{6,0},{7,1},{8,10},{9,11},{10,... | collective-permute-start | bytes 245768 | tf_op jit(solution)/shard_map/ppermute | solution.py:401
  102.5 5.5 %collective-permute-start.13 = (f32[160,128]{1,0:T(8,128)S(1)}, f32[160,128]{1,0:T(8,128)S(1)}, u32[]{:S(2)}, u32[]{:S(2)}) collective-permute-start(f32[160,128]{1,0:T(8,128)S(1)} %shard_map.45), channel_id=1, source_target_pairs={{0,4},{1,5},{2,6},{3,7},{4,0},{5,1},{6,2},{7,3},{8,12},{9,13},{10,... | collective-permute-start | bytes 245768 | tf_op jit(solution)/shard_map/ppermute | solution.py:401
  109.2 21.0 %all-to-all-start.1 = ((f32[16,160,128]{2,1,0:T(8,128)}), f32[16,160,128]{2,1,0:T(8,128)S(1)}, u32[]{:S(2)}, u32[]{:S(2)}) async-start(f32[16,160,128]{2,1,0:T(8,128)} %copy-done.1), calls=%async_computation.1 | async-start | bytes 2621440 | tf_op jit(solution)/shard_map/all_to_all | solution.py:459
  113.0 34.9 %collective-permute-start.11 = (f32[3,2,512,128]{3,2,1,0:T(8,128)}, f32[3,2,512,128]{3,2,1,0:T(8,128)}, u32[]{:S(2)}, u32[]{:S(2)}) collective-permute-start(f32[3,2,512,128]{3,2,1,0:T(8,128)} %copy-done.17), channel_id=1, source_target_pairs={{0,2},{1,3},{2,4},{3,5},{4,6},{5,7},{6,0},{7,1},{8,10},{9,11},{10,... | collective-permute-start | bytes 4718600 | tf_op jit(solution)/shard_map/ppermute | solution.py:401
  114.6 33.8 %collective-permute-start.17 = (f32[3,2,512,128]{3,2,1,0:T(8,128)}, f32[3,2,512,128]{3,2,1,0:T(8,128)}, u32[]{:S(2)}, u32[]{:S(2)}) collective-permute-start(f32[3,2,512,128]{3,2,1,0:T(8,128)} %copy-done.16), channel_id=1, source_target_pairs={{0,6},{1,7},{2,0},{3,1},{4,2},{5,3},{6,4},{7,5},{8,14},{9,15},{10,... | collective-permute-start | bytes 4718600 | tf_op jit(solution)/shard_map/ppermute | solution.py:401
  115.7 65.9 %collective-permute-start.16 = (f32[3,2,512,128]{3,2,1,0:T(8,128)}, f32[3,2,512,128]{3,2,1,0:T(8,128)}, u32[]{:S(2)}, u32[]{:S(2)}) collective-permute-start(f32[3,2,512,128]{3,2,1,0:T(8,128)} %copy-done.15), channel_id=1, source_target_pairs={{0,4},{1,5},{2,6},{3,7},{4,0},{5,1},{6,2},{7,3},{8,12},{9,13},{10,... | collective-permute-start | bytes 4718600 | tf_op jit(solution)/shard_map/ppermute | solution.py:401
  130.2 7.0 %collective-permute-start.18 = (f32[16,160,128]{2,1,0:T(8,128)S(1)}, f32[16,160,128]{2,1,0:T(8,128)S(1)}, u32[]{:S(2)}, u32[]{:S(2)}) collective-permute-start(f32[16,160,128]{2,1,0:T(8,128)S(1)} %all-to-all-done.1.mine_ref), channel_id=1, source_target_pairs={{0,1},{1,0},{2,3},{3,2},{4,5},{5,4},{6,7},{7,6},{8,9},{9,8},{10,11... | collective-permute-start | bytes 3932168 | tf_op jit(solution)/shard_map/ppermute | solution.py:397
  187.5 6.3 %collective-permute-start.19 = (f32[4,512,128]{2,1,0:T(8,128)S(1)}, f32[4,512,128]{2,1,0:T(8,128)S(1)}, u32[]{:S(2)}, u32[]{:S(2)}) collective-permute-start(f32[4,512,128]{2,1,0:T(8,128)S(1)} %get-tuple-element.74), channel_id=1, source_target_pairs={{0,1},{1,0},{2,3},{3,2},{4,5},{5,4},{6,7},{7,6},{8,9},{9,8},{10,11... | collective-permute-start | bytes 3145736 | tf_op jit(solution)/shard_map/ppermute | solution.py:397
  (15 other events, 338.9 us)

commit v6 on v5

--- a/solution.py
+++ b/solution.py
@@ -10,7 +10,9 @@
 VECTORS = 1024
 REACH = 2
 TILE = 256
-PAIRS = [(i, j) for i in range(4) for j in range(i, 4)]
+PAIRS = [(0, 0), (1, 1), (0, 1), (0, 2), (0, 3), (2, 2), (3, 3), (1, 2), (1, 3), (2, 3)]
+INNER_ROWS = 384
+EDGE_ROWS = 128
 SPAN = 2 * REACH + 1
 TOTAL = 256
 RING = 8
@@ -120,7 +122,16 @@
         out_ref[at % REACH] = first_of(apply_one(op_ref, wide_ref, elem), own_ref[elem])
 
 
-def second_edge_kernel(count, at_ref, op_ref, mid_ref, low_ref, high_ref, before_ref, after_ref, base_ref, done_ref, *refs):
+def deal(at_ref, all_ref, own_refs, other_ref):
+    z, c = at_ref[2], at_ref[3]
+    size = own_refs[0].shape[0]
+    for k in range(4):
+        chip = lax.rem(z + k, 4)
+        own_refs[k][...] = all_ref[pl.ds(pl.multiple_of((c * 4 + chip) * size, 128), size)]
+        other_ref[k] = all_ref[pl.ds(pl.multiple_of(((1 - c) * 4 + chip) * size, 128), size)]
+
+
+def second_edge_kernel(count, at_ref, op_ref, mid_ref, low_ref, high_ref, before_ref, after_ref, base_ref, *refs):
     own_refs, (other_ref, wide_ref, all_ref) = refs[:4], refs[4:]
     for r in range(REACH):
         spread(wide_ref, r, before_ref[r])
@@ -131,19 +142,12 @@
         spread(wide_ref, REACH + count + r, after_ref[r])
     for at, elem in enumerate(edges_of(count)):
         own = (low_ref if at < REACH else high_ref)[at % REACH]
-        all_ref[elem] = second_of(apply_one(op_ref, wide_ref, elem), own, base_ref[elem])
-    for at in range(count - 2 * REACH):
-        all_ref[REACH + at] = done_ref[at]
-    z, c = at_ref[2], at_ref[3]
-    half = count // 2
-    for k in range(4):
-        chip = lax.rem(z + k, 4)
-        for r in range(2):
-            other_ref[k, r * 256 : (r + 1) * 256] = all_ref[(1 - c) * half + chip * 2 + r]
-            own_refs[k][r * 256 : (r + 1) * 256] = all_ref[c * half + chip * 2 + r]
-
-
-def inner_kernel(count, op_ref, mid_ref, low_ref, high_ref, base_ref, out_ref, wide_ref):
+        all_ref[at * 256 : (at + 1) * 256] = second_of(apply_one(op_ref, wide_ref, elem), own, base_ref[elem])
+    deal(at_ref, all_ref, own_refs, other_ref)
+
+
+def inner_kernel(count, at_ref, op_ref, mid_ref, low_ref, high_ref, base_ref, *refs):
+    own_refs, (other_ref, wide_ref, all_ref) = refs[:4], refs[4:]
     for r in range(REACH):
         spread(wide_ref, REACH + r, low_ref[r])
         spread(wide_ref, count + r, high_ref[r])
@@ -154,10 +158,12 @@
         for u in range(4):
             at = 4 * g + u
             elem = REACH + at
-            out_ref[at] = second_of(apply_one(op_ref, wide_ref, elem), mid_ref[at], base_ref[elem])
+            rows = pl.ds(pl.multiple_of(at * 256, 256), 256)
+            all_ref[rows] = second_of(apply_one(op_ref, wide_ref, elem), mid_ref[at], base_ref[elem])
         return 0
 
     lax.fori_loop(0, (count - 2 * REACH) // 4, body, 0)
+    deal(at_ref, all_ref, own_refs, other_ref)
 
 
 VMEM_SPEC = pl.BlockSpec(memory_space=pltpu.VMEM)
@@ -214,32 +220,36 @@
     )
 
 
-def second_inner(op, mid, low, high, base):
+def second_inner(here, op, mid, low, high, base):
     count = base.shape[0]
-    return call(
-        functools.partial(inner_kernel, count), shaped(*mid.shape), [VMEM_SPEC] * 5,
-        [wide_scratch(count)], (op, mid, low, high, base), OPERATOR_LIMIT,
-    )
-
-
-def second_edges(here, op, mid, low, high, halos, base, done):
+    outs = call(
+        functools.partial(inner_kernel, count), (shaped(INNER_ROWS, 128),) * 4 + (shaped(4, INNER_ROWS, 128),),
+        [SMEM_SPEC] + [VMEM_SPEC] * 5,
+        [wide_scratch(count), pltpu.VMEM((8 * INNER_ROWS, 128), F32)],
+        (here, op, mid, low, high, base), OPERATOR_LIMIT,
+    )
+    return outs[:4], outs[4]
+
+
+def second_edges(here, op, mid, low, high, halos, base):
     count = base.shape[0]
-    chunk = shaped(512, 128)
     outs = call(
-        functools.partial(second_edge_kernel, count), (chunk,) * 4 + (shaped(4, 512, 128),),
-        [SMEM_SPEC] + [VMEM_SPEC] * 8,
-        [wide_scratch(count), pltpu.VMEM(base.shape, F32)],
-        (here, op, mid, low, high, *halos, base, done), OPERATOR_LIMIT,
+        functools.partial(second_edge_kernel, count), (shaped(EDGE_ROWS, 128),) * 4 + (shaped(4, EDGE_ROWS, 128),),
+        [SMEM_SPEC] + [VMEM_SPEC] * 7,
+        [wide_scratch(count), pltpu.VMEM((8 * EDGE_ROWS, 128), F32)],
+        (here, op, mid, low, high, *halos, base), OPERATOR_LIMIT,
     )
     return outs[:4], outs[4]
 
 
 def bulk_kernel(*refs):
-    own_refs, got_ref, out_refs = refs[:4], refs[4], refs[5:]
+    inner_refs, edge_refs, inner_got, edge_got, out_refs = refs[:4], refs[4:8], refs[8], refs[9], refs[10:]
     for k in range(1, 4):
         for i, m in enumerate(chunks_for(k)):
-            out_refs[k - 1][i, 0] = own_refs[m][...]
-            out_refs[k - 1][i, 1] = got_ref[m]
+            out_refs[k - 1][i, 0, :INNER_ROWS] = inner_refs[m][...]
+            out_refs[k - 1][i, 0, INNER_ROWS:] = edge_refs[m][...]
+            out_refs[k - 1][i, 1, :INNER_ROWS] = inner_got[m]
+            out_refs[k - 1][i, 1, INNER_ROWS:] = edge_got[m]
 
 
 def chunks_for(k):
@@ -264,6 +274,12 @@
 
 def lanes(start, size):
     return pl.ds(pl.multiple_of(start, size), size)
+
+
+def places_of(m):
+    if m < 2:
+        return [(3 * m, 0, 0), (3 * m + 1, 0, 1), (3 * m + 2, 1, 1)]
+    return [(6 + 4 * (m - 2) + 2 * a + b, a, b) for a in range(2) for b in range(2)]
 
 
 def half_of_gram(half, hi_ref, lo_ref, out_ref):
@@ -275,19 +291,26 @@
         left = jnp.concatenate([left_hi, left_hi, lo_ref[:, i]], axis=0)
         right = jnp.concatenate([right_hi, lo_ref[:, j], right_hi], axis=0)
         block = lax.dot_general(left, right, (((0,), (0,)), ((), ())), preferred_element_type=F32)
-        out_ref[2 * m] = block[:, :128]
-        out_ref[2 * m + 1] = block[:, 128:]
-
-
-def gram_send_kernel(at_ref, *refs):
-    owns, gots, (hi_ref, lo_ref, out_ref) = refs[:4], refs[4:8], refs[8:]
+        for at, a, b in places_of(m):
+            out_ref[at] = block[a * 128 : (a + 1) * 128, b * 128 : (b + 1) * 128]
+
+
+def gram_send_kernel(at_ref, inner_ref, edge_ref, inner_got, edge_got, *refs):
+    arrived, (hi_ref, lo_ref, out_ref) = refs[:12], refs[12:]
     z, c = at_ref[2], at_ref[3]
     for k in range(4):
         for j in range(2):
             band = lax.rem(z + 4 - k, 4) * 2 + lax.rem(c + j, 2)
-            hi, lo = split((owns, gots)[j][k][...])
-            hi_ref[:, lanes(band * 128, 128)] = hi
-            lo_ref[:, lanes(band * 128, 128)] = lo
+            if k:
+                inner, edge = arrived[6 * j + k - 1][...], arrived[6 * j + 3 + k - 1][...]
+            elif j:
+                inner, edge = inner_got[0], edge_got[0]
+            else:
+                inner, edge = inner_ref[...], edge_ref[...]
+            for value, rows in ((inner, slice(0, INNER_ROWS)), (edge, slice(INNER_ROWS, 512))):
+                hi, lo = split(value)
+                hi_ref[rows, lanes(band * 128, 128)] = hi
+                lo_ref[rows, lanes(band * 128, 128)] = lo
     half_of_gram(1 - c, hi_ref, lo_ref, out_ref)
 
 
@@ -301,33 +324,26 @@
 
 def poly_kernel(order, at_ref, mine_ref, theirs_ref, ph_ref, pl_ref, stretch_ref, gram_ref, nh_ref, nl_ref, poly_ref):
     z, c = at_ref[2], at_ref[3]
-    for ky in range(4):
-        for kx in range(4):
-            rows = slice((ky * 4 + kx) * 160, (ky * 4 + kx + 1) * 160)
-            gram_ref[c, rows] = mine_ref[ky * 4 + kx]
-            gram_ref[1 - c, rows] = theirs_ref[ky * 4 + kx]
-
-    def packed(n, h):
-        at = 2 * (n % 5) + h
-        return gram_ref[n // 5, at * 256 : (at + 1) * 256]
-
-    row = lax.broadcasted_iota(jnp.int32, (256, 128), 0)
-    col = lax.broadcasted_iota(jnp.int32, (256, 128), 1)
-    diag = jnp.zeros((256, 128), F32)
-    for n, (i, j) in enumerate(PAIRS):
-        if i == j:
-            for h in range(2):
-                diag += jnp.where(row == col + 128 * h, packed(n, h), 0.0)
+    gram_ref[c] = mine_ref[...]
+    gram_ref[1 - c] = theirs_ref[...]
+    row = lax.broadcasted_iota(jnp.int32, (128, 128), 0)
+    col = lax.broadcasted_iota(jnp.int32, (128, 128), 1)
+    diag = jnp.zeros((128, 128), F32)
+    for half in range(2):
+        for m in range(2):
+            for at, a, b in places_of(m):
+                if a == b:
+                    diag += jnp.where(row == col, gram_ref[half, at], 0.0)
     scale = jnp.sum(diag) / VECTORS
     for n, (i, j) in enumerate(PAIRS):
-        for h in range(2):
-            hi, lo = split(packed(n, h) / scale)
-            at = j * TILE + h * 128
-            nh_ref[i * TILE : (i + 1) * TILE, at : at + 128] = hi
-            nl_ref[i * TILE : (i + 1) * TILE, at : at + 128] = lo
-            if i != j:
-                nh_ref[at : at + 128, i * TILE : (i + 1) * TILE] = hi.T
-                nl_ref[at : at + 128, i * TILE : (i + 1) * TILE] = lo.T
+        for at, a, b in places_of(n % 5):
+            hi, lo = split(gram_ref[n // 5, at] / scale)
+            p, q = i * TILE + a * 128, j * TILE + b * 128
+            nh_ref[p : p + 128, q : q + 128] = hi
+            nl_ref[p : p + 128, q : q + 128] = lo
+            if p != q:
+                nh_ref[q : q + 128, p : p + 128] = hi.T
+                nl_ref[q : q + 128, p : p + 128] = lo.T
     stretch_ref[...] = jnp.sqrt(jnp.full((8, 128), order, F32) / scale)
     right = []
     for j in range(2):
@@ -352,16 +368,21 @@
 
 
 def turned_kernel(*refs):
-    owns, got_ref, part_owns, part_gots, bulks = refs[:4], refs[4], refs[5:8], refs[8:11], refs[11:14]
-    ph_ref, pl_ref, stretch_ref, mine_ref, theirs_ref = refs[14:]
+    inner_refs, edge_refs, inner_got, edge_got = refs[:4], refs[4:8], refs[8], refs[9]
+    arrived, bulks = refs[10:22], refs[22:25]
+    ph_ref, pl_ref, stretch_ref, mine_ref, theirs_ref = refs[25:]
 
     def piece(r, q, j):
         k = (4 - q) % 4
-        if q == 0:
-            return owns[r][...] if j == 0 else got_ref[r]
-        if r == 0:
-            return (part_owns, part_gots)[j][k - 1][...]
-        return bulks[k - 1][chunks_for(k).index((r + k) % 4), j]
+        if q == 0 and j == 0:
+            pair = (inner_refs[r][...], edge_refs[r][...])
+        elif q == 0:
+            pair = (inner_got[r], edge_got[r])
+        elif r == 0:
+            pair = (arrived[6 * j + k - 1][...], arrived[6 * j + 3 + k - 1][...])
+        else:
+            return bulks[k - 1][chunks_for(k).index((r + k) % 4), j]
+        return jnp.concatenate(pair, axis=0)
 
     ph, low = ph_ref[...], pl_ref[...]
     for r in range(4):
@@ -377,19 +398,32 @@
         theirs_ref[r] = out[:, 128:] * stretch
 
 
-def place_kernel(at_ref, mine_ref, got_ref, out_ref, sem):
+def place_kernel(theirs, at_ref, rows_ref, *refs):
+    out_ref, sem = refs[-2:]
     z, c = at_ref[2], at_ref[3]
+    half = 1 - c if theirs else c
     copies = []
     for k in range(4):
         chip = lax.rem(z + k, 4)
-        copies.append(pltpu.make_async_copy(mine_ref.at[k], out_ref.at[c * 4 + chip], sem.at[k]))
-        copies.append(pltpu.make_async_copy(got_ref.at[k], out_ref.at[(1 - c) * 4 + chip], sem.at[4 + k]))
+        inner = pl.ds(pl.multiple_of(512 + (half * 4 + chip) * INNER_ROWS, 128), INNER_ROWS)
+        edge = pl.ds(pl.multiple_of(half * 3584 + chip * EDGE_ROWS, 128), EDGE_ROWS)
+        copies.append(pltpu.make_async_copy(rows_ref.at[k, pl.ds(0, INNER_ROWS)], out_ref.at[inner], sem.at[k]))
+        copies.append(pltpu.make_async_copy(rows_ref.at[k, pl.ds(INNER_ROWS, EDGE_ROWS)], out_ref.at[edge], sem.at[4 + k]))
     for copy in copies:
         copy.start()
     for copy in copies:
         copy.wait()
 
 
+def place(here, rows, into=None):
+    extra = () if into is None else (into,)
+    return call(
+        functools.partial(place_kernel, into is not None), shaped(4096, 128), [SMEM_SPEC, ANY_SPEC] + [ANY_SPEC] * len(extra),
+        [pltpu.SemaphoreType.DMA((8,))], (here, rows, *extra), STEP_LIMIT,
+        out_specs=ANY_SPEC, input_output_aliases={2: 0} if extra else {},
+    )
+
+
 SHIFTS = (2, 1, 3)
 
 
@@ -405,7 +439,8 @@
     size = lax.axis_size("space")
     up = [(i, (i + 1) % size) for i in range(size)]
     down = [(j, i) for i, j in up]
-    return lax.ppermute(last, "space", up), lax.ppermute(first, "space", down)
+    before = lax.ppermute(last, "space", up)
+    return before, lax.ppermute(first, "space", down)
 
 
 def steps(vectors, blocks, neighbours):
@@ -421,35 +456,39 @@
     mid, op = build_operator(neighbours.T, here, blocks, start)
     low, high = first_edges(op, start, halos)
     halos = halos_of(low, high)
-    done = second_inner(op, mid, low, high, start)
-    own, other = second_edges(here, op, mid, low, high, halos, start, done)
+    inner, other = second_inner(here, op, mid, low, high, start)
+    inner_got = swap_cores(other)
+    arrived = {}
+    for j, rows in enumerate((inner, inner_got)):
+        for k in SHIFTS:
+            arrived[j, 0, k] = shift_z(rows[k], k)
+    edge, other = second_edges(here, op, mid, low, high, halos, start)
+    edge_got = swap_cores(other)
+    for j, rows in enumerate((edge, edge_got)):
+        for k in SHIFTS:
+            arrived[j, 1, k] = shift_z(rows[k], k)
+    arrived = [arrived[j, e, k] for j in range(2) for e in range(2) for k in (1, 2, 3)]
 
     share = elem_dev * basis // 8
-    got = swap_cores(other)
-    part_own = {k: shift_z(own[k], k) for k in SHIFTS}
-    part_got = {k: shift_z(got[k], k) for k in SHIFTS}
-    part_own[0], part_got[0] = own[0], got[0]
-    part_own = [part_own[k] for k in range(4)]
-    part_got = [part_got[k] for k in range(4)]
-
-    late_own, late_got, part_own, part_got = lax.optimization_barrier((own, got, part_own, part_got))
-    bulks = call(bulk_kernel, (shaped(3, 2, share, panel),) * 3, [VMEM_SPEC] * 5, [], (*late_own, late_got), STEP_LIMIT)
+    held = (*inner, *edge, inner_got, edge_got)
+    late, arrived = lax.optimization_barrier((held, arrived))
+    bulks = call(bulk_kernel, (shaped(3, 2, share, panel),) * 3, [VMEM_SPEC] * 10, [], late, STEP_LIMIT)
     sent = {}
     for k in (1, 3):
         sent[k] = shift_z(bulks[k - 1], k)
 
-    half = shaped(10, 256, 128)
+    half = shaped(18, 128, 128)
     wide = shaped(share, VECTORS, dtype=BF16)
     hi, lo, send = call(
-        gram_send_kernel, (wide, wide, half), [SMEM_SPEC] + [VMEM_SPEC] * 8, [],
-        (here, *part_own, *part_got), STEP_LIMIT,
+        gram_send_kernel, (wide, wide, half), [SMEM_SPEC] + [VMEM_SPEC] * 16, [],
+        (here, inner[0], edge[0], inner_got, edge_got, *arrived), STEP_LIMIT,
     )
     theirs = swap_cores(send)
     keep = call(gram_keep_kernel, half, [SMEM_SPEC] + [VMEM_SPEC] * 2, [], (here, hi, lo), STEP_LIMIT)
     total = call(add_kernel, half, [VMEM_SPEC] * 2, [], (keep, theirs), STEP_LIMIT)
-    pieces = total.reshape(16, 160, panel)
+    pieces = total.reshape(16, 144, panel)
     pieces = lax.all_to_all(pieces, "space", split_axis=0, concat_axis=0, tiled=True)
-    piece = call(fold_kernel, shaped(160, panel), [VMEM_SPEC], [], (pieces,), STEP_LIMIT)
+    piece = call(fold_kernel, shaped(144, panel), [VMEM_SPEC], [], (pieces,), STEP_LIMIT)
     sums = [shift_z(piece, k) for k in SHIFTS]
     piece = piece + sums[0] + (sums[1] + sums[2])
     late, piece = lax.optimization_barrier((bulks[1], piece))
@@ -457,13 +496,14 @@
     bulks = [sent[k] for k in (1, 2, 3)]
     copies = call(copy_kernel, shaped(*pieces.shape), [VMEM_SPEC], [], (piece,), STEP_LIMIT)
     mine = lax.all_to_all(copies, "space", split_axis=0, concat_axis=0, tiled=True)
+    mine = mine.reshape(half.shape)
     theirs = swap_cores(mine)
 
     poly = shaped(VECTORS, TILE, dtype=BF16)
     ph, low, stretch = call(
         functools.partial(poly_kernel, order), (poly, poly, shaped(8, 128)), [SMEM_SPEC] + [VMEM_SPEC] * 2,
         [
-            pltpu.VMEM((2, 2560, 128), F32),
+            pltpu.VMEM((2, *half.shape), F32),
             pltpu.VMEM((VECTORS, VECTORS), BF16),
             pltpu.VMEM((VECTORS, VECTORS), BF16),
             pltpu.VMEM((VECTORS, TILE), F32),
@@ -472,15 +512,11 @@
     )
     quarter = shaped(4, share, panel)
     mine, theirs = call(
-        turned_kernel, (quarter, quarter), [VMEM_SPEC] * 17, [],
-        (*own, got, *part_own[1:], *part_got[1:], *bulks, ph, low, stretch), TURN_LIMIT,
+        turned_kernel, (quarter, quarter), [VMEM_SPEC] * 28, [],
+        (*held, *arrived, *bulks, ph, low, stretch), TURN_LIMIT,
     )
     theirs = swap_cores(theirs)
-    placed = call(
-        place_kernel, shaped(8, share, panel), [SMEM_SPEC] + [ANY_SPEC] * 2, [pltpu.SemaphoreType.DMA((8,))],
-        (here, mine, theirs), STEP_LIMIT, out_specs=ANY_SPEC,
-    )
-    return placed.reshape(elem_dev * basis, panel)
+    return place(here, theirs, place(here, mine))
 
 
 def solution(mesh):

time: 196 us -> 206 us (1.051)
  starting transfers between devices: 37.5 us -> 48 us
  Pallas kernels: 42.4 us -> 44.9 us
    ppermute x12 -> x18, starting transfers between devices: 15 us -> 22.2 us  [shift_z(): return lax.ppermute(x, 'band', [(i, (i + 2 * k) % 8) for i in range(8)])]
    ppermute x4, waiting for transfers between devices: 4.64 us -> 10.8 us  [the longest x2 6.12 us: halos_of(): return (before, lax.ppermute(first, 'space', down))]
    ppermute x12 -> x18, waiting for transfers between devices: 61 us -> 56.1 us  [shift_z(): return lax.ppermute(x, 'band', [(i, (i + 2 * k) % 8) for i in range(8)])]
    ppermute x4 -> x5, starting transfers between devices: 11.4 us -> 14.6 us  [swap_cores(): return lax.ppermute(x, 'band', [(i, i ^ 1) for i in range(8)])]
    pallas_call x13 -> x14, Pallas kernels: 42.4 us -> 44.9 us  [call(): pl.pallas_call(kernel, out_shape=outs, in_specs=specs, out_specs=kwargs.p...]
    ppermute x4 -> x5, waiting for transfers between devices: 5.75 us -> 3.73 us  [swap_cores(): return lax.ppermute(x, 'band', [(i, i ^ 1) for i in range(8)])]
    unnamed x36 -> x58, local copies, waits for them, and re-layouts: 6.96 us -> 5.94 us
  transfers between devices with their start and end apart: 21 -> 28, of which waited for: 16 -> 14; matrix products, arithmetic and copies ran while one was open for 0% -> 0% of each run, Pallas kernels for 14% -> 13%
where the time goes in v6:
time: 206 us
  waiting for transfers between devices  84 us (41%)
  starting transfers between devices  48 us (23%)
  Pallas kernels  44.9 us (22%)
  blocking collectives  20.9 us (10%)
  local copies, waits for them, and re-layouts  7.06 us (3%)
    ppermute x18, waiting for transfers between devices, shift_z(): return lax.ppermute(x, 'band', [(i, (i + 2 * k) % 8) for i in range(8)])  56.1 us
    pallas_call x14, Pallas kernels, call(): pl.pallas_call(kernel, out_shape=outs, in_specs=specs, out_specs=kwargs.p...  44.9 us
    ppermute x18, starting transfers between devices, shift_z(): return lax.ppermute(x, 'band', [(i, (i + 2 * k) % 8) for i in range(8)])  22.2 us
    all_to_all x1, blocking collectives, steps(): lax.all_to_all(pieces, 'space', split_axis=0, concat_axis=0, tiled=True)  20.9 us
    ppermute x5, starting transfers between devices, swap_cores(): return lax.ppermute(x, 'band', [(i, i ^ 1) for i in range(8)])  14.6 us
    all_to_all x1, waiting for transfers between devices, steps(): lax.all_to_all(copies, 'space', split_axis=0, concat_axis=0, tiled=True)  13.3 us
    ppermute x2, waiting for transfers between devices, halos_of(): return (before, lax.ppermute(first, 'space', down))  6.12 us
    unnamed x58, local copies, waits for them, and re-layouts  5.94 us
  transfers between devices with their start and end apart: 28, of which 14 were waited for; matrix products, arithmetic and copies ran while one was open for 0% of the time, Pallas kernels for 13%

profile of v6, /device:TPU:1, one launch (start us, length us, event | category | flops | bytes accessed | tf_op | source)
XLA Modules:
  0.0 205.7 jit_solution(8223755871850534715)
XLA Ops:
  1.1 2.1 %collective-permute-start = (f32[2,256,128]{2,1,0:T(8,128)S(1)}, f32[2,256,128]{2,1,0:T(8,128)S(1)}, u32[]{:S(2)}, u32[]{:S(2)}) collective-permute-start(f32[2,256,128]{2,1,0:T(8,128)S(1)} %bitcast.31), channel_id=1, source_target_pairs={{0,8},{8,16},{16,24},{24,32},{32,40},{40,48},{48,56},{56,64},{64,7... | collective-permute-start | bytes 786440 | tf_op jit(solution)/shard_map/ppermute | solution.py:442
  3.2 3.8 %collective-permute-start.1 = (f32[2,256,128]{2,1,0:T(8,128)S(1)}, f32[2,256,128]{2,1,0:T(8,128)S(1)}, u32[]{:S(2)}, u32[]{:S(2)}) collective-permute-start(f32[2,256,128]{2,1,0:T(8,128)S(1)} %bitcast.30), channel_id=1, source_target_pairs={{8,0},{16,8},{24,16},{32,24},{40,32},{48,40},{56,48},{64,56},{72,6... | collective-permute-start | bytes 786440 | tf_op jit(solution)/shard_map/ppermute | solution.py:443
  9.3 16.5 %shard_map.37 = (f32[12,256,128]{2,1,0:T(8,128)S(1)}, bf16[16,512,1280]{2,1,0:T(8,128)(2,1)S(1)}) custom-call(s32[7,16]{1,0:T(8,128)S(1)} %bitcast.29, s32[4]{0:T(128)S(1)} %pad_add_fusion.at_ref, f32[16,7,256,256]{3,2,1,0:T(8,128)} %blocks_ref.1, f32[16,256,128]{2,1,0:T(8,128)S(1)} %bitcast.22), custom_call_target="tpu_custom_call" | custom-call | tf_op jit(solution)/shard_map/pallas_call | solution.py:180
  27.6 5.6 %shard_map.39 = (f32[384,128]{1,0:T(8,128)S(1)}, f32[384,128]{1,0:T(8,128)S(1)}, f32[384,128]{1,0:T(8,128)S(1)}, f32[384,128]{1,0:T(8,128)S(1)}, f32[4,384,128]{2,1,0:T(8,128)S(1)}) custom-call(s32[4]{0:T(128)S(1)} %pad_add_fusion.at_ref, bf16[16,512,1280]{2,1,0:T(8,128)(2,1)S(1)} %get-tuple-element.54.op_ref, ...), custom_call_target="tpu_custom_call" | custom-call | tf_op jit(solution)/shard_map/pallas_call | solution.py:180
  35.9 6.1 %collective-permute-done.3.after_ref = f32[2,256,128]{2,1,0:T(8,128)S(1)} collective-permute-done((f32[2,256,128]{2,1,0:T(8,128)S(1)}, f32[2,256,128]{2,1,0:T(8,128)S(1)}, u32[]{:S(2)}, u32[]{:S(2)}) %collective-permute-start.3) | collective-permute-done | bytes 262176 | tf_op jit(solution)/shard_map/ppermute | solution.py:443
  42.0 4.7 %collective-permute-done.2.before_ref = f32[2,256,128]{2,1,0:T(8,128)S(1)} collective-permute-done((f32[2,256,128]{2,1,0:T(8,128)S(1)}, f32[2,256,128]{2,1,0:T(8,128)S(1)}, u32[]{:S(2)}, u32[]{:S(2)}) %collective-permute-start.2) | collective-permute-done | bytes 262176 | tf_op jit(solution)/shard_map/ppermute | solution.py:442
  46.7 2.3 %shard_map.40 = (f32[128,128]{1,0:T(8,128)S(1)}, f32[128,128]{1,0:T(8,128)S(1)}, f32[128,128]{1,0:T(8,128)S(1)}, f32[128,128]{1,0:T(8,128)S(1)}, f32[4,128,128]{2,1,0:T(8,128)S(1)}) custom-call(s32[4]{0:T(128)S(1)} %pad_add_fusion.at_ref, bf16[16,512,1280]{2,1,0:T(8,128)(2,1)S(1)} %get-tuple-element.54.op_ref, ...), custom_call_target="tpu_custom_call" | custom-call | tf_op jit(solution)/shard_map/pallas_call | solution.py:180
  52.0 3.3 %collective-permute-start.7 = (f32[384,128]{1,0:T(8,128)S(1)}, f32[384,128]{1,0:T(8,128)S(1)}, u32[]{:S(2)}, u32[]{:S(2)}) collective-permute-start(f32[384,128]{1,0:T(8,128)S(1)} %get-tuple-element.82.refs_2_), channel_id=1, source_target_pairs={{0,4},{1,5},{2,6},{3,7},{4,0},{5,1},{6,2},{7,3},{8,12},{9,13},{10,... | collective-permute-start | bytes 589832 | tf_op jit(solution)/shard_map/ppermute | solution.py:435
  56.8 2.5 %collective-permute-done.6.refs_0_.refs_10_ = f32[384,128]{1,0:T(8,128)S(1)} collective-permute-done((f32[384,128]{1,0:T(8,128)S(1)}, f32[384,128]{1,0:T(8,128)S(1)}, u32[]{:S(2)}, u32[]{:S(2)}) %collective-permute-start.6) | collective-permute-done | bytes 196640 | tf_op jit(solution)/shard_map/ppermute | solution.py:435
  60.8 3.7 %collective-permute-done.7.refs_1_.refs_11_ = f32[384,128]{1,0:T(8,128)S(1)} collective-permute-done((f32[384,128]{1,0:T(8,128)S(1)}, f32[384,128]{1,0:T(8,128)S(1)}, u32[]{:S(2)}, u32[]{:S(2)}) %collective-permute-start.7) | collective-permute-done | bytes 196640 | tf_op jit(solution)/shard_map/ppermute | solution.py:435
  70.1 4.5 %collective-permute-done.11.refs_5_.refs_15_ = f32[128,128]{1,0:T(8,128)S(1)} collective-permute-done((f32[128,128]{1,0:T(8,128)S(1)}, f32[128,128]{1,0:T(8,128)S(1)}, u32[]{:S(2)}, u32[]{:S(2)}) %collective-permute-start.11) | collective-permute-done | bytes 65568 | tf_op jit(solution)/shard_map/ppermute | solution.py:435
  80.9 2.5 %shard_map.42 = (bf16[512,1024]{1,0:T(8,128)(2,1)S(1)}, bf16[512,1024]{1,0:T(8,128)(2,1)S(1)}, f32[18,128,128]{2,1,0:T(8,128)S(1)}) custom-call(s32[4]{0:T(128)S(1)} %pad_add_fusion.at_ref, f32[384,128]{1,0:T(8,128)S(1)} %get-tuple-element.80.refs_0_.inner_ref, f32[128,128]{1,0:T(8,128)S(1)} %get-tuple-element.84.refs_4_.edge_ref, ...), custom_call_target="tpu_custom_call" | custom-call | tf_op jit(solution)/shard_map/pallas_call | solution.py:180
  83.4 4.6 %collective-permute-start.19 = (f32[18,128,128]{2,1,0:T(8,128)S(1)}, f32[18,128,128]{2,1,0:T(8,128)S(1)}, u32[]{:S(2)}, u32[]{:S(2)}) collective-permute-start(f32[18,128,128]{2,1,0:T(8,128)S(1)} %get-tuple-element.94), channel_id=1, source_target_pairs={{0,1},{1,0},{2,3},{3,2},{4,5},{5,4},{6,7},{7,6},{8,9},{9,8},{10,11... | collective-permute-start | bytes 3538952 | tf_op jit(solution)/shard_map/ppermute | solution.py:431
  90.6 20.9 %all_to_all.10.parts_ref = f32[16,144,128]{2,1,0:T(8,128)S(1)} all-to-all(f32[16,144,128]{2,1,0:T(8,128)S(1)} %bitcast.28), channel_id=1, replica_groups=mesh['space'=16,'band'=8] {'space'}, dimensions={0} | all-to-all | bytes 2359296 | tf_op jit(solution)/shard_map/all_to_all | solution.py:490
  119.7 3.7 %all-to-all-start.1 = ((f32[16,144,128]{2,1,0:T(8,128)}), f32[16,144,128]{2,1,0:T(8,128)S(1)}, u32[]{:S(2)}, u32[]{:S(2)}) async-start(f32[16,144,128]{2,1,0:T(8,128)} %shard_map.46), calls=%async_computation.1 | async-start | bytes 2359296 | tf_op jit(solution)/shard_map/all_to_all | solution.py:498
  124.0 2.1 %collective-permute-start.24 = (f32[3,2,512,128]{3,2,1,0:T(8,128)}, f32[3,2,512,128]{3,2,1,0:T(8,128)}, u32[]{:S(2)}, u32[]{:S(2)}) collective-permute-start(f32[3,2,512,128]{3,2,1,0:T(8,128)} %copy-done.27), channel_id=1, source_target_pairs={{0,6},{1,7},{2,0},{3,1},{4,2},{5,3},{6,4},{7,5},{8,14},{9,15},{10,... | collective-permute-start | bytes 4718600 | tf_op jit(solution)/shard_map/ppermute | solution.py:435
  126.4 13.3 %all-to-all-done.1 = f32[16,144,128]{2,1,0:T(8,128)S(1)} async-done(((f32[16,144,128]{2,1,0:T(8,128)}), f32[16,144,128]{2,1,0:T(8,128)S(1)}, u32[]{:S(2)}, u32[]{:S(2)}) %all-to-all-start.1) | async-done | bytes 1179680 | tf_op jit(solution)/shard_map/all_to_all | solution.py:498
  139.8 3.9 %collective-permute-start.25 = (f32[18,128,128]{2,1,0:T(8,128)S(1)}, f32[18,128,128]{2,1,0:T(8,128)S(1)}, u32[]{:S(2)}, u32[]{:S(2)}) collective-permute-start(f32[18,128,128]{2,1,0:T(8,128)S(1)} %bitcast.26), channel_id=1, source_target_pairs={{0,1},{1,0},{2,3},{3,2},{4,5},{5,4},{6,7},{7,6},{8,9},{9,8},{10,11... | collective-permute-start | bytes 3538952 | tf_op jit(solution)/shard_map/ppermute | solution.py:431
  143.7 2.5 %collective-permute-done.25.theirs_ref = f32[18,128,128]{2,1,0:T(8,128)S(1)} collective-permute-done((f32[18,128,128]{2,1,0:T(8,128)S(1)}, f32[18,128,128]{2,1,0:T(8,128)S(1)}, u32[]{:S(2)}, u32[]{:S(2)}) %collective-permute-start.25) | collective-permute-done | bytes 1179680 | tf_op jit(solution)/shard_map/ppermute | solution.py:431
  146.2 3.8 %shard_map.47 = (bf16[1024,256]{1,0:T(8,128)(2,1)S(1)}, bf16[1024,256]{1,0:T(8,128)(2,1)S(1)}, f32[8,128]{1,0:T(8,128)S(1)}) custom-call(s32[4]{0:T(128)S(1)} %pad_add_fusion.at_ref, f32[18,128,128]{2,1,0:T(8,128)S(1)} %bitcast.27, f32[18,128,128]{2,1,0:T(8,128)S(1)} %collective-permute-done.25.theirs_ref), custom_call_target="tpu_custom_call" | custom-call | tf_op jit(solution)/shard_map/pallas_call | solution.py:180
  149.9 9.5 %collective-permute-done.18.refs_22_ = f32[3,2,512,128]{3,2,1,0:T(8,128)} collective-permute-done((f32[3,2,512,128]{3,2,1,0:T(8,128)}, f32[3,2,512,128]{3,2,1,0:T(8,128)}, u32[]{:S(2)}, u32[]{:S(2)}) %collective-permute-start.18) | collective-permute-done | bytes 1572896 | tf_op jit(solution)/shard_map/ppermute | solution.py:435
  159.4 32.4 %collective-permute-done.23.refs_23_ = f32[3,2,512,128]{3,2,1,0:T(8,128)} collective-permute-done((f32[3,2,512,128]{3,2,1,0:T(8,128)}, f32[3,2,512,128]{3,2,1,0:T(8,128)}, u32[]{:S(2)}, u32[]{:S(2)}) %collective-permute-start.23) | collective-permute-done | bytes 1572896 | tf_op jit(solution)/shard_map/ppermute | solution.py:435
  192.0 5.9 %shard_map.48 = (f32[4,512,128]{2,1,0:T(8,128)S(1)}, f32[4,512,128]{2,1,0:T(8,128)S(1)}) custom-call(f32[384,128]{1,0:T(8,128)S(1)} %get-tuple-element.80.refs_0_.inner_ref, f32[384,128]{1,0:T(8,128)S(1)} %get-tuple-element.81.refs_1_, f32[384,128]{1,0:T(8,128)S(1)} %get-tuple-element.82.refs_2_, f32[384,128]{1,0:T(8,128)S(1)} %get-tuple-element.83.refs_3_, ...), custom_call_target="tpu_custom_call" | custom-call | tf_op jit(solution)/shard_map/pallas_call | solution.py:180
  197.8 3.8 %collective-permute-start.26 = (f32[4,512,128]{2,1,0:T(8,128)S(1)}, f32[4,512,128]{2,1,0:T(8,128)S(1)}, u32[]{:S(2)}, u32[]{:S(2)}) collective-permute-start(f32[4,512,128]{2,1,0:T(8,128)S(1)} %get-tuple-element.101), channel_id=1, source_target_pairs={{0,1},{1,0},{2,3},{3,2},{4,5},{5,4},{6,7},{7,6},{8,9},{9,8},{10,11... | collective-permute-start | bytes 3145736 | tf_op jit(solution)/shard_map/ppermute | solution.py:431
  (110 shorter events, 41.0 us)
Async XLA Ops:
  1.1 24.8 %collective-permute-start = (f32[2,256,128]{2,1,0:T(8,128)S(1)}, f32[2,256,128]{2,1,0:T(8,128)S(1)}, u32[]{:S(2)}, u32[]{:S(2)}) collective-permute-start(f32[2,256,128]{2,1,0:T(8,128)S(1)} %bitcast.31), channel_id=1, source_target_pairs={{0,8},{8,16},{16,24},{24,32},{32,40},{40,48},{48,56},{56,64},{64,7... | collective-permute-start | bytes 786440 | tf_op jit(solution)/shard_map/ppermute | solution.py:442
  3.2 22.7 %collective-permute-start.1 = (f32[2,256,128]{2,1,0:T(8,128)S(1)}, f32[2,256,128]{2,1,0:T(8,128)S(1)}, u32[]{:S(2)}, u32[]{:S(2)}) collective-permute-start(f32[2,256,128]{2,1,0:T(8,128)S(1)} %bitcast.30), channel_id=1, source_target_pairs={{8,0},{16,8},{24,16},{32,24},{40,32},{48,40},{56,48},{64,56},{72,6... | collective-permute-start | bytes 786440 | tf_op jit(solution)/shard_map/ppermute | solution.py:443
  33.2 22.8 %collective-permute-start.4 = (f32[4,384,128]{2,1,0:T(8,128)S(1)}, f32[4,384,128]{2,1,0:T(8,128)S(1)}, u32[]{:S(2)}, u32[]{:S(2)}) collective-permute-start(f32[4,384,128]{2,1,0:T(8,128)S(1)} %get-tuple-element.66), channel_id=1, source_target_pairs={{0,1},{1,0},{2,3},{3,2},{4,5},{5,4},{6,7},{7,6},{8,9},{9,8},{10,11... | collective-permute-start | bytes 2359304 | tf_op jit(solution)/shard_map/ppermute | solution.py:431
  34.3 7.8 %collective-permute-start.3 = (f32[2,256,128]{2,1,0:T(8,128)S(1)}, f32[2,256,128]{2,1,0:T(8,128)S(1)}, u32[]{:S(2)}, u32[]{:S(2)}) collective-permute-start(f32[2,256,128]{2,1,0:T(8,128)S(1)} %get-tuple-element.56.low_ref), channel_id=1, source_target_pairs={{8,0},{16,8},{24,16},{32,24},{40,32},{48,40},{56,48},{64,56},{72,6... | collective-permute-start | bytes 786440 | tf_op jit(solution)/shard_map/ppermute | solution.py:443
  35.9 10.8 %collective-permute-start.2 = (f32[2,256,128]{2,1,0:T(8,128)S(1)}, f32[2,256,128]{2,1,0:T(8,128)S(1)}, u32[]{:S(2)}, u32[]{:S(2)}) collective-permute-start(f32[2,256,128]{2,1,0:T(8,128)S(1)} %get-tuple-element.57.high_ref), channel_id=1, source_target_pairs={{0,8},{8,16},{16,24},{24,32},{32,40},{40,48},{48,56},{56,64},{64,7... | collective-permute-start | bytes 786440 | tf_op jit(solution)/shard_map/ppermute | solution.py:442
  49.1 17.0 %collective-permute-start.5 = (f32[4,128,128]{2,1,0:T(8,128)S(1)}, f32[4,128,128]{2,1,0:T(8,128)S(1)}, u32[]{:S(2)}, u32[]{:S(2)}) collective-permute-start(f32[4,128,128]{2,1,0:T(8,128)S(1)} %get-tuple-element.67), channel_id=1, source_target_pairs={{0,1},{1,0},{2,3},{3,2},{4,5},{5,4},{6,7},{7,6},{8,9},{9,8},{10,11... | collective-permute-start | bytes 786440 | tf_op jit(solution)/shard_map/ppermute | solution.py:431
  50.4 8.9 %collective-permute-start.6 = (f32[384,128]{1,0:T(8,128)S(1)}, f32[384,128]{1,0:T(8,128)S(1)}, u32[]{:S(2)}, u32[]{:S(2)}) collective-permute-start(f32[384,128]{1,0:T(8,128)S(1)} %get-tuple-element.81.refs_1_), channel_id=1, source_target_pairs={{0,2},{1,3},{2,4},{3,5},{4,6},{5,7},{6,0},{7,1},{8,10},{9,11},{10,... | collective-permute-start | bytes 589832 | tf_op jit(solution)/shard_map/ppermute | solution.py:435
  52.0 12.5 %collective-permute-start.7 = (f32[384,128]{1,0:T(8,128)S(1)}, f32[384,128]{1,0:T(8,128)S(1)}, u32[]{:S(2)}, u32[]{:S(2)}) collective-permute-start(f32[384,128]{1,0:T(8,128)S(1)} %get-tuple-element.82.refs_2_), channel_id=1, source_target_pairs={{0,4},{1,5},{2,6},{3,7},{4,0},{5,1},{6,2},{7,3},{8,12},{9,13},{10,... | collective-permute-start | bytes 589832 | tf_op jit(solution)/shard_map/ppermute | solution.py:435
  55.3 9.2 %collective-permute-start.8 = (f32[384,128]{1,0:T(8,128)S(1)}, f32[384,128]{1,0:T(8,128)S(1)}, u32[]{:S(2)}, u32[]{:S(2)}) collective-permute-start(f32[384,128]{1,0:T(8,128)S(1)} %get-tuple-element.83.refs_3_), channel_id=1, source_target_pairs={{0,6},{1,7},{2,0},{3,1},{4,2},{5,3},{6,4},{7,5},{8,14},{9,15},{10,... | collective-permute-start | bytes 589832 | tf_op jit(solution)/shard_map/ppermute | solution.py:435
  56.1 11.7 %collective-permute-start.9 = (f32[128,128]{1,0:T(8,128)S(1)}, f32[128,128]{1,0:T(8,128)S(1)}, u32[]{:S(2)}, u32[]{:S(2)}) collective-permute-start(f32[128,128]{1,0:T(8,128)S(1)} %get-tuple-element.85.refs_5_), channel_id=1, source_target_pairs={{0,2},{1,3},{2,4},{3,5},{4,6},{5,7},{6,0},{7,1},{8,10},{9,11},{10,... | collective-permute-start | bytes 196616 | tf_op jit(solution)/shard_map/ppermute | solution.py:435
  59.3 9.8 %collective-permute-start.10 = (f32[128,128]{1,0:T(8,128)S(1)}, f32[128,128]{1,0:T(8,128)S(1)}, u32[]{:S(2)}, u32[]{:S(2)}) collective-permute-start(f32[128,128]{1,0:T(8,128)S(1)} %get-tuple-element.86.refs_6_), channel_id=1, source_target_pairs={{0,4},{1,5},{2,6},{3,7},{4,0},{5,1},{6,2},{7,3},{8,12},{9,13},{10,... | collective-permute-start | bytes 196616 | tf_op jit(solution)/shard_map/ppermute | solution.py:435
  64.5 16.3 %collective-permute-start.14 = (f32[384,128]{1,0:T(8,128)S(1)}, f32[384,128]{1,0:T(8,128)S(1)}, u32[]{:S(2)}, u32[]{:S(2)}) collective-permute-start(f32[384,128]{1,0:T(8,128)S(1)} %get-tuple-element.105), channel_id=1, source_target_pairs={{0,6},{1,7},{2,0},{3,1},{4,2},{5,3},{6,4},{7,5},{8,14},{9,15},{10,... | collective-permute-start | bytes 589832 | tf_op jit(solution)/shard_map/ppermute | solution.py:435
  64.5 16.3 %collective-permute-start.13 = (f32[384,128]{1,0:T(8,128)S(1)}, f32[384,128]{1,0:T(8,128)S(1)}, u32[]{:S(2)}, u32[]{:S(2)}) collective-permute-start(f32[384,128]{1,0:T(8,128)S(1)} %get-tuple-element.106), channel_id=1, source_target_pairs={{0,4},{1,5},{2,6},{3,7},{4,0},{5,1},{6,2},{7,3},{8,12},{9,13},{10,... | collective-permute-start | bytes 589832 | tf_op jit(solution)/shard_map/ppermute | solution.py:435
  66.1 14.7 %collective-permute-start.12 = (f32[384,128]{1,0:T(8,128)S(1)}, f32[384,128]{1,0:T(8,128)S(1)}, u32[]{:S(2)}, u32[]{:S(2)}) collective-permute-start(f32[384,128]{1,0:T(8,128)S(1)} %get-tuple-element.107), channel_id=1, source_target_pairs={{0,2},{1,3},{2,4},{3,5},{4,6},{5,7},{6,0},{7,1},{8,10},{9,11},{10,... | collective-permute-start | bytes 589832 | tf_op jit(solution)/shard_map/ppermute | solution.py:435
  67.8 6.9 %collective-permute-start.11 = (f32[128,128]{1,0:T(8,128)S(1)}, f32[128,128]{1,0:T(8,128)S(1)}, u32[]{:S(2)}, u32[]{:S(2)}) collective-permute-start(f32[128,128]{1,0:T(8,128)S(1)} %get-tuple-element.87.refs_7_), channel_id=1, source_target_pairs={{0,6},{1,7},{2,0},{3,1},{4,2},{5,3},{6,4},{7,5},{8,14},{9,15},{10,... | collective-permute-start | bytes 196616 | tf_op jit(solution)/shard_map/ppermute | solution.py:435
  69.1 7.4 %collective-permute-start.17 = (f32[128,128]{1,0:T(8,128)S(1)}, f32[128,128]{1,0:T(8,128)S(1)}, u32[]{:S(2)}, u32[]{:S(2)}) collective-permute-start(f32[128,128]{1,0:T(8,128)S(1)} %get-tuple-element.108), channel_id=1, source_target_pairs={{0,6},{1,7},{2,0},{3,1},{4,2},{5,3},{6,4},{7,5},{8,14},{9,15},{10,... | collective-permute-start | bytes 196616 | tf_op jit(solution)/shard_map/ppermute | solution.py:435
  83.4 7.1 %collective-permute-start.19 = (f32[18,128,128]{2,1,0:T(8,128)S(1)}, f32[18,128,128]{2,1,0:T(8,128)S(1)}, u32[]{:S(2)}, u32[]{:S(2)}) collective-permute-start(f32[18,128,128]{2,1,0:T(8,128)S(1)} %get-tuple-element.94), channel_id=1, source_target_pairs={{0,1},{1,0},{2,3},{3,2},{4,5},{5,4},{6,7},{7,6},{8,9},{9,8},{10,11... | collective-permute-start | bytes 3538952 | tf_op jit(solution)/shard_map/ppermute | solution.py:431
  111.6 6.5 %collective-permute-start.22 = (f32[144,128]{1,0:T(8,128)S(1)}, f32[144,128]{1,0:T(8,128)S(1)}, u32[]{:S(2)}, u32[]{:S(2)}) collective-permute-start(f32[144,128]{1,0:T(8,128)S(1)} %shard_map.45), channel_id=1, source_target_pairs={{0,6},{1,7},{2,0},{3,1},{4,2},{5,3},{6,4},{7,5},{8,14},{9,15},{10,... | collective-permute-start | bytes 221192 | tf_op jit(solution)/shard_map/ppermute | solution.py:435
  112.0 6.1 %collective-permute-start.21 = (f32[144,128]{1,0:T(8,128)S(1)}, f32[144,128]{1,0:T(8,128)S(1)}, u32[]{:S(2)}, u32[]{:S(2)}) collective-permute-start(f32[144,128]{1,0:T(8,128)S(1)} %shard_map.45), channel_id=1, source_target_pairs={{0,2},{1,3},{2,4},{3,5},{4,6},{5,7},{6,0},{7,1},{8,10},{9,11},{10,... | collective-permute-start | bytes 221192 | tf_op jit(solution)/shard_map/ppermute | solution.py:435
  119.7 20.0 %all-to-all-start.1 = ((f32[16,144,128]{2,1,0:T(8,128)}), f32[16,144,128]{2,1,0:T(8,128)S(1)}, u32[]{:S(2)}, u32[]{:S(2)}) async-start(f32[16,144,128]{2,1,0:T(8,128)} %shard_map.46), calls=%async_computation.1 | async-start | bytes 2359296 | tf_op jit(solution)/shard_map/all_to_all | solution.py:498
  123.4 36.0 %collective-permute-start.18 = (f32[3,2,512,128]{3,2,1,0:T(8,128)}, f32[3,2,512,128]{3,2,1,0:T(8,128)}, u32[]{:S(2)}, u32[]{:S(2)}) collective-permute-start(f32[3,2,512,128]{3,2,1,0:T(8,128)} %copy-done.28), channel_id=1, source_target_pairs={{0,2},{1,3},{2,4},{3,5},{4,6},{5,7},{6,0},{7,1},{8,10},{9,11},{10,... | collective-permute-start | bytes 4718600 | tf_op jit(solution)/shard_map/ppermute | solution.py:435
  124.0 35.4 %collective-permute-start.24 = (f32[3,2,512,128]{3,2,1,0:T(8,128)}, f32[3,2,512,128]{3,2,1,0:T(8,128)}, u32[]{:S(2)}, u32[]{:S(2)}) collective-permute-start(f32[3,2,512,128]{3,2,1,0:T(8,128)} %copy-done.27), channel_id=1, source_target_pairs={{0,6},{1,7},{2,0},{3,1},{4,2},{5,3},{6,4},{7,5},{8,14},{9,15},{10,... | collective-permute-start | bytes 4718600 | tf_op jit(solution)/shard_map/ppermute | solution.py:435
  126.2 65.7 %collective-permute-start.23 = (f32[3,2,512,128]{3,2,1,0:T(8,128)}, f32[3,2,512,128]{3,2,1,0:T(8,128)}, u32[]{:S(2)}, u32[]{:S(2)}) collective-permute-start(f32[3,2,512,128]{3,2,1,0:T(8,128)} %copy-done.26), channel_id=1, source_target_pairs={{0,4},{1,5},{2,6},{3,7},{4,0},{5,1},{6,2},{7,3},{8,12},{9,13},{10,... | collective-permute-start | bytes 4718600 | tf_op jit(solution)/shard_map/ppermute | solution.py:435
  139.8 6.3 %collective-permute-start.25 = (f32[18,128,128]{2,1,0:T(8,128)S(1)}, f32[18,128,128]{2,1,0:T(8,128)S(1)}, u32[]{:S(2)}, u32[]{:S(2)}) collective-permute-start(f32[18,128,128]{2,1,0:T(8,128)S(1)} %bitcast.26), channel_id=1, source_target_pairs={{0,1},{1,0},{2,3},{3,2},{4,5},{5,4},{6,7},{7,6},{8,9},{9,8},{10,11... | collective-permute-start | bytes 3538952 | tf_op jit(solution)/shard_map/ppermute | solution.py:431
  (33 other events, 907.0 us)

commit v7 on v6

--- a/solution.py
+++ b/solution.py
@@ -244,12 +244,23 @@
 
 def bulk_kernel(*refs):
     inner_refs, edge_refs, inner_got, edge_got, out_refs = refs[:4], refs[4:8], refs[8], refs[9], refs[10:]
-    for k in range(1, 4):
+    for k, out_ref in zip((1, 3), out_refs):
         for i, m in enumerate(chunks_for(k)):
-            out_refs[k - 1][i, 0, :INNER_ROWS] = inner_refs[m][...]
-            out_refs[k - 1][i, 0, INNER_ROWS:] = edge_refs[m][...]
-            out_refs[k - 1][i, 1, :INNER_ROWS] = inner_got[m]
-            out_refs[k - 1][i, 1, INNER_ROWS:] = edge_got[m]
+            out_ref[i, 0, :INNER_ROWS] = inner_refs[m][...]
+            out_ref[i, 0, INNER_ROWS:] = edge_refs[m][...]
+            out_ref[i, 1, :INNER_ROWS] = inner_got[m]
+            out_ref[i, 1, INNER_ROWS:] = edge_got[m]
+
+
+def relay_kernel(below_ref, above_ref, below_inner, below_edge, above_inner, above_edge, up_ref, down_ref):
+    up_ref[0] = below_ref[chunks_for(1).index(3), 0]
+    up_ref[1] = below_ref[chunks_for(1).index(0), 0]
+    up_ref[2, :INNER_ROWS] = below_inner[...]
+    up_ref[2, INNER_ROWS:] = below_edge[...]
+    down_ref[0, :INNER_ROWS] = above_inner[...]
+    down_ref[0, INNER_ROWS:] = above_edge[...]
+    down_ref[1] = above_ref[chunks_for(3).index(0), 1]
+    down_ref[2] = above_ref[chunks_for(3).index(1), 1]
 
 
 def chunks_for(k):
@@ -369,8 +380,8 @@
 
 def turned_kernel(*refs):
     inner_refs, edge_refs, inner_got, edge_got = refs[:4], refs[4:8], refs[8], refs[9]
-    arrived, bulks = refs[10:22], refs[22:25]
-    ph_ref, pl_ref, stretch_ref, mine_ref, theirs_ref = refs[25:]
+    arrived, bulks = refs[10:22], refs[22:26]
+    ph_ref, pl_ref, stretch_ref, mine_ref, theirs_ref = refs[26:]
 
     def piece(r, q, j):
         k = (4 - q) % 4
@@ -380,8 +391,10 @@
             pair = (inner_got[r], edge_got[r])
         elif r == 0:
             pair = (arrived[6 * j + k - 1][...], arrived[6 * j + 3 + k - 1][...])
+        elif q == 2:
+            return bulks[2 + j][r - 1]
         else:
-            return bulks[k - 1][chunks_for(k).index((r + k) % 4), j]
+            return bulks[k // 2][chunks_for(k).index((r + k) % 4), j]
         return jnp.concatenate(pair, axis=0)
 
     ph, low = ph_ref[...], pl_ref[...]
@@ -472,10 +485,10 @@
     share = elem_dev * basis // 8
     held = (*inner, *edge, inner_got, edge_got)
     late, arrived = lax.optimization_barrier((held, arrived))
-    bulks = call(bulk_kernel, (shaped(3, 2, share, panel),) * 3, [VMEM_SPEC] * 10, [], late, STEP_LIMIT)
-    sent = {}
-    for k in (1, 3):
-        sent[k] = shift_z(bulks[k - 1], k)
+    bulks = call(bulk_kernel, (shaped(3, 2, share, panel),) * 2, [VMEM_SPEC] * 10, [], late, STEP_LIMIT)
+    sent = []
+    for k, bulk in zip((1, 3), bulks):
+        sent.append(shift_z(bulk, k))
 
     half = shaped(18, 128, 128)
     wide = shaped(share, VECTORS, dtype=BF16)
@@ -491,9 +504,14 @@
     piece = call(fold_kernel, shaped(144, panel), [VMEM_SPEC], [], (pieces,), STEP_LIMIT)
     sums = [shift_z(piece, k) for k in SHIFTS]
     piece = piece + sums[0] + (sums[1] + sums[2])
-    late, piece = lax.optimization_barrier((bulks[1], piece))
-    sent[2] = shift_z(late, 2)
-    bulks = [sent[k] for k in (1, 2, 3)]
+    below, above, piece = lax.optimization_barrier((*sent, piece))
+    relays = call(
+        relay_kernel, (shaped(3, share, panel),) * 2, [VMEM_SPEC] * 6, [],
+        (below, above, arrived[0], arrived[3], arrived[8], arrived[11]), STEP_LIMIT,
+    )
+    bulks = [below, above]
+    for k, relay in zip((1, 3), relays):
+        bulks.append(shift_z(relay, k))
     copies = call(copy_kernel, shaped(*pieces.shape), [VMEM_SPEC], [], (piece,), STEP_LIMIT)
     mine = lax.all_to_all(copies, "space", split_axis=0, concat_axis=0, tiled=True)
     mine = mine.reshape(half.shape)
@@ -512,7 +530,7 @@
     )
     quarter = shaped(4, share, panel)
     mine, theirs = call(
-        turned_kernel, (quarter, quarter), [VMEM_SPEC] * 28, [],
+        turned_kernel, (quarter, quarter), [VMEM_SPEC] * 29, [],
         (*held, *arrived, *bulks, ph, low, stretch), TURN_LIMIT,
     )
     theirs = swap_cores(theirs)

time: 206 us -> 180 us (0.87)
  waiting for transfers between devices: 84 us -> 52.4 us
  blocking collectives: 20.9 us -> 40.9 us
  starting transfers between devices: 48 us -> 41.1 us
  local copies, waits for them, and re-layouts: 7.06 us -> 3.39 us
  Pallas kernels: 44.9 us -> 41.6 us
    all_to_all x0 -> x1, blocking collectives: none -> 20.1 us  [steps(): lax.all_to_all(copies, 'space', split_axis=0, concat_axis=0, tiled=True)]
    ppermute x18 -> x19, waiting for transfers between devices: 56.1 us -> 40.8 us  [shift_z(): return lax.ppermute(x, 'band', [(i, (i + 2 * k) % 8) for i in range(8)])]
    all_to_all x1 -> x0, waiting for transfers between devices: 13.3 us -> none  [steps(): lax.all_to_all(copies, 'space', split_axis=0, concat_axis=0, tiled=True)]
    ppermute x5, starting transfers between devices: 14.6 us -> 9.84 us  [swap_cores(): return lax.ppermute(x, 'band', [(i, i ^ 1) for i in range(8)])]
    all_to_all x1 -> x0, starting transfers between devices: 3.7 us -> none  [steps(): lax.all_to_all(copies, 'space', split_axis=0, concat_axis=0, tiled=True)]
    unnamed x58 -> x4, local copies, waits for them, and re-layouts: 5.94 us -> 2.28 us
    pallas_call x14 -> x15, Pallas kernels: 44.9 us -> 41.6 us  [call(): pl.pallas_call(kernel, out_shape=outs, in_specs=specs, out_specs=kwargs.p...]
    ppermute x5, waiting for transfers between devices: 3.73 us -> 0.72 us  [swap_cores(): return lax.ppermute(x, 'band', [(i, i ^ 1) for i in range(8)])]
  transfers between devices with their start and end apart: 28 -> 28, of which waited for: 14 -> 11; matrix products, arithmetic and copies ran while one was open for 0% -> 0% of each run, Pallas kernels for 13% -> 15%
where the time goes in v7:
time: 180 us
  waiting for transfers between devices  52.4 us (29%)
  Pallas kernels  41.6 us (23%)
  starting transfers between devices  41.1 us (23%)
  blocking collectives  40.9 us (23%)
  local copies, waits for them, and re-layouts  3.39 us (2%)
    pallas_call x15, Pallas kernels, call(): pl.pallas_call(kernel, out_shape=outs, in_specs=specs, out_specs=kwargs.p...  41.6 us
    ppermute x19, waiting for transfers between devices, shift_z(): return lax.ppermute(x, 'band', [(i, (i + 2 * k) % 8) for i in range(8)])  40.8 us
    ppermute x19, starting transfers between devices, shift_z(): return lax.ppermute(x, 'band', [(i, (i + 2 * k) % 8) for i in range(8)])  23.7 us
    all_to_all x1, blocking collectives, steps(): lax.all_to_all(pieces, 'space', split_axis=0, concat_axis=0, tiled=True)  20.7 us
    all_to_all x1, blocking collectives, steps(): lax.all_to_all(copies, 'space', split_axis=0, concat_axis=0, tiled=True)  20.1 us
    ppermute x5, starting transfers between devices, swap_cores(): return lax.ppermute(x, 'band', [(i, i ^ 1) for i in range(8)])  9.84 us
    ppermute x2, waiting for transfers between devices, halos_of(): return (before, lax.ppermute(first, 'space', down))  6.12 us
    ppermute x2, starting transfers between devices, halos_of(): return (before, lax.ppermute(first, 'space', down))  5.46 us
  transfers between devices with their start and end apart: 28, of which 11 were waited for; matrix products, arithmetic and copies ran while one was open for 0% of the time, Pallas kernels for 15%

profile of v7, /device:TPU:1, one launch (start us, length us, event | category | flops | bytes accessed | tf_op | source)
XLA Modules:
  0.0 179.8 jit_solution(10876091885620043479)
XLA Ops:
  1.1 2.1 %collective-permute-start = (f32[2,256,128]{2,1,0:T(8,128)S(1)}, f32[2,256,128]{2,1,0:T(8,128)S(1)}, u32[]{:S(2)}, u32[]{:S(2)}) collective-permute-start(f32[2,256,128]{2,1,0:T(8,128)S(1)} %bitcast.31), channel_id=1, source_target_pairs={{0,8},{8,16},{16,24},{24,32},{32,40},{40,48},{48,56},{56,64},{64,7... | collective-permute-start | bytes 786440 | tf_op jit(solution)/shard_map/ppermute | solution.py:455
  3.2 3.8 %collective-permute-start.1 = (f32[2,256,128]{2,1,0:T(8,128)S(1)}, f32[2,256,128]{2,1,0:T(8,128)S(1)}, u32[]{:S(2)}, u32[]{:S(2)}) collective-permute-start(f32[2,256,128]{2,1,0:T(8,128)S(1)} %bitcast.30), channel_id=1, source_target_pairs={{8,0},{16,8},{24,16},{32,24},{40,32},{48,40},{56,48},{64,56},{72,6... | collective-permute-start | bytes 786440 | tf_op jit(solution)/shard_map/ppermute | solution.py:456
  9.3 16.5 %shard_map.37 = (f32[12,256,128]{2,1,0:T(8,128)S(1)}, bf16[16,512,1280]{2,1,0:T(8,128)(2,1)S(1)}) custom-call(s32[7,16]{1,0:T(8,128)S(1)} %bitcast.29, s32[4]{0:T(128)S(1)} %pad_add_fusion.at_ref, f32[16,7,256,256]{3,2,1,0:T(8,128)} %blocks_ref.1, f32[16,256,128]{2,1,0:T(8,128)S(1)} %bitcast.22), custom_call_target="tpu_custom_call" | custom-call | tf_op jit(solution)/shard_map/pallas_call | solution.py:180
  27.6 5.7 %shard_map.39 = (f32[384,128]{1,0:T(8,128)S(1)}, f32[384,128]{1,0:T(8,128)S(1)}, f32[384,128]{1,0:T(8,128)S(1)}, f32[384,128]{1,0:T(8,128)S(1)}, f32[4,384,128]{2,1,0:T(8,128)S(1)}) custom-call(s32[4]{0:T(128)S(1)} %pad_add_fusion.at_ref, bf16[16,512,1280]{2,1,0:T(8,128)(2,1)S(1)} %get-tuple-element.56.op_ref, ...), custom_call_target="tpu_custom_call" | custom-call | tf_op jit(solution)/shard_map/pallas_call | solution.py:180
  36.0 6.1 %collective-permute-done.3.after_ref = f32[2,256,128]{2,1,0:T(8,128)S(1)} collective-permute-done((f32[2,256,128]{2,1,0:T(8,128)S(1)}, f32[2,256,128]{2,1,0:T(8,128)S(1)}, u32[]{:S(2)}, u32[]{:S(2)}) %collective-permute-start.3) | collective-permute-done | bytes 262176 | tf_op jit(solution)/shard_map/ppermute | solution.py:456
  42.1 4.7 %collective-permute-done.2.before_ref = f32[2,256,128]{2,1,0:T(8,128)S(1)} collective-permute-done((f32[2,256,128]{2,1,0:T(8,128)S(1)}, f32[2,256,128]{2,1,0:T(8,128)S(1)}, u32[]{:S(2)}, u32[]{:S(2)}) %collective-permute-start.2) | collective-permute-done | bytes 262176 | tf_op jit(solution)/shard_map/ppermute | solution.py:455
  46.8 2.3 %shard_map.40 = (f32[128,128]{1,0:T(8,128)S(1)}, f32[128,128]{1,0:T(8,128)S(1)}, f32[128,128]{1,0:T(8,128)S(1)}, f32[128,128]{1,0:T(8,128)S(1)}, f32[4,128,128]{2,1,0:T(8,128)S(1)}) custom-call(s32[4]{0:T(128)S(1)} %pad_add_fusion.at_ref, bf16[16,512,1280]{2,1,0:T(8,128)(2,1)S(1)} %get-tuple-element.56.op_ref, ...), custom_call_target="tpu_custom_call" | custom-call | tf_op jit(solution)/shard_map/pallas_call | solution.py:180
  52.1 3.3 %collective-permute-start.7 = (f32[384,128]{1,0:T(8,128)S(1)}, f32[384,128]{1,0:T(8,128)S(1)}, u32[]{:S(2)}, u32[]{:S(2)}) collective-permute-start(f32[384,128]{1,0:T(8,128)S(1)} %get-tuple-element.84.refs_2_), channel_id=1, source_target_pairs={{0,4},{1,5},{2,6},{3,7},{4,0},{5,1},{6,2},{7,3},{8,12},{9,13},{10,... | collective-permute-start | bytes 589832 | tf_op jit(solution)/shard_map/ppermute | solution.py:448
  56.9 2.5 %collective-permute-done.6.refs_0_.below_inner.refs_10_ = f32[384,128]{1,0:T(8,128)S(1)} collective-permute-done((f32[384,128]{1,0:T(8,128)S(1)}, f32[384,128]{1,0:T(8,128)S(1)}, u32[]{:S(2)}, u32[]{:S(2)}) %collective-permute-start.6) | collective-permute-done | bytes 196640 | tf_op jit(solution)/shard_map/ppermute | solution.py:448
  60.8 3.7 %collective-permute-done.7.refs_1_.refs_11_ = f32[384,128]{1,0:T(8,128)S(1)} collective-permute-done((f32[384,128]{1,0:T(8,128)S(1)}, f32[384,128]{1,0:T(8,128)S(1)}, u32[]{:S(2)}, u32[]{:S(2)}) %collective-permute-start.7) | collective-permute-done | bytes 196640 | tf_op jit(solution)/shard_map/ppermute | solution.py:448
  70.1 4.5 %collective-permute-done.11.refs_5_.refs_15_ = f32[128,128]{1,0:T(8,128)S(1)} collective-permute-done((f32[128,128]{1,0:T(8,128)S(1)}, f32[128,128]{1,0:T(8,128)S(1)}, u32[]{:S(2)}, u32[]{:S(2)}) %collective-permute-start.11) | collective-permute-done | bytes 65568 | tf_op jit(solution)/shard_map/ppermute | solution.py:448
  74.7 1.8 %collective-permute-start.16 = (f32[128,128]{1,0:T(8,128)S(1)}, f32[128,128]{1,0:T(8,128)S(1)}, u32[]{:S(2)}, u32[]{:S(2)}) collective-permute-start(f32[128,128]{1,0:T(8,128)S(1)} %get-tuple-element.113), channel_id=1, source_target_pairs={{0,4},{1,5},{2,6},{3,7},{4,0},{5,1},{6,2},{7,3},{8,12},{9,13},{10,... | collective-permute-start | bytes 196616 | tf_op jit(solution)/shard_map/ppermute | solution.py:448
  80.8 2.5 %shard_map.42 = (bf16[512,1024]{1,0:T(8,128)(2,1)S(1)}, bf16[512,1024]{1,0:T(8,128)(2,1)S(1)}, f32[18,128,128]{2,1,0:T(8,128)S(1)}) custom-call(s32[4]{0:T(128)S(1)} %pad_add_fusion.at_ref, f32[384,128]{1,0:T(8,128)S(1)} %get-tuple-element.82.refs_0_.inner_ref, f32[128,128]{1,0:T(8,128)S(1)} %get-tuple-element.86.refs_4_.edge_ref, ...), custom_call_target="tpu_custom_call" | custom-call | tf_op jit(solution)/shard_map/pallas_call | solution.py:180
  83.4 4.6 %collective-permute-start.20 = (f32[18,128,128]{2,1,0:T(8,128)S(1)}, f32[18,128,128]{2,1,0:T(8,128)S(1)}, u32[]{:S(2)}, u32[]{:S(2)}) collective-permute-start(f32[18,128,128]{2,1,0:T(8,128)S(1)} %get-tuple-element.96), channel_id=1, source_target_pairs={{0,1},{1,0},{2,3},{3,2},{4,5},{5,4},{6,7},{7,6},{8,9},{9,8},{10,11... | collective-permute-start | bytes 3538952 | tf_op jit(solution)/shard_map/ppermute | solution.py:444
  88.3 2.7 %collective-permute-start.19 = (f32[3,2,512,128]{3,2,1,0:T(8,128)S(1)}, f32[3,2,512,128]{3,2,1,0:T(8,128)S(1)}, u32[]{:S(2)}, u32[]{:S(2)}) collective-permute-start(f32[3,2,512,128]{3,2,1,0:T(8,128)S(1)} %get-tuple-element.93), channel_id=1, source_target_pairs={{0,6},{1,7},{2,0},{3,1},{4,2},{5,3},{6,4},{7,5},{8,14},{9,15},{10,... | collective-permute-start | bytes 4718600 | tf_op jit(solution)/shard_map/ppermute | solution.py:448
  91.0 1.9 %shard_map.43.a_ref = f32[18,128,128]{2,1,0:T(8,128)S(1)} custom-call(s32[4]{0:T(128)S(1)} %pad_add_fusion.at_ref, bf16[512,1024]{1,0:T(8,128)(2,1)S(1)} %get-tuple-element.94.hi_ref, bf16[512,1024]{1,0:T(8,128)(2,1)S(1)} %get-tuple-element.95.lo_ref), custom_call_target="tpu_custom_call" | custom-call | tf_op jit(solution)/shard_map/pallas_call | solution.py:180
  93.0 20.7 %all_to_all.10.parts_ref = f32[16,144,128]{2,1,0:T(8,128)S(1)} all-to-all(f32[16,144,128]{2,1,0:T(8,128)S(1)} %bitcast.28), channel_id=1, replica_groups=mesh['space'=16,'band'=8] {'space'}, dimensions={0} | all-to-all | bytes 2359296 | tf_op jit(solution)/shard_map/all_to_all | solution.py:503
  115.4 12.2 %collective-permute-done.23 = f32[144,128]{1,0:T(8,128)S(1)} collective-permute-done((f32[144,128]{1,0:T(8,128)S(1)}, f32[144,128]{1,0:T(8,128)S(1)}, u32[]{:S(2)}, u32[]{:S(2)}) %collective-permute-start.23) | collective-permute-done | bytes 73760 | tf_op jit(solution)/shard_map/ppermute | solution.py:448
  128.7 20.1 %all_to_all.11 = f32[16,144,128]{2,1,0:T(8,128)S(1)} all-to-all(f32[16,144,128]{2,1,0:T(8,128)S(1)} %shard_map.47), channel_id=1, replica_groups=mesh['space'=16,'band'=8] {'space'}, dimensions={0} | all-to-all | bytes 2359296 | tf_op jit(solution)/shard_map/all_to_all | solution.py:516
  148.8 2.0 %collective-permute-start.26 = (f32[18,128,128]{2,1,0:T(8,128)S(1)}, f32[18,128,128]{2,1,0:T(8,128)S(1)}, u32[]{:S(2)}, u32[]{:S(2)}) collective-permute-start(f32[18,128,128]{2,1,0:T(8,128)S(1)} %bitcast.26), channel_id=1, source_target_pairs={{0,1},{1,0},{2,3},{3,2},{4,5},{5,4},{6,7},{7,6},{8,9},{9,8},{10,11... | collective-permute-start | bytes 3538952 | tf_op jit(solution)/shard_map/ppermute | solution.py:444
  151.6 2.1 %collective-permute-start.25 = (f32[3,512,128]{2,1,0:T(8,128)S(1)}, f32[3,512,128]{2,1,0:T(8,128)S(1)}, u32[]{:S(2)}, u32[]{:S(2)}) collective-permute-start(f32[3,512,128]{2,1,0:T(8,128)S(1)} %get-tuple-element.100), channel_id=1, source_target_pairs={{0,6},{1,7},{2,0},{3,1},{4,2},{5,3},{6,4},{7,5},{8,14},{9,15},{10,... | collective-permute-start | bytes 2359304 | tf_op jit(solution)/shard_map/ppermute | solution.py:448
  153.7 3.7 %shard_map.48 = (bf16[1024,256]{1,0:T(8,128)(2,1)S(1)}, bf16[1024,256]{1,0:T(8,128)(2,1)S(1)}, f32[8,128]{1,0:T(8,128)S(1)}) custom-call(s32[4]{0:T(128)S(1)} %pad_add_fusion.at_ref, f32[18,128,128]{2,1,0:T(8,128)S(1)} %bitcast.27, f32[18,128,128]{2,1,0:T(8,128)S(1)} %collective-permute-done.26.theirs_ref), custom_call_target="tpu_custom_call" | custom-call | tf_op jit(solution)/shard_map/pallas_call | solution.py:180
  157.4 13.9 %collective-permute-done.24.refs_24_ = f32[3,512,128]{2,1,0:T(8,128)S(1)} collective-permute-done((f32[3,512,128]{2,1,0:T(8,128)S(1)}, f32[3,512,128]{2,1,0:T(8,128)S(1)}, u32[]{:S(2)}, u32[]{:S(2)}) %collective-permute-start.24) | collective-permute-done | bytes 786464 | tf_op jit(solution)/shard_map/ppermute | solution.py:448
  171.3 3.5 %shard_map.49 = (f32[4,512,128]{2,1,0:T(8,128)S(1)}, f32[4,512,128]{2,1,0:T(8,128)S(1)}) custom-call(f32[384,128]{1,0:T(8,128)S(1)} %get-tuple-element.82.refs_0_.inner_ref, f32[384,128]{1,0:T(8,128)S(1)} %get-tuple-element.83.refs_1_, f32[384,128]{1,0:T(8,128)S(1)} %get-tuple-element.84.refs_2_, f32[384,128]{1,0:T(8,128)S(1)} %get-tuple-element.85.refs_3_, ...), custom_call_target="tpu_custom_call" | custom-call | tf_op jit(solution)/shard_map/pallas_call | solution.py:180
  (58 shorter events, 32.5 us)
Async XLA Ops:
  1.1 24.8 %collective-permute-start = (f32[2,256,128]{2,1,0:T(8,128)S(1)}, f32[2,256,128]{2,1,0:T(8,128)S(1)}, u32[]{:S(2)}, u32[]{:S(2)}) collective-permute-start(f32[2,256,128]{2,1,0:T(8,128)S(1)} %bitcast.31), channel_id=1, source_target_pairs={{0,8},{8,16},{16,24},{24,32},{32,40},{40,48},{48,56},{56,64},{64,7... | collective-permute-start | bytes 786440 | tf_op jit(solution)/shard_map/ppermute | solution.py:455
  3.2 22.7 %collective-permute-start.1 = (f32[2,256,128]{2,1,0:T(8,128)S(1)}, f32[2,256,128]{2,1,0:T(8,128)S(1)}, u32[]{:S(2)}, u32[]{:S(2)}) collective-permute-start(f32[2,256,128]{2,1,0:T(8,128)S(1)} %bitcast.30), channel_id=1, source_target_pairs={{8,0},{16,8},{24,16},{32,24},{40,32},{48,40},{56,48},{64,56},{72,6... | collective-permute-start | bytes 786440 | tf_op jit(solution)/shard_map/ppermute | solution.py:456
  33.3 22.8 %collective-permute-start.4 = (f32[4,384,128]{2,1,0:T(8,128)S(1)}, f32[4,384,128]{2,1,0:T(8,128)S(1)}, u32[]{:S(2)}, u32[]{:S(2)}) collective-permute-start(f32[4,384,128]{2,1,0:T(8,128)S(1)} %get-tuple-element.68), channel_id=1, source_target_pairs={{0,1},{1,0},{2,3},{3,2},{4,5},{5,4},{6,7},{7,6},{8,9},{9,8},{10,11... | collective-permute-start | bytes 2359304 | tf_op jit(solution)/shard_map/ppermute | solution.py:444
  34.3 7.8 %collective-permute-start.3 = (f32[2,256,128]{2,1,0:T(8,128)S(1)}, f32[2,256,128]{2,1,0:T(8,128)S(1)}, u32[]{:S(2)}, u32[]{:S(2)}) collective-permute-start(f32[2,256,128]{2,1,0:T(8,128)S(1)} %get-tuple-element.58.low_ref), channel_id=1, source_target_pairs={{8,0},{16,8},{24,16},{32,24},{40,32},{48,40},{56,48},{64,56},{72,6... | collective-permute-start | bytes 786440 | tf_op jit(solution)/shard_map/ppermute | solution.py:456
  36.0 10.8 %collective-permute-start.2 = (f32[2,256,128]{2,1,0:T(8,128)S(1)}, f32[2,256,128]{2,1,0:T(8,128)S(1)}, u32[]{:S(2)}, u32[]{:S(2)}) collective-permute-start(f32[2,256,128]{2,1,0:T(8,128)S(1)} %get-tuple-element.59.high_ref), channel_id=1, source_target_pairs={{0,8},{8,16},{16,24},{24,32},{32,40},{40,48},{48,56},{56,64},{64,7... | collective-permute-start | bytes 786440 | tf_op jit(solution)/shard_map/ppermute | solution.py:455
  49.1 17.0 %collective-permute-start.5 = (f32[4,128,128]{2,1,0:T(8,128)S(1)}, f32[4,128,128]{2,1,0:T(8,128)S(1)}, u32[]{:S(2)}, u32[]{:S(2)}) collective-permute-start(f32[4,128,128]{2,1,0:T(8,128)S(1)} %get-tuple-element.69), channel_id=1, source_target_pairs={{0,1},{1,0},{2,3},{3,2},{4,5},{5,4},{6,7},{7,6},{8,9},{9,8},{10,11... | collective-permute-start | bytes 786440 | tf_op jit(solution)/shard_map/ppermute | solution.py:444
  50.4 8.9 %collective-permute-start.6 = (f32[384,128]{1,0:T(8,128)S(1)}, f32[384,128]{1,0:T(8,128)S(1)}, u32[]{:S(2)}, u32[]{:S(2)}) collective-permute-start(f32[384,128]{1,0:T(8,128)S(1)} %get-tuple-element.83.refs_1_), channel_id=1, source_target_pairs={{0,2},{1,3},{2,4},{3,5},{4,6},{5,7},{6,0},{7,1},{8,10},{9,11},{10,... | collective-permute-start | bytes 589832 | tf_op jit(solution)/shard_map/ppermute | solution.py:448
  52.1 12.5 %collective-permute-start.7 = (f32[384,128]{1,0:T(8,128)S(1)}, f32[384,128]{1,0:T(8,128)S(1)}, u32[]{:S(2)}, u32[]{:S(2)}) collective-permute-start(f32[384,128]{1,0:T(8,128)S(1)} %get-tuple-element.84.refs_2_), channel_id=1, source_target_pairs={{0,4},{1,5},{2,6},{3,7},{4,0},{5,1},{6,2},{7,3},{8,12},{9,13},{10,... | collective-permute-start | bytes 589832 | tf_op jit(solution)/shard_map/ppermute | solution.py:448
  55.4 9.2 %collective-permute-start.8 = (f32[384,128]{1,0:T(8,128)S(1)}, f32[384,128]{1,0:T(8,128)S(1)}, u32[]{:S(2)}, u32[]{:S(2)}) collective-permute-start(f32[384,128]{1,0:T(8,128)S(1)} %get-tuple-element.85.refs_3_), channel_id=1, source_target_pairs={{0,6},{1,7},{2,0},{3,1},{4,2},{5,3},{6,4},{7,5},{8,14},{9,15},{10,... | collective-permute-start | bytes 589832 | tf_op jit(solution)/shard_map/ppermute | solution.py:448
  56.1 11.7 %collective-permute-start.9 = (f32[128,128]{1,0:T(8,128)S(1)}, f32[128,128]{1,0:T(8,128)S(1)}, u32[]{:S(2)}, u32[]{:S(2)}) collective-permute-start(f32[128,128]{1,0:T(8,128)S(1)} %get-tuple-element.87.refs_5_), channel_id=1, source_target_pairs={{0,2},{1,3},{2,4},{3,5},{4,6},{5,7},{6,0},{7,1},{8,10},{9,11},{10,... | collective-permute-start | bytes 196616 | tf_op jit(solution)/shard_map/ppermute | solution.py:448
  59.4 9.8 %collective-permute-start.10 = (f32[128,128]{1,0:T(8,128)S(1)}, f32[128,128]{1,0:T(8,128)S(1)}, u32[]{:S(2)}, u32[]{:S(2)}) collective-permute-start(f32[128,128]{1,0:T(8,128)S(1)} %get-tuple-element.88.refs_6_), channel_id=1, source_target_pairs={{0,4},{1,5},{2,6},{3,7},{4,0},{5,1},{6,2},{7,3},{8,12},{9,13},{10,... | collective-permute-start | bytes 196616 | tf_op jit(solution)/shard_map/ppermute | solution.py:448
  64.5 16.3 %collective-permute-start.14 = (f32[384,128]{1,0:T(8,128)S(1)}, f32[384,128]{1,0:T(8,128)S(1)}, u32[]{:S(2)}, u32[]{:S(2)}) collective-permute-start(f32[384,128]{1,0:T(8,128)S(1)} %get-tuple-element.109), channel_id=1, source_target_pairs={{0,6},{1,7},{2,0},{3,1},{4,2},{5,3},{6,4},{7,5},{8,14},{9,15},{10,... | collective-permute-start | bytes 589832 | tf_op jit(solution)/shard_map/ppermute | solution.py:448
  64.5 16.3 %collective-permute-start.13 = (f32[384,128]{1,0:T(8,128)S(1)}, f32[384,128]{1,0:T(8,128)S(1)}, u32[]{:S(2)}, u32[]{:S(2)}) collective-permute-start(f32[384,128]{1,0:T(8,128)S(1)} %get-tuple-element.110), channel_id=1, source_target_pairs={{0,4},{1,5},{2,6},{3,7},{4,0},{5,1},{6,2},{7,3},{8,12},{9,13},{10,... | collective-permute-start | bytes 589832 | tf_op jit(solution)/shard_map/ppermute | solution.py:448
  66.2 14.7 %collective-permute-start.12 = (f32[384,128]{1,0:T(8,128)S(1)}, f32[384,128]{1,0:T(8,128)S(1)}, u32[]{:S(2)}, u32[]{:S(2)}) collective-permute-start(f32[384,128]{1,0:T(8,128)S(1)} %get-tuple-element.111), channel_id=1, source_target_pairs={{0,2},{1,3},{2,4},{3,5},{4,6},{5,7},{6,0},{7,1},{8,10},{9,11},{10,... | collective-permute-start | bytes 589832 | tf_op jit(solution)/shard_map/ppermute | solution.py:448
  67.8 6.9 %collective-permute-start.11 = (f32[128,128]{1,0:T(8,128)S(1)}, f32[128,128]{1,0:T(8,128)S(1)}, u32[]{:S(2)}, u32[]{:S(2)}) collective-permute-start(f32[128,128]{1,0:T(8,128)S(1)} %get-tuple-element.89.refs_7_), channel_id=1, source_target_pairs={{0,6},{1,7},{2,0},{3,1},{4,2},{5,3},{6,4},{7,5},{8,14},{9,15},{10,... | collective-permute-start | bytes 196616 | tf_op jit(solution)/shard_map/ppermute | solution.py:448
  69.1 7.4 %collective-permute-start.17 = (f32[128,128]{1,0:T(8,128)S(1)}, f32[128,128]{1,0:T(8,128)S(1)}, u32[]{:S(2)}, u32[]{:S(2)}) collective-permute-start(f32[128,128]{1,0:T(8,128)S(1)} %get-tuple-element.112), channel_id=1, source_target_pairs={{0,6},{1,7},{2,0},{3,1},{4,2},{5,3},{6,4},{7,5},{8,14},{9,15},{10,... | collective-permute-start | bytes 196616 | tf_op jit(solution)/shard_map/ppermute | solution.py:448
  83.4 9.4 %collective-permute-start.20 = (f32[18,128,128]{2,1,0:T(8,128)S(1)}, f32[18,128,128]{2,1,0:T(8,128)S(1)}, u32[]{:S(2)}, u32[]{:S(2)}) collective-permute-start(f32[18,128,128]{2,1,0:T(8,128)S(1)} %get-tuple-element.96), channel_id=1, source_target_pairs={{0,1},{1,0},{2,3},{3,2},{4,5},{5,4},{6,7},{7,6},{8,9},{9,8},{10,11... | collective-permute-start | bytes 3538952 | tf_op jit(solution)/shard_map/ppermute | solution.py:444
  88.2 40.4 %collective-permute-start.18 = (f32[3,2,512,128]{3,2,1,0:T(8,128)S(1)}, f32[3,2,512,128]{3,2,1,0:T(8,128)S(1)}, u32[]{:S(2)}, u32[]{:S(2)}) collective-permute-start(f32[3,2,512,128]{3,2,1,0:T(8,128)S(1)} %get-tuple-element.92), channel_id=1, source_target_pairs={{0,2},{1,3},{2,4},{3,5},{4,6},{5,7},{6,0},{7,1},{8,10},{9,11},{10,... | collective-permute-start | bytes 4718600 | tf_op jit(solution)/shard_map/ppermute | solution.py:448
  88.3 40.3 %collective-permute-start.19 = (f32[3,2,512,128]{3,2,1,0:T(8,128)S(1)}, f32[3,2,512,128]{3,2,1,0:T(8,128)S(1)}, u32[]{:S(2)}, u32[]{:S(2)}) collective-permute-start(f32[3,2,512,128]{3,2,1,0:T(8,128)S(1)} %get-tuple-element.93), channel_id=1, source_target_pairs={{0,6},{1,7},{2,0},{3,1},{4,2},{5,3},{6,4},{7,5},{8,14},{9,15},{10,... | collective-permute-start | bytes 4718600 | tf_op jit(solution)/shard_map/ppermute | solution.py:448
  113.8 13.8 %collective-permute-start.23 = (f32[144,128]{1,0:T(8,128)S(1)}, f32[144,128]{1,0:T(8,128)S(1)}, u32[]{:S(2)}, u32[]{:S(2)}) collective-permute-start(f32[144,128]{1,0:T(8,128)S(1)} %shard_map.45), channel_id=1, source_target_pairs={{0,6},{1,7},{2,0},{3,1},{4,2},{5,3},{6,4},{7,5},{8,14},{9,15},{10,... | collective-permute-start | bytes 221192 | tf_op jit(solution)/shard_map/ppermute | solution.py:448
  114.1 14.5 %collective-permute-start.22 = (f32[144,128]{1,0:T(8,128)S(1)}, f32[144,128]{1,0:T(8,128)S(1)}, u32[]{:S(2)}, u32[]{:S(2)}) collective-permute-start(f32[144,128]{1,0:T(8,128)S(1)} %shard_map.45), channel_id=1, source_target_pairs={{0,2},{1,3},{2,4},{3,5},{4,6},{5,7},{6,0},{7,1},{8,10},{9,11},{10,... | collective-permute-start | bytes 221192 | tf_op jit(solution)/shard_map/ppermute | solution.py:448
  115.3 13.3 %collective-permute-start.21 = (f32[144,128]{1,0:T(8,128)S(1)}, f32[144,128]{1,0:T(8,128)S(1)}, u32[]{:S(2)}, u32[]{:S(2)}) collective-permute-start(f32[144,128]{1,0:T(8,128)S(1)} %shard_map.45), channel_id=1, source_target_pairs={{0,4},{1,5},{2,6},{3,7},{4,0},{5,1},{6,2},{7,3},{8,12},{9,13},{10,... | collective-permute-start | bytes 221192 | tf_op jit(solution)/shard_map/ppermute | solution.py:448
  150.9 20.4 %collective-permute-start.24 = (f32[3,512,128]{2,1,0:T(8,128)S(1)}, f32[3,512,128]{2,1,0:T(8,128)S(1)}, u32[]{:S(2)}, u32[]{:S(2)}) collective-permute-start(f32[3,512,128]{2,1,0:T(8,128)S(1)} %get-tuple-element.99), channel_id=1, source_target_pairs={{0,2},{1,3},{2,4},{3,5},{4,6},{5,7},{6,0},{7,1},{8,10},{9,11},{10,... | collective-permute-start | bytes 2359304 | tf_op jit(solution)/shard_map/ppermute | solution.py:448
  151.6 19.7 %collective-permute-start.25 = (f32[3,512,128]{2,1,0:T(8,128)S(1)}, f32[3,512,128]{2,1,0:T(8,128)S(1)}, u32[]{:S(2)}, u32[]{:S(2)}) collective-permute-start(f32[3,512,128]{2,1,0:T(8,128)S(1)} %get-tuple-element.100), channel_id=1, source_target_pairs={{0,6},{1,7},{2,0},{3,1},{4,2},{5,3},{6,4},{7,5},{8,14},{9,15},{10,... | collective-permute-start | bytes 2359304 | tf_op jit(solution)/shard_map/ppermute | solution.py:448
  (6 other events, 19.3 us)

commit v8 on v7

--- a/solution.py
+++ b/solution.py
@@ -16,7 +16,7 @@
 SPAN = 2 * REACH + 1
 TOTAL = 256
 RING = 8
-BUILD_LIMIT = 26 << 20
+BUILD_LIMIT = 30 << 20
 STEP_LIMIT = 16 << 20
 OPERATOR_LIMIT = 8 << 20
 TURN_LIMIT = 32 << 20
@@ -41,8 +41,12 @@
 
 
 def apply_one(op_ref, wide_ref, elem):
+    return apply_left(op_ref[elem], wide_ref, elem)
+
+
+def apply_left(left, wide_ref, elem):
     near = wide_ref[pl.ds(elem, SPAN)].reshape(SPAN * 256, 256)
-    prod = dot(op_ref[elem], near)
+    prod = dot(left, near)
     return (prod[256:, 128:] + prod[256:, :128]) + (prod[:256, 128:] + prod[:256, :128])
 
 
@@ -54,7 +58,7 @@
     return 2.0 * (total - 0.5 * own) / 1.5 - base
 
 
-def build_kernel(count, near_ref, at_ref, blocks_ref, vectors_ref, step_ref, op_ref, wide_ref, ring_ref, sums_ref, own_ref, sem, own_sem):
+def build_kernel(count, near_ref, at_ref, blocks_ref, vectors_ref, step_ref, op_ref, wide_ref, ring_ref, own_ref, sums_a, sums_b, left_a, left_b, sem, own_sem):
     def fetch(n):
         elem = lax.rem(n + REACH, count)
         return pltpu.make_async_copy(blocks_ref.at[elem], ring_ref.at[lax.rem(n, RING)], sem.at[lax.rem(n, RING)])
@@ -68,42 +72,55 @@
     for r in range(count):
         spread(wide_ref, REACH + r, own_ref[r])
 
-    def combine(n, u):
+    def combine(n, sums_ref, left_ref):
         elem = lax.rem(n + REACH, count)
         at = lax.rem(n, RING)
-        fetch(n).wait()
-        sums_ref[u, 0] = ring_ref[at, 1]
-        sums_ref[u, SPAN - 1] = ring_ref[at, 2]
+        sums_ref[0] = ring_ref[at, 1]
+        sums_ref[SPAN - 1] = ring_ref[at, 2]
         for o in range(1, SPAN - 1):
-            sums_ref[u, o] = jnp.zeros((256, 256), F32)
+            sums_ref[o] = jnp.zeros((256, 256), F32)
         for k in (0, 3, 4, 5, 6):
             o = lax.rem(near_ref[k, elem] - first - elem + REACH + 2 * TOTAL, TOTAL)
-            sums_ref[u, o] = sums_ref[u, o] + ring_ref[at, k]
+            sums_ref[o] = sums_ref[o] + ring_ref[at, k]
         for o in range(SPAN):
-            hi, lo = split(sums_ref[u, o])
-            op_ref[elem, :256, o * 256 : (o + 1) * 256] = hi
-            op_ref[elem, 256:, o * 256 : (o + 1) * 256] = lo
-        return elem
+            hi, lo = split(sums_ref[o])
+            cols = slice(o * 256, (o + 1) * 256)
+            op_ref[elem, :256, cols] = hi
+            op_ref[elem, 256:, cols] = lo
+            left_ref[:256, cols] = hi
+            left_ref[256:, cols] = lo
 
     def refill(n):
         @pl.when(n + RING < count)
         def _():
             fetch(n + RING).start()
 
+    def step(n, left_ref):
+        total = apply_left(left_ref[...], wide_ref, n + REACH)
+        step_ref[n] = first_of(total, own_ref[n + REACH])
+
     def inner(g, _):
-        for u in range(2):
-            n = 2 * g + u
-            elem = combine(n, u)
-            refill(n)
-            step_ref[elem - REACH] = first_of(apply_one(op_ref, wide_ref, elem), own_ref[elem])
+        n = 2 * g
+        fetch(n + 1).wait()
+        fetch(n + 2).wait()
+        step(n, left_a)
+        combine(n + 1, sums_b, left_b)
+        step(n + 1, left_b)
+        combine(n + 2, sums_a, left_a)
+        refill(n + 1)
+        refill(n + 2)
         return 0
 
     def outer(n, _):
-        combine(n, 0)
+        fetch(n).wait()
+        combine(n, sums_a, left_a)
         return 0
 
+    fetch(0).wait()
+    combine(0, sums_a, left_a)
+    refill(0)
     lax.fori_loop(0, (count - 2 * REACH) // 2, inner, 0)
-    lax.fori_loop(count - 2 * REACH, count, outer, 0)
+    lax.fori_loop(count - 2 * REACH + 1, count, outer, 0)
 
 
 def edges_of(count):
@@ -201,8 +218,11 @@
         [
             wide_scratch(count),
             pltpu.VMEM((RING, 7, 256, 256), F32),
-            pltpu.VMEM((2, SPAN, 256, 256), F32),
             pltpu.VMEM(own.shape, F32),
+            pltpu.VMEM((SPAN, 256, 256), F32),
+            pltpu.VMEM((SPAN, 256, 256), F32),
+            pltpu.VMEM((512, SPAN * 256), BF16),
+            pltpu.VMEM((512, SPAN * 256), BF16),
             pltpu.SemaphoreType.DMA((RING,)),
             pltpu.SemaphoreType.DMA,
         ],
@@ -245,26 +265,31 @@
 def bulk_kernel(*refs):
     inner_refs, edge_refs, inner_got, edge_got, out_refs = refs[:4], refs[4:8], refs[8], refs[9], refs[10:]
     for k, out_ref in zip((1, 3), out_refs):
-        for i, m in enumerate(chunks_for(k)):
+        for i, m in enumerate(relayed_for(k)):
             out_ref[i, 0, :INNER_ROWS] = inner_refs[m][...]
             out_ref[i, 0, INNER_ROWS:] = edge_refs[m][...]
             out_ref[i, 1, :INNER_ROWS] = inner_got[m]
             out_ref[i, 1, INNER_ROWS:] = edge_got[m]
 
 
-def relay_kernel(below_ref, above_ref, below_inner, below_edge, above_inner, above_edge, up_ref, down_ref):
-    up_ref[0] = below_ref[chunks_for(1).index(3), 0]
-    up_ref[1] = below_ref[chunks_for(1).index(0), 0]
+def relay_kernel(below_ref, above_ref, below_inner, below_edge, above_inner, above_edge, inner_ref, edge_ref, inner_got, edge_got, up_ref, down_ref):
+    for out_ref in (up_ref, down_ref):
+        out_ref[3, :INNER_ROWS] = inner_ref[...]
+        out_ref[3, INNER_ROWS:] = edge_ref[...]
+        out_ref[4, :INNER_ROWS] = inner_got[2]
+        out_ref[4, INNER_ROWS:] = edge_got[2]
+    up_ref[0] = below_ref[relayed_for(1).index(3), 0]
+    up_ref[1] = below_ref[relayed_for(1).index(0), 0]
     up_ref[2, :INNER_ROWS] = below_inner[...]
     up_ref[2, INNER_ROWS:] = below_edge[...]
     down_ref[0, :INNER_ROWS] = above_inner[...]
     down_ref[0, INNER_ROWS:] = above_edge[...]
-    down_ref[1] = above_ref[chunks_for(3).index(0), 1]
-    down_ref[2] = above_ref[chunks_for(3).index(1), 1]
-
-
-def chunks_for(k):
-    return [m for m in range(4) if m != k]
+    down_ref[1] = above_ref[relayed_for(3).index(0), 1]
+    down_ref[2] = above_ref[relayed_for(3).index(1), 1]
+
+
+def relayed_for(k):
+    return [m for m in (0, 1, 3) if m != k]
 
 
 def add_kernel(a_ref, b_ref, out_ref):
@@ -393,8 +418,10 @@
             pair = (arrived[6 * j + k - 1][...], arrived[6 * j + 3 + k - 1][...])
         elif q == 2:
             return bulks[2 + j][r - 1]
+        elif (r + k) % 4 == 2:
+            return bulks[2 + k // 2][3 + j]
         else:
-            return bulks[k // 2][chunks_for(k).index((r + k) % 4), j]
+            return bulks[k // 2][relayed_for(k).index((r + k) % 4), j]
         return jnp.concatenate(pair, axis=0)
 
     ph, low = ph_ref[...], pl_ref[...]
@@ -485,7 +512,7 @@
     share = elem_dev * basis // 8
     held = (*inner, *edge, inner_got, edge_got)
     late, arrived = lax.optimization_barrier((held, arrived))
-    bulks = call(bulk_kernel, (shaped(3, 2, share, panel),) * 2, [VMEM_SPEC] * 10, [], late, STEP_LIMIT)
+    bulks = call(bulk_kernel, (shaped(2, 2, share, panel),) * 2, [VMEM_SPEC] * 10, [], late, STEP_LIMIT)
     sent = []
     for k, bulk in zip((1, 3), bulks):
         sent.append(shift_z(bulk, k))
@@ -506,8 +533,8 @@
     piece = piece + sums[0] + (sums[1] + sums[2])
     below, above, piece = lax.optimization_barrier((*sent, piece))
     relays = call(
-        relay_kernel, (shaped(3, share, panel),) * 2, [VMEM_SPEC] * 6, [],
-        (below, above, arrived[0], arrived[3], arrived[8], arrived[11]), STEP_LIMIT,
+        relay_kernel, (shaped(5, share, panel),) * 2, [VMEM_SPEC] * 10, [],
+        (below, above, arrived[0], arrived[3], arrived[8], arrived[11], inner[2], edge[2], inner_got, edge_got), STEP_LIMIT,
     )
     bulks = [below, above]
     for k, relay in zip((1, 3), relays):

time: 180 us -> 181 us (level)
  blocking collectives: 40.9 us -> 0 us
  waiting for transfers between devices: 52.4 us -> 68.3 us
  starting transfers between devices: 41.1 us -> 56.7 us
  Pallas kernels: 41.6 us -> 46.4 us
  local copies, waits for them, and re-layouts: 3.39 us -> 8.01 us
    all_to_all x2 -> x0, blocking collectives: 40.9 us -> none  [the longest x1 20.7 us: steps(): lax.all_to_all(pieces, 'space', split_axis=0, concat_axis=0, tiled=True)]
    all_to_all x0 -> x2, waiting for transfers between devices: none -> 21 us  [the longest x1 14.9 us: steps(): lax.all_to_all(pieces, 'space', split_axis=0, concat_axis=0, tiled=True)]
    all_to_all x0 -> x2, starting transfers between devices: none -> 9.36 us  [the longest x1 5.53 us: steps(): lax.all_to_all(copies, 'space', split_axis=0, concat_axis=0, tiled=True)]
    ppermute x19, waiting for transfers between devices: 40.8 us -> 32.6 us  [shift_z(): return lax.ppermute(x, 'band', [(i, (i + 2 * k) % 8) for i in range(8)])]
    ppermute x5, starting transfers between devices: 9.84 us -> 14.8 us  [swap_cores(): return lax.ppermute(x, 'band', [(i, i ^ 1) for i in range(8)])]
    pallas_call x15, Pallas kernels: 41.6 us -> 46.4 us  [call(): pl.pallas_call(kernel, out_shape=outs, in_specs=specs, out_specs=kwargs.p...]
    unnamed x4 -> x94, local copies, waits for them, and re-layouts: 2.28 us -> 6.89 us
    ppermute x5, waiting for transfers between devices: 0.72 us -> 3.8 us  [swap_cores(): return lax.ppermute(x, 'band', [(i, i ^ 1) for i in range(8)])]
  transfers between devices with their start and end apart: 28 -> 30, of which waited for: 11 -> 15; matrix products, arithmetic and copies ran while one was open for 0% -> 0% of each run, Pallas kernels for 15% -> 15%
where the time goes in v8:
time: 181 us; the launch traced here: 180 us
  waiting for transfers between devices  68.3 us (38%)
  starting transfers between devices  56.7 us (31%)
  Pallas kernels  46.4 us (26%)
  local copies, waits for them, and re-layouts  8.01 us (4%)
    pallas_call x15, Pallas kernels, call(): pl.pallas_call(kernel, out_shape=outs, in_specs=specs, out_specs=kwargs.p...  46.4 us
    ppermute x19, waiting for transfers between devices, shift_z(): return lax.ppermute(x, 'band', [(i, (i + 2 * k) % 8) for i in range(8)])  32.6 us
    ppermute x19, starting transfers between devices, shift_z(): return lax.ppermute(x, 'band', [(i, (i + 2 * k) % 8) for i in range(8)])  25 us
    all_to_all x1, waiting for transfers between devices, steps(): lax.all_to_all(pieces, 'space', split_axis=0, concat_axis=0, tiled=True)  14.9 us
    ppermute x5, starting transfers between devices, swap_cores(): return lax.ppermute(x, 'band', [(i, i ^ 1) for i in range(8)])  14.8 us
    unnamed x94, local copies, waits for them, and re-layouts  6.89 us
    ppermute x2, waiting for transfers between devices, halos_of(): return (before, lax.ppermute(first, 'space', down))  6.12 us
    all_to_all x1, waiting for transfers between devices, steps(): lax.all_to_all(copies, 'space', split_axis=0, concat_axis=0, tiled=True)  6.1 us
  transfers between devices with their start and end apart: 30, of which 15 were waited for; matrix products, arithmetic and copies ran while one was open for 0% of the time, Pallas kernels for 15%

profile of v8, /device:TPU:1, one launch (start us, length us, event | category | flops | bytes accessed | tf_op | source)
XLA Modules:
  0.0 180.5 jit_solution(4925692988993751331)
XLA Ops:
  3.2 3.8 %collective-permute-start.1 = (f32[2,256,128]{2,1,0:T(8,128)S(1)}, f32[2,256,128]{2,1,0:T(8,128)S(1)}, u32[]{:S(2)}, u32[]{:S(2)}) collective-permute-start(f32[2,256,128]{2,1,0:T(8,128)S(1)} %bitcast.29), channel_id=1, source_target_pairs={{8,0},{16,8},{24,16},{32,24},{40,32},{48,40},{56,48},{64,56},{72,6... | collective-permute-start | bytes 786440 | tf_op jit(solution)/shard_map/ppermute | solution.py:483
  9.3 13.4 %shard_map.37 = (f32[12,256,128]{2,1,0:T(8,128)S(1)}, bf16[16,512,1280]{2,1,0:T(8,128)(2,1)S(1)}) custom-call(s32[7,16]{1,0:T(8,128)S(1)} %bitcast.28, s32[4]{0:T(128)S(1)} %pad_add_fusion.at_ref, f32[16,7,256,256]{3,2,1,0:T(8,128)} %blocks_ref.1, f32[16,256,128]{2,1,0:T(8,128)S(1)} %bitcast.22), custom_call_target="tpu_custom_call" | custom-call | tf_op jit(solution)/shard_map/pallas_call | solution.py:197
  24.5 5.6 %shard_map.39 = (f32[384,128]{1,0:T(8,128)S(1)}, f32[384,128]{1,0:T(8,128)S(1)}, f32[384,128]{1,0:T(8,128)S(1)}, f32[384,128]{1,0:T(8,128)S(1)}, f32[4,384,128]{2,1,0:T(8,128)S(1)}) custom-call(s32[4]{0:T(128)S(1)} %pad_add_fusion.at_ref, bf16[16,512,1280]{2,1,0:T(8,128)(2,1)S(1)} %get-tuple-element.56.op_ref, ...), custom_call_target="tpu_custom_call" | custom-call | tf_op jit(solution)/shard_map/pallas_call | solution.py:197
  32.9 6.1 %collective-permute-done.3.after_ref = f32[2,256,128]{2,1,0:T(8,128)S(1)} collective-permute-done((f32[2,256,128]{2,1,0:T(8,128)S(1)}, f32[2,256,128]{2,1,0:T(8,128)S(1)}, u32[]{:S(2)}, u32[]{:S(2)}) %collective-permute-start.3) | collective-permute-done | bytes 262176 | tf_op jit(solution)/shard_map/ppermute | solution.py:483
  39.0 4.7 %collective-permute-done.2.before_ref = f32[2,256,128]{2,1,0:T(8,128)S(1)} collective-permute-done((f32[2,256,128]{2,1,0:T(8,128)S(1)}, f32[2,256,128]{2,1,0:T(8,128)S(1)}, u32[]{:S(2)}, u32[]{:S(2)}) %collective-permute-start.2) | collective-permute-done | bytes 262176 | tf_op jit(solution)/shard_map/ppermute | solution.py:482
  53.2 3.1 %collective-permute-done.6.refs_0_.below_inner.refs_10_ = f32[384,128]{1,0:T(8,128)S(1)} collective-permute-done((f32[384,128]{1,0:T(8,128)S(1)}, f32[384,128]{1,0:T(8,128)S(1)}, u32[]{:S(2)}, u32[]{:S(2)}) %collective-permute-start.6) | collective-permute-done | bytes 196640 | tf_op jit(solution)/shard_map/ppermute | solution.py:475
  57.5 4.8 %collective-permute-start.14 = (f32[384,128]{1,0:T(8,128)S(1)}, f32[384,128]{1,0:T(8,128)S(1)}, u32[]{:S(2)}, u32[]{:S(2)}) collective-permute-start(f32[384,128]{1,0:T(8,128)S(1)} %get-tuple-element.109), channel_id=1, source_target_pairs={{0,6},{1,7},{2,0},{3,1},{4,2},{5,3},{6,4},{7,5},{8,14},{9,15},{10,... | collective-permute-start | bytes 589832 | tf_op jit(solution)/shard_map/ppermute | solution.py:475
  63.0 2.7 %collective-permute-start.10 = (f32[128,128]{1,0:T(8,128)S(1)}, f32[128,128]{1,0:T(8,128)S(1)}, u32[]{:S(2)}, u32[]{:S(2)}) collective-permute-start(f32[128,128]{1,0:T(8,128)S(1)} %get-tuple-element.88.refs_6_.edge_ref), channel_id=1, source_target_pairs={{0,4},{1,5},{2,6},{3,7},{4,0},{5,1},{6,2},{7,3},{8,12},{9,13},{10,... | collective-permute-start | bytes 196616 | tf_op jit(solution)/shard_map/ppermute | solution.py:475
  67.6 6.0 %collective-permute-done.10.refs_4_.refs_14_ = f32[128,128]{1,0:T(8,128)S(1)} collective-permute-done((f32[128,128]{1,0:T(8,128)S(1)}, f32[128,128]{1,0:T(8,128)S(1)}, u32[]{:S(2)}, u32[]{:S(2)}) %collective-permute-start.10) | collective-permute-done | bytes 65568 | tf_op jit(solution)/shard_map/ppermute | solution.py:475
  73.6 4.6 %collective-permute-done.16.refs_10_.refs_20_ = f32[128,128]{1,0:T(8,128)S(1)} collective-permute-done((f32[128,128]{1,0:T(8,128)S(1)}, f32[128,128]{1,0:T(8,128)S(1)}, u32[]{:S(2)}, u32[]{:S(2)}) %collective-permute-start.16) | collective-permute-done | bytes 65568 | tf_op jit(solution)/shard_map/ppermute | solution.py:475
  78.7 2.5 %shard_map.42 = (bf16[512,1024]{1,0:T(8,128)(2,1)S(1)}, bf16[512,1024]{1,0:T(8,128)(2,1)S(1)}, f32[18,128,128]{2,1,0:T(8,128)S(1)}) custom-call(s32[4]{0:T(128)S(1)} %pad_add_fusion.at_ref, f32[384,128]{1,0:T(8,128)S(1)} %get-tuple-element.82.refs_0_.inner_ref, f32[128,128]{1,0:T(8,128)S(1)} %get-tuple-element.86.refs_4_.edge_ref, ...), custom_call_target="tpu_custom_call" | custom-call | tf_op jit(solution)/shard_map/pallas_call | solution.py:197
  81.4 4.7 %collective-permute-start.20 = (f32[18,128,128]{2,1,0:T(8,128)S(1)}, f32[18,128,128]{2,1,0:T(8,128)S(1)}, u32[]{:S(2)}, u32[]{:S(2)}) collective-permute-start(f32[18,128,128]{2,1,0:T(8,128)S(1)} %get-tuple-element.96), channel_id=1, source_target_pairs={{0,1},{1,0},{2,3},{3,2},{4,5},{5,4},{6,7},{7,6},{8,9},{9,8},{10,11... | collective-permute-start | bytes 3538952 | tf_op jit(solution)/shard_map/ppermute | solution.py:471
  89.7 3.8 %all-to-all-start = ((f32[16,144,128]{2,1,0:T(8,128)}), f32[16,144,128]{2,1,0:T(8,128)S(1)}, u32[]{:S(2)}, u32[]{:S(2)}) async-start(f32[16,144,128]{2,1,0:T(8,128)} %bitcast.14), calls=%async_computation | async-start | bytes 2359296 | tf_op jit(solution)/shard_map/all_to_all | solution.py:530
  95.0 2.7 %collective-permute-start.19 = (f32[2,2,512,128]{3,2,1,0:T(8,128)}, f32[2,2,512,128]{3,2,1,0:T(8,128)}, u32[]{:S(2)}, u32[]{:S(2)}) collective-permute-start(f32[2,2,512,128]{3,2,1,0:T(8,128)} %get-tuple-element.93), channel_id=1, source_target_pairs={{0,6},{1,7},{2,0},{3,1},{4,2},{5,3},{6,4},{7,5},{8,14},{9,15},{10,... | collective-permute-start | bytes 3145736 | tf_op jit(solution)/shard_map/ppermute | solution.py:475
  97.7 14.9 %all-to-all-done.parts_ref = f32[16,144,128]{2,1,0:T(8,128)S(1)} async-done(((f32[16,144,128]{2,1,0:T(8,128)}), f32[16,144,128]{2,1,0:T(8,128)S(1)}, u32[]{:S(2)}, u32[]{:S(2)}) %all-to-all-start) | async-done | bytes 1179680 | tf_op jit(solution)/shard_map/all_to_all | solution.py:530
  115.3 6.7 %collective-permute-done.23 = f32[144,128]{1,0:T(8,128)S(1)} collective-permute-done((f32[144,128]{1,0:T(8,128)S(1)}, f32[144,128]{1,0:T(8,128)S(1)}, u32[]{:S(2)}, u32[]{:S(2)}) %collective-permute-start.23) | collective-permute-done | bytes 73760 | tf_op jit(solution)/shard_map/ppermute | solution.py:475
  125.2 5.5 %all-to-all-start.1 = ((f32[16,144,128]{2,1,0:T(8,128)}), f32[16,144,128]{2,1,0:T(8,128)S(1)}, u32[]{:S(2)}, u32[]{:S(2)}) async-start(f32[16,144,128]{2,1,0:T(8,128)} %shard_map.47), calls=%async_computation.1 | async-start | bytes 2359296 | tf_op jit(solution)/shard_map/all_to_all | solution.py:543
  135.2 2.8 %shard_map.46 = (f32[5,512,128]{2,1,0:T(8,128)}, f32[5,512,128]{2,1,0:T(8,128)}) custom-call(f32[2,2,512,128]{3,2,1,0:T(8,128)S(1)} %collective-permute-done.18.below_ref.refs_22_, f32[2,2,512,128]{3,2,1,0:T(8,128)} %collective-permute-done.19.above_ref.refs_23_, f32[384,128]{1,0:T(8,128)S(1)} %copy-done.6, f32[128,128]{1,0:T(8,128)S(1)} %copy-done.24, ...), custom_call_target="tpu_custom_call" | custom-call | tf_op jit(solution)/shard_map/pallas_call | solution.py:197
  140.7 6.1 %all-to-all-done.1 = f32[16,144,128]{2,1,0:T(8,128)S(1)} async-done(((f32[16,144,128]{2,1,0:T(8,128)}), f32[16,144,128]{2,1,0:T(8,128)S(1)}, u32[]{:S(2)}, u32[]{:S(2)}) %all-to-all-start.1) | async-done | bytes 1179680 | tf_op jit(solution)/shard_map/all_to_all | solution.py:543
  146.9 4.3 %collective-permute-start.26 = (f32[18,128,128]{2,1,0:T(8,128)S(1)}, f32[18,128,128]{2,1,0:T(8,128)S(1)}, u32[]{:S(2)}, u32[]{:S(2)}) collective-permute-start(f32[18,128,128]{2,1,0:T(8,128)S(1)} %bitcast.26), channel_id=1, source_target_pairs={{0,1},{1,0},{2,3},{3,2},{4,5},{5,4},{6,7},{7,6},{8,9},{9,8},{10,11... | collective-permute-start | bytes 3538952 | tf_op jit(solution)/shard_map/ppermute | solution.py:471
  153.7 3.7 %shard_map.48 = (bf16[1024,256]{1,0:T(8,128)(2,1)S(1)}, bf16[1024,256]{1,0:T(8,128)(2,1)S(1)}, f32[8,128]{1,0:T(8,128)S(1)}) custom-call(s32[4]{0:T(128)S(1)} %pad_add_fusion.at_ref, f32[18,128,128]{2,1,0:T(8,128)S(1)} %bitcast.27, f32[18,128,128]{2,1,0:T(8,128)S(1)} %collective-permute-done.26.theirs_ref), custom_call_target="tpu_custom_call" | custom-call | tf_op jit(solution)/shard_map/pallas_call | solution.py:197
  157.4 9.8 %collective-permute-done.24.refs_24_ = f32[5,512,128]{2,1,0:T(8,128)} collective-permute-done((f32[5,512,128]{2,1,0:T(8,128)}, f32[5,512,128]{2,1,0:T(8,128)}, u32[]{:S(2)}, u32[]{:S(2)}) %collective-permute-start.24) | collective-permute-done | bytes 1310752 | tf_op jit(solution)/shard_map/ppermute | solution.py:475
  167.5 5.5 %shard_map.49 = (f32[4,512,128]{2,1,0:T(8,128)S(1)}, f32[4,512,128]{2,1,0:T(8,128)S(1)}) custom-call(f32[384,128]{1,0:T(8,128)S(1)} %get-tuple-element.82.refs_0_.inner_ref, f32[384,128]{1,0:T(8,128)S(1)} %copy-done.12, f32[384,128]{1,0:T(8,128)S(1)} %copy-done.4, f32[384,128]{1,0:T(8,128)S(1)} %copy-done.14, f32[128,128]{1,0:T(8,128)S(1)} %copy-done.31, ...), custom_call_target="tpu_custom_call" | custom-call | tf_op jit(solution)/shard_map/pallas_call | solution.py:197
  173.0 3.5 %collective-permute-start.27 = (f32[4,512,128]{2,1,0:T(8,128)S(1)}, f32[4,512,128]{2,1,0:T(8,128)S(1)}, u32[]{:S(2)}, u32[]{:S(2)}) collective-permute-start(f32[4,512,128]{2,1,0:T(8,128)S(1)} %get-tuple-element.105), channel_id=1, source_target_pairs={{0,1},{1,0},{2,3},{3,2},{4,5},{5,4},{6,7},{7,6},{8,9},{9,8},{10,11... | collective-permute-start | bytes 3145736 | tf_op jit(solution)/shard_map/ppermute | solution.py:471
  (150 shorter events, 48.0 us)
Async XLA Ops:
  1.1 21.7 %collective-permute-start = (f32[2,256,128]{2,1,0:T(8,128)S(1)}, f32[2,256,128]{2,1,0:T(8,128)S(1)}, u32[]{:S(2)}, u32[]{:S(2)}) collective-permute-start(f32[2,256,128]{2,1,0:T(8,128)S(1)} %bitcast.30), channel_id=1, source_target_pairs={{0,8},{8,16},{16,24},{24,32},{32,40},{40,48},{48,56},{56,64},{64,7... | collective-permute-start | bytes 786440 | tf_op jit(solution)/shard_map/ppermute | solution.py:482
  3.2 19.6 %collective-permute-start.1 = (f32[2,256,128]{2,1,0:T(8,128)S(1)}, f32[2,256,128]{2,1,0:T(8,128)S(1)}, u32[]{:S(2)}, u32[]{:S(2)}) collective-permute-start(f32[2,256,128]{2,1,0:T(8,128)S(1)} %bitcast.29), channel_id=1, source_target_pairs={{8,0},{16,8},{24,16},{32,24},{40,32},{48,40},{56,48},{64,56},{72,6... | collective-permute-start | bytes 786440 | tf_op jit(solution)/shard_map/ppermute | solution.py:483
  30.2 22.3 %collective-permute-start.4 = (f32[4,384,128]{2,1,0:T(8,128)S(1)}, f32[4,384,128]{2,1,0:T(8,128)S(1)}, u32[]{:S(2)}, u32[]{:S(2)}) collective-permute-start(f32[4,384,128]{2,1,0:T(8,128)S(1)} %get-tuple-element.68), channel_id=1, source_target_pairs={{0,1},{1,0},{2,3},{3,2},{4,5},{5,4},{6,7},{7,6},{8,9},{9,8},{10,11... | collective-permute-start | bytes 2359304 | tf_op jit(solution)/shard_map/ppermute | solution.py:471
  31.2 7.8 %collective-permute-start.3 = (f32[2,256,128]{2,1,0:T(8,128)S(1)}, f32[2,256,128]{2,1,0:T(8,128)S(1)}, u32[]{:S(2)}, u32[]{:S(2)}) collective-permute-start(f32[2,256,128]{2,1,0:T(8,128)S(1)} %get-tuple-element.58.low_ref), channel_id=1, source_target_pairs={{8,0},{16,8},{24,16},{32,24},{40,32},{48,40},{56,48},{64,56},{72,6... | collective-permute-start | bytes 786440 | tf_op jit(solution)/shard_map/ppermute | solution.py:483
  32.9 10.8 %collective-permute-start.2 = (f32[2,256,128]{2,1,0:T(8,128)S(1)}, f32[2,256,128]{2,1,0:T(8,128)S(1)}, u32[]{:S(2)}, u32[]{:S(2)}) collective-permute-start(f32[2,256,128]{2,1,0:T(8,128)S(1)} %get-tuple-element.59.high_ref), channel_id=1, source_target_pairs={{0,8},{8,16},{16,24},{24,32},{32,40},{40,48},{48,56},{56,64},{64,7... | collective-permute-start | bytes 786440 | tf_op jit(solution)/shard_map/ppermute | solution.py:482
  46.1 16.2 %collective-permute-start.5 = (f32[4,128,128]{2,1,0:T(8,128)S(1)}, f32[4,128,128]{2,1,0:T(8,128)S(1)}, u32[]{:S(2)}, u32[]{:S(2)}) collective-permute-start(f32[4,128,128]{2,1,0:T(8,128)S(1)} %get-tuple-element.69), channel_id=1, source_target_pairs={{0,1},{1,0},{2,3},{3,2},{4,5},{5,4},{6,7},{7,6},{8,9},{9,8},{10,11... | collective-permute-start | bytes 786440 | tf_op jit(solution)/shard_map/ppermute | solution.py:471
  47.4 8.9 %collective-permute-start.6 = (f32[384,128]{1,0:T(8,128)S(1)}, f32[384,128]{1,0:T(8,128)S(1)}, u32[]{:S(2)}, u32[]{:S(2)}) collective-permute-start(f32[384,128]{1,0:T(8,128)S(1)} %get-tuple-element.83.refs_1_), channel_id=1, source_target_pairs={{0,2},{1,3},{2,4},{3,5},{4,6},{5,7},{6,0},{7,1},{8,10},{9,11},{10,... | collective-permute-start | bytes 589832 | tf_op jit(solution)/shard_map/ppermute | solution.py:475
  49.0 8.5 %collective-permute-start.8 = (f32[384,128]{1,0:T(8,128)S(1)}, f32[384,128]{1,0:T(8,128)S(1)}, u32[]{:S(2)}, u32[]{:S(2)}) collective-permute-start(f32[384,128]{1,0:T(8,128)S(1)} %get-tuple-element.85.refs_3_), channel_id=1, source_target_pairs={{0,6},{1,7},{2,0},{3,1},{4,2},{5,3},{6,4},{7,5},{8,14},{9,15},{10,... | collective-permute-start | bytes 589832 | tf_op jit(solution)/shard_map/ppermute | solution.py:475
  51.2 11.2 %collective-permute-start.7 = (f32[384,128]{1,0:T(8,128)S(1)}, f32[384,128]{1,0:T(8,128)S(1)}, u32[]{:S(2)}, u32[]{:S(2)}) collective-permute-start(f32[384,128]{1,0:T(8,128)S(1)} %get-tuple-element.84.refs_2_.inner_ref), channel_id=1, source_target_pairs={{0,4},{1,5},{2,6},{3,7},{4,0},{5,1},{6,2},{7,3},{8,12},{9,13},{10,... | collective-permute-start | bytes 589832 | tf_op jit(solution)/shard_map/ppermute | solution.py:475
  52.5 10.6 %collective-permute-start.9 = (f32[128,128]{1,0:T(8,128)S(1)}, f32[128,128]{1,0:T(8,128)S(1)}, u32[]{:S(2)}, u32[]{:S(2)}) collective-permute-start(f32[128,128]{1,0:T(8,128)S(1)} %get-tuple-element.87.refs_5_), channel_id=1, source_target_pairs={{0,2},{1,3},{2,4},{3,5},{4,6},{5,7},{6,0},{7,1},{8,10},{9,11},{10,... | collective-permute-start | bytes 196616 | tf_op jit(solution)/shard_map/ppermute | solution.py:475
  56.3 9.4 %collective-permute-start.11 = (f32[128,128]{1,0:T(8,128)S(1)}, f32[128,128]{1,0:T(8,128)S(1)}, u32[]{:S(2)}, u32[]{:S(2)}) collective-permute-start(f32[128,128]{1,0:T(8,128)S(1)} %get-tuple-element.89.refs_7_), channel_id=1, source_target_pairs={{0,6},{1,7},{2,0},{3,1},{4,2},{5,3},{6,4},{7,5},{8,14},{9,15},{10,... | collective-permute-start | bytes 196616 | tf_op jit(solution)/shard_map/ppermute | solution.py:475
  57.5 21.1 %collective-permute-start.14 = (f32[384,128]{1,0:T(8,128)S(1)}, f32[384,128]{1,0:T(8,128)S(1)}, u32[]{:S(2)}, u32[]{:S(2)}) collective-permute-start(f32[384,128]{1,0:T(8,128)S(1)} %get-tuple-element.109), channel_id=1, source_target_pairs={{0,6},{1,7},{2,0},{3,1},{4,2},{5,3},{6,4},{7,5},{8,14},{9,15},{10,... | collective-permute-start | bytes 589832 | tf_op jit(solution)/shard_map/ppermute | solution.py:475
  62.3 16.3 %collective-permute-start.13 = (f32[384,128]{1,0:T(8,128)S(1)}, f32[384,128]{1,0:T(8,128)S(1)}, u32[]{:S(2)}, u32[]{:S(2)}) collective-permute-start(f32[384,128]{1,0:T(8,128)S(1)} %get-tuple-element.110), channel_id=1, source_target_pairs={{0,4},{1,5},{2,6},{3,7},{4,0},{5,1},{6,2},{7,3},{8,12},{9,13},{10,... | collective-permute-start | bytes 589832 | tf_op jit(solution)/shard_map/ppermute | solution.py:475
  62.3 16.3 %collective-permute-start.12 = (f32[384,128]{1,0:T(8,128)S(1)}, f32[384,128]{1,0:T(8,128)S(1)}, u32[]{:S(2)}, u32[]{:S(2)}) collective-permute-start(f32[384,128]{1,0:T(8,128)S(1)} %get-tuple-element.111), channel_id=1, source_target_pairs={{0,2},{1,3},{2,4},{3,5},{4,6},{5,7},{6,0},{7,1},{8,10},{9,11},{10,... | collective-permute-start | bytes 589832 | tf_op jit(solution)/shard_map/ppermute | solution.py:475
  63.0 10.5 %collective-permute-start.10 = (f32[128,128]{1,0:T(8,128)S(1)}, f32[128,128]{1,0:T(8,128)S(1)}, u32[]{:S(2)}, u32[]{:S(2)}) collective-permute-start(f32[128,128]{1,0:T(8,128)S(1)} %get-tuple-element.88.refs_6_.edge_ref), channel_id=1, source_target_pairs={{0,4},{1,5},{2,6},{3,7},{4,0},{5,1},{6,2},{7,3},{8,12},{9,13},{10,... | collective-permute-start | bytes 196616 | tf_op jit(solution)/shard_map/ppermute | solution.py:475
  89.7 22.9 %all-to-all-start = ((f32[16,144,128]{2,1,0:T(8,128)}), f32[16,144,128]{2,1,0:T(8,128)S(1)}, u32[]{:S(2)}, u32[]{:S(2)}) async-start(f32[16,144,128]{2,1,0:T(8,128)} %bitcast.14), calls=%async_computation | async-start | bytes 2359296 | tf_op jit(solution)/shard_map/all_to_all | solution.py:530
  95.0 29.0 %collective-permute-start.18 = (f32[2,2,512,128]{3,2,1,0:T(8,128)}, f32[2,2,512,128]{3,2,1,0:T(8,128)S(1)}, u32[]{:S(2)}, u32[]{:S(2)}) collective-permute-start(f32[2,2,512,128]{3,2,1,0:T(8,128)} %get-tuple-element.92), channel_id=1, source_target_pairs={{0,2},{1,3},{2,4},{3,5},{4,6},{5,7},{6,0},{7,1},{8,10},{9,11},{10,... | collective-permute-start | bytes 3145736 | tf_op jit(solution)/shard_map/ppermute | solution.py:475
  95.0 29.0 %collective-permute-start.19 = (f32[2,2,512,128]{3,2,1,0:T(8,128)}, f32[2,2,512,128]{3,2,1,0:T(8,128)}, u32[]{:S(2)}, u32[]{:S(2)}) collective-permute-start(f32[2,2,512,128]{3,2,1,0:T(8,128)} %get-tuple-element.93), channel_id=1, source_target_pairs={{0,6},{1,7},{2,0},{3,1},{4,2},{5,3},{6,4},{7,5},{8,14},{9,15},{10,... | collective-permute-start | bytes 3145736 | tf_op jit(solution)/shard_map/ppermute | solution.py:475
  112.7 9.3 %collective-permute-start.23 = (f32[144,128]{1,0:T(8,128)S(1)}, f32[144,128]{1,0:T(8,128)S(1)}, u32[]{:S(2)}, u32[]{:S(2)}) collective-permute-start(f32[144,128]{1,0:T(8,128)S(1)} %shard_map.45), channel_id=1, source_target_pairs={{0,6},{1,7},{2,0},{3,1},{4,2},{5,3},{6,4},{7,5},{8,14},{9,15},{10,... | collective-permute-start | bytes 221192 | tf_op jit(solution)/shard_map/ppermute | solution.py:475
  113.1 10.9 %collective-permute-start.22 = (f32[144,128]{1,0:T(8,128)S(1)}, f32[144,128]{1,0:T(8,128)S(1)}, u32[]{:S(2)}, u32[]{:S(2)}) collective-permute-start(f32[144,128]{1,0:T(8,128)S(1)} %shard_map.45), channel_id=1, source_target_pairs={{0,2},{1,3},{2,4},{3,5},{4,6},{5,7},{6,0},{7,1},{8,10},{9,11},{10,... | collective-permute-start | bytes 221192 | tf_op jit(solution)/shard_map/ppermute | solution.py:475
  114.3 9.7 %collective-permute-start.21 = (f32[144,128]{1,0:T(8,128)S(1)}, f32[144,128]{1,0:T(8,128)S(1)}, u32[]{:S(2)}, u32[]{:S(2)}) collective-permute-start(f32[144,128]{1,0:T(8,128)S(1)} %shard_map.45), channel_id=1, source_target_pairs={{0,4},{1,5},{2,6},{3,7},{4,0},{5,1},{6,2},{7,3},{8,12},{9,13},{10,... | collective-permute-start | bytes 221192 | tf_op jit(solution)/shard_map/ppermute | solution.py:475
  125.2 21.6 %all-to-all-start.1 = ((f32[16,144,128]{2,1,0:T(8,128)}), f32[16,144,128]{2,1,0:T(8,128)S(1)}, u32[]{:S(2)}, u32[]{:S(2)}) async-start(f32[16,144,128]{2,1,0:T(8,128)} %shard_map.47), calls=%async_computation.1 | async-start | bytes 2359296 | tf_op jit(solution)/shard_map/all_to_all | solution.py:543
  138.0 29.3 %collective-permute-start.24 = (f32[5,512,128]{2,1,0:T(8,128)}, f32[5,512,128]{2,1,0:T(8,128)}, u32[]{:S(2)}, u32[]{:S(2)}) collective-permute-start(f32[5,512,128]{2,1,0:T(8,128)} %get-tuple-element.99), channel_id=1, source_target_pairs={{0,2},{1,3},{2,4},{3,5},{4,6},{5,7},{6,0},{7,1},{8,10},{9,11},{10,... | collective-permute-start | bytes 3932168 | tf_op jit(solution)/shard_map/ppermute | solution.py:475
  139.0 28.3 %collective-permute-start.25 = (f32[5,512,128]{2,1,0:T(8,128)}, f32[5,512,128]{2,1,0:T(8,128)}, u32[]{:S(2)}, u32[]{:S(2)}) collective-permute-start(f32[5,512,128]{2,1,0:T(8,128)} %get-tuple-element.100), channel_id=1, source_target_pairs={{0,6},{1,7},{2,0},{3,1},{4,2},{5,3},{6,4},{7,5},{8,14},{9,15},{10,... | collective-permute-start | bytes 3932168 | tf_op jit(solution)/shard_map/ppermute | solution.py:475
  (53 other events, 850.6 us)

commit v9 on v8

--- a/solution.py
+++ b/solution.py
@@ -318,7 +318,7 @@
     return [(6 + 4 * (m - 2) + 2 * a + b, a, b) for a in range(2) for b in range(2)]
 
 
-def half_of_gram(half, hi_ref, lo_ref, out_ref):
+def half_of_gram(half, hi_ref, lo_ref, out_ref, start_ref=None):
     for m in range(5):
         (i0, j0), (i1, j1) = PAIRS[m], PAIRS[m + 5]
         i = lanes(jnp.where(half == 0, i0, i1) * TILE, TILE)
@@ -328,30 +328,36 @@
         right = jnp.concatenate([right_hi, lo_ref[:, j], right_hi], axis=0)
         block = lax.dot_general(left, right, (((0,), (0,)), ((), ())), preferred_element_type=F32)
         for at, a, b in places_of(m):
-            out_ref[at] = block[a * 128 : (a + 1) * 128, b * 128 : (b + 1) * 128]
-
-
-def gram_send_kernel(at_ref, inner_ref, edge_ref, inner_got, edge_got, *refs):
-    arrived, (hi_ref, lo_ref, out_ref) = refs[:12], refs[12:]
+            part = block[a * 128 : (a + 1) * 128, b * 128 : (b + 1) * 128]
+            out_ref[at] = part if start_ref is None else start_ref[at] + part
+
+
+def split_rows(at_ref, mine_ref, got_ref, arrived, hi_ref, lo_ref):
     z, c = at_ref[2], at_ref[3]
     for k in range(4):
         for j in range(2):
             band = lax.rem(z + 4 - k, 4) * 2 + lax.rem(c + j, 2)
-            if k:
-                inner, edge = arrived[6 * j + k - 1][...], arrived[6 * j + 3 + k - 1][...]
-            elif j:
-                inner, edge = inner_got[0], edge_got[0]
-            else:
-                inner, edge = inner_ref[...], edge_ref[...]
-            for value, rows in ((inner, slice(0, INNER_ROWS)), (edge, slice(INNER_ROWS, 512))):
-                hi, lo = split(value)
-                hi_ref[rows, lanes(band * 128, 128)] = hi
-                lo_ref[rows, lanes(band * 128, 128)] = lo
-    half_of_gram(1 - c, hi_ref, lo_ref, out_ref)
-
-
-def gram_keep_kernel(at_ref, hi_ref, lo_ref, out_ref):
-    half_of_gram(at_ref[3], hi_ref, lo_ref, out_ref)
+            value = arrived[3 * j + k - 1][...] if k else (got_ref[0] if j else mine_ref[...])
+            hi, lo = split(value)
+            hi_ref[:, lanes(band * 128, 128)] = hi
+            lo_ref[:, lanes(band * 128, 128)] = lo
+
+
+def gram_inner_kernel(at_ref, mine_ref, got_ref, *refs):
+    arrived, (send_ref, keep_ref, hi_ref, lo_ref) = refs[:6], refs[6:]
+    split_rows(at_ref, mine_ref, got_ref, arrived, hi_ref, lo_ref)
+    half_of_gram(1 - at_ref[3], hi_ref, lo_ref, send_ref)
+    half_of_gram(at_ref[3], hi_ref, lo_ref, keep_ref)
+
+
+def gram_send_kernel(at_ref, mine_ref, got_ref, *refs):
+    arrived, (start_ref, hi_ref, lo_ref, out_ref) = refs[:6], refs[6:]
+    split_rows(at_ref, mine_ref, got_ref, arrived, hi_ref, lo_ref)
+    half_of_gram(1 - at_ref[3], hi_ref, lo_ref, out_ref, start_ref)
+
+
+def gram_keep_kernel(at_ref, hi_ref, lo_ref, start_ref, out_ref):
+    half_of_gram(at_ref[3], hi_ref, lo_ref, out_ref, start_ref)
 
 
 def times_normed(hi, lo, nh, nl):
@@ -507,6 +513,12 @@
     for j, rows in enumerate((edge, edge_got)):
         for k in SHIFTS:
             arrived[j, 1, k] = shift_z(rows[k], k)
+    half = shaped(18, 128, 128)
+    wide = pltpu.VMEM((INNER_ROWS, VECTORS), BF16)
+    part_send, part_keep = call(
+        gram_inner_kernel, (half, half), [SMEM_SPEC] + [VMEM_SPEC] * 8, [wide, wide],
+        (here, inner[0], inner_got, *(arrived[j, 0, k] for j in range(2) for k in (1, 2, 3))), STEP_LIMIT,
+    )
     arrived = [arrived[j, e, k] for j in range(2) for e in range(2) for k in (1, 2, 3)]
 
     share = elem_dev * basis // 8
@@ -517,14 +529,13 @@
     for k, bulk in zip((1, 3), bulks):
         sent.append(shift_z(bulk, k))
 
-    half = shaped(18, 128, 128)
-    wide = shaped(share, VECTORS, dtype=BF16)
+    wide = shaped(EDGE_ROWS, VECTORS, dtype=BF16)
     hi, lo, send = call(
-        gram_send_kernel, (wide, wide, half), [SMEM_SPEC] + [VMEM_SPEC] * 16, [],
-        (here, inner[0], edge[0], inner_got, edge_got, *arrived), STEP_LIMIT,
+        gram_send_kernel, (wide, wide, half), [SMEM_SPEC] + [VMEM_SPEC] * 9, [],
+        (here, edge[0], edge_got, *arrived[3:6], *arrived[9:12], part_send), STEP_LIMIT,
     )
     theirs = swap_cores(send)
-    keep = call(gram_keep_kernel, half, [SMEM_SPEC] + [VMEM_SPEC] * 2, [], (here, hi, lo), STEP_LIMIT)
+    keep = call(gram_keep_kernel, half, [SMEM_SPEC] + [VMEM_SPEC] * 3, [], (here, hi, lo, part_keep), STEP_LIMIT)
     total = call(add_kernel, half, [VMEM_SPEC] * 2, [], (keep, theirs), STEP_LIMIT)
     pieces = total.reshape(16, 144, panel)
     pieces = lax.all_to_all(pieces, "space", split_axis=0, concat_axis=0, tiled=True)

time: 181 us -> 183 us (1.011)
    pallas_call x15 -> x16, Pallas kernels: 46.4 us -> 47.4 us  [call(): pl.pallas_call(kernel, out_shape=outs, in_specs=specs, out_specs=kwargs.p...]
where the time goes in v9:
time: 183 us; the launch traced here: 182 us
  waiting for transfers between devices  69.1 us (38%)
  starting transfers between devices  56.6 us (31%)
  Pallas kernels  47.4 us (26%)
  local copies, waits for them, and re-layouts  8.01 us (4%)
    pallas_call x16, Pallas kernels, call(): pl.pallas_call(kernel, out_shape=outs, in_specs=specs, out_specs=kwargs.p...  47.4 us
    ppermute x19, waiting for transfers between devices, shift_z(): return lax.ppermute(x, 'band', [(i, (i + 2 * k) % 8) for i in range(8)])  32.7 us
    ppermute x19, starting transfers between devices, shift_z(): return lax.ppermute(x, 'band', [(i, (i + 2 * k) % 8) for i in range(8)])  24.9 us
    all_to_all x1, waiting for transfers between devices, steps(): lax.all_to_all(pieces, 'space', split_axis=0, concat_axis=0, tiled=True)  14.9 us
    ppermute x5, starting transfers between devices, swap_cores(): return lax.ppermute(x, 'band', [(i, i ^ 1) for i in range(8)])  14.8 us
    unnamed x94, local copies, waits for them, and re-layouts  6.89 us
    ppermute x2, waiting for transfers between devices, halos_of(): return (before, lax.ppermute(first, 'space', down))  6.12 us
    all_to_all x1, waiting for transfers between devices, steps(): lax.all_to_all(copies, 'space', split_axis=0, concat_axis=0, tiled=True)  6.1 us
  transfers between devices with their start and end apart: 30, of which 15 were waited for; matrix products, arithmetic and copies ran while one was open for 0% of the time, Pallas kernels for 15%

profile of v9, /device:TPU:1, one launch (start us, length us, event | category | flops | bytes accessed | tf_op | source)
XLA Modules:
  0.0 182.1 jit_solution(14718436713256488327)
XLA Ops:
  3.2 3.8 %collective-permute-start.1 = (f32[2,256,128]{2,1,0:T(8,128)S(1)}, f32[2,256,128]{2,1,0:T(8,128)S(1)}, u32[]{:S(2)}, u32[]{:S(2)}) collective-permute-start(f32[2,256,128]{2,1,0:T(8,128)S(1)} %bitcast.29), channel_id=1, source_target_pairs={{8,0},{16,8},{24,16},{32,24},{40,32},{48,40},{56,48},{64,56},{72,6... | collective-permute-start | bytes 786440 | tf_op jit(solution)/shard_map/ppermute | solution.py:489
  9.3 13.4 %shard_map.37 = (f32[12,256,128]{2,1,0:T(8,128)S(1)}, bf16[16,512,1280]{2,1,0:T(8,128)(2,1)S(1)}) custom-call(s32[7,16]{1,0:T(8,128)S(1)} %bitcast.28, s32[4]{0:T(128)S(1)} %pad_add_fusion.at_ref, f32[16,7,256,256]{3,2,1,0:T(8,128)} %blocks_ref.1, f32[16,256,128]{2,1,0:T(8,128)S(1)} %bitcast.22), custom_call_target="tpu_custom_call" | custom-call | tf_op jit(solution)/shard_map/pallas_call | solution.py:197
  24.5 5.6 %shard_map.39 = (f32[384,128]{1,0:T(8,128)S(1)}, f32[384,128]{1,0:T(8,128)S(1)}, f32[384,128]{1,0:T(8,128)S(1)}, f32[384,128]{1,0:T(8,128)S(1)}, f32[4,384,128]{2,1,0:T(8,128)S(1)}) custom-call(s32[4]{0:T(128)S(1)} %pad_add_fusion.at_ref, bf16[16,512,1280]{2,1,0:T(8,128)(2,1)S(1)} %get-tuple-element.58.op_ref, ...), custom_call_target="tpu_custom_call" | custom-call | tf_op jit(solution)/shard_map/pallas_call | solution.py:197
  32.9 6.1 %collective-permute-done.3.after_ref = f32[2,256,128]{2,1,0:T(8,128)S(1)} collective-permute-done((f32[2,256,128]{2,1,0:T(8,128)S(1)}, f32[2,256,128]{2,1,0:T(8,128)S(1)}, u32[]{:S(2)}, u32[]{:S(2)}) %collective-permute-start.3) | collective-permute-done | bytes 262176 | tf_op jit(solution)/shard_map/ppermute | solution.py:489
  39.0 4.7 %collective-permute-done.2.before_ref = f32[2,256,128]{2,1,0:T(8,128)S(1)} collective-permute-done((f32[2,256,128]{2,1,0:T(8,128)S(1)}, f32[2,256,128]{2,1,0:T(8,128)S(1)}, u32[]{:S(2)}, u32[]{:S(2)}) %collective-permute-start.2) | collective-permute-done | bytes 262176 | tf_op jit(solution)/shard_map/ppermute | solution.py:488
  53.2 3.1 %collective-permute-done.6.refs_0_.below_inner.refs_10_ = f32[384,128]{1,0:T(8,128)S(1)} collective-permute-done((f32[384,128]{1,0:T(8,128)S(1)}, f32[384,128]{1,0:T(8,128)S(1)}, u32[]{:S(2)}, u32[]{:S(2)}) %collective-permute-start.6) | collective-permute-done | bytes 196640 | tf_op jit(solution)/shard_map/ppermute | solution.py:481
  57.5 4.8 %collective-permute-start.14 = (f32[384,128]{1,0:T(8,128)S(1)}, f32[384,128]{1,0:T(8,128)S(1)}, u32[]{:S(2)}, u32[]{:S(2)}) collective-permute-start(f32[384,128]{1,0:T(8,128)S(1)} %get-tuple-element.113), channel_id=1, source_target_pairs={{0,6},{1,7},{2,0},{3,1},{4,2},{5,3},{6,4},{7,5},{8,14},{9,15},{10,... | collective-permute-start | bytes 589832 | tf_op jit(solution)/shard_map/ppermute | solution.py:481
  63.0 2.7 %collective-permute-start.10 = (f32[128,128]{1,0:T(8,128)S(1)}, f32[128,128]{1,0:T(8,128)S(1)}, u32[]{:S(2)}, u32[]{:S(2)}) collective-permute-start(f32[128,128]{1,0:T(8,128)S(1)} %get-tuple-element.90.refs_6_.edge_ref), channel_id=1, source_target_pairs={{0,4},{1,5},{2,6},{3,7},{4,0},{5,1},{6,2},{7,3},{8,12},{9,13},{10,... | collective-permute-start | bytes 196616 | tf_op jit(solution)/shard_map/ppermute | solution.py:481
  67.5 6.0 %collective-permute-done.10.refs_1_.refs_14_ = f32[128,128]{1,0:T(8,128)S(1)} collective-permute-done((f32[128,128]{1,0:T(8,128)S(1)}, f32[128,128]{1,0:T(8,128)S(1)}, u32[]{:S(2)}, u32[]{:S(2)}) %collective-permute-start.10) | collective-permute-done | bytes 65568 | tf_op jit(solution)/shard_map/ppermute | solution.py:481
  73.6 4.6 %collective-permute-done.16.refs_4_.refs_20_ = f32[128,128]{1,0:T(8,128)S(1)} collective-permute-done((f32[128,128]{1,0:T(8,128)S(1)}, f32[128,128]{1,0:T(8,128)S(1)}, u32[]{:S(2)}, u32[]{:S(2)}) %collective-permute-start.16) | collective-permute-done | bytes 65568 | tf_op jit(solution)/shard_map/ppermute | solution.py:481
  78.7 3.0 %shard_map.42 = (f32[18,128,128]{2,1,0:T(8,128)S(1)}, f32[18,128,128]{2,1,0:T(8,128)S(1)}) custom-call(s32[4]{0:T(128)S(1)} %pad_add_fusion.at_ref, f32[384,128]{1,0:T(8,128)S(1)} %get-tuple-element.84.refs_0_.mine_ref, f32[4,384,128]{2,1,0:T(8,128)S(1)} %collective-permute-done.4.refs_8_.got_ref.inner_got, ...), custom_call_target="tpu_custom_call" | custom-call | tf_op jit(solution)/shard_map/pallas_call | solution.py:197
  83.1 4.7 %collective-permute-start.20 = (f32[18,128,128]{2,1,0:T(8,128)S(1)}, f32[18,128,128]{2,1,0:T(8,128)S(1)}, u32[]{:S(2)}, u32[]{:S(2)}) collective-permute-start(f32[18,128,128]{2,1,0:T(8,128)S(1)} %get-tuple-element.100), channel_id=1, source_target_pairs={{0,1},{1,0},{2,3},{3,2},{4,5},{5,4},{6,7},{7,6},{8,9},{9,8},{10,11... | collective-permute-start | bytes 3538952 | tf_op jit(solution)/shard_map/ppermute | solution.py:477
  91.4 3.8 %all-to-all-start = ((f32[16,144,128]{2,1,0:T(8,128)}), f32[16,144,128]{2,1,0:T(8,128)S(1)}, u32[]{:S(2)}, u32[]{:S(2)}) async-start(f32[16,144,128]{2,1,0:T(8,128)} %bitcast.14), calls=%async_computation | async-start | bytes 2359296 | tf_op jit(solution)/shard_map/all_to_all | solution.py:541
  96.7 2.7 %collective-permute-start.19 = (f32[2,2,512,128]{3,2,1,0:T(8,128)}, f32[2,2,512,128]{3,2,1,0:T(8,128)}, u32[]{:S(2)}, u32[]{:S(2)}) collective-permute-start(f32[2,2,512,128]{3,2,1,0:T(8,128)} %get-tuple-element.95), channel_id=1, source_target_pairs={{0,6},{1,7},{2,0},{3,1},{4,2},{5,3},{6,4},{7,5},{8,14},{9,15},{10,... | collective-permute-start | bytes 3145736 | tf_op jit(solution)/shard_map/ppermute | solution.py:481
  99.4 14.9 %all-to-all-done.parts_ref = f32[16,144,128]{2,1,0:T(8,128)S(1)} async-done(((f32[16,144,128]{2,1,0:T(8,128)}), f32[16,144,128]{2,1,0:T(8,128)S(1)}, u32[]{:S(2)}, u32[]{:S(2)}) %all-to-all-start) | async-done | bytes 1179680 | tf_op jit(solution)/shard_map/all_to_all | solution.py:541
  117.0 6.7 %collective-permute-done.23 = f32[144,128]{1,0:T(8,128)S(1)} collective-permute-done((f32[144,128]{1,0:T(8,128)S(1)}, f32[144,128]{1,0:T(8,128)S(1)}, u32[]{:S(2)}, u32[]{:S(2)}) %collective-permute-start.23) | collective-permute-done | bytes 73760 | tf_op jit(solution)/shard_map/ppermute | solution.py:481
  126.8 5.5 %all-to-all-start.1 = ((f32[16,144,128]{2,1,0:T(8,128)}), f32[16,144,128]{2,1,0:T(8,128)S(1)}, u32[]{:S(2)}, u32[]{:S(2)}) async-start(f32[16,144,128]{2,1,0:T(8,128)} %shard_map.48), calls=%async_computation.1 | async-start | bytes 2359296 | tf_op jit(solution)/shard_map/all_to_all | solution.py:554
  136.8 2.8 %shard_map.47 = (f32[5,512,128]{2,1,0:T(8,128)}, f32[5,512,128]{2,1,0:T(8,128)}) custom-call(f32[2,2,512,128]{3,2,1,0:T(8,128)S(1)} %collective-permute-done.18.below_ref.refs_22_, f32[2,2,512,128]{3,2,1,0:T(8,128)} %collective-permute-done.19.above_ref.refs_23_, f32[384,128]{1,0:T(8,128)S(1)} %copy-done.6, f32[128,128]{1,0:T(8,128)S(1)} %copy-done.24, ...), custom_call_target="tpu_custom_call" | custom-call | tf_op jit(solution)/shard_map/pallas_call | solution.py:197
  142.3 6.1 %all-to-all-done.1 = f32[16,144,128]{2,1,0:T(8,128)S(1)} async-done(((f32[16,144,128]{2,1,0:T(8,128)}), f32[16,144,128]{2,1,0:T(8,128)S(1)}, u32[]{:S(2)}, u32[]{:S(2)}) %all-to-all-start.1) | async-done | bytes 1179680 | tf_op jit(solution)/shard_map/all_to_all | solution.py:554
  148.6 4.3 %collective-permute-start.26 = (f32[18,128,128]{2,1,0:T(8,128)S(1)}, f32[18,128,128]{2,1,0:T(8,128)S(1)}, u32[]{:S(2)}, u32[]{:S(2)}) collective-permute-start(f32[18,128,128]{2,1,0:T(8,128)S(1)} %bitcast.26), channel_id=1, source_target_pairs={{0,1},{1,0},{2,3},{3,2},{4,5},{5,4},{6,7},{7,6},{8,9},{9,8},{10,11... | collective-permute-start | bytes 3538952 | tf_op jit(solution)/shard_map/ppermute | solution.py:477
  155.4 3.7 %shard_map.49 = (bf16[1024,256]{1,0:T(8,128)(2,1)S(1)}, bf16[1024,256]{1,0:T(8,128)(2,1)S(1)}, f32[8,128]{1,0:T(8,128)S(1)}) custom-call(s32[4]{0:T(128)S(1)} %pad_add_fusion.at_ref, f32[18,128,128]{2,1,0:T(8,128)S(1)} %bitcast.27, f32[18,128,128]{2,1,0:T(8,128)S(1)} %collective-permute-done.26.theirs_ref), custom_call_target="tpu_custom_call" | custom-call | tf_op jit(solution)/shard_map/pallas_call | solution.py:197
  159.1 9.8 %collective-permute-done.24.refs_24_ = f32[5,512,128]{2,1,0:T(8,128)} collective-permute-done((f32[5,512,128]{2,1,0:T(8,128)}, f32[5,512,128]{2,1,0:T(8,128)}, u32[]{:S(2)}, u32[]{:S(2)}) %collective-permute-start.24) | collective-permute-done | bytes 1310752 | tf_op jit(solution)/shard_map/ppermute | solution.py:481
  169.2 5.5 %shard_map.50 = (f32[4,512,128]{2,1,0:T(8,128)S(1)}, f32[4,512,128]{2,1,0:T(8,128)S(1)}) custom-call(f32[384,128]{1,0:T(8,128)S(1)} %get-tuple-element.84.refs_0_.mine_ref, f32[384,128]{1,0:T(8,128)S(1)} %copy-done.12, f32[384,128]{1,0:T(8,128)S(1)} %copy-done.4, f32[384,128]{1,0:T(8,128)S(1)} %copy-done.14, f32[128,128]{1,0:T(8,128)S(1)} %copy-done.31, ...), custom_call_target="tpu_custom_call" | custom-call | tf_op jit(solution)/shard_map/pallas_call | solution.py:197
  174.6 3.5 %collective-permute-start.27 = (f32[4,512,128]{2,1,0:T(8,128)S(1)}, f32[4,512,128]{2,1,0:T(8,128)S(1)}, u32[]{:S(2)}, u32[]{:S(2)}) collective-permute-start(f32[4,512,128]{2,1,0:T(8,128)S(1)} %get-tuple-element.109), channel_id=1, source_target_pairs={{0,1},{1,0},{2,3},{3,2},{4,5},{5,4},{6,7},{7,6},{8,9},{9,8},{10,11... | collective-permute-start | bytes 3145736 | tf_op jit(solution)/shard_map/ppermute | solution.py:477
  (151 shorter events, 49.2 us)
Async XLA Ops:
  1.1 21.7 %collective-permute-start = (f32[2,256,128]{2,1,0:T(8,128)S(1)}, f32[2,256,128]{2,1,0:T(8,128)S(1)}, u32[]{:S(2)}, u32[]{:S(2)}) collective-permute-start(f32[2,256,128]{2,1,0:T(8,128)S(1)} %bitcast.30), channel_id=1, source_target_pairs={{0,8},{8,16},{16,24},{24,32},{32,40},{40,48},{48,56},{56,64},{64,7... | collective-permute-start | bytes 786440 | tf_op jit(solution)/shard_map/ppermute | solution.py:488
  3.2 19.6 %collective-permute-start.1 = (f32[2,256,128]{2,1,0:T(8,128)S(1)}, f32[2,256,128]{2,1,0:T(8,128)S(1)}, u32[]{:S(2)}, u32[]{:S(2)}) collective-permute-start(f32[2,256,128]{2,1,0:T(8,128)S(1)} %bitcast.29), channel_id=1, source_target_pairs={{8,0},{16,8},{24,16},{32,24},{40,32},{48,40},{56,48},{64,56},{72,6... | collective-permute-start | bytes 786440 | tf_op jit(solution)/shard_map/ppermute | solution.py:489
  30.2 22.3 %collective-permute-start.4 = (f32[4,384,128]{2,1,0:T(8,128)S(1)}, f32[4,384,128]{2,1,0:T(8,128)S(1)}, u32[]{:S(2)}, u32[]{:S(2)}) collective-permute-start(f32[4,384,128]{2,1,0:T(8,128)S(1)} %get-tuple-element.70), channel_id=1, source_target_pairs={{0,1},{1,0},{2,3},{3,2},{4,5},{5,4},{6,7},{7,6},{8,9},{9,8},{10,11... | collective-permute-start | bytes 2359304 | tf_op jit(solution)/shard_map/ppermute | solution.py:477
  31.2 7.8 %collective-permute-start.3 = (f32[2,256,128]{2,1,0:T(8,128)S(1)}, f32[2,256,128]{2,1,0:T(8,128)S(1)}, u32[]{:S(2)}, u32[]{:S(2)}) collective-permute-start(f32[2,256,128]{2,1,0:T(8,128)S(1)} %get-tuple-element.60.low_ref), channel_id=1, source_target_pairs={{8,0},{16,8},{24,16},{32,24},{40,32},{48,40},{56,48},{64,56},{72,6... | collective-permute-start | bytes 786440 | tf_op jit(solution)/shard_map/ppermute | solution.py:489
  32.9 10.8 %collective-permute-start.2 = (f32[2,256,128]{2,1,0:T(8,128)S(1)}, f32[2,256,128]{2,1,0:T(8,128)S(1)}, u32[]{:S(2)}, u32[]{:S(2)}) collective-permute-start(f32[2,256,128]{2,1,0:T(8,128)S(1)} %get-tuple-element.61.high_ref), channel_id=1, source_target_pairs={{0,8},{8,16},{16,24},{24,32},{32,40},{40,48},{48,56},{56,64},{64,7... | collective-permute-start | bytes 786440 | tf_op jit(solution)/shard_map/ppermute | solution.py:488
  46.1 16.2 %collective-permute-start.5 = (f32[4,128,128]{2,1,0:T(8,128)S(1)}, f32[4,128,128]{2,1,0:T(8,128)S(1)}, u32[]{:S(2)}, u32[]{:S(2)}) collective-permute-start(f32[4,128,128]{2,1,0:T(8,128)S(1)} %get-tuple-element.71), channel_id=1, source_target_pairs={{0,1},{1,0},{2,3},{3,2},{4,5},{5,4},{6,7},{7,6},{8,9},{9,8},{10,11... | collective-permute-start | bytes 786440 | tf_op jit(solution)/shard_map/ppermute | solution.py:477
  47.4 8.9 %collective-permute-start.6 = (f32[384,128]{1,0:T(8,128)S(1)}, f32[384,128]{1,0:T(8,128)S(1)}, u32[]{:S(2)}, u32[]{:S(2)}) collective-permute-start(f32[384,128]{1,0:T(8,128)S(1)} %get-tuple-element.85.refs_1_), channel_id=1, source_target_pairs={{0,2},{1,3},{2,4},{3,5},{4,6},{5,7},{6,0},{7,1},{8,10},{9,11},{10,... | collective-permute-start | bytes 589832 | tf_op jit(solution)/shard_map/ppermute | solution.py:481
  49.0 8.5 %collective-permute-start.8 = (f32[384,128]{1,0:T(8,128)S(1)}, f32[384,128]{1,0:T(8,128)S(1)}, u32[]{:S(2)}, u32[]{:S(2)}) collective-permute-start(f32[384,128]{1,0:T(8,128)S(1)} %get-tuple-element.87.refs_3_), channel_id=1, source_target_pairs={{0,6},{1,7},{2,0},{3,1},{4,2},{5,3},{6,4},{7,5},{8,14},{9,15},{10,... | collective-permute-start | bytes 589832 | tf_op jit(solution)/shard_map/ppermute | solution.py:481
  51.2 11.2 %collective-permute-start.7 = (f32[384,128]{1,0:T(8,128)S(1)}, f32[384,128]{1,0:T(8,128)S(1)}, u32[]{:S(2)}, u32[]{:S(2)}) collective-permute-start(f32[384,128]{1,0:T(8,128)S(1)} %get-tuple-element.86.refs_2_.inner_ref), channel_id=1, source_target_pairs={{0,4},{1,5},{2,6},{3,7},{4,0},{5,1},{6,2},{7,3},{8,12},{9,13},{10,... | collective-permute-start | bytes 589832 | tf_op jit(solution)/shard_map/ppermute | solution.py:481
  52.5 10.6 %collective-permute-start.9 = (f32[128,128]{1,0:T(8,128)S(1)}, f32[128,128]{1,0:T(8,128)S(1)}, u32[]{:S(2)}, u32[]{:S(2)}) collective-permute-start(f32[128,128]{1,0:T(8,128)S(1)} %get-tuple-element.89.refs_5_), channel_id=1, source_target_pairs={{0,2},{1,3},{2,4},{3,5},{4,6},{5,7},{6,0},{7,1},{8,10},{9,11},{10,... | collective-permute-start | bytes 196616 | tf_op jit(solution)/shard_map/ppermute | solution.py:481
  56.3 9.4 %collective-permute-start.11 = (f32[128,128]{1,0:T(8,128)S(1)}, f32[128,128]{1,0:T(8,128)S(1)}, u32[]{:S(2)}, u32[]{:S(2)}) collective-permute-start(f32[128,128]{1,0:T(8,128)S(1)} %get-tuple-element.91.refs_7_), channel_id=1, source_target_pairs={{0,6},{1,7},{2,0},{3,1},{4,2},{5,3},{6,4},{7,5},{8,14},{9,15},{10,... | collective-permute-start | bytes 196616 | tf_op jit(solution)/shard_map/ppermute | solution.py:481
  57.5 21.1 %collective-permute-start.14 = (f32[384,128]{1,0:T(8,128)S(1)}, f32[384,128]{1,0:T(8,128)S(1)}, u32[]{:S(2)}, u32[]{:S(2)}) collective-permute-start(f32[384,128]{1,0:T(8,128)S(1)} %get-tuple-element.113), channel_id=1, source_target_pairs={{0,6},{1,7},{2,0},{3,1},{4,2},{5,3},{6,4},{7,5},{8,14},{9,15},{10,... | collective-permute-start | bytes 589832 | tf_op jit(solution)/shard_map/ppermute | solution.py:481
  62.3 16.3 %collective-permute-start.13 = (f32[384,128]{1,0:T(8,128)S(1)}, f32[384,128]{1,0:T(8,128)S(1)}, u32[]{:S(2)}, u32[]{:S(2)}) collective-permute-start(f32[384,128]{1,0:T(8,128)S(1)} %get-tuple-element.114), channel_id=1, source_target_pairs={{0,4},{1,5},{2,6},{3,7},{4,0},{5,1},{6,2},{7,3},{8,12},{9,13},{10,... | collective-permute-start | bytes 589832 | tf_op jit(solution)/shard_map/ppermute | solution.py:481
  62.3 16.3 %collective-permute-start.12 = (f32[384,128]{1,0:T(8,128)S(1)}, f32[384,128]{1,0:T(8,128)S(1)}, u32[]{:S(2)}, u32[]{:S(2)}) collective-permute-start(f32[384,128]{1,0:T(8,128)S(1)} %get-tuple-element.115), channel_id=1, source_target_pairs={{0,2},{1,3},{2,4},{3,5},{4,6},{5,7},{6,0},{7,1},{8,10},{9,11},{10,... | collective-permute-start | bytes 589832 | tf_op jit(solution)/shard_map/ppermute | solution.py:481
  63.0 10.5 %collective-permute-start.10 = (f32[128,128]{1,0:T(8,128)S(1)}, f32[128,128]{1,0:T(8,128)S(1)}, u32[]{:S(2)}, u32[]{:S(2)}) collective-permute-start(f32[128,128]{1,0:T(8,128)S(1)} %get-tuple-element.90.refs_6_.edge_ref), channel_id=1, source_target_pairs={{0,4},{1,5},{2,6},{3,7},{4,0},{5,1},{6,2},{7,3},{8,12},{9,13},{10,... | collective-permute-start | bytes 196616 | tf_op jit(solution)/shard_map/ppermute | solution.py:481
  91.4 22.9 %all-to-all-start = ((f32[16,144,128]{2,1,0:T(8,128)}), f32[16,144,128]{2,1,0:T(8,128)S(1)}, u32[]{:S(2)}, u32[]{:S(2)}) async-start(f32[16,144,128]{2,1,0:T(8,128)} %bitcast.14), calls=%async_computation | async-start | bytes 2359296 | tf_op jit(solution)/shard_map/all_to_all | solution.py:541
  96.7 29.0 %collective-permute-start.18 = (f32[2,2,512,128]{3,2,1,0:T(8,128)}, f32[2,2,512,128]{3,2,1,0:T(8,128)S(1)}, u32[]{:S(2)}, u32[]{:S(2)}) collective-permute-start(f32[2,2,512,128]{3,2,1,0:T(8,128)} %get-tuple-element.94), channel_id=1, source_target_pairs={{0,2},{1,3},{2,4},{3,5},{4,6},{5,7},{6,0},{7,1},{8,10},{9,11},{10,... | collective-permute-start | bytes 3145736 | tf_op jit(solution)/shard_map/ppermute | solution.py:481
  96.7 29.0 %collective-permute-start.19 = (f32[2,2,512,128]{3,2,1,0:T(8,128)}, f32[2,2,512,128]{3,2,1,0:T(8,128)}, u32[]{:S(2)}, u32[]{:S(2)}) collective-permute-start(f32[2,2,512,128]{3,2,1,0:T(8,128)} %get-tuple-element.95), channel_id=1, source_target_pairs={{0,6},{1,7},{2,0},{3,1},{4,2},{5,3},{6,4},{7,5},{8,14},{9,15},{10,... | collective-permute-start | bytes 3145736 | tf_op jit(solution)/shard_map/ppermute | solution.py:481
  114.4 9.3 %collective-permute-start.23 = (f32[144,128]{1,0:T(8,128)S(1)}, f32[144,128]{1,0:T(8,128)S(1)}, u32[]{:S(2)}, u32[]{:S(2)}) collective-permute-start(f32[144,128]{1,0:T(8,128)S(1)} %shard_map.46), channel_id=1, source_target_pairs={{0,6},{1,7},{2,0},{3,1},{4,2},{5,3},{6,4},{7,5},{8,14},{9,15},{10,... | collective-permute-start | bytes 221192 | tf_op jit(solution)/shard_map/ppermute | solution.py:481
  114.8 10.9 %collective-permute-start.22 = (f32[144,128]{1,0:T(8,128)S(1)}, f32[144,128]{1,0:T(8,128)S(1)}, u32[]{:S(2)}, u32[]{:S(2)}) collective-permute-start(f32[144,128]{1,0:T(8,128)S(1)} %shard_map.46), channel_id=1, source_target_pairs={{0,2},{1,3},{2,4},{3,5},{4,6},{5,7},{6,0},{7,1},{8,10},{9,11},{10,... | collective-permute-start | bytes 221192 | tf_op jit(solution)/shard_map/ppermute | solution.py:481
  115.9 9.7 %collective-permute-start.21 = (f32[144,128]{1,0:T(8,128)S(1)}, f32[144,128]{1,0:T(8,128)S(1)}, u32[]{:S(2)}, u32[]{:S(2)}) collective-permute-start(f32[144,128]{1,0:T(8,128)S(1)} %shard_map.46), channel_id=1, source_target_pairs={{0,4},{1,5},{2,6},{3,7},{4,0},{5,1},{6,2},{7,3},{8,12},{9,13},{10,... | collective-permute-start | bytes 221192 | tf_op jit(solution)/shard_map/ppermute | solution.py:481
  126.8 21.6 %all-to-all-start.1 = ((f32[16,144,128]{2,1,0:T(8,128)}), f32[16,144,128]{2,1,0:T(8,128)S(1)}, u32[]{:S(2)}, u32[]{:S(2)}) async-start(f32[16,144,128]{2,1,0:T(8,128)} %shard_map.48), calls=%async_computation.1 | async-start | bytes 2359296 | tf_op jit(solution)/shard_map/all_to_all | solution.py:554
  139.7 29.3 %collective-permute-start.24 = (f32[5,512,128]{2,1,0:T(8,128)}, f32[5,512,128]{2,1,0:T(8,128)}, u32[]{:S(2)}, u32[]{:S(2)}) collective-permute-start(f32[5,512,128]{2,1,0:T(8,128)} %get-tuple-element.103), channel_id=1, source_target_pairs={{0,2},{1,3},{2,4},{3,5},{4,6},{5,7},{6,0},{7,1},{8,10},{9,11},{10,... | collective-permute-start | bytes 3932168 | tf_op jit(solution)/shard_map/ppermute | solution.py:481
  140.7 28.3 %collective-permute-start.25 = (f32[5,512,128]{2,1,0:T(8,128)}, f32[5,512,128]{2,1,0:T(8,128)}, u32[]{:S(2)}, u32[]{:S(2)}) collective-permute-start(f32[5,512,128]{2,1,0:T(8,128)} %get-tuple-element.104), channel_id=1, source_target_pairs={{0,6},{1,7},{2,0},{3,1},{4,2},{5,3},{6,4},{7,5},{8,14},{9,15},{10,... | collective-permute-start | bytes 3932168 | tf_op jit(solution)/shard_map/ppermute | solution.py:481
  (53 other events, 885.3 us)

commit v10 on v9

--- a/solution.py
+++ b/solution.py
@@ -58,19 +58,18 @@
     return 2.0 * (total - 0.5 * own) / 1.5 - base
 
 
-def build_kernel(count, near_ref, at_ref, blocks_ref, vectors_ref, step_ref, op_ref, wide_ref, ring_ref, own_ref, sums_a, sums_b, left_a, left_b, sem, own_sem):
+def build_kernel(count, table_ref, at_ref, blocks_ref, vectors_ref, step_ref, op_ref, wide_ref, ring_ref, own_ref, sums_a, sums_b, left_a, left_b, near_ref, sem, own_sem, near_sem):
     def fetch(n):
         elem = lax.rem(n + REACH, count)
         return pltpu.make_async_copy(blocks_ref.at[elem], ring_ref.at[lax.rem(n, RING)], sem.at[lax.rem(n, RING)])
 
     first = (at_ref[1] * 4 + at_ref[0]) * count
     load = pltpu.make_async_copy(vectors_ref, own_ref, own_sem)
+    table = pltpu.make_async_copy(table_ref, near_ref, near_sem)
+    table.start()
     load.start()
-    for n in range(RING):
+    for n in range(2):
         fetch(n).start()
-    load.wait()
-    for r in range(count):
-        spread(wide_ref, REACH + r, own_ref[r])
 
     def combine(n, sums_ref, left_ref):
         elem = lax.rem(n + REACH, count)
@@ -116,9 +115,15 @@
         combine(n, sums_a, left_a)
         return 0
 
+    table.wait()
     fetch(0).wait()
+    for n in range(2, RING):
+        fetch(n).start()
     combine(0, sums_a, left_a)
     refill(0)
+    load.wait()
+    for r in range(count):
+        spread(wide_ref, REACH + r, own_ref[r])
     lax.fori_loop(0, (count - 2 * REACH) // 2, inner, 0)
     lax.fori_loop(count - 2 * REACH + 1, count, outer, 0)
 
@@ -214,7 +219,7 @@
     return call(
         functools.partial(build_kernel, count),
         (shaped(count - 2 * REACH, 256, 128), shaped(count, 512, SPAN * 256, dtype=BF16)),
-        [SMEM_SPEC, SMEM_SPEC, HBM_SPEC, HBM_SPEC],
+        [HBM_SPEC, SMEM_SPEC, HBM_SPEC, HBM_SPEC],
         [
             wide_scratch(count),
             pltpu.VMEM((RING, 7, 256, 256), F32),
@@ -223,7 +228,9 @@
             pltpu.VMEM((SPAN, 256, 256), F32),
             pltpu.VMEM((512, SPAN * 256), BF16),
             pltpu.VMEM((512, SPAN * 256), BF16),
+            pltpu.SMEM(near.shape, jnp.int32),
             pltpu.SemaphoreType.DMA((RING,)),
+            pltpu.SemaphoreType.DMA,
             pltpu.SemaphoreType.DMA,
         ],
         (near, here, blocks, own),
@@ -499,7 +506,7 @@
 
     start = vectors.reshape(elem_dev, basis, panel)
     halos = halos_of(start[:REACH], start[-REACH:])
-    mid, op = build_operator(neighbours.T, here, blocks, start)
+    mid, op = build_operator(pltpu.with_memory_space_constraint(neighbours.T, pltpu.HBM), here, blocks, pltpu.with_memory_space_constraint(start, pltpu.HBM))
     low, high = first_edges(op, start, halos)
     halos = halos_of(low, high)
     inner, other = second_inner(here, op, mid, low, high, start)

time: 183 us -> 181 us (0.989)
  local copies, waits for them, and re-layouts: 8.01 us -> 5.73 us
    unnamed x94 -> x90, local copies, waits for them, and re-layouts: 6.89 us -> 4.61 us
where the time goes in v10:
time: 181 us
  waiting for transfers between devices  69.1 us (38%)
  starting transfers between devices  56.6 us (31%)
  Pallas kernels  48.1 us (27%)
  local copies, waits for them, and re-layouts  5.73 us (3%)
    pallas_call x16, Pallas kernels, call(): pl.pallas_call(kernel, out_shape=outs, in_specs=specs, out_specs=kwargs.p...  48.1 us
    ppermute x19, waiting for transfers between devices, shift_z(): return lax.ppermute(x, 'band', [(i, (i + 2 * k) % 8) for i in range(8)])  32.7 us
    ppermute x19, starting transfers between devices, shift_z(): return lax.ppermute(x, 'band', [(i, (i + 2 * k) % 8) for i in range(8)])  24.9 us
    all_to_all x1, waiting for transfers between devices, steps(): lax.all_to_all(pieces, 'space', split_axis=0, concat_axis=0, tiled=True)  14.9 us
    ppermute x5, starting transfers between devices, swap_cores(): return lax.ppermute(x, 'band', [(i, i ^ 1) for i in range(8)])  14.8 us
    ppermute x2, waiting for transfers between devices, halos_of(): return (before, lax.ppermute(first, 'space', down))  6.12 us
    all_to_all x1, waiting for transfers between devices, steps(): lax.all_to_all(copies, 'space', split_axis=0, concat_axis=0, tiled=True)  6.11 us
    all_to_all x1, starting transfers between devices, steps(): lax.all_to_all(copies, 'space', split_axis=0, concat_axis=0, tiled=True)  5.53 us
  transfers between devices with their start and end apart: 30, of which 15 were waited for; matrix products, arithmetic and copies ran while one was open for 0% of the time, Pallas kernels for 15%

profile of v10, /device:TPU:1, one launch (start us, length us, event | category | flops | bytes accessed | tf_op | source)
XLA Modules:
  0.0 180.6 jit_solution(5254522661577468959)
XLA Ops:
  3.2 3.8 %collective-permute-start.1 = (f32[2,256,128]{2,1,0:T(8,128)S(1)}, f32[2,256,128]{2,1,0:T(8,128)S(1)}, u32[]{:S(2)}, u32[]{:S(2)}) collective-permute-start(f32[2,256,128]{2,1,0:T(8,128)S(1)} %bitcast.28), channel_id=1, source_target_pairs={{8,0},{16,8},{24,16},{32,24},{40,32},{48,40},{56,48},{64,56},{72,6... | collective-permute-start | bytes 786440 | tf_op jit(solution)/shard_map/ppermute | solution.py:496
  7.0 14.2 %shard_map.37 = (f32[12,256,128]{2,1,0:T(8,128)S(1)}, bf16[16,512,1280]{2,1,0:T(8,128)(2,1)S(1)}) custom-call(s32[7,16]{1,0:T(8,128)} %bitcast.30, s32[4]{0:T(128)S(1)} %pad_add_fusion.at_ref, f32[16,7,256,256]{3,2,1,0:T(8,128)} %blocks_ref.1, f32[16,256,128]{2,1,0:T(8,128)} %bitcast.22), custom_call_target="tpu_custom_call" | custom-call | tf_op jit(solution)/shard_map/pallas_call | solution.py:202
  23.0 5.6 %shard_map.39 = (f32[384,128]{1,0:T(8,128)S(1)}, f32[384,128]{1,0:T(8,128)S(1)}, f32[384,128]{1,0:T(8,128)S(1)}, f32[384,128]{1,0:T(8,128)S(1)}, f32[4,384,128]{2,1,0:T(8,128)S(1)}) custom-call(s32[4]{0:T(128)S(1)} %pad_add_fusion.at_ref, bf16[16,512,1280]{2,1,0:T(8,128)(2,1)S(1)} %get-tuple-element.58.op_ref, ...), custom_call_target="tpu_custom_call" | custom-call | tf_op jit(solution)/shard_map/pallas_call | solution.py:202
  31.4 6.1 %collective-permute-done.3.after_ref = f32[2,256,128]{2,1,0:T(8,128)S(1)} collective-permute-done((f32[2,256,128]{2,1,0:T(8,128)S(1)}, f32[2,256,128]{2,1,0:T(8,128)S(1)}, u32[]{:S(2)}, u32[]{:S(2)}) %collective-permute-start.3) | collective-permute-done | bytes 262176 | tf_op jit(solution)/shard_map/ppermute | solution.py:496
  37.5 4.7 %collective-permute-done.2.before_ref = f32[2,256,128]{2,1,0:T(8,128)S(1)} collective-permute-done((f32[2,256,128]{2,1,0:T(8,128)S(1)}, f32[2,256,128]{2,1,0:T(8,128)S(1)}, u32[]{:S(2)}, u32[]{:S(2)}) %collective-permute-start.2) | collective-permute-done | bytes 262176 | tf_op jit(solution)/shard_map/ppermute | solution.py:495
  51.7 3.1 %collective-permute-done.6.refs_0_.below_inner.refs_10_ = f32[384,128]{1,0:T(8,128)S(1)} collective-permute-done((f32[384,128]{1,0:T(8,128)S(1)}, f32[384,128]{1,0:T(8,128)S(1)}, u32[]{:S(2)}, u32[]{:S(2)}) %collective-permute-start.6) | collective-permute-done | bytes 196640 | tf_op jit(solution)/shard_map/ppermute | solution.py:488
  56.0 4.8 %collective-permute-start.14 = (f32[384,128]{1,0:T(8,128)S(1)}, f32[384,128]{1,0:T(8,128)S(1)}, u32[]{:S(2)}, u32[]{:S(2)}) collective-permute-start(f32[384,128]{1,0:T(8,128)S(1)} %get-tuple-element.113), channel_id=1, source_target_pairs={{0,6},{1,7},{2,0},{3,1},{4,2},{5,3},{6,4},{7,5},{8,14},{9,15},{10,... | collective-permute-start | bytes 589832 | tf_op jit(solution)/shard_map/ppermute | solution.py:488
  61.5 2.7 %collective-permute-start.10 = (f32[128,128]{1,0:T(8,128)S(1)}, f32[128,128]{1,0:T(8,128)S(1)}, u32[]{:S(2)}, u32[]{:S(2)}) collective-permute-start(f32[128,128]{1,0:T(8,128)S(1)} %get-tuple-element.90.refs_6_.edge_ref), channel_id=1, source_target_pairs={{0,4},{1,5},{2,6},{3,7},{4,0},{5,1},{6,2},{7,3},{8,12},{9,13},{10,... | collective-permute-start | bytes 196616 | tf_op jit(solution)/shard_map/ppermute | solution.py:488
  65.9 6.0 %collective-permute-done.10.refs_1_.refs_14_ = f32[128,128]{1,0:T(8,128)S(1)} collective-permute-done((f32[128,128]{1,0:T(8,128)S(1)}, f32[128,128]{1,0:T(8,128)S(1)}, u32[]{:S(2)}, u32[]{:S(2)}) %collective-permute-start.10) | collective-permute-done | bytes 65568 | tf_op jit(solution)/shard_map/ppermute | solution.py:488
  72.1 4.6 %collective-permute-done.16.refs_4_.refs_20_ = f32[128,128]{1,0:T(8,128)S(1)} collective-permute-done((f32[128,128]{1,0:T(8,128)S(1)}, f32[128,128]{1,0:T(8,128)S(1)}, u32[]{:S(2)}, u32[]{:S(2)}) %collective-permute-start.16) | collective-permute-done | bytes 65568 | tf_op jit(solution)/shard_map/ppermute | solution.py:488
  77.1 3.0 %shard_map.42 = (f32[18,128,128]{2,1,0:T(8,128)S(1)}, f32[18,128,128]{2,1,0:T(8,128)S(1)}) custom-call(s32[4]{0:T(128)S(1)} %pad_add_fusion.at_ref, f32[384,128]{1,0:T(8,128)S(1)} %get-tuple-element.84.refs_0_.mine_ref, f32[4,384,128]{2,1,0:T(8,128)S(1)} %collective-permute-done.4.refs_8_.got_ref.inner_got, ...), custom_call_target="tpu_custom_call" | custom-call | tf_op jit(solution)/shard_map/pallas_call | solution.py:202
  81.5 4.7 %collective-permute-start.20 = (f32[18,128,128]{2,1,0:T(8,128)S(1)}, f32[18,128,128]{2,1,0:T(8,128)S(1)}, u32[]{:S(2)}, u32[]{:S(2)}) collective-permute-start(f32[18,128,128]{2,1,0:T(8,128)S(1)} %get-tuple-element.100), channel_id=1, source_target_pairs={{0,1},{1,0},{2,3},{3,2},{4,5},{5,4},{6,7},{7,6},{8,9},{9,8},{10,11... | collective-permute-start | bytes 3538952 | tf_op jit(solution)/shard_map/ppermute | solution.py:484
  89.8 3.8 %all-to-all-start = ((f32[16,144,128]{2,1,0:T(8,128)}), f32[16,144,128]{2,1,0:T(8,128)S(1)}, u32[]{:S(2)}, u32[]{:S(2)}) async-start(f32[16,144,128]{2,1,0:T(8,128)} %bitcast.14), calls=%async_computation | async-start | bytes 2359296 | tf_op jit(solution)/shard_map/all_to_all | solution.py:548
  95.2 2.7 %collective-permute-start.19 = (f32[2,2,512,128]{3,2,1,0:T(8,128)}, f32[2,2,512,128]{3,2,1,0:T(8,128)}, u32[]{:S(2)}, u32[]{:S(2)}) collective-permute-start(f32[2,2,512,128]{3,2,1,0:T(8,128)} %get-tuple-element.95), channel_id=1, source_target_pairs={{0,6},{1,7},{2,0},{3,1},{4,2},{5,3},{6,4},{7,5},{8,14},{9,15},{10,... | collective-permute-start | bytes 3145736 | tf_op jit(solution)/shard_map/ppermute | solution.py:488
  97.8 14.9 %all-to-all-done.parts_ref = f32[16,144,128]{2,1,0:T(8,128)S(1)} async-done(((f32[16,144,128]{2,1,0:T(8,128)}), f32[16,144,128]{2,1,0:T(8,128)S(1)}, u32[]{:S(2)}, u32[]{:S(2)}) %all-to-all-start) | async-done | bytes 1179680 | tf_op jit(solution)/shard_map/all_to_all | solution.py:548
  115.4 6.7 %collective-permute-done.23 = f32[144,128]{1,0:T(8,128)S(1)} collective-permute-done((f32[144,128]{1,0:T(8,128)S(1)}, f32[144,128]{1,0:T(8,128)S(1)}, u32[]{:S(2)}, u32[]{:S(2)}) %collective-permute-start.23) | collective-permute-done | bytes 73760 | tf_op jit(solution)/shard_map/ppermute | solution.py:488
  125.3 5.5 %all-to-all-start.1 = ((f32[16,144,128]{2,1,0:T(8,128)}), f32[16,144,128]{2,1,0:T(8,128)S(1)}, u32[]{:S(2)}, u32[]{:S(2)}) async-start(f32[16,144,128]{2,1,0:T(8,128)} %shard_map.48), calls=%async_computation.1 | async-start | bytes 2359296 | tf_op jit(solution)/shard_map/all_to_all | solution.py:561
  135.3 2.8 %shard_map.47 = (f32[5,512,128]{2,1,0:T(8,128)}, f32[5,512,128]{2,1,0:T(8,128)}) custom-call(f32[2,2,512,128]{3,2,1,0:T(8,128)S(1)} %collective-permute-done.18.below_ref.refs_22_, f32[2,2,512,128]{3,2,1,0:T(8,128)} %collective-permute-done.19.above_ref.refs_23_, f32[384,128]{1,0:T(8,128)S(1)} %copy-done.5, f32[128,128]{1,0:T(8,128)S(1)} %copy-done.23, ...), custom_call_target="tpu_custom_call" | custom-call | tf_op jit(solution)/shard_map/pallas_call | solution.py:202
  140.8 6.1 %all-to-all-done.1 = f32[16,144,128]{2,1,0:T(8,128)S(1)} async-done(((f32[16,144,128]{2,1,0:T(8,128)}), f32[16,144,128]{2,1,0:T(8,128)S(1)}, u32[]{:S(2)}, u32[]{:S(2)}) %all-to-all-start.1) | async-done | bytes 1179680 | tf_op jit(solution)/shard_map/all_to_all | solution.py:561
  147.0 4.3 %collective-permute-start.26 = (f32[18,128,128]{2,1,0:T(8,128)S(1)}, f32[18,128,128]{2,1,0:T(8,128)S(1)}, u32[]{:S(2)}, u32[]{:S(2)}) collective-permute-start(f32[18,128,128]{2,1,0:T(8,128)S(1)} %bitcast.26), channel_id=1, source_target_pairs={{0,1},{1,0},{2,3},{3,2},{4,5},{5,4},{6,7},{7,6},{8,9},{9,8},{10,11... | collective-permute-start | bytes 3538952 | tf_op jit(solution)/shard_map/ppermute | solution.py:484
  153.8 3.7 %shard_map.49 = (bf16[1024,256]{1,0:T(8,128)(2,1)S(1)}, bf16[1024,256]{1,0:T(8,128)(2,1)S(1)}, f32[8,128]{1,0:T(8,128)S(1)}) custom-call(s32[4]{0:T(128)S(1)} %pad_add_fusion.at_ref, f32[18,128,128]{2,1,0:T(8,128)S(1)} %bitcast.27, f32[18,128,128]{2,1,0:T(8,128)S(1)} %collective-permute-done.26.theirs_ref), custom_call_target="tpu_custom_call" | custom-call | tf_op jit(solution)/shard_map/pallas_call | solution.py:202
  157.6 9.8 %collective-permute-done.24.refs_24_ = f32[5,512,128]{2,1,0:T(8,128)} collective-permute-done((f32[5,512,128]{2,1,0:T(8,128)}, f32[5,512,128]{2,1,0:T(8,128)}, u32[]{:S(2)}, u32[]{:S(2)}) %collective-permute-start.24) | collective-permute-done | bytes 1310752 | tf_op jit(solution)/shard_map/ppermute | solution.py:488
  167.6 5.5 %shard_map.50 = (f32[4,512,128]{2,1,0:T(8,128)S(1)}, f32[4,512,128]{2,1,0:T(8,128)S(1)}) custom-call(f32[384,128]{1,0:T(8,128)S(1)} %get-tuple-element.84.refs_0_.mine_ref, f32[384,128]{1,0:T(8,128)S(1)} %copy-done.11, f32[384,128]{1,0:T(8,128)S(1)} %copy-done.3, f32[384,128]{1,0:T(8,128)S(1)} %copy-done.13, f32[128,128]{1,0:T(8,128)S(1)} %copy-done.30, ...), custom_call_target="tpu_custom_call" | custom-call | tf_op jit(solution)/shard_map/pallas_call | solution.py:202
  173.1 3.5 %collective-permute-start.27 = (f32[4,512,128]{2,1,0:T(8,128)S(1)}, f32[4,512,128]{2,1,0:T(8,128)S(1)}, u32[]{:S(2)}, u32[]{:S(2)}) collective-permute-start(f32[4,512,128]{2,1,0:T(8,128)S(1)} %get-tuple-element.109), channel_id=1, source_target_pairs={{0,1},{1,0},{2,3},{3,2},{4,5},{5,4},{6,7},{7,6},{8,9},{9,8},{10,11... | collective-permute-start | bytes 3145736 | tf_op jit(solution)/shard_map/ppermute | solution.py:484
  (147 shorter events, 46.8 us)
Async XLA Ops:
  1.1 20.2 %collective-permute-start = (f32[2,256,128]{2,1,0:T(8,128)S(1)}, f32[2,256,128]{2,1,0:T(8,128)S(1)}, u32[]{:S(2)}, u32[]{:S(2)}) collective-permute-start(f32[2,256,128]{2,1,0:T(8,128)S(1)} %bitcast.29), channel_id=1, source_target_pairs={{0,8},{8,16},{16,24},{24,32},{32,40},{40,48},{48,56},{56,64},{64,7... | collective-permute-start | bytes 786440 | tf_op jit(solution)/shard_map/ppermute | solution.py:495
  3.2 18.1 %collective-permute-start.1 = (f32[2,256,128]{2,1,0:T(8,128)S(1)}, f32[2,256,128]{2,1,0:T(8,128)S(1)}, u32[]{:S(2)}, u32[]{:S(2)}) collective-permute-start(f32[2,256,128]{2,1,0:T(8,128)S(1)} %bitcast.28), channel_id=1, source_target_pairs={{8,0},{16,8},{24,16},{32,24},{40,32},{48,40},{56,48},{64,56},{72,6... | collective-permute-start | bytes 786440 | tf_op jit(solution)/shard_map/ppermute | solution.py:496
  28.7 22.2 %collective-permute-start.4 = (f32[4,384,128]{2,1,0:T(8,128)S(1)}, f32[4,384,128]{2,1,0:T(8,128)S(1)}, u32[]{:S(2)}, u32[]{:S(2)}) collective-permute-start(f32[4,384,128]{2,1,0:T(8,128)S(1)} %get-tuple-element.70), channel_id=1, source_target_pairs={{0,1},{1,0},{2,3},{3,2},{4,5},{5,4},{6,7},{7,6},{8,9},{9,8},{10,11... | collective-permute-start | bytes 2359304 | tf_op jit(solution)/shard_map/ppermute | solution.py:484
  29.7 7.8 %collective-permute-start.3 = (f32[2,256,128]{2,1,0:T(8,128)S(1)}, f32[2,256,128]{2,1,0:T(8,128)S(1)}, u32[]{:S(2)}, u32[]{:S(2)}) collective-permute-start(f32[2,256,128]{2,1,0:T(8,128)S(1)} %get-tuple-element.60.low_ref), channel_id=1, source_target_pairs={{8,0},{16,8},{24,16},{32,24},{40,32},{48,40},{56,48},{64,56},{72,6... | collective-permute-start | bytes 786440 | tf_op jit(solution)/shard_map/ppermute | solution.py:496
  31.4 10.8 %collective-permute-start.2 = (f32[2,256,128]{2,1,0:T(8,128)S(1)}, f32[2,256,128]{2,1,0:T(8,128)S(1)}, u32[]{:S(2)}, u32[]{:S(2)}) collective-permute-start(f32[2,256,128]{2,1,0:T(8,128)S(1)} %get-tuple-element.61.high_ref), channel_id=1, source_target_pairs={{0,8},{8,16},{16,24},{24,32},{32,40},{40,48},{48,56},{56,64},{64,7... | collective-permute-start | bytes 786440 | tf_op jit(solution)/shard_map/ppermute | solution.py:495
  44.5 16.2 %collective-permute-start.5 = (f32[4,128,128]{2,1,0:T(8,128)S(1)}, f32[4,128,128]{2,1,0:T(8,128)S(1)}, u32[]{:S(2)}, u32[]{:S(2)}) collective-permute-start(f32[4,128,128]{2,1,0:T(8,128)S(1)} %get-tuple-element.71), channel_id=1, source_target_pairs={{0,1},{1,0},{2,3},{3,2},{4,5},{5,4},{6,7},{7,6},{8,9},{9,8},{10,11... | collective-permute-start | bytes 786440 | tf_op jit(solution)/shard_map/ppermute | solution.py:484
  45.8 8.9 %collective-permute-start.6 = (f32[384,128]{1,0:T(8,128)S(1)}, f32[384,128]{1,0:T(8,128)S(1)}, u32[]{:S(2)}, u32[]{:S(2)}) collective-permute-start(f32[384,128]{1,0:T(8,128)S(1)} %get-tuple-element.85.refs_1_), channel_id=1, source_target_pairs={{0,2},{1,3},{2,4},{3,5},{4,6},{5,7},{6,0},{7,1},{8,10},{9,11},{10,... | collective-permute-start | bytes 589832 | tf_op jit(solution)/shard_map/ppermute | solution.py:488
  47.5 8.5 %collective-permute-start.8 = (f32[384,128]{1,0:T(8,128)S(1)}, f32[384,128]{1,0:T(8,128)S(1)}, u32[]{:S(2)}, u32[]{:S(2)}) collective-permute-start(f32[384,128]{1,0:T(8,128)S(1)} %get-tuple-element.87.refs_3_), channel_id=1, source_target_pairs={{0,6},{1,7},{2,0},{3,1},{4,2},{5,3},{6,4},{7,5},{8,14},{9,15},{10,... | collective-permute-start | bytes 589832 | tf_op jit(solution)/shard_map/ppermute | solution.py:488
  49.6 11.2 %collective-permute-start.7 = (f32[384,128]{1,0:T(8,128)S(1)}, f32[384,128]{1,0:T(8,128)S(1)}, u32[]{:S(2)}, u32[]{:S(2)}) collective-permute-start(f32[384,128]{1,0:T(8,128)S(1)} %get-tuple-element.86.refs_2_.inner_ref), channel_id=1, source_target_pairs={{0,4},{1,5},{2,6},{3,7},{4,0},{5,1},{6,2},{7,3},{8,12},{9,13},{10,... | collective-permute-start | bytes 589832 | tf_op jit(solution)/shard_map/ppermute | solution.py:488
  50.9 10.6 %collective-permute-start.9 = (f32[128,128]{1,0:T(8,128)S(1)}, f32[128,128]{1,0:T(8,128)S(1)}, u32[]{:S(2)}, u32[]{:S(2)}) collective-permute-start(f32[128,128]{1,0:T(8,128)S(1)} %get-tuple-element.89.refs_5_), channel_id=1, source_target_pairs={{0,2},{1,3},{2,4},{3,5},{4,6},{5,7},{6,0},{7,1},{8,10},{9,11},{10,... | collective-permute-start | bytes 196616 | tf_op jit(solution)/shard_map/ppermute | solution.py:488
  54.8 9.4 %collective-permute-start.11 = (f32[128,128]{1,0:T(8,128)S(1)}, f32[128,128]{1,0:T(8,128)S(1)}, u32[]{:S(2)}, u32[]{:S(2)}) collective-permute-start(f32[128,128]{1,0:T(8,128)S(1)} %get-tuple-element.91.refs_7_), channel_id=1, source_target_pairs={{0,6},{1,7},{2,0},{3,1},{4,2},{5,3},{6,4},{7,5},{8,14},{9,15},{10,... | collective-permute-start | bytes 196616 | tf_op jit(solution)/shard_map/ppermute | solution.py:488
  56.0 21.1 %collective-permute-start.14 = (f32[384,128]{1,0:T(8,128)S(1)}, f32[384,128]{1,0:T(8,128)S(1)}, u32[]{:S(2)}, u32[]{:S(2)}) collective-permute-start(f32[384,128]{1,0:T(8,128)S(1)} %get-tuple-element.113), channel_id=1, source_target_pairs={{0,6},{1,7},{2,0},{3,1},{4,2},{5,3},{6,4},{7,5},{8,14},{9,15},{10,... | collective-permute-start | bytes 589832 | tf_op jit(solution)/shard_map/ppermute | solution.py:488
  60.8 16.3 %collective-permute-start.13 = (f32[384,128]{1,0:T(8,128)S(1)}, f32[384,128]{1,0:T(8,128)S(1)}, u32[]{:S(2)}, u32[]{:S(2)}) collective-permute-start(f32[384,128]{1,0:T(8,128)S(1)} %get-tuple-element.114), channel_id=1, source_target_pairs={{0,4},{1,5},{2,6},{3,7},{4,0},{5,1},{6,2},{7,3},{8,12},{9,13},{10,... | collective-permute-start | bytes 589832 | tf_op jit(solution)/shard_map/ppermute | solution.py:488
  60.8 16.3 %collective-permute-start.12 = (f32[384,128]{1,0:T(8,128)S(1)}, f32[384,128]{1,0:T(8,128)S(1)}, u32[]{:S(2)}, u32[]{:S(2)}) collective-permute-start(f32[384,128]{1,0:T(8,128)S(1)} %get-tuple-element.115), channel_id=1, source_target_pairs={{0,2},{1,3},{2,4},{3,5},{4,6},{5,7},{6,0},{7,1},{8,10},{9,11},{10,... | collective-permute-start | bytes 589832 | tf_op jit(solution)/shard_map/ppermute | solution.py:488
  61.5 10.5 %collective-permute-start.10 = (f32[128,128]{1,0:T(8,128)S(1)}, f32[128,128]{1,0:T(8,128)S(1)}, u32[]{:S(2)}, u32[]{:S(2)}) collective-permute-start(f32[128,128]{1,0:T(8,128)S(1)} %get-tuple-element.90.refs_6_.edge_ref), channel_id=1, source_target_pairs={{0,4},{1,5},{2,6},{3,7},{4,0},{5,1},{6,2},{7,3},{8,12},{9,13},{10,... | collective-permute-start | bytes 196616 | tf_op jit(solution)/shard_map/ppermute | solution.py:488
  89.8 22.9 %all-to-all-start = ((f32[16,144,128]{2,1,0:T(8,128)}), f32[16,144,128]{2,1,0:T(8,128)S(1)}, u32[]{:S(2)}, u32[]{:S(2)}) async-start(f32[16,144,128]{2,1,0:T(8,128)} %bitcast.14), calls=%async_computation | async-start | bytes 2359296 | tf_op jit(solution)/shard_map/all_to_all | solution.py:548
  95.2 29.0 %collective-permute-start.18 = (f32[2,2,512,128]{3,2,1,0:T(8,128)}, f32[2,2,512,128]{3,2,1,0:T(8,128)S(1)}, u32[]{:S(2)}, u32[]{:S(2)}) collective-permute-start(f32[2,2,512,128]{3,2,1,0:T(8,128)} %get-tuple-element.94), channel_id=1, source_target_pairs={{0,2},{1,3},{2,4},{3,5},{4,6},{5,7},{6,0},{7,1},{8,10},{9,11},{10,... | collective-permute-start | bytes 3145736 | tf_op jit(solution)/shard_map/ppermute | solution.py:488
  95.2 29.0 %collective-permute-start.19 = (f32[2,2,512,128]{3,2,1,0:T(8,128)}, f32[2,2,512,128]{3,2,1,0:T(8,128)}, u32[]{:S(2)}, u32[]{:S(2)}) collective-permute-start(f32[2,2,512,128]{3,2,1,0:T(8,128)} %get-tuple-element.95), channel_id=1, source_target_pairs={{0,6},{1,7},{2,0},{3,1},{4,2},{5,3},{6,4},{7,5},{8,14},{9,15},{10,... | collective-permute-start | bytes 3145736 | tf_op jit(solution)/shard_map/ppermute | solution.py:488
  112.8 9.3 %collective-permute-start.23 = (f32[144,128]{1,0:T(8,128)S(1)}, f32[144,128]{1,0:T(8,128)S(1)}, u32[]{:S(2)}, u32[]{:S(2)}) collective-permute-start(f32[144,128]{1,0:T(8,128)S(1)} %shard_map.46), channel_id=1, source_target_pairs={{0,6},{1,7},{2,0},{3,1},{4,2},{5,3},{6,4},{7,5},{8,14},{9,15},{10,... | collective-permute-start | bytes 221192 | tf_op jit(solution)/shard_map/ppermute | solution.py:488
  113.2 10.9 %collective-permute-start.22 = (f32[144,128]{1,0:T(8,128)S(1)}, f32[144,128]{1,0:T(8,128)S(1)}, u32[]{:S(2)}, u32[]{:S(2)}) collective-permute-start(f32[144,128]{1,0:T(8,128)S(1)} %shard_map.46), channel_id=1, source_target_pairs={{0,2},{1,3},{2,4},{3,5},{4,6},{5,7},{6,0},{7,1},{8,10},{9,11},{10,... | collective-permute-start | bytes 221192 | tf_op jit(solution)/shard_map/ppermute | solution.py:488
  114.4 9.7 %collective-permute-start.21 = (f32[144,128]{1,0:T(8,128)S(1)}, f32[144,128]{1,0:T(8,128)S(1)}, u32[]{:S(2)}, u32[]{:S(2)}) collective-permute-start(f32[144,128]{1,0:T(8,128)S(1)} %shard_map.46), channel_id=1, source_target_pairs={{0,4},{1,5},{2,6},{3,7},{4,0},{5,1},{6,2},{7,3},{8,12},{9,13},{10,... | collective-permute-start | bytes 221192 | tf_op jit(solution)/shard_map/ppermute | solution.py:488
  125.3 21.6 %all-to-all-start.1 = ((f32[16,144,128]{2,1,0:T(8,128)}), f32[16,144,128]{2,1,0:T(8,128)S(1)}, u32[]{:S(2)}, u32[]{:S(2)}) async-start(f32[16,144,128]{2,1,0:T(8,128)} %shard_map.48), calls=%async_computation.1 | async-start | bytes 2359296 | tf_op jit(solution)/shard_map/all_to_all | solution.py:561
  138.1 29.3 %collective-permute-start.24 = (f32[5,512,128]{2,1,0:T(8,128)}, f32[5,512,128]{2,1,0:T(8,128)}, u32[]{:S(2)}, u32[]{:S(2)}) collective-permute-start(f32[5,512,128]{2,1,0:T(8,128)} %get-tuple-element.103), channel_id=1, source_target_pairs={{0,2},{1,3},{2,4},{3,5},{4,6},{5,7},{6,0},{7,1},{8,10},{9,11},{10,... | collective-permute-start | bytes 3932168 | tf_op jit(solution)/shard_map/ppermute | solution.py:488
  139.1 28.3 %collective-permute-start.25 = (f32[5,512,128]{2,1,0:T(8,128)}, f32[5,512,128]{2,1,0:T(8,128)}, u32[]{:S(2)}, u32[]{:S(2)}) collective-permute-start(f32[5,512,128]{2,1,0:T(8,128)} %get-tuple-element.104), channel_id=1, source_target_pairs={{0,6},{1,7},{2,0},{3,1},{4,2},{5,3},{6,4},{7,5},{8,14},{9,15},{10,... | collective-permute-start | bytes 3932168 | tf_op jit(solution)/shard_map/ppermute | solution.py:488
  (51 other events, 883.6 us)
